TPU v7x, 32 devices: a whole 2x2x4 slice. The times are simulated.
32 devices in a mesh: dp: 8 (over y, x, core), mp: 4 (over z).
Axes of the slice: x: 2, y: 2, z: 4, core: 2. Of those that a mesh axis runs over, the one named last changes fastest.
Arguments:
- tokens: bfloat16 [16, 512, 768], P('dp'), may hold values from -6 to 6
- lengths: int32 [16], P('dp'), may hold values from 40 to 512, as said below
- coords: int32 [16, 2, 512], P('dp'), may hold values from 0 to 999
- w_qkv: bfloat16 [3, 768, 768], P(None, None, 'mp'), may hold values from -0.375 to 0.375
- w_pos: bfloat16 [2, 768, 768], P(None, None, 'mp'), may hold values from -0.375 to 0.375
- w_out: bfloat16 [768, 768], P('mp'), may hold values from -0.875 to 0.875
- b_out: float32 [768], replicated, may hold values from -3 to 3
- gain_one: float32 [768], replicated, may hold values from 0.5 to 1.5
- shift_one: float32 [768], replicated, may hold values from -3 to 3
- w_in: bfloat16 [768, 3072], P(None, 'mp'), may hold values from -0.21875 to 0.21875
- b_in: float32 [3072], P('mp'), may hold values from -3 to 3
- w_back: bfloat16 [3072, 768], P('mp'), may hold values from -0.109375 to 0.109375
- b_back: float32 [768], replicated, may hold values from -3 to 3
- gain_two: float32 [768], replicated, may hold values from 0.5 to 1.5
- shift_two: float32 [768], replicated, may hold values from -3 to 3
- cotangent: bfloat16 [16, 512, 768], P('dp'), may hold values from -6 to 6
Outputs:
- layer_out: bfloat16 [16, 512, 768], P('dp')
- grad_tokens: float32 [16, 512, 768], P('dp')
- grad_w_qkv: float32 [3, 768, 768], P(None, None, 'mp')
- grad_w_pos: float32 [2, 768, 768], P(None, None, 'mp')
- grad_w_out: float32 [768, 768], P('mp')
- grad_b_out: float32 [768], replicated
- grad_gain_one: float32 [768], replicated
- grad_shift_one: float32 [768], replicated
- grad_w_in: float32 [768, 3072], P(None, 'mp')
- grad_b_in: float32 [3072], P('mp')
- grad_w_back: float32 [3072, 768], P('mp')
- grad_b_back: float32 [768], replicated
- grad_gain_two: float32 [768], replicated
- grad_shift_two: float32 [768], replicated
Inputs may be any that keep to these rules, and one draw needn't show every extreme that they name: `lengths`: in every draw some page has all 512 tokens real.
All inputs are finite; a program needn't handle non-finite values.
Results may differ from a plain program's by a relative error of at most 0.015.
Values sent between devices are 32-bit elements; how exact they have to be, the bound alone decides.
No kernel may reach another device: no remote copies, remote signals or barrier semaphores. Data moves between devices by JAX's collectives and lax.ppermute only.
A program may use at most 128 MiB of HBM per device.

v0:
```python
from functools import partial
import math

import jax
import jax.numpy as jnp
from jax import lax
from jax.sharding import PartitionSpec as P

HEAD_DIM = 64


def sinusoid(coords, model_width):
    quarter = model_width // 4
    frequency = jnp.exp(jnp.arange(quarter, dtype=jnp.float32) * (-math.log(10000.0) / quarter))
    position = coords.astype(jnp.float32)
    phases = position[:, :, None] * frequency
    sin_cos = jnp.concatenate([jnp.sin(phases), jnp.cos(phases)], axis=2)
    return jnp.concatenate([sin_cos[0], sin_cos[1]], axis=1)


def layer_norm(values, norm_gain, norm_shift):
    center = values - jnp.mean(values, axis=-1, keepdims=True)
    spread = jnp.mean(center * center, axis=-1, keepdims=True)
    return center * lax.rsqrt(spread + 1e-05) * norm_gain + norm_shift


def exact_gelu(values):
    return jax.nn.gelu(values, approximate=False)


def page_scores(queries, key_rows, pos_query, pos_key, page_length):
    factor = 1.0 / math.sqrt(3.0 * queries.shape[2])
    scores = jnp.einsum("ihd,jhd->hij", queries, key_rows, preferred_element_type=jnp.float32)
    scores = scores + jnp.einsum(
        "ihd,jhd->hij", queries, pos_key, preferred_element_type=jnp.float32
    )
    scores = scores + jnp.einsum(
        "ihd,jhd->hij", pos_query, key_rows, preferred_element_type=jnp.float32
    )
    scores = scores * factor
    visible = jnp.arange(queries.shape[0]) < page_length
    return jnp.where(visible[None, None, :], scores, -1e30)


def attend_page(inputs):
    queries, key_rows, value_rows, pos_query, pos_key, page_length = inputs
    scores = page_scores(queries, key_rows, pos_query, pos_key, page_length)
    highest = jnp.max(scores, axis=2, keepdims=True)
    totals = jnp.sum(jnp.exp(scores - highest), axis=2, keepdims=True)
    log_total = highest + jnp.log(totals)
    weights = jnp.exp(scores - log_total).astype(jnp.bfloat16)
    mixed = jnp.einsum("hij,jhd->ihd", weights, value_rows, preferred_element_type=jnp.float32)
    return (mixed.astype(jnp.bfloat16), log_total)


def page_backward(inputs):
    queries, key_rows, value_rows, pos_query, pos_key, page_length, log_total, d_mixed = inputs
    factor = 1.0 / math.sqrt(3.0 * queries.shape[2])
    scores = page_scores(queries, key_rows, pos_query, pos_key, page_length)
    probs = jnp.exp(scores - log_total)
    weights = probs.astype(jnp.bfloat16)
    d_values = jnp.einsum("hij,ihd->jhd", weights, d_mixed, preferred_element_type=jnp.float32)
    d_probs = jnp.einsum("ihd,jhd->hij", d_mixed, value_rows, preferred_element_type=jnp.float32)
    d_scores = (probs * (d_probs - jnp.sum(d_probs * probs, axis=2, keepdims=True))).astype(
        jnp.bfloat16
    )
    by_key = jnp.einsum("hij,jhd->ihd", d_scores, key_rows, preferred_element_type=jnp.float32)
    by_pos_key = jnp.einsum("hij,jhd->ihd", d_scores, pos_key, preferred_element_type=jnp.float32)
    by_query = jnp.einsum("hij,ihd->jhd", d_scores, queries, preferred_element_type=jnp.float32)
    by_pos_query = jnp.einsum(
        "hij,ihd->jhd", d_scores, pos_query, preferred_element_type=jnp.float32
    )
    d_queries = ((by_key + by_pos_key) * factor).astype(jnp.bfloat16)
    d_pos_query = (by_key * factor).astype(jnp.bfloat16)
    d_keys = ((by_query + by_pos_query) * factor).astype(jnp.bfloat16)
    d_pos_key = (by_query * factor).astype(jnp.bfloat16)
    return (d_queries, d_keys, d_values.astype(jnp.bfloat16), d_pos_query, d_pos_key)


def forward(
    token_rows,
    position,
    lengths,
    w_qkv,
    w_pos,
    w_out,
    b_out,
    gain_one,
    shift_one,
    w_in,
    b_in,
    w_back,
    b_back,
    gain_two,
    shift_two,
):
    page_count = lengths.shape[0]
    page_len = token_rows.shape[0] // page_count
    heads_here = w_qkv.shape[2] // HEAD_DIM

    def split_heads(values):
        return values.astype(jnp.bfloat16).reshape(page_count, page_len, heads_here, HEAD_DIM)

    queries = split_heads(jnp.dot(token_rows, w_qkv[0], preferred_element_type=jnp.float32))
    key_rows = split_heads(jnp.dot(token_rows, w_qkv[1], preferred_element_type=jnp.float32))
    value_rows = split_heads(jnp.dot(token_rows, w_qkv[2], preferred_element_type=jnp.float32))
    pos_query = split_heads(jnp.dot(position, w_pos[0], preferred_element_type=jnp.float32))
    pos_key = split_heads(jnp.dot(position, w_pos[1], preferred_element_type=jnp.float32))
    mixed, log_total = lax.map(
        attend_page, (queries, key_rows, value_rows, pos_query, pos_key, lengths)
    )
    mixed = mixed.reshape(page_count * page_len, heads_here * HEAD_DIM)
    branch = lax.psum(jnp.dot(mixed, w_out, preferred_element_type=jnp.float32), "mp") + b_out
    first = token_rows.astype(jnp.float32) + branch
    normed = layer_norm(first, gain_one, shift_one)
    normed_low = normed.astype(jnp.bfloat16)
    hidden_pre = jnp.dot(normed_low, w_in, preferred_element_type=jnp.float32) + b_in
    hidden = exact_gelu(hidden_pre).astype(jnp.bfloat16)
    feed = lax.psum(jnp.dot(hidden, w_back, preferred_element_type=jnp.float32), "mp") + b_back
    second = normed + feed
    output = layer_norm(second, gain_two, shift_two)
    saved = (
        queries,
        key_rows,
        value_rows,
        pos_query,
        pos_key,
        mixed,
        log_total,
        first,
        normed,
        normed_low,
        hidden_pre,
        hidden,
        second,
    )
    return (output, saved)


def body(
    tokens,
    lengths,
    coords,
    w_qkv,
    w_pos,
    w_out,
    b_out,
    gain_one,
    shift_one,
    w_in,
    b_in,
    w_back,
    b_back,
    gain_two,
    shift_two,
    cotangent,
):
    page_count, page_len, model_width = tokens.shape
    token_rows = tokens.reshape(page_count * page_len, model_width)
    position = jax.vmap(partial(sinusoid, model_width=model_width))(coords)
    position = position.astype(jnp.bfloat16).reshape(page_count * page_len, model_width)
    weights_all = (
        w_qkv,
        w_pos,
        w_out,
        b_out,
        gain_one,
        shift_one,
        w_in,
        b_in,
        w_back,
        b_back,
        gain_two,
        shift_two,
    )
    output, saved = forward(token_rows, position, lengths, *weights_all)
    unused_output, saved = forward(token_rows, position, lengths, *weights_all)
    (
        queries,
        key_rows,
        value_rows,
        pos_query,
        pos_key,
        mixed,
        log_total,
        first,
        normed,
        normed_low,
        hidden_pre,
        hidden,
        second,
    ) = saved
    heads_here = w_qkv.shape[2] // HEAD_DIM
    d_output = cotangent.reshape(page_count * page_len, model_width).astype(jnp.float32)
    unused_two, pull_two = jax.vjp(layer_norm, second, gain_two, shift_two)
    d_second, d_gain_two, d_shift_two = pull_two(d_output)
    d_feed = d_second.astype(jnp.bfloat16)
    d_b_back = jnp.sum(d_feed.astype(jnp.float32), axis=0)
    d_w_back = jnp.dot(hidden.T, d_feed, preferred_element_type=jnp.float32)
    d_hidden = jnp.dot(d_feed, w_back.T, preferred_element_type=jnp.float32)
    unused_gelu, pull_gelu = jax.vjp(exact_gelu, hidden_pre)
    d_pre = pull_gelu(d_hidden)[0].astype(jnp.bfloat16)
    d_b_in = jnp.sum(d_pre.astype(jnp.float32), axis=0)
    d_w_in = jnp.dot(normed_low.T, d_pre, preferred_element_type=jnp.float32)
    ffn_terms = (d_w_in, d_b_in, d_w_back, d_b_back, d_gain_two, d_shift_two)
    d_normed = d_second + lax.psum(jnp.dot(d_pre, w_in.T, preferred_element_type=jnp.float32), "mp")
    unused_one, pull_one = jax.vjp(layer_norm, first, gain_one, shift_one)
    d_first, d_gain_one, d_shift_one = pull_one(d_normed)
    d_branch = d_first.astype(jnp.bfloat16)
    d_b_out = jnp.sum(d_branch.astype(jnp.float32), axis=0)
    d_w_out = jnp.dot(mixed.T, d_branch, preferred_element_type=jnp.float32)
    d_mixed = jnp.dot(d_branch, w_out.T, preferred_element_type=jnp.float32).astype(jnp.bfloat16)
    d_mixed = d_mixed.reshape(page_count, page_len, heads_here, HEAD_DIM)
    head_grads = lax.map(
        page_backward,
        (queries, key_rows, value_rows, pos_query, pos_key, lengths, log_total, d_mixed),
    )
    flat_grads = [
        piece.reshape(page_count * page_len, heads_here * HEAD_DIM) for piece in head_grads
    ]
    d_queries, d_keys, d_values, d_pos_query, d_pos_key = flat_grads
    d_w_qkv = jnp.stack(
        [
            jnp.dot(token_rows.T, d_queries, preferred_element_type=jnp.float32),
            jnp.dot(token_rows.T, d_keys, preferred_element_type=jnp.float32),
            jnp.dot(token_rows.T, d_values, preferred_element_type=jnp.float32),
        ]
    )
    d_w_pos = jnp.stack(
        [
            jnp.dot(position.T, d_pos_query, preferred_element_type=jnp.float32),
            jnp.dot(position.T, d_pos_key, preferred_element_type=jnp.float32),
        ]
    )
    input_part = jnp.dot(d_queries, w_qkv[0].T, preferred_element_type=jnp.float32)
    input_part = input_part + jnp.dot(d_keys, w_qkv[1].T, preferred_element_type=jnp.float32)
    input_part = input_part + jnp.dot(d_values, w_qkv[2].T, preferred_element_type=jnp.float32)
    d_tokens = d_first + lax.psum(input_part, "mp")
    summed = lax.psum(
        (
            d_w_qkv,
            d_w_pos,
            d_w_out,
            d_b_out,
            d_gain_one,
            d_shift_one,
            d_w_in,
            d_b_in,
            d_w_back,
            d_b_back,
            d_gain_two,
            d_shift_two,
        ),
        "dp",
    )
    attn_terms = summed[:6]
    ffn_terms = summed[6:]
    sum_w_qkv, sum_w_pos, sum_w_out, sum_b_out, sum_gain_one, sum_shift_one = attn_terms
    sum_w_in, sum_b_in, sum_w_back, sum_b_back, sum_gain_two, sum_shift_two = ffn_terms
    layer_out = output.astype(jnp.bfloat16).reshape(page_count, page_len, model_width)
    grad_tokens = d_tokens.reshape(page_count, page_len, model_width)
    return (
        layer_out,
        grad_tokens,
        sum_w_qkv,
        sum_w_pos,
        sum_w_out,
        sum_b_out,
        sum_gain_one,
        sum_shift_one,
        sum_w_in,
        sum_b_in,
        sum_w_back,
        sum_b_back,
        sum_gain_two,
        sum_shift_two,
    )


def solution(mesh):
    placed = (
        P("dp", None, None),
        P("dp"),
        P("dp", None, None),
        P(None, None, "mp"),
        P(None, None, "mp"),
        P("mp", None),
        P(),
        P(),
        P(),
        P(None, "mp"),
        P("mp"),
        P("mp", None),
        P(),
        P(),
        P(),
        P("dp", None, None),
    )
    return jax.shard_map(
        body,
        mesh=mesh,
        in_specs=placed,
        out_specs=(
            P("dp", None, None),
            P("dp", None, None),
            P(None, None, "mp"),
            P(None, None, "mp"),
            P("mp", None),
            P(),
            P(),
            P(),
            P(None, "mp"),
            P("mp"),
            P("mp", None),
            P(),
            P(),
            P(),
        ),
        check_vma=False,
    )
```

profile of v0, /device:TPU:0, one launch (start us, length us, event | category | flops | bytes accessed | tf_op | source)
XLA Modules:
  0.0 978.8 jit_solution(5172779278769250379)
XLA Ops:
  8.0 8.2 multiply_sine_fusion
  17.3 1.4 convolution_convert_fusion.1
  18.7 1.4 convolution_convert_fusion.2
  21.5 1.4 convolution_convert_fusion.3
  22.9 1.3 reshape.241
  24.3 1.3 reshape.240
  26.3 1.3 reshape.239
  27.6 9.5 while.41
  38.4 3.3 fusion.207
  41.7 10.7 %all-reduce.12.cloned.1.call-start = ((), (), s32[]{:S(2)}) async-start(), calls=%async_computation.1 | async-start | bytes 6291456 | tf_op jit(solution)/shard_map/psum | solution.py:119
  52.4 113.2 %all-reduce.10.cloned.1.call-done = f32[1024,768]{1,0:T(8,128)} async-done(((f32[1024,768]{1,0:T(8,128)}), f32[1024,768]{1,0:T(8,128)}) %all-reduce.10.cloned.1.call-update) | async-done | bytes 3145744 | tf_op jit(solution)/shard_map/psum | solution.py:113
  165.6 2.8 fusion.199
  170.0 9.7 multiply_convert_fusion.3
  180.9 3.0 fusion.208
  184.0 9.5 while.40
  194.0 3.3 fusion.206
  197.3 106.9 %all-reduce.12.cloned.1.call-done = f32[1024,768]{1,0:T(8,128)} async-done(((f32[1024,768]{1,0:T(8,128)}), f32[1024,768]{1,0:T(8,128)}) %all-reduce.12.cloned.1.call-update) | async-done | bytes 3145744 | tf_op jit(solution)/shard_map/psum | solution.py:119
  304.2 3.8 fusion.197
  309.5 1.8 fusion.120
  311.3 1.5 fusion.196
  312.8 1.6 copy-done.6
  316.2 2.8 convert_reduce_fusion.2
  320.2 3.1 fusion.209
  323.7 221.9 %all-reduce.18.cloned.1.call-done = (f32[1024,768]{1,0:T(8,128)}, f32[1024,768]{1,0:T(8,128)}) async-done(((f32[1024,768]{1,0:T(8,128)}, f32[1024,768]{1,0:T(8,128)}), (f32[1024,768]{1,0:T(8,128)}, f32[1024,768]{1,0:T(8,128)})) %all-reduce.18.cloned.1.call-update) | async-done | bytes 6291472 | tf_op jit(solution)/shard_map/psum | solution.py:113
  545.6 5.3 multiply_reduce_fusion.1
  551.0 1.5 fusion.194
  552.5 1.6 copy-done.8
  562.9 18.8 %while.42 = (s32[]{:T(128)}, bf16[2,512,3,64]{1,3,2,0:T(8,128)(2,1)}, bf16[2,512,3,64]{1,3,2,0:T(8,128)(2,1)}, bf16[2,512,3,64]{1,3,2,0:T(8,128)(2,1)}, bf16[2,5...) while((s32[]{:T(128)}, ...), condition=%wide.region_27.28_spmd, body=%wide.region_25.27_spmd.sunk | while | flops 915700736 | bytes 57108952 | solution.py:214
  581.7 1.5 copy.80
  583.3 1.4 copy.79
  585.2 2.3 fusion.145
  587.6 2.3 fusion.148
  590.4 1.6 copy-done.7
  593.1 12.6 %fusion.141 = f32[1024,768]{1,0:T(8,128)} fusion(bf16[768,768]{1,0:T(8,128)(2,1)} %param.33, bf16[768,768]{1,0:T(8,128)(2,1)S(1)} %copy-done, f32[1024,768]{1,0:T(8,128)} %copy-done.7, f32[768]{0:T(1024)} %param.32, f32[768]{0:T(1024)} %param.30, f32[768]{0:T(1024)S(1)} %copy-done.43, f32[1024]{0:T(1024)} %add_rsqrt_fusion.1, f32[1024]{0:T(1024)} %copy-done.49), kind=kOutput, calls=%fused_computation.204 | convolution fusion | flops 2471755776 | bytes 8668160 | tf_op jit(solution)/shard_map/dot_general | solution.py:119
  605.7 5.2 add_add_fusion.2
  611.1 5.0 fusion.211
  616.1 3.3 fusion.203
  624.3 1.3 pad_maximum_fusion
  625.7 1.3 fusion.210
  627.1 1.3 copy-done.10
  628.7 26.0 %all-reduce = (f32[768]{0:T(1024)}, f32[768]{0:T(1024)}, f32[768]{0:T(1024)}, f32[768]{0:T(1024)}, f32[768]{0:T(1024)}, /*index=5*/f32[768]{0:T(1024)}, f32[768]{0:T(1024)}) all-reduce(f32[768]{0:T(1024)S(1)} %copy-done.56, f32[768]{0:T(1024)S(1)} %copy-done.51, f32[768]{0:T(1024)S(1)} %copy-done.52, ...), channel_id=1, replica_groups=mesh['dp'=8,'mp'=4] {'dp'}, use_global_device_ids=true, to_apply=%region_33.34 | all-reduce | flops 5376 | bytes 43008 | tf_op jit(solution)/shard_map/psum | solution.py:239
  654.8 178.5 %all-reduce.16.cloned.1.call-done = (f32[1024,768]{1,0:T(8,128)}, f32[1024,768]{1,0:T(8,128)}) async-done(((f32[1024,768]{1,0:T(8,128)}, f32[1024,768]{1,0:T(8,128)}), (f32[1024,768]{1,0:T(8,128)}, f32[1024,768]{1,0:T(8,128)})) %all-reduce.16.cloned.1.call-update) | async-done | bytes 6291472 | tf_op jit(solution)/shard_map/psum | solution.py:119
  833.3 6.9 fusion.193
  840.9 1.7 add_convert_fusion.1
  842.6 121.9 %all-reduce.14.cloned.1.call-done = (f32[3,768,192]{1,2,0:T(8,128)}, f32[2,768,192]{1,2,0:T(8,128)}, f32[192,768]{1,0:T(8,128)}, f32[768,768]{1,0:T(8,128)}, f32[768,768]{1,0:T(8,128)}) async-done(((f32[3,768,192]{1,2,0:T(8,128)}, f32[2,768,192]{1,2,0:T(8,128)}, f32[192,768]{1,0:T(8,128)}, f32[768,768]{1,0:T(8,128)}, f32[768,768]{1,0:T(8,128)}), (f32[3,768,192]{1,2,0:T(8,128)}, f32[2,768,192]{1,2,0:T(8,128)}, ...) | async-done | bytes 8257552 | tf_op jit(solution)/shard_map/psum | solution.py:239
  964.5 2.9 copy.151
  969.3 1.4 copy.154
  970.7 1.4 copy.155
  (309 shorter events, 69.2 us)
Async XLA Ops:
  7.2 162.8 %copy-start = (bf16[768,768]{1,0:T(8,128)(2,1)S(1)}, bf16[768,768]{1,0:T(8,128)(2,1)}, u32[]{:S(2)}) copy-start(bf16[768,768]{1,0:T(8,128)(2,1)} %param.31) | copy-start | bytes 3538948
  7.2 158.4 %all-reduce.10.cloned.1.call-start = ((), (), s32[]{:S(2)}) async-start(), calls=%async_computation | async-start | bytes 6291456 | tf_op jit(solution)/shard_map/psum | solution.py:113
  17.0 3.1 copy-start.36
  17.0 3.1 copy-start.38
  17.3 2.8 copy-start.4
  17.3 2.8 copy-start.34
  37.2 4.5 copy-start.41
  38.4 127.2 %copy-start.53 = (f32[768]{0:T(1024)S(1)}, f32[768]{0:T(1024)}, u32[]{:S(2)}) copy-start(f32[768]{0:T(1024)} %param.28) | copy-start | bytes 9220
  41.7 262.5 %all-reduce.12.cloned.1.call-start = ((), (), s32[]{:S(2)}) async-start(), calls=%async_computation.1 | async-start | bytes 6291456 | tf_op jit(solution)/shard_map/psum | solution.py:119
  168.5 11.2 %copy-start.1 = (f32[1024,768]{1,0:T(8,128)}, f32[1024,768]{1,0:T(8,128)S(1)}, u32[]{:S(2)}) copy-start(f32[1024,768]{1,0:T(8,128)S(1)} %get-tuple-element.355) | copy-start | bytes 9437188
  170.0 10.8 %copy-start.66 = (bf16[768,768]{1,0:T(8,128)(2,1)S(1)}, bf16[768,768]{1,0:T(8,128)(2,1)}, u32[]{:S(2)}) copy-start(bf16[768,768]{1,0:T(8,128)(2,1)} %param.33) | copy-start | bytes 3538948
  183.9 361.7 %all-reduce.18.cloned.1.call-start = ((), (), s32[]{:S(2)}) async-start(), calls=%async_computation.4 | async-start | bytes 12582912 | tf_op jit(solution)/shard_map/psum | solution.py:113
  193.9 110.3 %copy-start.61 = (f32[768]{0:T(1024)S(1)}, f32[768]{0:T(1024)}, u32[]{:S(2)}) copy-start(f32[768]{0:T(1024)} %param.34) | copy-start | bytes 9220
  311.2 4.1 copy-start.78
  312.7 2.6 copy-start.67
  312.8 2.6 copy-start.70
  312.8 3.5 copy-start.77
  315.3 3.7 copy-start.31
  323.2 510.1 %all-reduce.16.cloned.1.call-start = ((), (), s32[]{:S(2)}) async-start(), calls=%async_computation.3 | async-start | bytes 12582912 | tf_op jit(solution)/shard_map/psum | solution.py:119
  545.6 5.3 copy-start.46
  545.6 5.3 copy-start.2
  552.5 3.8 copy-start.33
  552.5 2.6 copy-start.47
  581.7 3.0 copy-start.22
  581.7 3.5 copy-start.35
  585.2 4.7 copy-start.15
  585.2 4.6 copy-start.5
  585.2 4.6 copy-start.17
  585.2 4.6 copy-start.54
  590.4 2.1 copy-start.49
  611.0 353.5 %all-reduce.14.cloned.1.call-start = ((), (), s32[]{:S(2)}) async-start(), calls=%async_computation.2 | async-start | bytes 16515072 | tf_op jit(solution)/shard_map/psum | solution.py:239
  611.0 5.1 copy-start.3
  611.0 5.1 copy-start.59
  611.1 5.0 copy-start.76
  616.1 3.3 copy-start.30
  616.1 3.8 copy-start.27
  623.9 1.8 copy-start.12
  623.9 1.8 copy-start.14
  627.0 1.7 copy-start.56
  627.0 206.3 %copy-start.48 = (f32[1024]{0:T(1024)S(1)}, f32[1024]{0:T(1024)}, u32[]{:S(2)}) copy-start(f32[1024]{0:T(1024)} %copy-done.47) | copy-start | bytes 12292
  627.0 206.3 %copy-start.50 = (f32[1024]{0:T(1024)S(1)}, f32[1024]{0:T(1024)}, u32[]{:S(2)}) copy-start(f32[1024]{0:T(1024)} %copy-done.49) | copy-start | bytes 12292
  627.0 206.3 %copy-start.60 = (f32[768]{0:T(1024)S(1)}, f32[768]{0:T(1024)}, u32[]{:S(2)}) copy-start(f32[768]{0:T(1024)} %param.30) | copy-start | bytes 9220
  627.1 206.3 %copy-start.62 = (f32[768]{0:T(1024)S(1)}, f32[768]{0:T(1024)}, u32[]{:S(2)}) copy-start(f32[768]{0:T(1024)} %param.34) | copy-start | bytes 9220
  627.1 206.2 %copy-start.63 = (f32[1024]{0:T(1024)S(1)}, f32[1024]{0:T(1024)}, u32[]{:S(2)}) copy-start(f32[1024]{0:T(1024)} %add_rsqrt_fusion.1) | copy-start | bytes 12292
  964.5 3.0 copy-start.32
  964.5 4.0 copy-start.40
  964.5 4.8 copy-start.19
  968.5 2.2 copy-start.18
  (48 other events, 64.0 us)
Sparse Core Ops, SparseCore 0:
  41.8 123.7 all-reduce.9
  184.0 120.1 all-reduce.11
  323.4 222.2 all-reduce.17
  611.1 222.1 all-reduce.15
  838.8 125.6 all-reduce.13
where the time goes:
time: 986 us; the launch traced here: 979 us
  waiting for transfers between devices  743 us (75%)
  matrix products  90.5 us (9%)
  other arithmetic  49.8 us (5%)
  local copies, waits for them, and re-layouts  43.2 us (4%)
  blocking collectives  26 us (3%)
  between operations  14.9 us (2%)
  starting transfers between devices  11.3 us (1%)
    psum x2, waiting for transfers between devices, forward(): lax.psum(jnp.dot(mixed, w_out, preferred_element_type=jnp.float32), 'mp')  335 us
    psum x2, waiting for transfers between devices, forward(): lax.psum(jnp.dot(hidden, w_back, preferred_element_type=jnp.float32), 'mp')  285 us
    psum x1, waiting for transfers between devices, body(): lax.psum((d_w_qkv, d_w_pos, d_w_out, d_b_out, d_gain_one, d_shift_one, d_...  122 us
    psum x1, blocking collectives, body(): lax.psum((d_w_qkv, d_w_pos, d_w_out, d_b_out, d_gain_one, d_shift_one, d_...  26 us
    unnamed x146, local copies, waits for them, and re-layouts  22.1 us
  transfers between devices with their start and end apart: 5, of which 5 were waited for; matrix products, arithmetic and copies ran while one was open for 4% of the time, Pallas kernels for 0%

commit v1 on v0

--- a/solution.py
+++ b/solution.py
@@ -174,7 +174,6 @@
         shift_two,
     )
     output, saved = forward(token_rows, position, lengths, *weights_all)
-    unused_output, saved = forward(token_rows, position, lengths, *weights_all)
     (
         queries,
         key_rows,

time: 986 us -> 768 us (0.78)
  waiting for transfers between devices: 743 us -> 567 us
  matrix products: 90.5 us -> 66.2 us
  starting transfers between devices: 11.3 us -> 0.84 us
    psum x2 -> x1, waiting for transfers between devices: 335 us -> 124 us  [forward(): lax.psum(jnp.dot(mixed, w_out, preferred_element_type=jnp.float32), 'mp')]
    psum x0 -> x2, waiting for transfers between devices: none -> 196 us  [the longest x1 120 us: body(): lax.psum(jnp.dot(d_pre, w_in.T, preferred_element_type=jnp.float32), 'mp')]
    psum x2 -> x1, waiting for transfers between devices: 285 us -> 120 us  [forward(): lax.psum(jnp.dot(hidden, w_back, preferred_element_type=jnp.float32), 'mp')]
    dot_general x2 -> x1, matrix products: 15.7 us -> 3.07 us  [forward(): jnp.dot(hidden, w_back, preferred_element_type=jnp.float32)]
    psum x2 -> x1, starting transfers between devices: 11.2 us -> 0.21 us  [forward(): lax.psum(jnp.dot(hidden, w_back, preferred_element_type=jnp.float32), 'mp')]
    unnamed x146 -> x115, local copies, waits for them, and re-layouts: 22.1 us -> 19.5 us
  transfers between devices with their start and end apart: 5 -> 5, of which waited for: 5 -> 5; matrix products, arithmetic and copies ran while one was open for 4% -> 3% of each run, Pallas kernels for 0% -> 0%
where the time goes in v1:
time: 768 us; the launch traced here: 760 us
  waiting for transfers between devices  567 us (74%)
  matrix products  66.2 us (9%)
  other arithmetic  44.3 us (6%)
  local copies, waits for them, and re-layouts  40.9 us (5%)
  blocking collectives  26.2 us (3%)
  between operations  14.9 us (2%)
    psum x1, waiting for transfers between devices, body(): lax.psum((d_w_qkv, d_w_pos, d_w_out, d_b_out, d_gain_one, d_shift_one, d_...  126 us
    psum x1, waiting for transfers between devices, forward(): lax.psum(jnp.dot(mixed, w_out, preferred_element_type=jnp.float32), 'mp')  124 us
    psum x1, waiting for transfers between devices, forward(): lax.psum(jnp.dot(hidden, w_back, preferred_element_type=jnp.float32), 'mp')  120 us
    psum x1, waiting for transfers between devices, body(): lax.psum(jnp.dot(d_pre, w_in.T, preferred_element_type=jnp.float32), 'mp')  120 us
    psum x1, waiting for transfers between devices, body(): d_tokens = d_first + lax.psum(input_part, 'mp')  76.3 us
    psum x1, blocking collectives, body(): lax.psum((d_w_qkv, d_w_pos, d_w_out, d_b_out, d_gain_one, d_shift_one, d_...  26.2 us
    unnamed x115, local copies, waits for them, and re-layouts  19.5 us
  transfers between devices with their start and end apart: 5, of which 5 were waited for; matrix products, arithmetic and copies ran while one was open for 3% of the time, Pallas kernels for 0%

profile of v1, /device:TPU:0, one launch (start us, length us, event | category | flops | bytes accessed | tf_op | source)
XLA Modules:
  0.0 760.3 jit_solution(17825696523205868860)
XLA Ops:
  7.8 2.9 convolution_convert_fusion.3
  10.7 2.1 convolution_convert_fusion.4
  12.9 1.6 convolution_convert_fusion.5
  14.5 8.2 %multiply_sine_fusion = (bf16[2,2,512,192]{3,2,1,0:T(8,128)(2,1)S(1)}, bf16[2,2,512,192]{3,2,1,0:T(8,128)(2,1)S(1)}) fusion(f32[192]{0:T(256)S(1)} %copy-done.47, f32[2,2,512]{2,1,0:T(2,128)S(1)} %convert_element_type.111), kind=kLoop, calls=%fused_computation.137 | loop fusion | flops 1179648 | bytes 1581824 | tf_op jit(solution)/shard_map/vmap()/sin | solution.py:17
  23.8 1.4 convolution_convert_fusion.1
  25.3 1.4 convolution_convert_fusion.2
  27.7 1.3 reshape.196
  29.0 1.3 reshape.195
  30.4 10.8 %while.30 = (s32[]{:T(128)}, bf16[2,512,3,64]{1,3,2,0:T(8,128)(2,1)S(1)}, f32[2,3,512,1]{2,1,3,0:T(4,128)S(1)}, bf16[2,512,3,64]{1,3,2,0:T(8,128)(2,1)S(1)}, s32...) while((s32[]{:T(128)}, ...), condition=%wide.region_3.4_spmd, body=%wide.region_0.3_spmd.sunk | while | flops 409828352 | bytes 23657600 | solution.py:109
  41.7 3.3 fusion.129
  45.2 123.7 %all-reduce.8.cloned.1.call-done = f32[1024,768]{1,0:T(8,128)} async-done(((f32[1024,768]{1,0:T(8,128)}), f32[1024,768]{1,0:T(8,128)}) %all-reduce.8.cloned.1.call-update) | async-done | bytes 3145744 | tf_op jit(solution)/shard_map/psum | solution.py:113
  168.9 2.8 fusion.123
  173.3 9.6 %multiply_convert_fusion.3 = (bf16[1024,768]{1,0:T(8,128)(2,1)S(1)}, f32[1024,768]{1,0:T(8,128)}, f32[1024,768]{1,0:T(8,128)}) fusion(f32[768]{0:T(1024)S(1)} %copy-done.51, bf16[768,768]{1,0:T(8,128)(2,1)S(1)} %copy-done, f32[1024,768]{1,0:T(8,128)S(1)} %get-tuple-element.272, f32[768]{0:T(1024)S(1)} %copy-done.44, f32[768]{0:T(1024)S(1)} %copy-done.32, ...), kind=kOutput, calls=%fused_computation.119 | convolution fusion | flops 1263796224 | bytes 12207104 | tf_op jit(solution)/shard_map/dot_general | solution.py:117
  184.1 3.1 fusion.130
  187.3 120.2 %all-reduce.10.cloned.1.call-done = f32[1024,768]{1,0:T(8,128)} async-done(((f32[1024,768]{1,0:T(8,128)}), f32[1024,768]{1,0:T(8,128)}) %all-reduce.10.cloned.1.call-update) | async-done | bytes 3145744 | tf_op jit(solution)/shard_map/psum | solution.py:119
  307.5 3.9 fusion.121
  312.7 1.8 fusion.92
  314.5 2.6 fusion.120
  317.2 1.7 copy-done.5
  320.5 2.8 convert_reduce_fusion.2
  324.5 3.1 fusion.131
  327.9 120.0 %all-reduce.12.cloned.1.call-done = f32[1024,768]{1,0:T(8,128)} async-done(((f32[1024,768]{1,0:T(8,128)}), f32[1024,768]{1,0:T(8,128)}) %all-reduce.12.cloned.1.call-update) | async-done | bytes 3145744 | tf_op jit(solution)/shard_map/psum | solution.py:205
  447.9 5.2 multiply_reduce_fusion.1
  453.1 2.8 fusion.119
  456.0 1.6 copy-done.4
  463.9 22.3 %while.31 = (s32[]{:T(128)}, bf16[2,512,3,64]{1,3,2,0:T(8,128)(2,1)}, bf16[2,512,3,64]{1,3,2,0:T(8,128)(2,1)}, bf16[2,512,3,64]{1,3,2,0:T(8,128)(2,1)}, bf16[2,5...) while((s32[]{:T(128)}, ...), condition=%wide.region_17.18_spmd, body=%wide.region_15.17_spmd.sunk | while | flops 915700736 | bytes 53913936 | solution.py:213
  463.9 1.3 dynamic_slice.183
  467.9 1.3 subtract_exponential_fusion.2
  469.1 1.3 fusion.227
  475.0 1.3 dynamic_slice.183
  479.0 1.3 subtract_exponential_fusion.2
  480.2 1.3 fusion.227
  486.2 1.5 copy.65
  487.7 1.4 copy.66
  489.1 1.4 copy.67
  491.9 2.3 add_add_fusion.2
  494.5 4.9 fusion.133
  499.4 3.3 fusion.126
  507.7 1.3 pad_maximum_fusion
  509.0 1.3 fusion.132
  510.4 1.3 copy-done.9
  512.0 26.2 %all-reduce = (f32[768]{0:T(1024)}, f32[768]{0:T(1024)}, f32[768]{0:T(1024)}, f32[768]{0:T(1024)}, f32[768]{0:T(1024)}, /*index=5*/f32[768]{0:T(1024)}, f32[768]{0:T(1024)}) all-reduce(f32[768]{0:T(1024)S(1)} %copy-done.38, f32[768]{0:T(1024)S(1)} %copy-done.35, f32[768]{0:T(1024)S(1)} %copy-done.36, ...), channel_id=1, replica_groups=mesh['dp'=8,'mp'=4] {'dp'}, use_global_device_ids=true, to_apply=%region_23.24 | all-reduce | flops 5376 | bytes 43008 | tf_op jit(solution)/shard_map/psum | solution.py:238
  538.2 76.3 %all-reduce.14.cloned.1.call-done = f32[1024,768]{1,0:T(8,128)} async-done(((f32[1024,768]{1,0:T(8,128)}), f32[1024,768]{1,0:T(8,128)}) %all-reduce.14.cloned.1.call-update) | async-done | bytes 3145744 | tf_op jit(solution)/shard_map/psum | solution.py:237
  614.5 4.9 add_add_fusion.5
  619.3 126.4 %all-reduce.16.cloned.1.call-done = (f32[3,768,192]{1,2,0:T(8,128)}, f32[2,768,192]{1,2,0:T(8,128)}, f32[192,768]{1,0:T(8,128)}, f32[768,768]{1,0:T(8,128)}, f32[768,768]{1,0:T(8,128)}) async-done(((f32[3,768,192]{1,2,0:T(8,128)}, f32[2,768,192]{1,2,0:T(8,128)}, f32[192,768]{1,0:T(8,128)}, f32[768,768]{1,0:T(8,128)}, f32[768,768]{1,0:T(8,128)}), (f32[3,768,192]{1,2,0:T(8,128)}, f32[2,768,192]{1,2,0:T(8,128)}, ...) | async-done | bytes 8257552 | tf_op jit(solution)/shard_map/psum | solution.py:238
  745.7 2.9 copy.127
  750.5 1.4 copy.130
  751.9 1.4 copy.131
  (225 shorter events, 50.6 us)
Async XLA Ops:
  7.2 166.1 %copy-start = (bf16[768,768]{1,0:T(8,128)(2,1)S(1)}, bf16[768,768]{1,0:T(8,128)(2,1)}, u32[]{:S(2)}) copy-start(bf16[768,768]{1,0:T(8,128)(2,1)} %param.29) | copy-start | bytes 3538948
  7.2 5.7 copy-start.6
  7.2 161.7 %all-reduce.8.cloned.1.call-start = ((), (), s32[]{:S(2)}) async-start(), calls=%async_computation | async-start | bytes 6291456 | tf_op jit(solution)/shard_map/psum | solution.py:113
  7.8 6.7 copy-start.41
  7.8 6.7 copy-start.47
  23.5 1.7 copy-start.24
  23.5 1.7 copy-start.26
  23.8 2.8 copy-start.29
  41.2 3.8 copy-start.31
  45.0 262.5 %all-reduce.10.cloned.1.call-start = ((), (), s32[]{:S(2)}) async-start(), calls=%async_computation.1 | async-start | bytes 6291456 | tf_op jit(solution)/shard_map/psum | solution.py:119
  171.7 11.2 %copy-start.2 = (f32[1024,768]{1,0:T(8,128)}, f32[1024,768]{1,0:T(8,128)S(1)}, u32[]{:S(2)}) copy-start(f32[1024,768]{1,0:T(8,128)S(1)} %get-tuple-element.272) | copy-start | bytes 9437188
  171.7 1.5 copy-start.32
  171.8 1.5 copy-start.44
  173.3 10.8 %copy-start.48 = (bf16[768,768]{1,0:T(8,128)(2,1)S(1)}, bf16[768,768]{1,0:T(8,128)(2,1)}, u32[]{:S(2)}) copy-start(bf16[768,768]{1,0:T(8,128)(2,1)} %param.31) | copy-start | bytes 3538948
  187.2 120.3 %copy-start.42 = (f32[768]{0:T(1024)S(1)}, f32[768]{0:T(1024)}, u32[]{:S(2)}) copy-start(f32[768]{0:T(1024)} %param.32) | copy-start | bytes 9220
  187.2 260.7 %all-reduce.12.cloned.1.call-start = ((), (), s32[]{:S(2)}) async-start(), calls=%async_computation.2 | async-start | bytes 6291456 | tf_op jit(solution)/shard_map/psum | solution.py:205
  311.9 2.7 copy-start.43
  314.5 5.2 copy-start.57
  317.1 1.7 copy-start.5
  317.1 2.6 copy-start.49
  317.1 2.6 copy-start.52
  317.1 3.4 copy-start.56
  319.8 3.6 copy-start.21
  327.6 125.5 %copy-start.34 = (f32[1024]{0:T(1024)S(1)}, f32[1024]{0:T(1024)}, u32[]{:S(2)}) copy-start(f32[1024]{0:T(1024)} %copy-done.33) | copy-start | bytes 12292
  327.6 286.8 %all-reduce.14.cloned.1.call-start = ((), (), s32[]{:S(2)}) async-start(), calls=%async_computation.3 | async-start | bytes 6291456 | tf_op jit(solution)/shard_map/psum | solution.py:237
  456.0 1.7 copy-start.4
  456.0 3.8 copy-start.30
  471.9 1.6 copy-start.19
  483.0 1.6 copy-start.19
  486.2 4.5 copy-start.23
  494.2 5.2 copy-start.45
  494.2 251.5 %all-reduce.16.cloned.1.call-start = ((), (), s32[]{:S(2)}) async-start(), calls=%async_computation.4 | async-start | bytes 16515072 | tf_op jit(solution)/shard_map/psum | solution.py:238
  494.5 4.9 copy-start.3
  494.5 4.9 copy-start.55
  499.4 3.8 copy-start.16
  504.6 1.6 copy-start.7
  507.2 1.8 copy-start.11
  510.3 1.7 copy-start.35
  510.3 1.7 copy-start.36
  510.3 1.7 copy-start.37
  510.3 1.7 copy-start.38
  510.3 1.7 copy-start.40
  510.3 1.7 copy-start.46
  745.7 3.0 copy-start.22
  745.7 4.0 copy-start.28
  745.7 4.8 copy-start.13
  749.7 2.2 copy-start.12
  750.5 2.8 copy-start.1
  (21 other events, 23.8 us)
Sparse Core Ops, SparseCore 0:
  45.1 123.7 all-reduce.7
  187.3 120.0 all-reduce.9
  327.8 120.0 all-reduce.11
  494.3 120.0 all-reduce.13
  619.9 125.7 all-reduce.15

commit v2 on v1

v2 whole, which is shorter than its diff:
```python
from functools import partial
import math

import jax
import jax.numpy as jnp
import numpy as np
from jax import lax
from jax.experimental import pallas as pl
from jax.experimental.pallas import tpu as pltpu
from jax.sharding import PartitionSpec as P

HEAD_DIM = 64
STEP = 32
NEAR = 1
FAR = 2
MASKED = -1e30


def mm(left, right):
    return jnp.dot(left, right, preferred_element_type=jnp.float32)


def mm_nt(left, right):
    return lax.dot_general(
        left, right, (((1,), (1,)), ((), ())), preferred_element_type=jnp.float32
    )


def mm_tn(left, right):
    return lax.dot_general(
        left, right, (((0,), (0,)), ((), ())), preferred_element_type=jnp.float32
    )


def angle_tables(model_width):
    quarter = model_width // 4
    rate = np.exp(np.arange(quarter) * (-math.log(10000.0) / quarter))
    fine = np.arange(STEP)[:, None] * rate
    coarse = fine * STEP
    zero = np.zeros((STEP, 2 * quarter))
    table = np.concatenate(
        [
            np.concatenate([np.sin(coarse), np.cos(coarse), zero], axis=1),
            np.concatenate([zero, np.sin(fine), np.cos(fine)], axis=1),
        ],
        axis=0,
    )
    parts = []
    rest = table
    for _ in range(3):
        part = rest.astype(jnp.bfloat16)
        parts.append(part)
        rest = rest - part.astype(np.float64)
    return np.concatenate(parts, axis=0)


def sinusoid(coords, model_width):
    quarter = model_width // 4
    table = jnp.asarray(angle_tables(model_width))
    slot = lax.broadcasted_iota(jnp.int32, (coords.shape[0], 2 * STEP), 1)
    hit = (slot == (coords // STEP)[:, None]) | (slot == (coords % STEP)[:, None] + STEP)
    hit = hit.astype(jnp.bfloat16)
    looked = mm(jnp.concatenate([hit, hit, hit], axis=1), table)
    sin_a, cos_a, sin_b, cos_b = [looked[:, k * quarter : (k + 1) * quarter] for k in range(4)]
    return jnp.concatenate([sin_a * cos_b + cos_a * sin_b, cos_a * cos_b - sin_a * sin_b], axis=1)


def head_of(ref, index, head):
    return ref[index, :, head * HEAD_DIM : (head + 1) * HEAD_DIM]


def probs_t(q, k, pq, pk, length, factor):
    left = jnp.concatenate([k, pk, k], axis=1)
    right = jnp.concatenate([q, q, pq], axis=1)
    scores = mm_nt(left, right) * factor
    visible = lax.broadcasted_iota(jnp.int32, scores.shape, 0) < length
    scores = jnp.where(visible, scores, MASKED)
    raised = jnp.exp(scores - jnp.max(scores, axis=0, keepdims=True))
    return raised * (1.0 / jnp.sum(raised, axis=0, keepdims=True))


def attend_kernel(heads, lengths_ref, x_ref, pos_ref, wqkv_ref, wpos_ref, mixed_ref, proj_ref):
    length = lengths_ref[pl.program_id(0)]
    factor = 1.0 / math.sqrt(3.0 * HEAD_DIM)
    rows = x_ref[0]
    for part in range(3):
        proj_ref[0, part] = mm(rows, wqkv_ref[part]).astype(jnp.bfloat16)
    position = pos_ref[0]
    for part in range(2):
        proj_ref[0, 3 + part] = mm(position, wpos_ref[part]).astype(jnp.bfloat16)
    here = proj_ref.at[0]
    for head in range(heads):
        q, k, v, pq, pk = [head_of(here, part, head) for part in range(5)]
        weights = probs_t(q, k, pq, pk, length, factor).astype(jnp.bfloat16)
        mixed = mm_tn(v, weights)
        mixed = mixed.astype(jnp.bfloat16).astype(jnp.float32)
        mixed_ref[0, :, head * HEAD_DIM : (head + 1) * HEAD_DIM] = mixed.T


def attend(lengths, tokens, position, w_qkv, w_pos):
    pages, length, width = tokens.shape
    columns = w_qkv.shape[2]
    page = lambda i, lens: (i, 0, 0)
    whole = lambda i, lens: (0, 0, 0)
    return pl.pallas_call(
        partial(attend_kernel, columns // HEAD_DIM),
        out_shape=(
            jax.ShapeDtypeStruct((pages, length, columns), jnp.float32),
            jax.ShapeDtypeStruct((pages, 5, length, columns), jnp.bfloat16),
        ),
        grid_spec=pltpu.PrefetchScalarGridSpec(
            num_scalar_prefetch=1,
            grid=(pages,),
            in_specs=[
                pl.BlockSpec((1, length, width), page),
                pl.BlockSpec((1, length, width), page),
                pl.BlockSpec(w_qkv.shape, whole),
                pl.BlockSpec(w_pos.shape, whole),
            ],
            out_specs=[
                pl.BlockSpec((1, length, columns), page),
                pl.BlockSpec((1, 5, length, columns), lambda i, lens: (i, 0, 0, 0)),
            ],
        ),
        compiler_params=pltpu.CompilerParams(vmem_limit_bytes=40 << 20),
        cost_estimate=pl.CostEstimate(
            flops=2 * pages * length * columns * (5 * width + 4 * length),
            transcendentals=pages * length * length * columns // HEAD_DIM,
            bytes_accessed=pages * length * (4 * width + 14 * columns),
        ),
        name="attend",
    )(lengths, tokens, position, w_qkv, w_pos)


def attend_back_kernel(heads, scalars_ref, own_ref, far_ref, dm_ref, d_ref, dp_ref):
    length = scalars_ref[1]
    factor = 1.0 / math.sqrt(3.0 * HEAD_DIM)
    columns = heads * HEAD_DIM
    for side, here in enumerate((own_ref.at[0], far_ref)):
        for head in range(heads):
            q, k, v, pq, pk = [head_of(here, part, head) for part in range(5)]
            at = side * columns + head * HEAD_DIM
            dm = dm_ref[:, at : at + HEAD_DIM]
            probs = probs_t(q, k, pq, pk, length, factor)
            weights = probs.astype(jnp.bfloat16)
            d_values = mm(weights, dm)
            d_probs = mm_nt(v, dm)
            inner = jnp.sum(d_probs * probs, axis=0, keepdims=True)
            d_scores = (probs * (d_probs - inner)).astype(jnp.bfloat16)
            by_queries = mm(d_scores, jnp.concatenate([q, pq], axis=1))
            by_query, by_pos_query = by_queries[:, :HEAD_DIM], by_queries[:, HEAD_DIM:]
            by_keys = mm_tn(jnp.concatenate([k, pk], axis=1), d_scores).T
            by_key, by_pos_key = by_keys[:, :HEAD_DIM], by_keys[:, HEAD_DIM:]
            grads = (
                ((by_key + by_pos_key) * factor, 0, d_ref, 3),
                ((by_query + by_pos_query) * factor, 1, d_ref, 3),
                (d_values, 2, d_ref, 3),
                (by_key * factor, 0, dp_ref, 2),
                (by_query * factor, 1, dp_ref, 2),
            )
            for value, part, ref, parts in grads:
                to = (side * parts + part) * columns + head * HEAD_DIM
                ref[:, to : to + HEAD_DIM] = value.astype(jnp.bfloat16)


def attend_back(scalars, proj, far_proj, d_mixed):
    pages, parts, length, columns = proj.shape
    heads = columns // HEAD_DIM
    return pl.pallas_call(
        partial(attend_back_kernel, heads),
        out_shape=(
            jax.ShapeDtypeStruct((length, 6 * columns), jnp.bfloat16),
            jax.ShapeDtypeStruct((length, 4 * columns), jnp.bfloat16),
        ),
        grid_spec=pltpu.PrefetchScalarGridSpec(
            num_scalar_prefetch=1,
            grid=(1,),
            in_specs=[
                pl.BlockSpec((1, parts, length, columns), lambda i, s: (s[0], 0, 0, 0)),
                pl.BlockSpec((parts, length, columns), lambda i, s: (0, 0, 0)),
                pl.BlockSpec((length, 2 * columns), lambda i, s: (0, 0)),
            ],
            out_specs=[
                pl.BlockSpec((length, 6 * columns), lambda i, s: (0, 0)),
                pl.BlockSpec((length, 4 * columns), lambda i, s: (0, 0)),
            ],
        ),
        compiler_params=pltpu.CompilerParams(vmem_limit_bytes=40 << 20),
        cost_estimate=pl.CostEstimate(
            flops=2 * 2 * heads * length * length * HEAD_DIM * 9,
            transcendentals=2 * heads * length * length,
            bytes_accessed=length * columns * 44,
        ),
        name="attend_back",
    )(scalars, proj, far_proj, d_mixed)


def norm_parts(values):
    center = values - jnp.mean(values, axis=-1, keepdims=True)
    spread = jnp.mean(center * center, axis=-1, keepdims=True)
    scale = lax.rsqrt(spread + 1e-05)
    return center * scale, scale


def norm_back(grad, gain, xhat, scale):
    up = grad * gain
    mean = jnp.mean(up, axis=-1, keepdims=True)
    along = jnp.mean(up * xhat, axis=-1, keepdims=True)
    return scale * (up - mean - xhat * along)


def column_sum(values):
    return jnp.sum(values.astype(jnp.float32), axis=0)


def body(
    dp_size,
    mp_size,
    tokens,
    lengths,
    coords,
    w_qkv,
    w_pos,
    w_out,
    b_out,
    gain_one,
    shift_one,
    w_in,
    b_in,
    w_back,
    b_back,
    gain_two,
    shift_two,
    cotangent,
):
    pages, length, width = tokens.shape
    columns = w_qkv.shape[2]
    units = w_in.shape[1]
    here = lax.axis_index("mp")
    low = here & 1
    page = here >> 1
    group = lax.axis_index("dp")
    f32, bf16 = jnp.float32, jnp.bfloat16

    one = jnp.where(lengths[0] > 0, 1.0, 0.0).astype(f32)

    def arrived(value):
        return value * one

    def swap(value, bit):
        pairs = [(i, i ^ bit) for i in range(mp_size)]
        return lax.ppermute(value, "mp", pairs)

    def my_rows(value):
        rows = value.shape[0] // dp_size
        return lax.dynamic_slice_in_dim(value, group * rows, rows, 0)

    def gather(value):
        return arrived(lax.all_gather(value, "dp", axis=0, tiled=True))

    def take(value, index):
        return lax.dynamic_index_in_dim(value, index, 0, keepdims=False)

    out_rows = swap(my_rows(w_out).astype(f32), FAR)
    w_out_far = gather(out_rows).astype(bf16)
    unit_rows = jnp.concatenate([my_rows(w_in), my_rows(w_back)], axis=0).astype(f32)
    far_rows = swap(jnp.concatenate([unit_rows, b_in[None], jnp.zeros((7, units), f32)], axis=0), FAR)
    b_in_far = far_rows[unit_rows.shape[0]]
    blocks = gather(far_rows[: unit_rows.shape[0]]).reshape(dp_size, unit_rows.shape[0], -1)
    in_rows = width // dp_size
    w_in_far = blocks[:, :in_rows].reshape(width, units).astype(bf16)
    w_back_far = blocks[:, in_rows:].reshape(units, width).astype(bf16)
    head_rows = jnp.concatenate(
        [my_rows(w_qkv.reshape(-1, columns)), my_rows(w_pos.reshape(-1, columns))], axis=0
    ).astype(f32)
    blocks = gather(swap(head_rows, FAR)).reshape(dp_size, head_rows.shape[0], columns)
    qkv_rows = 3 * width // dp_size
    w_qkv_far = blocks[:, :qkv_rows].reshape(3, width, columns).astype(bf16)
    w_pos_far = blocks[:, qkv_rows:].reshape(2, width, columns).astype(bf16)

    position = [
        sinusoid(coords[:, axis].reshape(-1), width).astype(bf16) for axis in range(2)
    ]
    position = jnp.concatenate(position, axis=1).reshape(pages, length, width)
    mixed_all, proj = attend(lengths, tokens, position, w_qkv, w_pos)

    mixed_far = arrived(swap(take(mixed_all, 1 - page), FAR))
    mixed = jnp.concatenate([take(mixed_all, page), mixed_far], axis=1).astype(bf16)
    w_out_two = jnp.concatenate([w_out, w_out_far], axis=0)
    w_in_two = jnp.concatenate([w_in, w_in_far], axis=1)
    w_back_two = jnp.concatenate([w_back, w_back_far], axis=0)
    b_in_two = jnp.concatenate([b_in, b_in_far], axis=0)
    rows = take(tokens, page)
    pos_rows = take(position, page)
    grad_out = take(cotangent, page).astype(f32)

    part = mm(mixed, w_out_two)
    first = rows.astype(f32) + (part + swap(part, NEAR) + b_out)
    xhat_one, scale_one = norm_parts(first)
    normed = xhat_one * gain_one + shift_one
    normed_low = normed.astype(bf16)
    hidden_pre = mm(normed_low, w_in_two) + b_in_two
    cdf = 0.5 * (1.0 + lax.erf(hidden_pre * math.sqrt(0.5)))
    hidden = (hidden_pre * cdf).astype(bf16)
    part = mm(hidden, w_back_two)
    slope = cdf + hidden_pre * (
        jnp.exp(-0.5 * hidden_pre * hidden_pre) * (1.0 / math.sqrt(2.0 * math.pi))
    )
    second = normed + (part + swap(part, NEAR) + b_back)
    xhat_two, scale_two = norm_parts(second)
    d_second = norm_back(grad_out, gain_two, xhat_two, scale_two)
    d_feed = d_second.astype(bf16)
    d_hidden = mm_nt(d_feed, w_back_two)
    d_pre = (d_hidden * slope).astype(bf16)
    part = mm_nt(d_pre, w_in_two)
    d_normed = d_second + (part + swap(part, NEAR))

    half = length // 2

    def half_of(value, index):
        return lax.dynamic_slice_in_dim(value, index * half, half, 0)

    def spread(mine, other):
        both = jnp.stack([mine, other])
        rest = swap(both, NEAR)
        out = jnp.stack([jnp.where(low == 0, both, rest), jnp.where(low == 0, rest, both)], axis=1)
        out = out.reshape(pages, length, width)
        return jnp.where(page == 0, out, out[::-1])

    output = xhat_two * gain_two + shift_two
    mine = half_of(output, low)
    layer_out = arrived(spread(mine, swap(mine, FAR))).astype(bf16)

    def to_blocks(value):
        return value.reshape(dp_size, -1, value.shape[1])

    def in_first(rows_of):
        value = jnp.stack(rows_of + [jnp.zeros_like(rows_of[0])] * (8 - len(rows_of)))
        return jnp.concatenate(
            [value[None], jnp.zeros((dp_size - 1,) + value.shape, f32)], axis=0
        )

    def reduce_two(own, far):
        both = jnp.concatenate(own + far, axis=1)
        total = lax.psum_scatter(
            both.reshape(-1, both.shape[2]), "dp", scatter_dimension=0, tiled=True
        )
        cut = total.shape[0] // 2
        total = total[:cut] + swap(total[cut:], FAR)
        return lax.all_gather(total, "dp", axis=0, tiled=True).reshape(dp_size, cut, -1)

    d_w_back = mm_tn(hidden, d_feed)
    d_w_in = [mm_tn(normed_low, d_pre[:, :units]), mm_tn(normed_low, d_pre[:, units:])]
    d_b_in = column_sum(d_pre)
    vectors = [
        column_sum(d_feed),
        jnp.sum(grad_out * xhat_two, axis=0),
        jnp.sum(grad_out, axis=0),
    ]
    ffn = reduce_two(
        [to_blocks(d_w_in[0]), to_blocks(d_w_back[:units]), in_first([d_b_in[:units]] + vectors)],
        [to_blocks(d_w_in[1]), to_blocks(d_w_back[units:]), in_first([d_b_in[units:]] + vectors)],
    )
    grad_w_in = ffn[:, :in_rows].reshape(width, units)
    grad_w_back = ffn[:, in_rows : in_rows + units // dp_size].reshape(units, width)
    vectors = ffn[0, in_rows + units // dp_size :]
    grad_b_in, grad_b_back, grad_gain_two, grad_shift_two = vectors[0], vectors[1], vectors[2], vectors[3]

    d_first = norm_back(d_normed, gain_one, xhat_one, scale_one)
    d_branch = d_first.astype(bf16)
    d_mixed = mm_nt(d_branch, w_out_two).astype(bf16)
    far_proj = [mm(rows, w_qkv_far[k]).astype(bf16) for k in range(3)]
    far_proj += [mm(pos_rows, w_pos_far[k]).astype(bf16) for k in range(2)]
    scalars = jnp.stack([page, take(lengths, page)])
    d_heads, d_pos = attend_back(scalars, proj, jnp.stack(far_proj), d_mixed)
    part = mm_nt(d_heads[:, : 3 * columns], jnp.concatenate(list(w_qkv), axis=1))
    part = part + mm_nt(d_heads[:, 3 * columns :], jnp.concatenate(list(w_qkv_far), axis=1))
    mine = half_of(part, low) + swap(half_of(part, 1 - low), NEAR) + half_of(d_first, low)
    grad_tokens = spread(mine, swap(mine, FAR))

    d_w_out = mm_tn(mixed, d_branch)
    vectors = [
        column_sum(d_branch),
        jnp.sum(d_normed * xhat_one, axis=0),
        jnp.sum(d_normed, axis=0),
    ]
    vectors = in_first(vectors)
    grads_x = mm_tn(rows, d_heads)
    grads_p = mm_tn(pos_rows, d_pos)
    attn = reduce_two(
        [to_blocks(d_w_out[:columns]), vectors],
        [to_blocks(d_w_out[columns:]), vectors],
    )
    out_block = columns // dp_size
    grad_w_out = attn[:, :out_block].reshape(columns, width)
    grad_b_out, grad_gain_one, grad_shift_one = [attn[0, out_block + k] for k in range(3)]

    def reduce_columns(value):
        total = lax.psum_scatter(value, "dp", scatter_dimension=0, tiled=True)
        cut = total.shape[1] // 2
        total = total[:, :cut] + swap(total[:, cut:], FAR)
        return lax.all_gather(total, "dp", axis=0, tiled=True)

    grads_x = reduce_columns(grads_x)
    grads_p = reduce_columns(grads_p)
    grad_w_qkv = jnp.stack([grads_x[:, k * columns : (k + 1) * columns] for k in range(3)])
    grad_w_pos = jnp.stack([grads_p[:, k * columns : (k + 1) * columns] for k in range(2)])
    return (
        layer_out,
        grad_tokens,
        grad_w_qkv,
        grad_w_pos,
        grad_w_out,
        grad_b_out,
        grad_gain_one,
        grad_shift_one,
        grad_w_in,
        grad_b_in,
        grad_w_back,
        grad_b_back,
        grad_gain_two,
        grad_shift_two,
    )


def solution(mesh):
    placed = (
        P("dp", None, None),
        P("dp"),
        P("dp", None, None),
        P(None, None, "mp"),
        P(None, None, "mp"),
        P("mp", None),
        P(),
        P(),
        P(),
        P(None, "mp"),
        P("mp"),
        P("mp", None),
        P(),
        P(),
        P(),
        P("dp", None, None),
    )
    return jax.shard_map(
        partial(body, mesh.shape["dp"], mesh.shape["mp"]),
        mesh=mesh,
        in_specs=placed,
        out_specs=(
            P("dp", None, None),
            P("dp", None, None),
            P(None, None, "mp"),
            P(None, None, "mp"),
            P("mp", None),
            P(),
            P(),
            P(),
            P(None, "mp"),
            P("mp"),
            P("mp", None),
            P(),
            P(),
            P(),
        ),
        check_vma=False,
    )
```

time: 768 us -> 642 us (0.84)
  waiting for transfers between devices: 567 us -> 396 us
  local copies, waits for them, and re-layouts: 40.9 us -> 75.9 us
  starting transfers between devices: 0.84 us -> 34.5 us
  matrix products: 66.2 us -> 37 us
  Pallas kernels: 0 us -> 15 us
    psum x5 -> x0, waiting for transfers between devices: 567 us -> none  [the longest x1 126 us: body(): lax.psum((d_w_qkv, d_w_pos, d_w_out, d_b_out, d_gain_one, d_shift_one, d_...]
    ppermute x0 -> x16, waiting for transfers between devices: none -> 273 us  [swap(): return lax.ppermute(value, 'mp', pairs)]
    reduce_scatter x0 -> x4, waiting for transfers between devices: none -> 123 us  [the longest x2 65.4 us: reduce_two(): lax.psum_scatter(both.reshape(-1, both.shape[2]), 'dp', scatter_dimension...]
    ppermute x0 -> x16, starting transfers between devices: none -> 33.6 us  [swap(): return lax.ppermute(value, 'mp', pairs)]
    dot_general x48 -> x25, matrix products: 66.2 us -> 37 us  [the longest x14 17.2 us: mm(): return jnp.dot(left, right, preferred_element_type=jnp.float32)]
    psum x1 -> x0, blocking collectives: 26.2 us -> none  [body(): lax.psum((d_w_qkv, d_w_pos, d_w_out, d_b_out, d_gain_one, d_shift_one, d_...]
    slice x1 -> x20, local copies, waits for them, and re-layouts: 0.16 us -> 23.3 us  [the longest x3 5.28 us: body(): far_proj += [mm(pos_rows, w_pos_far[k]).astype(bf16) for k in range(2)]]
    all_gather x0 -> x2, blocking collectives: none -> 20.9 us  [the longest x1 10.5 us: reduce_two(): lax.all_gather(total, 'dp', axis=0, tiled=True).reshape(dp_size, cut, -1)]
  transfers between devices with their start and end apart: 5 -> 25, of which waited for: 5 -> 15; matrix products, arithmetic and copies ran while one was open for 3% -> 19% of each run, Pallas kernels for 0% -> 1%
where the time goes in v2:
time: 642 us; the launch traced here: 633 us
  waiting for transfers between devices  396 us (62%)
  local copies, waits for them, and re-layouts  75.9 us (12%)
  other arithmetic  37.1 us (6%)
  matrix products  37 us (6%)
  starting transfers between devices  34.5 us (5%)
  blocking collectives  20.9 us (3%)
  between operations  16.1 us (3%)
  Pallas kernels  15 us (2%)
    ppermute x16, waiting for transfers between devices, swap(): return lax.ppermute(value, 'mp', pairs)  273 us
    reduce_scatter x2, waiting for transfers between devices, reduce_two(): lax.psum_scatter(both.reshape(-1, both.shape[2]), 'dp', scatter_dimension...  65.4 us
    reduce_scatter x2, waiting for transfers between devices, reduce_columns(): total = lax.psum_scatter(value, 'dp', scatter_dimension=0, tiled=True)  57.3 us
    ppermute x16, starting transfers between devices, swap(): return lax.ppermute(value, 'mp', pairs)  33.6 us
    unnamed x125, local copies, waits for them, and re-layouts  28.5 us
    dot_general x14, matrix products, mm(): return jnp.dot(left, right, preferred_element_type=jnp.float32)  17.2 us
  transfers between devices with their start and end apart: 25, of which 15 were waited for; matrix products, arithmetic and copies ran while one was open for 19% of the time, Pallas kernels for 1%

profile of v2, /device:TPU:0, one launch (start us, length us, event | category | flops | bytes accessed | tf_op | source)
XLA Modules:
  0.0 632.6 jit_solution(4737269136532318899)
XLA Ops:
  9.2 4.1 collective-permute-start.3
  13.3 27.0 %collective-permute-done.3 = f32[200,768]{1,0:T(8,128)S(1)} collective-permute-done((f32[200,768]{1,0:T(8,128)S(1)}, f32[200,768]{1,0:T(8,128)S(1)}, u32[]{:S(2)}, u32[]{:S(2)}) %collective-permute-start.3) | collective-permute-done | bytes 614432 | tf_op jit(solution)/shard_map/ppermute | solution.py:252
  47.2 2.0 add_add_fusion
  54.4 2.0 add_add_fusion.1
  58.8 2.4 pad_maximum_fusion.5.pos_ref
  61.2 7.6 %attend.1 = (f32[2,512,192]{2,1,0:T(8,128)S(1)}, bf16[2,5,512,192]{3,2,1,0:T(8,128)(2,1)S(1)}) custom-call(s32[2]{0:T(128)S(1)} %copy-done.3, bf16[2,512,768]{2,1,0:T(8,128)(2,1)S(1)} %copy-done.1, bf16[2,512,768]{2,1,0:T(8,128)(2,1)S(1)} %pad_maximum_fusion.5.pos_ref, bf16[3,768,192]{2,1,0:T(8,128)(2,1)S(1)} %copy.86.wqkv_ref, ...), custom_call_target="tpu_custom_call" | custom-call | flops 2315255808 | bytes 5898240 | tf_op jit(solution)/shard_map/attend/pallas_call | solution.py:105
  72.1 2.9 collective-permute-start
  77.3 10.4 %all_gather.21 = f32[192,768]{1,0:T(8,128)S(1)} all-gather(f32[24,768]{1,0:T(8,128)} %collective-permute-done.1), channel_id=1, replica_groups=mesh['dp'=8,'mp'=4] {'dp'}, dimensions={0}, use_global_device_ids=true | all-gather | bytes 663552 | tf_op jit(solution)/shard_map/all_gather | solution.py:259
  87.8 9.9 %collective-permute-done = f32[512,192]{1,0:T(8,128)} collective-permute-done((f32[512,192]{1,0:T(8,128)}, f32[512,192]{1,0:T(8,128)}, u32[]{:S(2)}, u32[]{:S(2)}) %collective-permute-start) | collective-permute-done | bytes 393248 | tf_op jit(solution)/shard_map/ppermute | solution.py:252
  102.1 2.3 copy.107
  106.5 3.4 collective-permute-start.7
  109.9 33.7 %collective-permute-done.7 = f32[480,192]{0,1:T(8,128)} collective-permute-done((f32[480,192]{0,1:T(8,128)S(1)}, f32[480,192]{0,1:T(8,128)}, u32[]{:S(2)}, u32[]{:S(2)}) %collective-permute-start.7) | collective-permute-done | bytes 368672 | tf_op jit(solution)/shard_map/ppermute | solution.py:252
  145.0 2.2 fusion.120
  148.8 2.7 multiply_convert_fusion
  156.5 4.4 collective-permute-start.4
  161.6 33.3 %collective-permute-done.4 = f32[512,768]{1,0:T(8,128)S(1)} collective-permute-done((f32[512,768]{1,0:T(8,128)S(1)}, f32[512,768]{1,0:T(8,128)S(1)}, u32[]{:S(2)}, u32[]{:S(2)}) %collective-permute-start.4) | collective-permute-done | bytes 1572896 | tf_op jit(solution)/shard_map/ppermute | solution.py:252
  198.9 4.1 convert_reduce_fusion
  203.0 2.6 fusion.17
  207.3 2.3 multiply_convert_fusion.1
  212.0 2.6 copy.91
  214.6 2.2 fusion.124
  217.8 2.0 squeeze.68
  219.8 2.0 copy.95
  221.9 2.0 squeeze.67
  227.2 13.9 %collective-permute-done.8 = f32[512,768]{1,0:T(8,128)} collective-permute-done((f32[512,768]{1,0:T(8,128)}, f32[512,768]{1,0:T(8,128)}, u32[]{:S(2)}, u32[]{:S(2)}) %collective-permute-start.8) | collective-permute-done | bytes 1572896 | tf_op jit(solution)/shard_map/ppermute | solution.py:252
  241.1 2.7 multiply_reduce_fusion
  246.2 7.4 %attend_back.1 = (bf16[512,1152]{1,0:T(8,128)(2,1)S(1)}, bf16[512,768]{1,0:T(8,128)(2,1)S(1)}) custom-call(s32[2]{0:T(128)S(1)} %pad_add_fusion.scalars_ref, bf16[2,5,512,192]{3,2,1,0:T(8,128)(2,1)S(1)} %copy-done.7, bf16[5,512,192]{2,1,0:T(8,128)(2,1)S(1)} %fusion.23.far_ref, bf16[512,384]{1,0:T(8,128)(2,1)S(1)} %convolution_convert_fusion.dm_ref), custom_call_target="tpu_custom_call" | custom-call | flops 1811939328 | bytes 4325376 | tf_op jit(solution)/shard_map/attend_back/pallas_call | solution.py:169
  254.6 2.5 fusion.46
  258.3 3.1 fusion.50
  263.1 2.2 fusion.43
  280.8 17.8 %reduce-scatter.7.cloned.1.call-done = f32[96,768]{1,0:T(8,128)} async-done(((f32[768,768]{1,0:T(8,128)}), f32[96,768]{1,0:T(8,128)}) %reduce-scatter.7.cloned.1.call-update) | async-done | bytes 294928 | tf_op jit(solution)/shard_map/reduce_scatter | solution.py:399
  299.5 2.5 collective-permute-start.13
  302.0 7.3 %collective-permute-done.13 = f32[96,384]{1,0:T(8,128)S(1)} collective-permute-done((f32[96,384]{1,0:T(8,128)S(1)}, f32[96,384]{1,0:T(8,128)S(1)}, u32[]{:S(2)}, u32[]{:S(2)}) %collective-permute-start.13) | collective-permute-done | bytes 147488 | tf_op jit(solution)/shard_map/ppermute | solution.py:252
  310.9 39.5 %reduce-scatter.5.cloned.1.call-done = f32[96,1152]{1,0:T(8,128)} async-done(((f32[768,1152]{1,0:T(8,128)}), f32[96,1152]{1,0:T(8,128)}) %reduce-scatter.5.cloned.1.call-update) | async-done | bytes 442384 | tf_op jit(solution)/shard_map/reduce_scatter | solution.py:399
  351.5 2.5 collective-permute-start.12
  354.0 11.5 %collective-permute-done.12 = f32[96,576]{1,0:T(8,128)S(1)} collective-permute-done((f32[96,576]{1,0:T(8,128)S(1)}, f32[96,576]{1,0:T(8,128)S(1)}, u32[]{:S(2)}, u32[]{:S(2)}) %collective-permute-start.12) | collective-permute-done | bytes 221216 | tf_op jit(solution)/shard_map/ppermute | solution.py:252
  367.2 65.3 %reduce-scatter.11.cloned.1.call-done = f32[400,768]{1,0:T(8,128)} async-done(((f32[3200,768]{1,0:T(8,128)}), f32[400,768]{1,0:T(8,128)}) %reduce-scatter.11.cloned.1.call-update) | async-done | bytes 1228816 | tf_op jit(solution)/shard_map/reduce_scatter | solution.py:345
  433.8 2.5 collective-permute-start.15
  436.3 27.3 %collective-permute-done.15 = f32[200,768]{1,0:T(8,128)S(1)} collective-permute-done((f32[200,768]{1,0:T(8,128)S(1)}, f32[200,768]{1,0:T(8,128)S(1)}, u32[]{:S(2)}, u32[]{:S(2)}) %collective-permute-start.15) | collective-permute-done | bytes 614432 | tf_op jit(solution)/shard_map/ppermute | solution.py:252
  469.4 3.9 collective-permute-start.9
  473.4 30.6 %collective-permute-done.5 = f32[256,768]{1,0:T(8,128)S(1)} collective-permute-done((f32[256,768]{1,0:T(8,128)S(1)}, f32[256,768]{1,0:T(8,128)S(1)}, u32[]{:S(2)}, u32[]{:S(2)}) %collective-permute-start.5) | collective-permute-done | bytes 786464 | tf_op jit(solution)/shard_map/ppermute | solution.py:252
  507.3 47.5 %collective-permute-done.10 = f32[256,768]{1,0:T(8,128)S(1)} collective-permute-done((f32[256,768]{1,0:T(8,128)S(1)}, f32[256,768]{1,0:T(8,128)S(1)}, u32[]{:S(2)}, u32[]{:S(2)}) %collective-permute-start.10) | collective-permute-done | bytes 786464 | tf_op jit(solution)/shard_map/ppermute | solution.py:252
  556.2 3.8 collective-permute-start.11
  564.8 30.8 %collective-permute-done.14 = f32[32,768]{1,0:T(8,128)S(1)} collective-permute-done((f32[32,768]{1,0:T(8,128)S(1)}, f32[32,768]{1,0:T(8,128)S(1)}, u32[]{:S(2)}, u32[]{:S(2)}) %collective-permute-start.14) | collective-permute-done | bytes 98336 | tf_op jit(solution)/shard_map/ppermute | solution.py:252
  595.6 10.5 %all_gather.26 = f32[256,768]{1,0:T(8,128)S(1)} all-gather(f32[32,768]{1,0:T(8,128)S(1)} %slice_add_fusion.3), channel_id=1, replica_groups=mesh['dp'=8,'mp'=4] {'dp'}, dimensions={0}, use_global_device_ids=true | all-gather | bytes 884736 | tf_op jit(solution)/shard_map/all_gather | solution.py:350
  609.9 1.9 reverse_select_fusion
  615.0 2.1 slice_bitcast_fusion.4
  620.6 5.0 fusion.121
  (273 shorter events, 102.6 us)
Async XLA Ops:
  7.2 141.6 %all-gather.7.cloned.1.call-start = ((), (), s32[]{:S(2)}) async-start(), calls=%async_computation.4 | async-start | bytes 5308416 | tf_op jit(solution)/shard_map/all_gather | solution.py:259
  9.1 34.4 %copy-start.30 = (bf16[2,768,192]{1,2,0:T(8,128)(2,1)S(1)}, bf16[2,768,192]{1,2,0:T(8,128)(2,1)}, u32[]{:S(2)}) copy-start(bf16[2,768,192]{1,2,0:T(8,128)(2,1)} %param.22) | copy-start | bytes 1769476
  9.2 34.6 %copy-start.20 = (bf16[3,768,192]{1,2,0:T(8,128)(2,1)S(1)}, bf16[3,768,192]{1,2,0:T(8,128)(2,1)}, u32[]{:S(2)}) copy-start(bf16[3,768,192]{1,2,0:T(8,128)(2,1)} %param.21) | copy-start | bytes 2654212
  9.2 31.1 %collective-permute-start.3 = (f32[200,768]{1,0:T(8,128)S(1)}, f32[200,768]{1,0:T(8,128)S(1)}, u32[]{:S(2)}, u32[]{:S(2)}) collective-permute-start(f32[200,768]{1,0:T(8,128)S(1)} %maximum_maximum_fusion), channel_id=1, source_target_pairs={{0,2},{1,3},{2,0},{3,1},{4,6},{5,7},{6,4},{7,5},{8,10},{9,11},{10,... | collective-permute-start | bytes 1843208 | tf_op jit(solution)/shard_map/ppermute | solution.py:252
  42.0 165.3 %all-gather.15.cloned.1.call-start = ((), (), s32[]{:S(2)}) async-start(), calls=%async_computation.12 | async-start | bytes 3538944 | tf_op jit(solution)/shard_map/all_gather | solution.py:259
  43.5 33.8 %collective-permute-start.1 = (f32[24,768]{1,0:T(8,128)}, f32[24,768]{1,0:T(8,128)}, u32[]{:S(2)}, u32[]{:S(2)}) collective-permute-start(f32[24,768]{1,0:T(8,128)} %dynamic-slice_convert_fusion.1), channel_id=1, source_target_pairs={{0,2},{1,3},{2,0},{3,1},{4,6},{5,7},{6,4},{7,5},{8,10},{9,11},{10,... | collective-permute-start | bytes 221192 | tf_op jit(solution)/shard_map/ppermute | solution.py:252
  58.8 2.4 copy-start.3
  72.1 26.6 %copy-start.36 = (bf16[192,768]{1,0:T(8,128)(2,1)S(1)}, bf16[192,768]{1,0:T(8,128)(2,1)}, u32[]{:S(2)}) copy-start(bf16[192,768]{1,0:T(8,128)(2,1)} %param.23) | copy-start | bytes 884740
  72.1 25.6 %collective-permute-start = (f32[512,192]{1,0:T(8,128)}, f32[512,192]{1,0:T(8,128)}, u32[]{:S(2)}, u32[]{:S(2)}) collective-permute-start(f32[512,192]{1,0:T(8,128)} %dynamic-slice_bitcast_fusion), channel_id=1, source_target_pairs={{0,2},{1,3},{2,0},{3,1},{4,6},{5,7},{6,4},{7,5},{8,10},{9,11},{10,... | collective-permute-start | bytes 1179656 | tf_op jit(solution)/shard_map/ppermute | solution.py:252
  76.0 24.4 %copy-start.32 = (bf16[512,192]{1,0:T(8,128)(2,1)}, bf16[512,192]{1,0:T(8,128)(2,1)S(1)}, u32[]{:S(2)}) copy-start(bf16[512,192]{1,0:T(8,128)(2,1)S(1)} %fusion.77) | copy-start | bytes 589828
  87.8 13.5 %copy-start.31 = (bf16[2,768,192]{1,2,0:T(8,128)(2,1)S(1)}, bf16[2,768,192]{1,2,0:T(8,128)(2,1)}, u32[]{:S(2)}) copy-start(bf16[2,768,192]{1,2,0:T(8,128)(2,1)} %param.22) | copy-start | bytes 1769476
  98.7 3.3 copy-start.34
  100.5 44.5 %collective-permute-start.2 = (f32[512,768]{1,0:T(8,128)}, f32[512,768]{1,0:T(8,128)}, u32[]{:S(2)}, u32[]{:S(2)}) collective-permute-start(f32[512,768]{1,0:T(8,128)} %fusion.66), channel_id=1, source_target_pairs={{0,1},{1,0},{2,3},{3,2},{4,5},{5,4},{6,7},{7,6},{8,9},{9,8},{10,11... | collective-permute-start | bytes 4718600 | tf_op jit(solution)/shard_map/ppermute | solution.py:252
  102.1 42.9 %copy-start.51 = (f32[768]{0:T(1024)S(1)}, f32[768]{0:T(1024)}, u32[]{:S(2)}) copy-start(f32[768]{0:T(1024)} %param.28) | copy-start | bytes 9220
  102.1 42.9 %copy-start.2 = (bf16[2,512,768]{2,1,0:T(8,128)(2,1)S(1)}, bf16[2,512,768]{2,1,0:T(8,128)(2,1)}, u32[]{:S(2)}) copy-start(bf16[2,512,768]{2,1,0:T(8,128)(2,1)} %x_ref.1) | copy-start | bytes 4718596
  102.1 43.0 %copy-start.53 = (f32[768]{0:T(1024)S(1)}, f32[768]{0:T(1024)}, u32[]{:S(2)}) copy-start(f32[768]{0:T(1024)} %param.24) | copy-start | bytes 9220
  106.5 37.2 %collective-permute-start.7 = (f32[480,192]{0,1:T(8,128)S(1)}, f32[480,192]{0,1:T(8,128)}, u32[]{:S(2)}, u32[]{:S(2)}) collective-permute-start(f32[480,192]{0,1:T(8,128)S(1)} %maximum_convert_fusion.1), channel_id=1, source_target_pairs={{0,2},{1,3},{2,0},{3,1},{4,6},{5,7},{6,4},{7,5},{8,10},{9,11},{10,... | collective-permute-start | bytes 1105928 | tf_op jit(solution)/shard_map/ppermute | solution.py:252
  143.7 154.9 %reduce-scatter.7.cloned.1.call-start = ((), (), s32[]{:S(2)}) async-start(), calls=%async_computation.7 | async-start | bytes 2654208 | tf_op jit(solution)/shard_map/reduce_scatter | solution.py:399
  155.1 39.8 %copy-start.54 = (f32[768]{0:T(1024)S(1)}, f32[768]{0:T(1024)}, u32[]{:S(2)}) copy-start(f32[768]{0:T(1024)} %param.30) | copy-start | bytes 9220
  156.5 38.4 %collective-permute-start.4 = (f32[512,768]{1,0:T(8,128)S(1)}, f32[512,768]{1,0:T(8,128)S(1)}, u32[]{:S(2)}, u32[]{:S(2)}) collective-permute-start(f32[512,768]{1,0:T(8,128)S(1)} %fusion.16), channel_id=1, source_target_pairs={{0,1},{1,0},{2,3},{3,2},{4,5},{5,4},{6,7},{7,6},{8,9},{9,8},{10,11... | collective-permute-start | bytes 4718600 | tf_op jit(solution)/shard_map/ppermute | solution.py:252
  198.9 4.1 copy-start.14
  203.0 2.6 copy-start.56
  205.6 35.5 %collective-permute-start.8 = (f32[512,768]{1,0:T(8,128)}, f32[512,768]{1,0:T(8,128)}, u32[]{:S(2)}, u32[]{:S(2)}) collective-permute-start(f32[512,768]{1,0:T(8,128)} %fusion.17), channel_id=1, source_target_pairs={{0,1},{1,0},{2,3},{3,2},{4,5},{5,4},{6,7},{7,6},{8,9},{9,8},{10,11... | collective-permute-start | bytes 4718600 | tf_op jit(solution)/shard_map/ppermute | solution.py:252
  225.8 15.2 %copy-start.15 = (f32[512,768]{1,0:T(8,128)S(1)}, f32[512,768]{1,0:T(8,128)}, u32[]{:S(2)}) copy-start(f32[512,768]{1,0:T(8,128)} %copy-done.14) | copy-start | bytes 4718596
  226.4 14.7 %copy-start.10 = (f32[512,768]{1,0:T(8,128)S(1)}, f32[512,768]{1,0:T(8,128)}, u32[]{:S(2)}) copy-start(f32[512,768]{1,0:T(8,128)} %copy-done.8) | copy-start | bytes 4718596
  243.8 2.4 copy-start.7
  244.3 9.3 %copy-start.12 = (f32[512,768]{1,0:T(8,128)}, f32[512,768]{1,0:T(8,128)S(1)}, u32[]{:S(2)}) copy-start(f32[512,768]{1,0:T(8,128)S(1)} %get-tuple-element.95) | copy-start | bytes 4718596
  257.1 93.3 %reduce-scatter.5.cloned.1.call-start = ((), (), s32[]{:S(2)}) async-start(), calls=%async_computation.5 | async-start | bytes 3981312 | tf_op jit(solution)/shard_map/reduce_scatter | solution.py:399
  261.5 171.1 %reduce-scatter.11.cloned.1.call-start = ((), (), s32[]{:S(2)}) async-start(), calls=%async_computation.10 | async-start | bytes 11059200 | tf_op jit(solution)/shard_map/reduce_scatter | solution.py:345
  265.3 2.9 copy-start.29
  277.2 285.1 %reduce-scatter.9.cloned.1.call-start = ((), (), s32[]{:S(2)}) async-start(), calls=%async_computation.9 | async-start | bytes 1769472 | tf_op jit(solution)/shard_map/reduce_scatter | solution.py:345
  280.7 331.1 %all-gather.11.cloned.1.call-start = ((), (), s32[]{:S(2)}) async-start(), calls=%async_computation.8 | async-start | bytes 1327104 | tf_op jit(solution)/shard_map/all_gather | solution.py:402
  299.5 9.7 %collective-permute-start.13 = (f32[96,384]{1,0:T(8,128)S(1)}, f32[96,384]{1,0:T(8,128)S(1)}, u32[]{:S(2)}, u32[]{:S(2)}) collective-permute-start(f32[96,384]{1,0:T(8,128)S(1)} %slice.264), channel_id=1, source_target_pairs={{0,2},{1,3},{2,0},{3,1},{4,6},{5,7},{6,4},{7,5},{8,10},{9,11},{10,... | collective-permute-start | bytes 442376 | tf_op jit(solution)/shard_map/ppermute | solution.py:252
  310.9 304.1 %all-gather.9.cloned.1.call-start = ((), (), s32[]{:S(2)}) async-start(), calls=%async_computation.6 | async-start | bytes 2211840 | tf_op jit(solution)/shard_map/all_gather | solution.py:402
  351.5 13.9 %collective-permute-start.12 = (f32[96,576]{1,0:T(8,128)S(1)}, f32[96,576]{1,0:T(8,128)S(1)}, u32[]{:S(2)}, u32[]{:S(2)}) collective-permute-start(f32[96,576]{1,0:T(8,128)S(1)} %slice.259), channel_id=1, source_target_pairs={{0,2},{1,3},{2,0},{3,1},{4,6},{5,7},{6,4},{7,5},{8,10},{9,11},{10,... | collective-permute-start | bytes 663560 | tf_op jit(solution)/shard_map/ppermute | solution.py:252
  367.2 251.9 %all-gather.13.cloned.1.call-start = ((), (), s32[]{:S(2)}) async-start(), calls=%async_computation.11 | async-start | bytes 5529600 | tf_op jit(solution)/shard_map/all_gather | solution.py:350
  432.6 30.9 %copy-start.38 = (f32[400,768]{1,0:T(8,128)S(1)}, f32[400,768]{1,0:T(8,128)}, u32[]{:S(2)}) copy-start(f32[400,768]{1,0:T(8,128)} %reduce-scatter.11.cloned.1.call-done) | copy-start | bytes 3686404
  433.8 29.7 %collective-permute-start.15 = (f32[200,768]{1,0:T(8,128)S(1)}, f32[200,768]{1,0:T(8,128)S(1)}, u32[]{:S(2)}, u32[]{:S(2)}) collective-permute-start(f32[200,768]{1,0:T(8,128)S(1)} %slice.282), channel_id=1, source_target_pairs={{0,2},{1,3},{2,0},{3,1},{4,6},{5,7},{6,4},{7,5},{8,10},{9,11},{10,... | collective-permute-start | bytes 1843208 | tf_op jit(solution)/shard_map/ppermute | solution.py:252
  467.5 36.5 %collective-permute-start.5 = (f32[256,768]{1,0:T(8,128)S(1)}, f32[256,768]{1,0:T(8,128)S(1)}, u32[]{:S(2)}, u32[]{:S(2)}) collective-permute-start(f32[256,768]{1,0:T(8,128)S(1)} %fusion.45), channel_id=1, source_target_pairs={{0,2},{1,3},{2,0},{3,1},{4,6},{5,7},{6,4},{7,5},{8,10},{9,11},{10,... | collective-permute-start | bytes 2359304 | tf_op jit(solution)/shard_map/ppermute | solution.py:252
  469.4 36.6 %collective-permute-start.9 = (f32[256,768]{1,0:T(8,128)S(1)}, f32[256,768]{1,0:T(8,128)S(1)}, u32[]{:S(2)}, u32[]{:S(2)}) collective-permute-start(f32[256,768]{1,0:T(8,128)S(1)} %constant_dynamic-slice_fusion), channel_id=1, source_target_pairs={{0,1},{1,0},{2,3},{3,2},{4,5},{5,4},{6,7},{7,6},{8,9},{9,8},{10,11... | collective-permute-start | bytes 2359304 | tf_op jit(solution)/shard_map/ppermute | solution.py:252
  505.3 54.7 %collective-permute-start.6 = (f32[2,256,768]{2,1,0:T(8,128)}, f32[2,256,768]{2,1,0:T(8,128)}, u32[]{:S(2)}, u32[]{:S(2)}) collective-permute-start(f32[2,256,768]{2,1,0:T(8,128)} %pad_maximum_fusion.6), channel_id=1, source_target_pairs={{0,1},{1,0},{2,3},{3,2},{4,5},{5,4},{6,7},{7,6},{8,9},{9,8},{10,11... | collective-permute-start | bytes 4718600 | tf_op jit(solution)/shard_map/ppermute | solution.py:252
  506.1 50.0 %copy-start.21 = (f32[256,768]{1,0:T(8,128)}, f32[256,768]{1,0:T(8,128)S(1)}, u32[]{:S(2)}) copy-start(f32[256,768]{1,0:T(8,128)S(1)} %dynamic-slice_add_fusion) | copy-start | bytes 2359300
  506.1 48.6 %collective-permute-start.10 = (f32[256,768]{1,0:T(8,128)S(1)}, f32[256,768]{1,0:T(8,128)S(1)}, u32[]{:S(2)}, u32[]{:S(2)}) collective-permute-start(f32[256,768]{1,0:T(8,128)S(1)} %dynamic-slice_add_fusion), channel_id=1, source_target_pairs={{0,2},{1,3},{2,0},{3,1},{4,6},{5,7},{6,4},{7,5},{8,10},{9,11},{10,... | collective-permute-start | bytes 2359304 | tf_op jit(solution)/shard_map/ppermute | solution.py:252
  556.2 51.4 %collective-permute-start.11 = (f32[2,256,768]{2,1,0:T(8,128)}, f32[2,256,768]{2,1,0:T(8,128)}, u32[]{:S(2)}, u32[]{:S(2)}) collective-permute-start(f32[2,256,768]{2,1,0:T(8,128)} %pad_maximum_fusion.7), channel_id=1, source_target_pairs={{0,1},{1,0},{2,3},{3,2},{4,5},{5,4},{6,7},{7,6},{8,9},{9,8},{10,11... | collective-permute-start | bytes 4718600 | tf_op jit(solution)/shard_map/ppermute | solution.py:252
  563.2 32.4 %collective-permute-start.14 = (f32[32,768]{1,0:T(8,128)S(1)}, f32[32,768]{1,0:T(8,128)S(1)}, u32[]{:S(2)}, u32[]{:S(2)}) collective-permute-start(f32[32,768]{1,0:T(8,128)S(1)} %slice.270), channel_id=1, source_target_pairs={{0,2},{1,3},{2,0},{3,1},{4,6},{5,7},{6,4},{7,5},{8,10},{9,11},{10,... | collective-permute-start | bytes 294920 | tf_op jit(solution)/shard_map/ppermute | solution.py:252
  563.2 32.4 %copy-start.45 = (f32[64,768]{1,0:T(8,128)S(1)}, f32[64,768]{1,0:T(8,128)}, u32[]{:S(2)}) copy-start(f32[64,768]{1,0:T(8,128)} %reduce-scatter.9.cloned.1.call-done) | copy-start | bytes 589828
  564.8 42.8 %copy-start.22 = (f32[256,768]{1,0:T(8,128)S(1)}, f32[256,768]{1,0:T(8,128)}, u32[]{:S(2)}) copy-start(f32[256,768]{1,0:T(8,128)} %copy-done.21) | copy-start | bytes 2359300
  564.8 42.8 %copy-start.27 = (f32[256,768]{1,0:T(8,128)S(1)}, f32[256,768]{1,0:T(8,128)}, u32[]{:S(2)}) copy-start(f32[256,768]{1,0:T(8,128)} %copy-done.26) | copy-start | bytes 2359300
  (35 other events, 49.6 us)
Sparse Core Ops, SparseCore 0:
  42.1 40.1 all-gather.6
  143.8 33.9 all-gather.14
  257.2 41.3 reduce-scatter.6
  302.3 48.0 reduce-scatter.4
  354.3 78.2 reduce-scatter.10
  436.7 38.4 reduce-scatter.8
  477.1 24.0 all-gather.10
  503.3 27.3 all-gather.8
  532.7 39.7 all-gather.12

commit v3 on v2

--- a/solution.py
+++ b/solution.py
@@ -10,7 +10,8 @@
 from jax.sharding import PartitionSpec as P
 
 HEAD_DIM = 64
-STEP = 32
+STEP_BITS = 5
+STEP = 1 << STEP_BITS
 NEAR = 1
 FAR = 2
 MASKED = -1e30
@@ -54,13 +55,13 @@
     return np.concatenate(parts, axis=0)
 
 
-def sinusoid(coords, model_width):
-    quarter = model_width // 4
-    table = jnp.asarray(angle_tables(model_width))
-    slot = lax.broadcasted_iota(jnp.int32, (coords.shape[0], 2 * STEP), 1)
-    hit = (slot == (coords // STEP)[:, None]) | (slot == (coords % STEP)[:, None] + STEP)
-    hit = hit.astype(jnp.bfloat16)
-    looked = mm(jnp.concatenate([hit, hit, hit], axis=1), table)
+def sinusoid(coord, table_ref):
+    quarter = table_ref.shape[1] // 4
+    slot = lax.broadcasted_iota(jnp.int32, (2 * STEP, coord.shape[1]), 0)
+    coarse = coord >> STEP_BITS
+    fine = (coord & (STEP - 1)) + STEP
+    hit = ((slot == coarse) | (slot == fine)).astype(jnp.float32).astype(jnp.bfloat16)
+    looked = mm_tn(jnp.concatenate([hit, hit, hit], axis=0), table_ref[...])
     sin_a, cos_a, sin_b, cos_b = [looked[:, k * quarter : (k + 1) * quarter] for k in range(4)]
     return jnp.concatenate([sin_a * cos_b + cos_a * sin_b, cos_a * cos_b - sin_a * sin_b], axis=1)
 
@@ -79,13 +80,17 @@
     return raised * (1.0 / jnp.sum(raised, axis=0, keepdims=True))
 
 
-def attend_kernel(heads, lengths_ref, x_ref, pos_ref, wqkv_ref, wpos_ref, mixed_ref, proj_ref):
+def attend_kernel(
+    heads, lengths_ref, x_ref, coords_ref, table_ref, wqkv_ref, wpos_ref, mixed_ref, proj_ref, pos_ref
+):
     length = lengths_ref[pl.program_id(0)]
     factor = 1.0 / math.sqrt(3.0 * HEAD_DIM)
     rows = x_ref[0]
     for part in range(3):
         proj_ref[0, part] = mm(rows, wqkv_ref[part]).astype(jnp.bfloat16)
-    position = pos_ref[0]
+    sides = [sinusoid(coords_ref[0, axis : axis + 1], table_ref) for axis in range(2)]
+    position = jnp.concatenate(sides, axis=1).astype(jnp.bfloat16)
+    pos_ref[0] = position
     for part in range(2):
         proj_ref[0, 3 + part] = mm(position, wpos_ref[part]).astype(jnp.bfloat16)
     here = proj_ref.at[0]
@@ -97,7 +102,7 @@
         mixed_ref[0, :, head * HEAD_DIM : (head + 1) * HEAD_DIM] = mixed.T
 
 
-def attend(lengths, tokens, position, w_qkv, w_pos):
+def attend(lengths, tokens, coords, table, w_qkv, w_pos):
     pages, length, width = tokens.shape
     columns = w_qkv.shape[2]
     page = lambda i, lens: (i, 0, 0)
@@ -107,32 +112,35 @@
         out_shape=(
             jax.ShapeDtypeStruct((pages, length, columns), jnp.float32),
             jax.ShapeDtypeStruct((pages, 5, length, columns), jnp.bfloat16),
+            jax.ShapeDtypeStruct((pages, length, width), jnp.bfloat16),
         ),
         grid_spec=pltpu.PrefetchScalarGridSpec(
             num_scalar_prefetch=1,
             grid=(pages,),
             in_specs=[
                 pl.BlockSpec((1, length, width), page),
-                pl.BlockSpec((1, length, width), page),
+                pl.BlockSpec((1,) + coords.shape[1:], page),
+                pl.BlockSpec(table.shape, lambda i, lens: (0, 0)),
                 pl.BlockSpec(w_qkv.shape, whole),
                 pl.BlockSpec(w_pos.shape, whole),
             ],
             out_specs=[
                 pl.BlockSpec((1, length, columns), page),
                 pl.BlockSpec((1, 5, length, columns), lambda i, lens: (i, 0, 0, 0)),
+                pl.BlockSpec((1, length, width), page),
             ],
         ),
-        compiler_params=pltpu.CompilerParams(vmem_limit_bytes=40 << 20),
+        compiler_params=pltpu.CompilerParams(vmem_limit_bytes=48 << 20),
         cost_estimate=pl.CostEstimate(
             flops=2 * pages * length * columns * (5 * width + 4 * length),
             transcendentals=pages * length * length * columns // HEAD_DIM,
             bytes_accessed=pages * length * (4 * width + 14 * columns),
         ),
         name="attend",
-    )(lengths, tokens, position, w_qkv, w_pos)
-
-
-def attend_back_kernel(heads, scalars_ref, own_ref, far_ref, dm_ref, d_ref, dp_ref):
+    )(lengths, tokens, coords, table, w_qkv, w_pos)
+
+
+def attend_back_kernel(heads, scalars_ref, own_ref, far_ref, dm_ref, d_ref):
     length = scalars_ref[1]
     factor = 1.0 / math.sqrt(3.0 * HEAD_DIM)
     columns = heads * HEAD_DIM
@@ -152,15 +160,14 @@
             by_keys = mm_tn(jnp.concatenate([k, pk], axis=1), d_scores).T
             by_key, by_pos_key = by_keys[:, :HEAD_DIM], by_keys[:, HEAD_DIM:]
             grads = (
-                ((by_key + by_pos_key) * factor, 0, d_ref, 3),
-                ((by_query + by_pos_query) * factor, 1, d_ref, 3),
-                (d_values, 2, d_ref, 3),
-                (by_key * factor, 0, dp_ref, 2),
-                (by_query * factor, 1, dp_ref, 2),
+                (by_key + by_pos_key) * factor,
+                (by_query + by_pos_query) * factor,
+                d_values,
+                by_key * factor,
+                by_query * factor,
             )
-            for value, part, ref, parts in grads:
-                to = (side * parts + part) * columns + head * HEAD_DIM
-                ref[:, to : to + HEAD_DIM] = value.astype(jnp.bfloat16)
+            for part, value in enumerate(grads):
+                d_ref[part, :, at : at + HEAD_DIM] = value.astype(jnp.bfloat16)
 
 
 def attend_back(scalars, proj, far_proj, d_mixed):
@@ -168,10 +175,7 @@
     heads = columns // HEAD_DIM
     return pl.pallas_call(
         partial(attend_back_kernel, heads),
-        out_shape=(
-            jax.ShapeDtypeStruct((length, 6 * columns), jnp.bfloat16),
-            jax.ShapeDtypeStruct((length, 4 * columns), jnp.bfloat16),
-        ),
+        out_shape=jax.ShapeDtypeStruct((parts, length, 2 * columns), jnp.bfloat16),
         grid_spec=pltpu.PrefetchScalarGridSpec(
             num_scalar_prefetch=1,
             grid=(1,),
@@ -180,10 +184,7 @@
                 pl.BlockSpec((parts, length, columns), lambda i, s: (0, 0, 0)),
                 pl.BlockSpec((length, 2 * columns), lambda i, s: (0, 0)),
             ],
-            out_specs=[
-                pl.BlockSpec((length, 6 * columns), lambda i, s: (0, 0)),
-                pl.BlockSpec((length, 4 * columns), lambda i, s: (0, 0)),
-            ],
+            out_specs=pl.BlockSpec((parts, length, 2 * columns), lambda i, s: (0, 0, 0)),
         ),
         compiler_params=pltpu.CompilerParams(vmem_limit_bytes=40 << 20),
         cost_estimate=pl.CostEstimate(
@@ -193,6 +194,89 @@
         ),
         name="attend_back",
     )(scalars, proj, far_proj, d_mixed)
+
+
+def weight_grads_kernel(count, scalars_ref, x_ref, pos_ref, d_ref, db_ref, mixed_ref, vec_ref, out_ref):
+    group = scalars_ref[0]
+    rows = x_ref.shape[1] // count
+    pairs = [(x_ref, d_ref.at[k]) for k in range(3)]
+    pairs += [(pos_ref, d_ref.at[k]) for k in range(3, 5)]
+    pairs += [(db_ref, mixed_ref)]
+    for part, (left, right) in enumerate(pairs):
+        product = mm_tn(left[...], right[...])
+        for block in range(count):
+            out_ref[block ^ group, part * rows : (part + 1) * rows] = product[
+                block * rows : (block + 1) * rows
+            ]
+    for block in range(count):
+        out_ref[block ^ group, len(pairs) * rows :] = (
+            vec_ref[...] if block == 0 else jnp.zeros_like(vec_ref)
+        )
+
+
+def weight_grads(count, scalars, rows, pos_rows, d_heads, d_branch, mixed, vectors):
+    length, width = rows.shape
+    wide = d_heads.shape[2]
+    block = 6 * (width // count) + vectors.shape[0]
+    return pl.pallas_call(
+        partial(weight_grads_kernel, count),
+        out_shape=jax.ShapeDtypeStruct((count, block, wide), jnp.float32),
+        in_specs=[pl.BlockSpec(memory_space=pltpu.SMEM)] + [pl.BlockSpec(memory_space=pltpu.VMEM)] * 6,
+        out_specs=pl.BlockSpec(memory_space=pltpu.VMEM),
+        compiler_params=pltpu.CompilerParams(vmem_limit_bytes=48 << 20),
+        cost_estimate=pl.CostEstimate(
+            flops=12 * length * width * wide,
+            transcendentals=0,
+            bytes_accessed=4 * count * block * wide + 10 * length * wide + 6 * length * width,
+        ),
+        name="weight_grads",
+    )(scalars, rows, pos_rows, d_heads, d_branch, mixed, vectors)
+
+
+def place_grads_kernel(scalars_ref, low_ref, high_ref, qkv_ref, pos_ref, out_ref, vec_ref, turned):
+    group = scalars_ref[0]
+    half = low_ref.shape[0]
+    count = 2 * half
+    rows = qkv_ref.shape[1] // count
+    for block in range(count):
+        place = block ^ group
+        index = place >> 1
+        upper = (place & 1) == 1
+        at = slice(block * rows, (block + 1) * rows)
+        for part in range(6):
+            cut = slice(part * rows, (part + 1) * rows)
+            value = jnp.where(upper, high_ref[index, cut], low_ref[index, cut])
+            if part < 3:
+                qkv_ref[part, at] = value
+            elif part < 5:
+                pos_ref[part - 3, at] = value
+            else:
+                turned[at] = value
+        if block == 0:
+            vec_ref[...] = jnp.where(upper, high_ref[index, 6 * rows :], low_ref[index, 6 * rows :])
+    out_ref[...] = turned[...].T
+
+
+def place_grads(scalars, low, high, width):
+    columns = low.shape[2]
+    vec_rows = low.shape[1] - 6 * (width // (2 * low.shape[0]))
+    return pl.pallas_call(
+        place_grads_kernel,
+        out_shape=(
+            jax.ShapeDtypeStruct((3, width, columns), jnp.float32),
+            jax.ShapeDtypeStruct((2, width, columns), jnp.float32),
+            jax.ShapeDtypeStruct((columns, width), jnp.float32),
+            jax.ShapeDtypeStruct((vec_rows, columns), jnp.float32),
+        ),
+        in_specs=[pl.BlockSpec(memory_space=pltpu.SMEM)] + [pl.BlockSpec(memory_space=pltpu.VMEM)] * 2,
+        out_specs=[pl.BlockSpec(memory_space=pltpu.VMEM)] * 4,
+        scratch_shapes=[pltpu.VMEM((width, columns), jnp.float32)],
+        compiler_params=pltpu.CompilerParams(vmem_limit_bytes=40 << 20),
+        cost_estimate=pl.CostEstimate(
+            flops=0, transcendentals=0, bytes_accessed=16 * low.size
+        ),
+        name="place_grads",
+    )(scalars, low, high)
 
 
 def norm_parts(values):
@@ -261,31 +345,29 @@
     def take(value, index):
         return lax.dynamic_index_in_dim(value, index, 0, keepdims=False)
 
+    def group_swap(value, bit):
+        pairs = [(i, i ^ bit) for i in range(dp_size)]
+        return lax.ppermute(value, "dp", pairs)
+
+    def after(value, *others):
+        return lax.optimization_barrier((value,) + others)[0]
+
     out_rows = swap(my_rows(w_out).astype(f32), FAR)
     w_out_far = gather(out_rows).astype(bf16)
     unit_rows = jnp.concatenate([my_rows(w_in), my_rows(w_back)], axis=0).astype(f32)
     far_rows = swap(jnp.concatenate([unit_rows, b_in[None], jnp.zeros((7, units), f32)], axis=0), FAR)
+
+    table = jnp.asarray(angle_tables(width))
+    mixed_all, proj, position = attend(lengths, tokens, coords, table, w_qkv, w_pos)
+    far_rows = after(far_rows, mixed_all)
     b_in_far = far_rows[unit_rows.shape[0]]
     blocks = gather(far_rows[: unit_rows.shape[0]]).reshape(dp_size, unit_rows.shape[0], -1)
     in_rows = width // dp_size
     w_in_far = blocks[:, :in_rows].reshape(width, units).astype(bf16)
     w_back_far = blocks[:, in_rows:].reshape(units, width).astype(bf16)
-    head_rows = jnp.concatenate(
-        [my_rows(w_qkv.reshape(-1, columns)), my_rows(w_pos.reshape(-1, columns))], axis=0
-    ).astype(f32)
-    blocks = gather(swap(head_rows, FAR)).reshape(dp_size, head_rows.shape[0], columns)
-    qkv_rows = 3 * width // dp_size
-    w_qkv_far = blocks[:, :qkv_rows].reshape(3, width, columns).astype(bf16)
-    w_pos_far = blocks[:, qkv_rows:].reshape(2, width, columns).astype(bf16)
-
-    position = [
-        sinusoid(coords[:, axis].reshape(-1), width).astype(bf16) for axis in range(2)
-    ]
-    position = jnp.concatenate(position, axis=1).reshape(pages, length, width)
-    mixed_all, proj = attend(lengths, tokens, position, w_qkv, w_pos)
-
-    mixed_far = arrived(swap(take(mixed_all, 1 - page), FAR))
-    mixed = jnp.concatenate([take(mixed_all, page), mixed_far], axis=1).astype(bf16)
+
+    mixed_far = swap(take(mixed_all, 1 - page), FAR)
+    mixed = jnp.concatenate([take(mixed_all, page), arrived(mixed_far)], axis=1).astype(bf16)
     w_out_two = jnp.concatenate([w_out, w_out_far], axis=0)
     w_in_two = jnp.concatenate([w_in, w_in_far], axis=1)
     w_back_two = jnp.concatenate([w_back, w_back_far], axis=0)
@@ -295,7 +377,18 @@
     grad_out = take(cotangent, page).astype(f32)
 
     part = mm(mixed, w_out_two)
-    first = rows.astype(f32) + (part + swap(part, NEAR) + b_out)
+    other = swap(part, NEAR)
+    head_rows = jnp.concatenate(
+        [my_rows(w_qkv.reshape(-1, columns)), my_rows(w_pos.reshape(-1, columns))], axis=0
+    )
+    head_rows = swap(after(head_rows, part).astype(f32), FAR)
+    head_rows = after(head_rows, other)
+    blocks = gather(head_rows).reshape(dp_size, head_rows.shape[0], columns)
+    qkv_rows = 3 * width // dp_size
+    w_qkv_far = blocks[:, :qkv_rows].reshape(3, width, columns).astype(bf16)
+    w_pos_far = blocks[:, qkv_rows:].reshape(2, width, columns).astype(bf16)
+
+    first = rows.astype(f32) + (part + other + b_out)
     xhat_one, scale_one = norm_parts(first)
     normed = xhat_one * gain_one + shift_one
     normed_low = normed.astype(bf16)
@@ -313,41 +406,26 @@
     d_hidden = mm_nt(d_feed, w_back_two)
     d_pre = (d_hidden * slope).astype(bf16)
     part = mm_nt(d_pre, w_in_two)
-    d_normed = d_second + (part + swap(part, NEAR))
+    other = swap(part, NEAR)
+    d_normed = d_second + (part + other)
 
     half = length // 2
 
     def half_of(value, index):
         return lax.dynamic_slice_in_dim(value, index * half, half, 0)
 
-    def spread(mine, other):
-        both = jnp.stack([mine, other])
-        rest = swap(both, NEAR)
+    def spread(mine, far, rest):
+        both = jnp.stack([mine, far])
         out = jnp.stack([jnp.where(low == 0, both, rest), jnp.where(low == 0, rest, both)], axis=1)
         out = out.reshape(pages, length, width)
         return jnp.where(page == 0, out, out[::-1])
 
-    output = xhat_two * gain_two + shift_two
-    mine = half_of(output, low)
-    layer_out = arrived(spread(mine, swap(mine, FAR))).astype(bf16)
-
     def to_blocks(value):
         return value.reshape(dp_size, -1, value.shape[1])
 
     def in_first(rows_of):
         value = jnp.stack(rows_of + [jnp.zeros_like(rows_of[0])] * (8 - len(rows_of)))
-        return jnp.concatenate(
-            [value[None], jnp.zeros((dp_size - 1,) + value.shape, f32)], axis=0
-        )
-
-    def reduce_two(own, far):
-        both = jnp.concatenate(own + far, axis=1)
-        total = lax.psum_scatter(
-            both.reshape(-1, both.shape[2]), "dp", scatter_dimension=0, tiled=True
-        )
-        cut = total.shape[0] // 2
-        total = total[:cut] + swap(total[cut:], FAR)
-        return lax.all_gather(total, "dp", axis=0, tiled=True).reshape(dp_size, cut, -1)
+        return jnp.concatenate([value[None], jnp.zeros((dp_size - 1,) + value.shape, f32)], axis=0)
 
     d_w_back = mm_tn(hidden, d_feed)
     d_w_in = [mm_tn(normed_low, d_pre[:, :units]), mm_tn(normed_low, d_pre[:, units:])]
@@ -357,14 +435,10 @@
         jnp.sum(grad_out * xhat_two, axis=0),
         jnp.sum(grad_out, axis=0),
     ]
-    ffn = reduce_two(
-        [to_blocks(d_w_in[0]), to_blocks(d_w_back[:units]), in_first([d_b_in[:units]] + vectors)],
-        [to_blocks(d_w_in[1]), to_blocks(d_w_back[units:]), in_first([d_b_in[units:]] + vectors)],
-    )
-    grad_w_in = ffn[:, :in_rows].reshape(width, units)
-    grad_w_back = ffn[:, in_rows : in_rows + units // dp_size].reshape(units, width)
-    vectors = ffn[0, in_rows + units // dp_size :]
-    grad_b_in, grad_b_back, grad_gain_two, grad_shift_two = vectors[0], vectors[1], vectors[2], vectors[3]
+    own = [to_blocks(d_w_in[0]), to_blocks(d_w_back[:units]), in_first([d_b_in[:units]] + vectors)]
+    far = [to_blocks(d_w_in[1]), to_blocks(d_w_back[units:]), in_first([d_b_in[units:]] + vectors)]
+    ffn = jnp.concatenate(own + far, axis=1)
+    ffn = lax.psum_scatter(ffn.reshape(-1, width), "dp", scatter_dimension=0, tiled=True)
 
     d_first = norm_back(d_normed, gain_one, xhat_one, scale_one)
     d_branch = d_first.astype(bf16)
@@ -372,39 +446,85 @@
     far_proj = [mm(rows, w_qkv_far[k]).astype(bf16) for k in range(3)]
     far_proj += [mm(pos_rows, w_pos_far[k]).astype(bf16) for k in range(2)]
     scalars = jnp.stack([page, take(lengths, page)])
-    d_heads, d_pos = attend_back(scalars, proj, jnp.stack(far_proj), d_mixed)
-    part = mm_nt(d_heads[:, : 3 * columns], jnp.concatenate(list(w_qkv), axis=1))
-    part = part + mm_nt(d_heads[:, 3 * columns :], jnp.concatenate(list(w_qkv_far), axis=1))
-    mine = half_of(part, low) + swap(half_of(part, 1 - low), NEAR) + half_of(d_first, low)
-    grad_tokens = spread(mine, swap(mine, FAR))
-
-    d_w_out = mm_tn(mixed, d_branch)
-    vectors = [
-        column_sum(d_branch),
-        jnp.sum(d_normed * xhat_one, axis=0),
-        jnp.sum(d_normed, axis=0),
+    d_heads = attend_back(scalars, proj, jnp.stack(far_proj), d_mixed)
+    part = mm_nt(d_heads[0], jnp.concatenate([w_qkv[0], w_qkv_far[0]], axis=1))
+    for k in (1, 2):
+        part = part + mm_nt(d_heads[k], jnp.concatenate([w_qkv[k], w_qkv_far[k]], axis=1))
+
+    chunks = 2
+    piece = half // chunks
+
+    def pieces(value):
+        return [value[k * piece : (k + 1) * piece] for k in range(chunks)]
+
+    sent = [swap(value, NEAR) for value in pieces(half_of(part, 1 - low))]
+    base = pieces(half_of(part, low) + half_of(d_first, low))
+    mine = [value + other_value for value, other_value in zip(base, sent)]
+    far_mine = [swap(value, FAR) for value in mine]
+    rest = [swap(jnp.stack(pair), NEAR) for pair in zip(mine, far_mine)]
+    grad_tokens = spread(
+        jnp.concatenate(mine, axis=0), jnp.concatenate(far_mine, axis=0), jnp.concatenate(rest, axis=1)
+    )
+
+    output = xhat_two * gain_two + shift_two
+    out_mine = after(half_of(output, low), other)
+    out_far = after(swap(out_mine, FAR), d_heads)
+    out_rest = swap(after(jnp.stack([out_mine, out_far]), mine[-1]), NEAR)
+    out_rest = after(out_rest, far_mine[-1])
+    layer_out = arrived(spread(out_mine, out_far, out_rest)).astype(bf16)
+
+    vectors = jnp.stack(
+        [column_sum(d_branch), jnp.sum(d_normed * xhat_one, axis=0), jnp.sum(d_normed, axis=0)]
+    ).reshape(-1, columns)
+    vectors = jnp.pad(vectors, ((0, -vectors.shape[0] % 8), (0, 0)))
+    vectors = jnp.concatenate([vectors, vectors], axis=1)
+    scalars = jnp.reshape(group, (1,))
+    total = weight_grads(dp_size, scalars, rows, pos_rows, d_heads, d_branch, mixed, vectors)
+
+    bits = [1 << k for k in range(dp_size.bit_length() - 1)]
+
+    def fold(value, bit_list, axis):
+        shape = value.shape[1:]
+        for bit in bit_list:
+            value = value.reshape(((-1, 2) if axis else (2, -1)) + shape)
+            kept, given = (value[:, 0], value[:, 1]) if axis else (value[0], value[1])
+            value = kept + group_swap(given, bit)
+        return value.reshape(shape)
+
+    def unfold(value, bit_list, axis):
+        shape = value.shape
+        value = value[None]
+        for bit in bit_list:
+            value = jnp.stack([value, group_swap(value, bit)], axis=axis).reshape((-1,) + shape)
+        return value
+
+    cut = total.shape[1] // 16 * 8
+    total = total.reshape(dp_size // 2, 2, total.shape[1], -1)
+    total = total[:, 0] + group_swap(total[:, 1], bits[0])
+    more = bits[1:]
+    upper = fold(total[:, :cut], more, 1)
+    lower = fold(total[:, cut:], more[::-1], 0)
+    total = jnp.concatenate([upper, lower], axis=0)
+    total = total[:, :columns] + swap(total[:, columns:], FAR)
+    upper = unfold(total[:cut], more, 0)
+    lower = unfold(total[cut:], more[::-1], 1)
+    total = jnp.concatenate([upper, lower], axis=1)
+    grad_w_qkv, grad_w_pos, grad_w_out, vectors = place_grads(
+        scalars, total, group_swap(total, bits[0]), width
+    )
+    vectors = vectors.reshape(-1)
+    grad_b_out, grad_gain_one, grad_shift_one = [
+        vectors[k * width : (k + 1) * width] for k in range(3)
     ]
-    vectors = in_first(vectors)
-    grads_x = mm_tn(rows, d_heads)
-    grads_p = mm_tn(pos_rows, d_pos)
-    attn = reduce_two(
-        [to_blocks(d_w_out[:columns]), vectors],
-        [to_blocks(d_w_out[columns:]), vectors],
-    )
-    out_block = columns // dp_size
-    grad_w_out = attn[:, :out_block].reshape(columns, width)
-    grad_b_out, grad_gain_one, grad_shift_one = [attn[0, out_block + k] for k in range(3)]
-
-    def reduce_columns(value):
-        total = lax.psum_scatter(value, "dp", scatter_dimension=0, tiled=True)
-        cut = total.shape[1] // 2
-        total = total[:, :cut] + swap(total[:, cut:], FAR)
-        return lax.all_gather(total, "dp", axis=0, tiled=True)
-
-    grads_x = reduce_columns(grads_x)
-    grads_p = reduce_columns(grads_p)
-    grad_w_qkv = jnp.stack([grads_x[:, k * columns : (k + 1) * columns] for k in range(3)])
-    grad_w_pos = jnp.stack([grads_p[:, k * columns : (k + 1) * columns] for k in range(2)])
+
+    ffn = after(ffn, mine[-1])
+    count = ffn.shape[0] // 2
+    ffn = ffn[:count] + swap(ffn[count:], FAR)
+    ffn = lax.all_gather(ffn, "dp", axis=0, tiled=True).reshape(dp_size, count, -1)
+    grad_w_in = ffn[:, :in_rows].reshape(width, units)
+    grad_w_back = ffn[:, in_rows : in_rows + units // dp_size].reshape(units, width)
+    vectors = ffn[0, in_rows + units // dp_size :]
+    grad_b_in, grad_b_back, grad_gain_two, grad_shift_two = vectors[0], vectors[1], vectors[2], vectors[3]
     return (
         layer_out,
         grad_tokens,

time: 642 us -> 584 us (0.910)
  waiting for transfers between devices: 396 us -> 328 us
  local copies, waits for them, and re-layouts: 75.9 us -> 94.4 us
  matrix products: 37 us -> 24.4 us
  Pallas kernels: 15 us -> 25.3 us
  blocking collectives: 20.9 us -> 12.8 us
    reduce_scatter x4 -> x1, waiting for transfers between devices: 123 us -> 0.01 us  [body(): lax.psum_scatter(ffn.reshape(-1, width), 'dp', scatter_dimension=0, tiled...]
    ppermute x0 -> x10, waiting for transfers between devices: none -> 46.6 us  [group_swap(): return lax.ppermute(value, 'dp', pairs)]
    ppermute x16 -> x17, starting transfers between devices: 33.6 us -> 22.1 us  [swap(): return lax.ppermute(value, 'mp', pairs)]
    all_gather x1 -> x0, blocking collectives: 10.5 us -> none  [reduce_two(): lax.all_gather(total, 'dp', axis=0, tiled=True).reshape(dp_size, cut, -1)]
    ppermute x0 -> x10, starting transfers between devices: none -> 9.8 us  [group_swap(): return lax.ppermute(value, 'dp', pairs)]
    dot_general x14 -> x8, matrix products: 17.2 us -> 8.34 us  [mm(): return jnp.dot(left, right, preferred_element_type=jnp.float32)]
    ppermute x0 -> x4, local copies, waits for them, and re-layouts: none -> 7.74 us  [the longest x3 5.67 us: group_swap(): return lax.ppermute(value, 'dp', pairs)]
    pallas_call x1 -> x3, Pallas kernels: 7.4 us -> 14.8 us  [the longest x1 7.56 us: attend_back(): pl.pallas_call(partial(attend_back_kernel, heads), out_shape=jax.ShapeDty...]
  transfers between devices with their start and end apart: 25 -> 31, of which waited for: 15 -> 19; matrix products, arithmetic and copies ran while one was open for 19% -> 21% of each run, Pallas kernels for 1% -> 4%
where the time goes in v3:
time: 584 us; the launch traced here: 575 us
  waiting for transfers between devices  328 us (56%)
  local copies, waits for them, and re-layouts  94.4 us (16%)
  other arithmetic  42.8 us (7%)
  starting transfers between devices  32.3 us (6%)
  Pallas kernels  25.3 us (4%)
  matrix products  24.4 us (4%)
  between operations  15.6 us (3%)
  blocking collectives  12.8 us (2%)
    ppermute x17, waiting for transfers between devices, swap(): return lax.ppermute(value, 'mp', pairs)  277 us
    ppermute x10, waiting for transfers between devices, group_swap(): return lax.ppermute(value, 'dp', pairs)  46.6 us
    unnamed x145, local copies, waits for them, and re-layouts  33.7 us
    ppermute x17, starting transfers between devices, swap(): return lax.ppermute(value, 'mp', pairs)  22.1 us
    all_gather x1, blocking collectives, gather(): return arrived(lax.all_gather(value, 'dp', axis=0, tiled=True))  12.8 us
  transfers between devices with their start and end apart: 31, of which 19 were waited for; matrix products, arithmetic and copies ran while one was open for 21% of the time, Pallas kernels for 4%

profile of v3, /device:TPU:0, one launch (start us, length us, event | category | flops | bytes accessed | tf_op | source)
XLA Modules:
  0.0 575.2 jit_solution(15428064214872656075)
XLA Ops:
  10.1 4.0 collective-permute-start.3
  15.0 10.5 %attend.1 = (f32[2,512,192]{2,1,0:T(8,128)S(1)}, bf16[2,5,512,192]{3,2,1,0:T(8,128)(2,1)}, bf16[2,512,768]{2,1,0:T(8,128)(2,1)S(1)}) custom-call(s32[2]{0:T(128)S(1)} %copy-done.5, bf16[2,512,768]{2,1,0:T(8,128)(2,1)} %x_ref.1, s32[2,2,512]{2,1,0:T(2,128)S(1)} %copy-done.6, bf16[192,768]{1,0:T(8,128)(2,1)S(1)} %copy-done.7, ...), custom_call_target="tpu_custom_call" | custom-call | flops 2315255808 | bytes 5898240 | tf_op jit(solution)/shard_map/attend/pallas_call | solution.py:110
  26.7 14.8 %collective-permute-done.3 = f32[200,768]{1,0:T(8,128)} collective-permute-done((f32[200,768]{1,0:T(8,128)}, f32[200,768]{1,0:T(8,128)}, u32[]{:S(2)}, u32[]{:S(2)}) %collective-permute-start.3) | collective-permute-done | bytes 614432 | tf_op jit(solution)/shard_map/ppermute | solution.py:336
  44.4 2.9 collective-permute-start
  48.6 2.5 collective-permute-done.1
  51.1 12.8 %all_gather.12 = f32[192,768]{1,0:T(8,128)S(1)} all-gather(f32[24,768]{1,0:T(8,128)S(1)} %collective-permute-done.1), channel_id=1, replica_groups=mesh['dp'=8,'mp'=4] {'dp'}, dimensions={0}, use_global_device_ids=true | all-gather | bytes 663552 | tf_op jit(solution)/shard_map/all_gather | solution.py:343
  64.0 8.2 %collective-permute-done = f32[512,192]{1,0:T(8,128)S(1)} collective-permute-done((f32[512,192]{1,0:T(8,128)}, f32[512,192]{1,0:T(8,128)S(1)}, u32[]{:S(2)}, u32[]{:S(2)}) %collective-permute-start) | collective-permute-done | bytes 393248 | tf_op jit(solution)/shard_map/ppermute | solution.py:336
  73.9 34.3 %collective-permute-done.2 = f32[512,768]{1,0:T(8,128)S(1)} collective-permute-done((f32[512,768]{1,0:T(8,128)S(1)}, f32[512,768]{1,0:T(8,128)S(1)}, u32[]{:S(2)}, u32[]{:S(2)}) %collective-permute-start.2) | collective-permute-done | bytes 1572896 | tf_op jit(solution)/shard_map/ppermute | solution.py:336
  110.0 2.7 multiply_convert_fusion
  115.3 3.4 multiply_convert_fusion.2
  118.7 2.5 fusion.17
  127.0 3.3 collective-permute-start.7
  131.6 31.2 %collective-permute-done.7 = f32[480,192]{0,1:T(8,128)S(1)} collective-permute-done((f32[480,192]{0,1:T(8,128)S(1)}, f32[480,192]{0,1:T(8,128)S(1)}, u32[]{:S(2)}, u32[]{:S(2)}) %collective-permute-start.7) | collective-permute-done | bytes 368672 | tf_op jit(solution)/shard_map/ppermute | solution.py:336
  164.1 2.9 fusion.74
  172.3 4.8 convert_reduce_fusion
  177.1 2.6 fusion.36
  195.2 3.7 all-gather.9.cloned.1.call-done
  198.9 2.5 multiply_convert_fusion.1
  201.6 2.6 fusion.18
  208.1 2.1 copy.157
  210.2 2.1 copy.163
  212.3 2.1 squeeze.102
  214.4 2.1 copy.161
  216.5 2.1 squeeze.101
  222.9 18.2 %collective-permute-done.5 = f32[512,768]{1,0:T(8,128)} collective-permute-done((f32[512,768]{1,0:T(8,128)}, f32[512,768]{1,0:T(8,128)}, u32[]{:S(2)}, u32[]{:S(2)}) %collective-permute-start.5) | collective-permute-done | bytes 1572896 | tf_op jit(solution)/shard_map/ppermute | solution.py:336
  241.1 3.0 multiply_reduce_fusion
  249.4 7.6 %attend_back.1.d_ref = bf16[5,512,384]{2,1,0:T(8,128)(2,1)S(1)} custom-call(s32[2]{0:T(128)S(1)} %pad_add_fusion.scalars_ref, bf16[2,5,512,192]{3,2,1,0:T(8,128)(2,1)S(1)} %copy-done.10, bf16[5,512,192]{2,1,0:T(8,128)(2,1)S(1)} %copy-done.9, bf16[512,384]{1,0:T(8,128)(2,1)S(1)} %convolution_convert_fusion.dm_ref), custom_call_target="tpu_custom_call" | custom-call | flops 1811939328 | bytes 4325376 | tf_op jit(solution)/shard_map/attend_back/pallas_call | solution.py:176
  257.0 5.8 %weight_grads.1 = f32[8,592,384]{2,1,0:T(8,128)} custom-call(s32[1]{0:T(128)} %bitcast.41.scalars_ref, bf16[512,768]{1,0:T(8,128)(2,1)S(1)} %get-tuple-element.150.x_ref, bf16[512,768]{1,0:T(8,128)(2,1)S(1)} %dynamic-slice_bitcast_fusion.pos_ref, bf16[5,512,384]{2,1,0:T(8,128)(2,1)S(1)} %attend_back.1.d_ref, bf16[512,768]{1,0:T(8,128)(2,1)S(1)} %get-tuple-element.142.db_ref, ...), custom_call_target="tpu_custom_call" | custom-call | flops 1811939328 | bytes 11599872 | tf_op jit(solution)/shard_map/weight_grads/pallas_call | solution.py:221
  262.8 5.0 slice_bitcast_fusion
  273.4 10.0 %collective-permute-done.11 = f32[128,768]{1,0:T(8,128)S(1)} collective-permute-done((f32[128,768]{1,0:T(8,128)}, f32[128,768]{1,0:T(8,128)S(1)}, u32[]{:S(2)}, u32[]{:S(2)}) %collective-permute-start.11) | collective-permute-done | bytes 393248 | tf_op jit(solution)/shard_map/ppermute | solution.py:336
  283.4 8.0 %collective-permute-done.8 = f32[128,768]{1,0:T(8,128)} collective-permute-done((f32[128,768]{1,0:T(8,128)}, f32[128,768]{1,0:T(8,128)}, u32[]{:S(2)}, u32[]{:S(2)}) %collective-permute-start.8) | collective-permute-done | bytes 393248 | tf_op jit(solution)/shard_map/ppermute | solution.py:336
  294.5 2.4 collective-permute-start.26
  296.9 27.1 %collective-permute-done.26 = f32[200,768]{1,0:T(8,128)S(1)} collective-permute-done((f32[200,768]{1,0:T(8,128)S(1)}, f32[200,768]{1,0:T(8,128)S(1)}, u32[]{:S(2)}, u32[]{:S(2)}) %collective-permute-start.26) | collective-permute-done | bytes 614432 | tf_op jit(solution)/shard_map/ppermute | solution.py:336
  325.0 3.5 fusion
  330.3 26.2 %collective-permute-done.18 = f32[2,296,384]{2,1,0:T(8,128)S(1)} collective-permute-done((f32[2,296,384]{2,1,0:T(8,128)S(1)}, f32[2,296,384]{2,1,0:T(8,128)S(1)}, u32[]{:S(2)}, u32[]{:S(2)}) %collective-permute-start.18) | collective-permute-done | bytes 909344 | tf_op jit(solution)/shard_map/ppermute | solution.py:350
  358.2 2.5 collective-permute-start.17
  360.7 18.1 %collective-permute-done.19 = f32[1,296,384]{2,1,0:T(8,128)S(1)} collective-permute-done((f32[1,296,384]{2,1,0:T(8,128)S(1)}, f32[1,296,384]{2,1,0:T(8,128)S(1)}, u32[]{:S(2)}, u32[]{:S(2)}) %collective-permute-start.19) | collective-permute-done | bytes 454688 | tf_op jit(solution)/shard_map/ppermute | solution.py:350
  381.9 2.7 collective-permute-start.6
  384.9 47.0 %collective-permute-done.20 = f32[592,192]{0,1:T(8,128)} collective-permute-done((f32[592,192]{0,1:T(8,128)}, f32[592,192]{0,1:T(8,128)}, u32[]{:S(2)}, u32[]{:S(2)}) %collective-permute-start.20) | collective-permute-done | bytes 454688 | tf_op jit(solution)/shard_map/ppermute | solution.py:336
  431.9 2.1 copy.174
  438.2 27.3 %collective-permute-done.12 = f32[128,768]{1,0:T(8,128)S(1)} collective-permute-done((f32[128,768]{1,0:T(8,128)S(1)}, f32[128,768]{1,0:T(8,128)S(1)}, u32[]{:S(2)}, u32[]{:S(2)}) %collective-permute-start.12) | collective-permute-done | bytes 393248 | tf_op jit(solution)/shard_map/ppermute | solution.py:336
  470.8 2.1 copy.175
  475.2 2.0 collective-permute-start.9
  477.3 1.9 pad_maximum_fusion.15
  490.4 48.3 %collective-permute-done.14 = f32[2,128,768]{2,1,0:T(8,128)} collective-permute-done((f32[2,128,768]{2,1,0:T(8,128)}, f32[2,128,768]{2,1,0:T(8,128)}, u32[]{:S(2)}, u32[]{:S(2)}) %collective-permute-start.14) | collective-permute-done | bytes 786464 | tf_op jit(solution)/shard_map/ppermute | solution.py:336
  546.8 3.1 copy.181.high_ref
  555.5 3.0 copy.182
  563.5 5.0 fusion.76
  (309 shorter events, 115.1 us)
Async XLA Ops:
  7.2 6.9 %copy-start.32 = (bf16[2,768,192]{1,2,0:T(8,128)(2,1)S(1)}, bf16[2,768,192]{1,2,0:T(8,128)(2,1)}, u32[]{:S(2)}) copy-start(bf16[2,768,192]{1,2,0:T(8,128)(2,1)} %param.21) | copy-start | bytes 1769476
  7.2 102.8 %all-gather.5.cloned.1.call-start = ((), (), s32[]{:S(2)}) async-start(), calls=%async_computation.1 | async-start | bytes 5308416 | tf_op jit(solution)/shard_map/all_gather | solution.py:343
  10.1 31.4 %collective-permute-start.3 = (f32[200,768]{1,0:T(8,128)}, f32[200,768]{1,0:T(8,128)}, u32[]{:S(2)}, u32[]{:S(2)}) collective-permute-start(f32[200,768]{1,0:T(8,128)} %maximum_maximum_fusion), channel_id=1, source_target_pairs={{0,2},{1,3},{2,0},{3,1},{4,6},{5,7},{6,4},{7,5},{8,10},{9,11},{10,... | collective-permute-start | bytes 1843208 | tf_op jit(solution)/shard_map/ppermute | solution.py:336
  26.7 16.8 %copy-start.49 = (bf16[192,768]{1,0:T(8,128)(2,1)S(1)}, bf16[192,768]{1,0:T(8,128)(2,1)}, u32[]{:S(2)}) copy-start(bf16[192,768]{1,0:T(8,128)(2,1)} %param.22) | copy-start | bytes 884740
  43.4 155.5 %all-gather.9.cloned.1.call-start = ((), (), s32[]{:S(2)}) async-start(), calls=%async_computation.4 | async-start | bytes 3538944 | tf_op jit(solution)/shard_map/all_gather | solution.py:343
  43.5 7.6 %collective-permute-start.1 = (f32[24,768]{1,0:T(8,128)S(1)}, f32[24,768]{1,0:T(8,128)S(1)}, u32[]{:S(2)}, u32[]{:S(2)}) collective-permute-start(f32[24,768]{1,0:T(8,128)S(1)} %dynamic-slice_convert_fusion.1), channel_id=1, source_target_pairs={{0,2},{1,3},{2,0},{3,1},{4,6},{5,7},{6,4},{7,5},{8,10},{9,11},{10,... | collective-permute-start | bytes 221192 | tf_op jit(solution)/shard_map/ppermute | solution.py:336
  44.4 27.8 %collective-permute-start = (f32[512,192]{1,0:T(8,128)}, f32[512,192]{1,0:T(8,128)S(1)}, u32[]{:S(2)}, u32[]{:S(2)}) collective-permute-start(f32[512,192]{1,0:T(8,128)} %dynamic-slice_bitcast_fusion.2), channel_id=1, source_target_pairs={{0,2},{1,3},{2,0},{3,1},{4,6},{5,7},{6,4},{7,5},{8,10},{9,11},{10,... | collective-permute-start | bytes 1179656 | tf_op jit(solution)/shard_map/ppermute | solution.py:336
  64.0 9.1 %copy-start.41 = (bf16[192,768]{1,0:T(8,128)(2,1)}, bf16[192,768]{1,0:T(8,128)(2,1)S(1)}, u32[]{:S(2)}) copy-start(bf16[192,768]{1,0:T(8,128)(2,1)S(1)} %multiply_convert_fusion.3) | copy-start | bytes 884740
  72.3 35.9 %copy-start.48 = (bf16[2,512,768]{2,1,0:T(8,128)(2,1)S(1)}, bf16[2,512,768]{2,1,0:T(8,128)(2,1)}, u32[]{:S(2)}) copy-start(bf16[2,512,768]{2,1,0:T(8,128)(2,1)} %x_ref.1) | copy-start | bytes 4718596
  72.3 35.9 %copy-start.62 = (f32[768]{0:T(1024)S(1)}, f32[768]{0:T(1024)}, u32[]{:S(2)}) copy-start(f32[768]{0:T(1024)} %param.23) | copy-start | bytes 9220
  73.0 35.1 %collective-permute-start.2 = (f32[512,768]{1,0:T(8,128)S(1)}, f32[512,768]{1,0:T(8,128)S(1)}, u32[]{:S(2)}, u32[]{:S(2)}) collective-permute-start(f32[512,768]{1,0:T(8,128)S(1)} %fusion.59), channel_id=1, source_target_pairs={{0,1},{1,0},{2,3},{3,2},{4,5},{5,4},{6,7},{7,6},{8,9},{9,8},{10,11... | collective-permute-start | bytes 4718600 | tf_op jit(solution)/shard_map/ppermute | solution.py:336
  109.9 76.6 %copy-start.54 = (f32[512]{0:T(512)}, f32[512]{0:T(512)S(1)}, u32[]{:S(2)}) copy-start(f32[512]{0:T(512)S(1)} %add_rsqrt_fusion.1) | copy-start | bytes 6148
  112.9 5.8 %copy-start.43 = (bf16[8,96,768]{2,1,0:T(8,128)(2,1)}, bf16[8,96,768]{2,1,0:T(8,128)(2,1)S(1)}, u32[]{:S(2)}) copy-start(bf16[8,96,768]{2,1,0:T(8,128)(2,1)S(1)} %get-tuple-element.160) | copy-start | bytes 3538948
  112.9 5.8 %copy-start.45 = (bf16[8,96,768]{2,1,0:T(8,128)(2,1)}, bf16[8,96,768]{2,1,0:T(8,128)(2,1)S(1)}, u32[]{:S(2)}) copy-start(bf16[8,96,768]{2,1,0:T(8,128)(2,1)S(1)} %get-tuple-element.159) | copy-start | bytes 3538948
  121.2 42.9 %collective-permute-start.4 = (f32[512,768]{1,0:T(8,128)}, f32[512,768]{1,0:T(8,128)}, u32[]{:S(2)}, u32[]{:S(2)}) collective-permute-start(f32[512,768]{1,0:T(8,128)} %fusion.17), channel_id=1, source_target_pairs={{0,1},{1,0},{2,3},{3,2},{4,5},{5,4},{6,7},{7,6},{8,9},{9,8},{10,11... | collective-permute-start | bytes 4718600 | tf_op jit(solution)/shard_map/ppermute | solution.py:336
  124.8 39.3 %copy-start.63 = (f32[768]{0:T(1024)S(1)}, f32[768]{0:T(1024)}, u32[]{:S(2)}) copy-start(f32[768]{0:T(1024)} %param.29) | copy-start | bytes 9220
  127.0 35.8 %collective-permute-start.7 = (f32[480,192]{0,1:T(8,128)S(1)}, f32[480,192]{0,1:T(8,128)S(1)}, u32[]{:S(2)}, u32[]{:S(2)}) collective-permute-start(f32[480,192]{0,1:T(8,128)S(1)} %convert_element_type.95), channel_id=1, source_target_pairs={{0,2},{1,3},{2,0},{3,1},{4,6},{5,7},{6,4},{7,5},{8,10},{9,11},{10,... | collective-permute-start | bytes 1105928 | tf_op jit(solution)/shard_map/ppermute | solution.py:336
  163.6 129.6 %reduce-scatter.2.cloned.1.call-start = ((), (), s32[]{:S(2)}) async-start(), calls=%async_computation.2 | async-start | bytes 11059200 | tf_op jit(solution)/shard_map/reduce_scatter | solution.py:441
  170.4 6.6 %copy-start.15 = (f32[512,768]{1,0:T(8,128)}, f32[512,768]{1,0:T(8,128)S(1)}, u32[]{:S(2)}) copy-start(f32[512,768]{1,0:T(8,128)S(1)} %get-tuple-element.140) | copy-start | bytes 4718596
  192.3 369.7 %all-gather.7.cloned.1.call-start = ((), (), s32[]{:S(2)}) async-start(), calls=%async_computation.3 | async-start | bytes 5529600 | tf_op jit(solution)/shard_map/all_gather | solution.py:523
  195.2 6.2 %copy-start.44 = (bf16[8,96,768]{2,1,0:T(8,128)(2,1)S(1)}, bf16[8,96,768]{2,1,0:T(8,128)(2,1)}, u32[]{:S(2)}) copy-start(bf16[8,96,768]{2,1,0:T(8,128)(2,1)} %copy-done.43) | copy-start | bytes 3538948
  204.2 36.9 %collective-permute-start.5 = (f32[512,768]{1,0:T(8,128)}, f32[512,768]{1,0:T(8,128)}, u32[]{:S(2)}, u32[]{:S(2)}) collective-permute-start(f32[512,768]{1,0:T(8,128)} %fusion.18), channel_id=1, source_target_pairs={{0,1},{1,0},{2,3},{3,2},{4,5},{5,4},{6,7},{7,6},{8,9},{9,8},{10,11... | collective-permute-start | bytes 4718600 | tf_op jit(solution)/shard_map/ppermute | solution.py:336
  220.4 20.7 %copy-start.14 = (f32[512,768]{1,0:T(8,128)S(1)}, f32[512,768]{1,0:T(8,128)}, u32[]{:S(2)}) copy-start(f32[512,768]{1,0:T(8,128)} %copy-done.11) | copy-start | bytes 4718596
  220.4 20.7 %copy-start.17 = (f32[512,768]{1,0:T(8,128)S(1)}, f32[512,768]{1,0:T(8,128)}, u32[]{:S(2)}) copy-start(f32[512,768]{1,0:T(8,128)} %copy-done.15) | copy-start | bytes 4718596
  220.4 20.7 %copy-start.55 = (f32[512]{0:T(512)S(1)}, f32[512]{0:T(512)}, u32[]{:S(2)}) copy-start(f32[512]{0:T(512)} %copy-done.54) | copy-start | bytes 6148
  267.8 57.2 %collective-permute-start.15 = (f32[4,592,384]{2,1,0:T(8,128)}, f32[4,592,384]{2,1,0:T(8,128)}, u32[]{:S(2)}, u32[]{:S(2)}) collective-permute-start(f32[4,592,384]{2,1,0:T(8,128)} %slice_bitcast_fusion), channel_id=1, source_target_pairs={{0,4},{4,0},{8,12},{12,8},{16,20},{20,16},{24,28},{28,24},{1,5},{5... | collective-permute-start | bytes 10911752 | tf_op jit(solution)/shard_map/ppermute | solution.py:350
  271.2 12.2 %collective-permute-start.11 = (f32[128,768]{1,0:T(8,128)}, f32[128,768]{1,0:T(8,128)S(1)}, u32[]{:S(2)}, u32[]{:S(2)}) collective-permute-start(f32[128,768]{1,0:T(8,128)} %get-tuple-element.161), channel_id=1, source_target_pairs={{0,1},{1,0},{2,3},{3,2},{4,5},{5,4},{6,7},{7,6},{8,9},{9,8},{10,11... | collective-permute-start | bytes 1179656 | tf_op jit(solution)/shard_map/ppermute | solution.py:336
  272.6 18.8 %collective-permute-start.8 = (f32[128,768]{1,0:T(8,128)}, f32[128,768]{1,0:T(8,128)}, u32[]{:S(2)}, u32[]{:S(2)}) collective-permute-start(f32[128,768]{1,0:T(8,128)} %get-tuple-element.162), channel_id=1, source_target_pairs={{0,1},{1,0},{2,3},{3,2},{4,5},{5,4},{6,7},{7,6},{8,9},{9,8},{10,11... | collective-permute-start | bytes 1179656 | tf_op jit(solution)/shard_map/ppermute | solution.py:336
  293.2 172.3 %copy-start.25 = (f32[128,768]{1,0:T(8,128)}, f32[128,768]{1,0:T(8,128)S(1)}, u32[]{:S(2)}) copy-start(f32[128,768]{1,0:T(8,128)S(1)} %get-tuple-element.171) | copy-start | bytes 1179652
  293.2 30.7 %copy-start.40 = (f32[400,768]{1,0:T(8,128)S(1)}, f32[400,768]{1,0:T(8,128)}, u32[]{:S(2)}) copy-start(f32[400,768]{1,0:T(8,128)} %reduce-scatter.2.cloned.1.call-done) | copy-start | bytes 3686404
  294.5 29.5 %collective-permute-start.26 = (f32[200,768]{1,0:T(8,128)S(1)}, f32[200,768]{1,0:T(8,128)S(1)}, u32[]{:S(2)}, u32[]{:S(2)}) collective-permute-start(f32[200,768]{1,0:T(8,128)S(1)} %slice.245), channel_id=1, source_target_pairs={{0,2},{1,3},{2,0},{3,1},{4,6},{5,7},{6,4},{7,5},{8,10},{9,11},{10,... | collective-permute-start | bytes 1843208 | tf_op jit(solution)/shard_map/ppermute | solution.py:336
  328.6 27.9 %collective-permute-start.18 = (f32[2,296,384]{2,1,0:T(8,128)S(1)}, f32[2,296,384]{2,1,0:T(8,128)S(1)}, u32[]{:S(2)}, u32[]{:S(2)}) collective-permute-start(f32[2,296,384]{2,1,0:T(8,128)S(1)} %slice.276), channel_id=1, source_target_pairs={{0,16},{4,20},{8,24},{12,28},{16,0},{20,4},{24,8},{28,12},{1,17},{... | collective-permute-start | bytes 2727944 | tf_op jit(solution)/shard_map/ppermute | solution.py:350
  329.8 28.2 %collective-permute-start.16 = (f32[2,296,384]{2,1,0:T(8,128)S(1)}, f32[2,296,384]{2,1,0:T(8,128)S(1)}, u32[]{:S(2)}, u32[]{:S(2)}) collective-permute-start(f32[2,296,384]{2,1,0:T(8,128)S(1)} %slice_bitcast_fusion.2), channel_id=1, source_target_pairs={{0,8},{4,12},{8,0},{12,4},{16,24},{20,28},{24,16},{28,20},{1,9},{5... | collective-permute-start | bytes 2727944 | tf_op jit(solution)/shard_map/ppermute | solution.py:350
  356.7 22.1 %collective-permute-start.19 = (f32[1,296,384]{2,1,0:T(8,128)S(1)}, f32[1,296,384]{2,1,0:T(8,128)S(1)}, u32[]{:S(2)}, u32[]{:S(2)}) collective-permute-start(f32[1,296,384]{2,1,0:T(8,128)S(1)} %slice.278), channel_id=1, source_target_pairs={{0,8},{4,12},{8,0},{12,4},{16,24},{20,28},{24,16},{28,20},{1,9},{5... | collective-permute-start | bytes 1363976 | tf_op jit(solution)/shard_map/ppermute | solution.py:350
  358.2 21.3 %collective-permute-start.17 = (f32[1,296,384]{2,1,0:T(8,128)S(1)}, f32[1,296,384]{2,1,0:T(8,128)S(1)}, u32[]{:S(2)}, u32[]{:S(2)}) collective-permute-start(f32[1,296,384]{2,1,0:T(8,128)S(1)} %slice_bitcast_fusion.4), channel_id=1, source_target_pairs={{0,16},{4,20},{8,24},{12,28},{16,0},{20,4},{24,8},{28,12},{1,17},{... | collective-permute-start | bytes 1363976 | tf_op jit(solution)/shard_map/ppermute | solution.py:350
  381.5 50.3 %collective-permute-start.20 = (f32[592,192]{0,1:T(8,128)}, f32[592,192]{0,1:T(8,128)}, u32[]{:S(2)}, u32[]{:S(2)}) collective-permute-start(f32[592,192]{0,1:T(8,128)} %copy.173), channel_id=1, source_target_pairs={{0,2},{1,3},{2,0},{3,1},{4,6},{5,7},{6,4},{7,5},{8,10},{9,11},{10,... | collective-permute-start | bytes 1363976 | tf_op jit(solution)/shard_map/ppermute | solution.py:336
  381.9 84.7 %collective-permute-start.6 = (f32[256,768]{1,0:T(8,128)S(1)}, f32[256,768]{1,0:T(8,128)S(1)}, u32[]{:S(2)}, u32[]{:S(2)}) collective-permute-start(f32[256,768]{1,0:T(8,128)S(1)} %fusion.38), channel_id=1, source_target_pairs={{0,2},{1,3},{2,0},{3,1},{4,6},{5,7},{6,4},{7,5},{8,10},{9,11},{10,... | collective-permute-start | bytes 2359304 | tf_op jit(solution)/shard_map/ppermute | solution.py:336
  384.6 81.0 %collective-permute-start.12 = (f32[128,768]{1,0:T(8,128)S(1)}, f32[128,768]{1,0:T(8,128)S(1)}, u32[]{:S(2)}, u32[]{:S(2)}) collective-permute-start(f32[128,768]{1,0:T(8,128)S(1)} %get-tuple-element.171), channel_id=1, source_target_pairs={{0,2},{1,3},{2,0},{3,1},{4,6},{5,7},{6,4},{7,5},{8,10},{9,11},{10,... | collective-permute-start | bytes 1179656 | tf_op jit(solution)/shard_map/ppermute | solution.py:336
  436.0 30.6 %collective-permute-start.23 = (f32[1,296,192]{2,1,0:T(8,128)S(1)}, f32[1,296,192]{2,1,0:T(8,128)S(1)}, u32[]{:S(2)}, u32[]{:S(2)}) collective-permute-start(f32[1,296,192]{2,1,0:T(8,128)S(1)} %get-tuple-element.177), channel_id=1, source_target_pairs={{0,16},{4,20},{8,24},{12,28},{16,0},{20,4},{24,8},{28,12},{1,17},{... | collective-permute-start | bytes 681992 | tf_op jit(solution)/shard_map/ppermute | solution.py:350
  436.6 40.7 %collective-permute-start.10 = (f32[128,768]{1,0:T(8,128)S(1)}, f32[128,768]{1,0:T(8,128)}, u32[]{:S(2)}, u32[]{:S(2)}) collective-permute-start(f32[128,768]{1,0:T(8,128)S(1)} %copy-done.26), channel_id=1, source_target_pairs={{0,2},{1,3},{2,0},{3,1},{4,6},{5,7},{6,4},{7,5},{8,10},{9,11},{10,... | collective-permute-start | bytes 1179656 | tf_op jit(solution)/shard_map/ppermute | solution.py:336
  436.6 32.3 %collective-permute-start.21 = (f32[1,296,192]{2,1,0:T(8,128)}, f32[1,296,192]{2,1,0:T(8,128)}, u32[]{:S(2)}, u32[]{:S(2)}) collective-permute-start(f32[1,296,192]{2,1,0:T(8,128)} %get-tuple-element.176), channel_id=1, source_target_pairs={{0,8},{4,12},{8,0},{12,4},{16,24},{20,28},{24,16},{28,20},{1,9},{5... | collective-permute-start | bytes 681992 | tf_op jit(solution)/shard_map/ppermute | solution.py:350
  466.6 23.8 %collective-permute-start.13 = (f32[2,128,768]{2,1,0:T(8,128)}, f32[2,128,768]{2,1,0:T(8,128)}, u32[]{:S(2)}, u32[]{:S(2)}) collective-permute-start(f32[2,128,768]{2,1,0:T(8,128)} %pad_maximum_fusion.14), channel_id=1, source_target_pairs={{0,1},{1,0},{2,3},{3,2},{4,5},{5,4},{6,7},{7,6},{8,9},{9,8},{10,11... | collective-permute-start | bytes 2359304 | tf_op jit(solution)/shard_map/ppermute | solution.py:336
  466.6 7.4 %copy-start.28 = (f32[256,768]{1,0:T(8,128)}, f32[256,768]{1,0:T(8,128)S(1)}, u32[]{:S(2)}) copy-start(f32[256,768]{1,0:T(8,128)S(1)} %collective-permute-done.6) | copy-start | bytes 2359300
  467.8 11.4 %collective-permute-start.24 = (f32[2,296,192]{1,2,0:T(8,128)}, f32[2,296,192]{1,2,0:T(8,128)}, u32[]{:S(2)}, u32[]{:S(2)}) collective-permute-start(f32[2,296,192]{1,2,0:T(8,128)} %copy.177), channel_id=1, source_target_pairs={{0,8},{4,12},{8,0},{12,4},{16,24},{20,28},{24,16},{28,20},{1,9},{5... | collective-permute-start | bytes 1363976 | tf_op jit(solution)/shard_map/ppermute | solution.py:350
  472.9 10.4 %collective-permute-start.22 = (f32[2,296,192]{1,2,0:T(8,128)}, f32[2,296,192]{1,2,0:T(8,128)}, u32[]{:S(2)}, u32[]{:S(2)}) collective-permute-start(f32[2,296,192]{1,2,0:T(8,128)} %copy.175), channel_id=1, source_target_pairs={{0,16},{4,20},{8,24},{12,28},{16,0},{20,4},{24,8},{28,12},{1,17},{... | collective-permute-start | bytes 1363976 | tf_op jit(solution)/shard_map/ppermute | solution.py:350
  475.2 67.6 %collective-permute-start.9 = (f32[2,256,768]{2,1,0:T(8,128)}, f32[2,256,768]{2,1,0:T(8,128)}, u32[]{:S(2)}, u32[]{:S(2)}) collective-permute-start(f32[2,256,768]{2,1,0:T(8,128)} %pad_maximum_fusion.5), channel_id=1, source_target_pairs={{0,1},{1,0},{2,3},{3,2},{4,5},{5,4},{6,7},{7,6},{8,9},{9,8},{10,11... | collective-permute-start | bytes 4718600 | tf_op jit(solution)/shard_map/ppermute | solution.py:336
  479.2 59.5 %collective-permute-start.14 = (f32[2,128,768]{2,1,0:T(8,128)}, f32[2,128,768]{2,1,0:T(8,128)}, u32[]{:S(2)}, u32[]{:S(2)}) collective-permute-start(f32[2,128,768]{2,1,0:T(8,128)} %pad_maximum_fusion.15), channel_id=1, source_target_pairs={{0,1},{1,0},{2,3},{3,2},{4,5},{5,4},{6,7},{7,6},{8,9},{9,8},{10,11... | collective-permute-start | bytes 2359304 | tf_op jit(solution)/shard_map/ppermute | solution.py:336
  488.1 58.7 %collective-permute-start.25 = (f32[4,592,192]{1,2,0:T(8,128)}, f32[4,592,192]{1,2,0:T(8,128)}, u32[]{:S(2)}, u32[]{:S(2)}) collective-permute-start(f32[4,592,192]{1,2,0:T(8,128)} %copy.180), channel_id=1, source_target_pairs={{0,4},{4,0},{8,12},{12,8},{16,20},{20,16},{24,28},{28,24},{1,5},{5... | collective-permute-start | bytes 5455880 | tf_op jit(solution)/shard_map/ppermute | solution.py:350
  (51 other events, 115.0 us)
Sparse Core Ops, SparseCore 0:
  43.5 40.7 all-gather.4
  163.7 35.1 all-gather.8
  202.5 78.3 reduce-scatter.1
  325.1 56.3 all-gather.6

commit v4 on v3

v4 whole, which is shorter than its diff:
```python
from functools import partial
import math

import jax
import jax.numpy as jnp
import numpy as np
from jax import lax
from jax.experimental import pallas as pl
from jax.experimental.pallas import tpu as pltpu
from jax.sharding import PartitionSpec as P

HEAD_DIM = 64
STEP_BITS = 5
STEP = 1 << STEP_BITS
NEAR = 1
FAR = 2
MASKED = -1e30


def mm(left, right):
    return jnp.dot(left, right, preferred_element_type=jnp.float32)


def mm_nt(left, right):
    return lax.dot_general(
        left, right, (((1,), (1,)), ((), ())), preferred_element_type=jnp.float32
    )


def mm_tn(left, right):
    return lax.dot_general(
        left, right, (((0,), (0,)), ((), ())), preferred_element_type=jnp.float32
    )


def angle_tables(model_width):
    quarter = model_width // 4
    rate = np.exp(np.arange(quarter) * (-math.log(10000.0) / quarter))
    fine = np.arange(STEP)[:, None] * rate
    coarse = fine * STEP
    zero = np.zeros((STEP, 2 * quarter))
    table = np.concatenate(
        [
            np.concatenate([np.sin(coarse), np.cos(coarse), zero], axis=1),
            np.concatenate([zero, np.sin(fine), np.cos(fine)], axis=1),
        ],
        axis=0,
    )
    parts = []
    rest = table
    for _ in range(3):
        part = rest.astype(jnp.bfloat16)
        parts.append(part)
        rest = rest - part.astype(np.float64)
    return np.concatenate(parts, axis=0)


def sinusoid(coord, table_ref):
    quarter = table_ref.shape[1] // 4
    slot = lax.broadcasted_iota(jnp.int32, (2 * STEP, coord.shape[1]), 0)
    coarse = coord >> STEP_BITS
    fine = (coord & (STEP - 1)) + STEP
    hit = ((slot == coarse) | (slot == fine)).astype(jnp.float32).astype(jnp.bfloat16)
    looked = mm_tn(jnp.concatenate([hit, hit, hit], axis=0), table_ref[...])
    sin_a, cos_a, sin_b, cos_b = [looked[:, k * quarter : (k + 1) * quarter] for k in range(4)]
    return jnp.concatenate([sin_a * cos_b + cos_a * sin_b, cos_a * cos_b - sin_a * sin_b], axis=1)


def head_of(ref, index, head):
    return ref[index, :, head * HEAD_DIM : (head + 1) * HEAD_DIM]


def probs_t(q, k, pq, pk, length, factor):
    left = jnp.concatenate([k, pk, k], axis=1)
    right = jnp.concatenate([q, q, pq], axis=1)
    scores = mm_nt(left, right) * factor
    visible = lax.broadcasted_iota(jnp.int32, scores.shape, 0) < length
    scores = jnp.where(visible, scores, MASKED)
    raised = jnp.exp(scores - jnp.max(scores, axis=0, keepdims=True))
    return raised * (1.0 / jnp.sum(raised, axis=0, keepdims=True))


def attend_kernel(
    heads, keep, scalars_ref, x_ref, coords_ref, table_ref, wqkv_ref, wpos_ref, mixed_ref, *kept
):
    length = scalars_ref[1]
    factor = 1.0 / math.sqrt(3.0 * HEAD_DIM)
    proj_ref, pos_ref = kept
    rows = x_ref[0]
    for part in range(3):
        proj_ref[part] = mm(rows, wqkv_ref[part]).astype(jnp.bfloat16)
    sides = [sinusoid(coords_ref[0, axis : axis + 1], table_ref) for axis in range(2)]
    position = jnp.concatenate(sides, axis=1).astype(jnp.bfloat16)
    if keep:
        pos_ref[...] = position
    for part in range(2):
        proj_ref[3 + part] = mm(position, wpos_ref[part]).astype(jnp.bfloat16)
    for head in range(heads):
        q, k, v, pq, pk = [head_of(proj_ref, part, head) for part in range(5)]
        weights = probs_t(q, k, pq, pk, length, factor).astype(jnp.bfloat16)
        mixed = mm_tn(v, weights).T
        mixed = mixed.astype(jnp.bfloat16).astype(mixed_ref.dtype)
        mixed_ref[:, head * HEAD_DIM : (head + 1) * HEAD_DIM] = mixed


def attend(keep, scalars, tokens, coords, table, w_qkv, w_pos):
    pages, length, width = tokens.shape
    columns = w_qkv.shape[2]
    whole = lambda *shape: pl.BlockSpec(shape, lambda i, s: (0,) * len(shape))
    proj = jax.ShapeDtypeStruct((5, length, columns), jnp.bfloat16)
    pos = jax.ShapeDtypeStruct((length, width), jnp.bfloat16)
    mixed = jax.ShapeDtypeStruct((length, columns), jnp.bfloat16 if keep else jnp.float32)
    shapes = (mixed, proj, pos) if keep else (mixed,)
    return pl.pallas_call(
        partial(attend_kernel, columns // HEAD_DIM, keep),
        out_shape=shapes,
        grid_spec=pltpu.PrefetchScalarGridSpec(
            num_scalar_prefetch=1,
            grid=(1,),
            in_specs=[
                pl.BlockSpec((1, length, width), lambda i, s: (s[0], 0, 0)),
                pl.BlockSpec((1,) + coords.shape[1:], lambda i, s: (s[0], 0, 0)),
                whole(*table.shape),
                whole(*w_qkv.shape),
                whole(*w_pos.shape),
            ],
            out_specs=[whole(*shape.shape) for shape in shapes],
            scratch_shapes=[]
            if keep
            else [pltpu.VMEM(proj.shape, proj.dtype), pltpu.VMEM((8, 128), jnp.bfloat16)],
        ),
        compiler_params=pltpu.CompilerParams(vmem_limit_bytes=40 << 20),
        cost_estimate=pl.CostEstimate(
            flops=2 * length * columns * (5 * width + 4 * length),
            transcendentals=length * length * columns // HEAD_DIM,
            bytes_accessed=length * (4 * width + 14 * columns),
        ),
        name="attend",
    )(scalars, tokens, coords, table, w_qkv, w_pos)


def norm_parts(values):
    center = values - jnp.mean(values, axis=-1, keepdims=True)
    spread = jnp.mean(center * center, axis=-1, keepdims=True)
    scale = lax.rsqrt(spread + 1e-05)
    return center * scale, scale


def norm_back(grad, gain, xhat, scale):
    up = grad * gain
    mean = jnp.mean(up, axis=-1, keepdims=True)
    along = jnp.mean(up * xhat, axis=-1, keepdims=True)
    return scale * (up - mean - xhat * along)


def column_sum(values):
    return jnp.sum(values.astype(jnp.float32), axis=0, keepdims=True)


def feed_kernel(
    scalars_ref, x_ref, part_ref, other_ref, b_out_ref, gain_ref, shift_ref, w_in_ref, w_in_far_ref, b_in_ref,
    w_back_ref, w_back_far_ref, next_ref, xhat_ref, scale_ref, low_ref, hidden_ref, slope_ref,
):
    first = x_ref[0].astype(jnp.float32) + (part_ref[...] + other_ref[...] + b_out_ref[...])
    xhat, scale = norm_parts(first)
    low = (xhat * gain_ref[...] + shift_ref[...]).astype(jnp.bfloat16)
    xhat_ref[...] = xhat
    scale_ref[...] = scale
    low_ref[...] = low
    units = w_in_ref.shape[1]
    total = None
    for side, (into, back) in enumerate(((w_in_ref, w_back_ref), (w_in_far_ref, w_back_far_ref))):
        at = slice(side * units, (side + 1) * units)
        pre = mm(low, into[...]) + b_in_ref[side : side + 1]
        cdf = 0.5 * (1.0 + lax.erf(pre * math.sqrt(0.5)))
        hidden = (pre * cdf).astype(jnp.bfloat16)
        hidden_ref[:, at] = hidden
        slope_ref[:, at] = cdf + pre * (jnp.exp(-0.5 * pre * pre) * (1.0 / math.sqrt(2.0 * math.pi)))
        product = mm(hidden, back[...])
        total = product if total is None else total + product
    next_ref[...] = total


def feed_back_kernel(
    scalars_ref, cot_ref, part_ref, other_ref, xhat_ref, slope_ref, gain_one_ref, shift_one_ref, b_back_ref,
    gain_ref, shift_ref, w_in_ref, w_in_far_ref, w_back_ref, w_back_far_ref,
    next_ref, second_ref, feed_ref, pre_ref, out_ref, sums_ref, sums_in_ref,
):
    normed = xhat_ref[...] * gain_one_ref[...] + shift_one_ref[...]
    second = normed + (part_ref[...] + other_ref[...] + b_back_ref[...])
    xhat, scale = norm_parts(second)
    out_ref[...] = xhat * gain_ref[...] + shift_ref[...]
    grad = cot_ref[0].astype(jnp.float32)
    d_second = norm_back(grad, gain_ref[...], xhat, scale)
    second_ref[...] = d_second
    d_feed = d_second.astype(jnp.bfloat16)
    feed_ref[...] = d_feed
    sums_ref[0:1] = column_sum(d_feed)
    sums_ref[1:2] = column_sum(grad * xhat)
    sums_ref[2:3] = column_sum(grad)
    units = w_in_ref.shape[1]
    total = None
    for side, (into, back) in enumerate(((w_in_ref, w_back_ref), (w_in_far_ref, w_back_far_ref))):
        at = slice(side * units, (side + 1) * units)
        d_pre = (mm_nt(d_feed, back[...]) * slope_ref[:, at]).astype(jnp.bfloat16)
        pre_ref[:, at] = d_pre
        sums_in_ref[side : side + 1] = column_sum(d_pre)
        product = mm_nt(d_pre, into[...])
        total = product if total is None else total + product
    next_ref[...] = total


def on_chunk(kernel, name, chunk, scalars, pages_array, rows, arrays, shapes):
    length, width = pages_array.shape[1:]
    whole = lambda shape: pl.BlockSpec(shape, lambda i, s: (0,) * len(shape))
    return pl.pallas_call(
        kernel,
        out_shape=shapes,
        grid_spec=pltpu.PrefetchScalarGridSpec(
            num_scalar_prefetch=1,
            grid=(1,),
            in_specs=[pl.BlockSpec((1, rows, width), lambda i, s: (s[0], chunk, 0))]
            + [whole(array.shape) for array in arrays],
            out_specs=[whole(shape.shape) for shape in shapes],
        ),
        compiler_params=pltpu.CompilerParams(vmem_limit_bytes=48 << 20),
        cost_estimate=pl.CostEstimate(
            flops=16 * rows * width * width, transcendentals=2 * rows * width, bytes_accessed=40 * rows * width
        ),
        name=name,
    )(scalars, pages_array, *arrays)


def feed_grads_kernel(count, low_ref, pre_ref, hidden_ref, feed_ref, out_ref):
    rows = out_ref.shape[2]

    def put(left, right):
        product = mm_tn(left[...], right[...])
        for block in range(count):
            out_ref[block, 0] = product[block * rows : (block + 1) * rows]

    @pl.when(pl.program_id(0) % 2 == 0)
    def _():
        put(low_ref, pre_ref)

    @pl.when(pl.program_id(0) % 2 == 1)
    def _():
        put(hidden_ref, feed_ref)


def feed_grads(count, low, d_pre, hidden, d_feed):
    length, width = low.shape
    units = hidden.shape[1] // 2
    return pl.pallas_call(
        partial(feed_grads_kernel, count),
        out_shape=jax.ShapeDtypeStruct((count, 4, width // count, units), jnp.float32),
        grid_spec=pl.GridSpec(
            grid=(4,),
            in_specs=[
                pl.BlockSpec((length, width), lambda i: (0, 0)),
                pl.BlockSpec((length, units), lambda i: (0, i // 2)),
                pl.BlockSpec((length, units), lambda i: (0, i // 2)),
                pl.BlockSpec((length, width), lambda i: (0, 0)),
            ],
            out_specs=pl.BlockSpec((count, 1, width // count, units), lambda i: (0, i, 0, 0)),
        ),
        compiler_params=pltpu.CompilerParams(vmem_limit_bytes=40 << 20),
        cost_estimate=pl.CostEstimate(
            flops=8 * length * width * units, transcendentals=0, bytes_accessed=16 * width * units
        ),
        name="feed_grads",
    )(low, d_pre, hidden, d_feed)


def far_proj_kernel(count, x_ref, pos_ref, blocks_ref, proj_ref, wqkv_ref):
    width = x_ref.shape[1]
    rows = width // count
    for part in range(5):
        weight = jnp.concatenate([blocks_ref[block, part] for block in range(count)], axis=0)
        weight = weight.astype(jnp.bfloat16)
        if part < 3:
            wqkv_ref[part] = weight
        left = x_ref if part < 3 else pos_ref
        proj_ref[part] = mm(left[...], weight).astype(jnp.bfloat16)


def far_proj(rows, pos_rows, blocks):
    count, parts, block_rows, columns = blocks.shape
    length, width = rows.shape
    whole = lambda shape: pl.BlockSpec(shape, lambda i: (0,) * len(shape))
    shapes = (
        jax.ShapeDtypeStruct((parts, length, columns), jnp.bfloat16),
        jax.ShapeDtypeStruct((3, width, columns), jnp.bfloat16),
    )
    return pl.pallas_call(
        partial(far_proj_kernel, count),
        out_shape=shapes,
        grid_spec=pl.GridSpec(
            grid=(1,),
            in_specs=[whole(rows.shape), whole(pos_rows.shape), whole(blocks.shape)],
            out_specs=[whole(shape.shape) for shape in shapes],
        ),
        compiler_params=pltpu.CompilerParams(vmem_limit_bytes=40 << 20),
        cost_estimate=pl.CostEstimate(
            flops=2 * parts * length * width * columns, transcendentals=0, bytes_accessed=4 * blocks.size
        ),
        name="far_proj",
    )(rows, pos_rows, blocks)


def attend_back_kernel(
    heads, scalars_ref, part_a, part_b, other_a, other_b, second_a, second_b, xhat_a, xhat_b, scale_a, scale_b,
    gain_ref, w_out_ref, w_out_far_ref, own_ref, far_ref, wqkv_ref, wqkv_far_ref,
    send_ref, base_ref, d_ref, branch_ref, sums_ref, dm_ref, first_ref,
):
    length, low = scalars_ref[1], scalars_ref[2]
    factor = 1.0 / math.sqrt(3.0 * HEAD_DIM)
    columns = heads * HEAD_DIM
    half = part_a.shape[0]
    sums = None
    chunks = ((part_a, other_a, second_a, xhat_a, scale_a), (part_b, other_b, second_b, xhat_b, scale_b))
    for index, (part, other, second, xhat, scale) in enumerate(chunks):
        at = slice(index * half, (index + 1) * half)
        d_normed = second[...] + (part[...] + other[...])
        d_first = norm_back(d_normed, gain_ref[...], xhat[...], scale[...])
        first_ref[at] = d_first
        d_branch = d_first.astype(jnp.bfloat16)
        branch_ref[at] = d_branch
        some = (column_sum(d_branch), column_sum(d_normed * xhat[...]), column_sum(d_normed))
        sums = some if sums is None else tuple(x + y for x, y in zip(sums, some))
        dm_ref[at, :columns] = mm_nt(d_branch, w_out_ref[...]).astype(jnp.bfloat16)
        dm_ref[at, columns:] = mm_nt(d_branch, w_out_far_ref[...]).astype(jnp.bfloat16)
    for index, value in enumerate(sums):
        sums_ref[index : index + 1] = value
    for side, here in enumerate((own_ref, far_ref)):
        for head in range(heads):
            q, k, v, pq, pk = [head_of(here, part, head) for part in range(5)]
            at = side * columns + head * HEAD_DIM
            dm = dm_ref[:, at : at + HEAD_DIM]
            probs = probs_t(q, k, pq, pk, length, factor)
            weights = probs.astype(jnp.bfloat16)
            d_values = mm(weights, dm)
            d_probs = mm_nt(v, dm)
            inner = jnp.sum(d_probs * probs, axis=0, keepdims=True)
            d_scores = (probs * (d_probs - inner)).astype(jnp.bfloat16)
            by_queries = mm(d_scores, jnp.concatenate([q, pq], axis=1))
            by_query, by_pos_query = by_queries[:, :HEAD_DIM], by_queries[:, HEAD_DIM:]
            by_keys = mm_tn(jnp.concatenate([k, pk], axis=1), d_scores).T
            by_key, by_pos_key = by_keys[:, :HEAD_DIM], by_keys[:, HEAD_DIM:]
            grads = (
                (by_key + by_pos_key) * factor,
                (by_query + by_pos_query) * factor,
                d_values,
                by_key * factor,
                by_query * factor,
            )
            for part, value in enumerate(grads):
                d_ref[part, :, at : at + HEAD_DIM] = value.astype(jnp.bfloat16)
    for index, ref in enumerate((base_ref, send_ref)):
        at = pl.multiple_of(jnp.where(low == index, 0, half), half)
        at = pl.ds(at, half)
        total = first_ref[at] if index == 0 else None
        for part in range(3):
            for side, weights in enumerate((wqkv_ref, wqkv_far_ref)):
                left = d_ref[part, at, side * columns : (side + 1) * columns]
                product = mm_nt(left, weights[part])
                total = product if total is None else total + product
        ref[...] = total


def attend_back(scalars, arrays):
    proj = arrays[13]
    parts, length, columns = proj.shape
    half, width = arrays[0].shape
    heads = columns // HEAD_DIM
    whole = lambda shape: pl.BlockSpec(shape, lambda i, s: (0,) * len(shape))
    shapes = (
        jax.ShapeDtypeStruct((half, width), jnp.float32),
        jax.ShapeDtypeStruct((half, width), jnp.float32),
        jax.ShapeDtypeStruct((parts, length, 2 * columns), jnp.bfloat16),
        jax.ShapeDtypeStruct((length, width), jnp.bfloat16),
        jax.ShapeDtypeStruct((3, width), jnp.float32),
    )
    return pl.pallas_call(
        partial(attend_back_kernel, heads),
        out_shape=shapes,
        grid_spec=pltpu.PrefetchScalarGridSpec(
            num_scalar_prefetch=1,
            grid=(1,),
            in_specs=[whole(array.shape) for array in arrays],
            out_specs=[whole(shape.shape) for shape in shapes],
            scratch_shapes=[
                pltpu.VMEM((length, 2 * columns), jnp.bfloat16),
                pltpu.VMEM((length, width), jnp.float32),
            ],
        ),
        compiler_params=pltpu.CompilerParams(vmem_limit_bytes=48 << 20),
        cost_estimate=pl.CostEstimate(
            flops=2 * 2 * heads * length * length * HEAD_DIM * 9 + 20 * length * width * columns,
            transcendentals=2 * heads * length * length,
            bytes_accessed=40 * length * width,
        ),
        name="attend_back",
    )(scalars, *arrays)


def weight_grads_kernel(
    count, scalars_ref, x_ref, pos_ref, d_ref, db_ref, mixed_ref, far_ref, vec_ref, keep_ref, send_ref
):
    group = scalars_ref[0]
    rows = x_ref.shape[1] // count
    mixed = jnp.concatenate([mixed_ref[...], far_ref[...]], axis=1)
    lefts = [x_ref] * 3 + [pos_ref] * 2 + [db_ref]
    odd = group & 1
    for part, left in enumerate(lefts):
        product = mm_tn(left[...], d_ref[part] if part < 5 else mixed)
        at = slice(part * rows, (part + 1) * rows)
        for block in range(count):
            ref, place = (keep_ref, send_ref)[block & 1], (block ^ group) >> 1
            value = product[block * rows : (block + 1) * rows]

            @pl.when(odd == (block & 1))
            def _():
                keep_ref[place, at] = value

            @pl.when(odd != (block & 1))
            def _():
                send_ref[place, at] = value

    at = slice(6 * rows, None)
    keep_ref[:, at] = jnp.zeros((count // 2,) + vec_ref.shape, jnp.float32)
    send_ref[:, at] = jnp.zeros((count // 2,) + vec_ref.shape, jnp.float32)

    @pl.when(odd == 0)
    def _():
        keep_ref[group >> 1, at] = vec_ref[...]

    @pl.when(odd == 1)
    def _():
        send_ref[group >> 1, at] = vec_ref[...]


def weight_grads(count, scalars, rows, pos_rows, d_heads, d_branch, mixed, mixed_far, vectors):
    length, width = rows.shape
    wide = d_heads.shape[2]
    block = 6 * (width // count) + vectors.shape[0]
    shape = jax.ShapeDtypeStruct((count // 2, block, wide), jnp.float32)
    return pl.pallas_call(
        partial(weight_grads_kernel, count),
        out_shape=(shape, shape),
        in_specs=[pl.BlockSpec(memory_space=pltpu.SMEM)] + [pl.BlockSpec(memory_space=pltpu.VMEM)] * 7,
        out_specs=[pl.BlockSpec(memory_space=pltpu.VMEM)] * 2,
        compiler_params=pltpu.CompilerParams(vmem_limit_bytes=48 << 20),
        cost_estimate=pl.CostEstimate(
            flops=12 * length * width * wide,
            transcendentals=0,
            bytes_accessed=4 * count * block * wide + 10 * length * wide + 6 * length * width,
        ),
        name="weight_grads",
    )(scalars, rows, pos_rows, d_heads, d_branch, mixed, mixed_far, vectors)


def place_grads_kernel(
    order, scalars_ref, low_a_ref, low_b_ref, high_a_ref, high_b_ref, qkv_ref, pos_ref, out_ref, vec_ref, turned
):
    group = scalars_ref[0]
    count = 2 * low_a_ref.shape[0]
    rows = qkv_ref.shape[1] // count
    cut = low_a_ref.shape[1]

    def read(place, start, stop):
        upper = (place & 1) == 1
        index = place >> 1
        pieces = []
        if start < cut:
            at = slice(start, min(stop, cut))
            pieces.append(jnp.where(upper, high_a_ref[index, at], low_a_ref[index, at]))
        if stop > cut:
            at = slice(max(start, cut) - cut, stop - cut)
            turned_index = 0
            for bit in range(len(order)):
                turned_index = turned_index | (((index >> bit) & 1) << order[bit])
            pieces.append(jnp.where(upper, high_b_ref[turned_index, at], low_b_ref[turned_index, at]))
        return jnp.concatenate(pieces, axis=0) if len(pieces) > 1 else pieces[0]

    for block in range(count):
        place = block ^ group
        at = slice(block * rows, (block + 1) * rows)
        for part in range(6):
            value = read(place, part * rows, (part + 1) * rows)
            if part < 3:
                qkv_ref[part, at] = value
            elif part < 5:
                pos_ref[part - 3, at] = value
            else:
                turned[at] = value
        if block == 0:
            vec_ref[...] = read(place, 6 * rows, cut + low_b_ref.shape[1])
    out_ref[...] = turned[...].T


def place_grads(scalars, parts, width, vec_rows):
    columns = parts[0].shape[2]
    bits = parts[0].shape[0].bit_length() - 1
    whole = lambda shape: pl.BlockSpec(shape, lambda i: (0,) * len(shape))
    shapes = (
        jax.ShapeDtypeStruct((3, width, columns), jnp.float32),
        jax.ShapeDtypeStruct((2, width, columns), jnp.float32),
        jax.ShapeDtypeStruct((columns, width), jnp.float32),
        jax.ShapeDtypeStruct((vec_rows, columns), jnp.float32),
    )
    return pl.pallas_call(
        partial(place_grads_kernel, tuple(range(bits))[::-1]),
        out_shape=shapes,
        grid_spec=pl.GridSpec(
            grid=(1,),
            in_specs=[pl.BlockSpec(memory_space=pltpu.SMEM)] + [whole(part.shape) for part in parts],
            out_specs=[whole(shape.shape) for shape in shapes],
            scratch_shapes=[pltpu.VMEM((width, columns), jnp.float32)],
        ),
        compiler_params=pltpu.CompilerParams(vmem_limit_bytes=40 << 20),
        cost_estimate=pl.CostEstimate(
            flops=0, transcendentals=0, bytes_accessed=32 * width * columns * 3
        ),
        name="place_grads",
    )(scalars, *parts)


def body(
    dp_size,
    mp_size,
    tokens,
    lengths,
    coords,
    w_qkv,
    w_pos,
    w_out,
    b_out,
    gain_one,
    shift_one,
    w_in,
    b_in,
    w_back,
    b_back,
    gain_two,
    shift_two,
    cotangent,
):
    pages, length, width = tokens.shape
    columns = w_qkv.shape[2]
    units = w_in.shape[1]
    here = lax.axis_index("mp")
    low = here & 1
    page = here >> 1
    group = lax.axis_index("dp")
    f32, bf16 = jnp.float32, jnp.bfloat16
    half = length // 2
    one = jnp.where(lengths[0] > 0, 1.0, 0.0).astype(f32)

    def arrived(value):
        return value * one

    def swap(value, bit):
        pairs = [(i, i ^ bit) for i in range(mp_size)]
        return lax.ppermute(value, "mp", pairs)

    def group_swap(value, bit):
        pairs = [(i, i ^ bit) for i in range(dp_size)]
        return lax.ppermute(value, "dp", pairs)

    def my_rows(value):
        rows = value.shape[0] // dp_size
        return lax.dynamic_slice_in_dim(value, group * rows, rows, 0)

    def gather(value):
        return lax.all_gather(value, "dp", axis=0, tiled=True)

    def take(value, index):
        return lax.dynamic_index_in_dim(value, index, 0, keepdims=False)

    def after(value, *others):
        return lax.optimization_barrier((value,) + others)[0]

    def row(value):
        return value.reshape(1, -1)

    chunk_rows = lambda value: [value[:half], value[half:]]

    unit_rows = jnp.concatenate([my_rows(w_in), my_rows(w_back)], axis=0).astype(f32)
    tail = jnp.concatenate([row(b_in), jnp.zeros((7, units), f32)], axis=0)
    far_rows = swap(jnp.concatenate([unit_rows, tail], axis=0), FAR)
    out_rows = swap(my_rows(w_out).astype(f32), FAR)

    table = jnp.asarray(angle_tables(width))
    mine_scalars = jnp.stack([page, take(lengths, page), low])
    their_scalars = jnp.stack([1 - page, take(lengths, 1 - page), low])
    (mixed_send,) = attend(False, their_scalars, tokens, coords, table, w_qkv, w_pos)
    mixed_far = swap(mixed_send, FAR)
    far_rows = after(far_rows, mixed_send)
    tokens_later = after(tokens, far_rows)
    mixed, proj, pos_rows = attend(True, mine_scalars, tokens_later, coords, table, w_qkv, w_pos)
    w_out_far = arrived(gather(after(out_rows, mixed_send))).astype(bf16)
    count = unit_rows.shape[0]
    b_in_two = jnp.stack([b_in, far_rows[count]])
    blocks = arrived(gather(far_rows[:count])).reshape(dp_size, count, -1)
    in_rows = width // dp_size
    w_in_far = blocks[:, :in_rows].reshape(width, units).astype(bf16)
    w_back_far = blocks[:, in_rows:].reshape(units, width).astype(bf16)

    mixed_far = arrived(mixed_far).astype(bf16)
    part = [
        mm(own, w_out) + mm(far, w_out_far) for own, far in zip(chunk_rows(mixed), chunk_rows(mixed_far))
    ]
    other = [swap(value, NEAR) for value in part]
    head_rows = jnp.concatenate([w_qkv, w_pos], axis=0)
    head_rows = lax.dynamic_slice_in_dim(after(head_rows, part[1]), group * in_rows, in_rows, 1)
    head_rows = swap(head_rows.astype(f32), FAR)

    rows_of = jax.ShapeDtypeStruct((half, width), f32)
    rows_low = jax.ShapeDtypeStruct((half, width), bf16)
    units_of = jax.ShapeDtypeStruct((half, 2 * units), f32)
    units_low = jax.ShapeDtypeStruct((half, 2 * units), bf16)
    scale_of = jax.ShapeDtypeStruct((half, 1), f32)
    fed = []
    for index in range(2):
        arrays = [part[index], other[index], row(b_out), row(gain_one), row(shift_one)]
        arrays += [w_in, w_in_far, b_in_two, w_back, w_back_far]
        shapes = (rows_of, rows_of, scale_of, rows_low, units_low, units_of)
        fed.append(
            on_chunk(feed_kernel, "feed", index, mine_scalars, tokens, half, arrays, shapes)
        )
    part = [value[0] for value in fed]
    other = [swap(value, NEAR) for value in part]
    head_rows = after(head_rows, other[0])
    blocks = gather(head_rows.reshape(-1, columns)).reshape(dp_size, 5, in_rows, columns)
    back = []
    for index in range(2):
        arrays = [part[index], other[index], fed[index][1], fed[index][5], row(gain_one), row(shift_one)]
        arrays += [row(b_back), row(gain_two), row(shift_two), w_in, w_in_far, w_back, w_back_far]
        shapes = (rows_of, rows_of, rows_low, units_low, rows_of)
        shapes += (jax.ShapeDtypeStruct((3, width), f32), jax.ShapeDtypeStruct((2, units), f32))
        back.append(
            on_chunk(feed_back_kernel, "feed_back", index, mine_scalars, cotangent, half, arrays, shapes)
        )
    part = [value[0] for value in back]
    other = [swap(value, NEAR) for value in part]

    rows = take(tokens, page)
    proj_far, w_qkv_far = far_proj(rows, pos_rows, after(blocks, part[1]))
    both = lambda index, source: jnp.concatenate([source[0][index], source[1][index]], axis=0)
    d_feed = after(both(2, back), other[0])
    ffn = feed_grads(dp_size, both(3, fed), both(3, back), both(4, fed), d_feed)
    ffn = lax.psum_scatter(ffn.reshape(-1, units), "dp", scatter_dimension=0, tiled=True)

    arrays = part + other + [back[0][1], back[1][1], fed[0][1], fed[1][1], fed[0][2], fed[1][2]]
    arrays += [row(gain_one), w_out, w_out_far]
    arrays += [proj, proj_far, w_qkv, w_qkv_far]
    send, base, d_heads, d_branch, sums = attend_back(mine_scalars, arrays)

    chunks = 2
    piece = half // chunks

    def pieces(value):
        return [value[k * piece : (k + 1) * piece] for k in range(chunks)]

    def spread(mine, far, rest):
        both = jnp.stack([mine, far])
        out = jnp.stack([jnp.where(low == 0, both, rest), jnp.where(low == 0, rest, both)], axis=1)
        out = out.reshape(pages, length, width)
        return jnp.where(page == 0, out, out[::-1])

    sent = [swap(value, NEAR) for value in pieces(send)]
    mine = [value + other_value for value, other_value in zip(pieces(base), sent)]
    far_mine = [swap(value, FAR) for value in mine]
    rest = [swap(jnp.stack(pair), NEAR) for pair in zip(mine, far_mine)]
    grad_tokens = spread(
        jnp.concatenate(mine, axis=0), jnp.concatenate(far_mine, axis=0), jnp.concatenate(rest, axis=1)
    )

    out_mine = jnp.where(low == 0, back[0][4], back[1][4])
    out_mine = after(out_mine, other[1])
    out_far = after(swap(out_mine, FAR), send)
    out_rest = swap(after(jnp.stack([out_mine, out_far]), mine[-1]), NEAR)
    out_rest = after(out_rest, far_mine[-1])
    layer_out = arrived(spread(out_mine, out_far, out_rest)).astype(bf16)

    vectors = jnp.concatenate([sums, back[0][5] + back[1][5]], axis=0)
    vectors = vectors.reshape(-1, columns)
    vectors = jnp.concatenate([vectors, vectors], axis=1)
    d_b_in = (back[0][6] + back[1][6]).reshape(2, -1, columns)
    vectors = jnp.concatenate([vectors, jnp.concatenate([d_b_in[0], d_b_in[1]], axis=1)], axis=0)
    vectors = jnp.pad(vectors, ((0, -vectors.shape[0] % 16), (0, 0)))
    scalars = jnp.reshape(group, (1,))
    keep, give = weight_grads(
        dp_size, scalars, rows, pos_rows, d_heads, d_branch, mixed, mixed_far, vectors
    )
    bits = [1 << k for k in range(dp_size.bit_length() - 1)]

    def fold(value, bit_list, axis):
        shape = value.shape[1:]
        for bit in bit_list:
            value = value.reshape(((-1, 2) if axis else (2, -1)) + shape)
            kept, given = (value[:, 0], value[:, 1]) if axis else (value[0], value[1])
            value = kept + group_swap(given, bit)
        return value.reshape(shape)

    def unfold(value, bit_list):
        value = value[None]
        for bit in bit_list:
            value = jnp.concatenate([value, group_swap(value, bit)], axis=0)
        return value

    cut = keep.shape[1] // 16 * 8
    total = keep + group_swap(give, bits[0])
    more = bits[1:]
    upper = fold(total[:, :cut], more, 1)
    lower = fold(total[:, cut:], more[::-1], 0)
    total = jnp.concatenate([upper, lower], axis=0)
    total = total[:, :columns] + swap(total[:, columns:], FAR)
    upper = unfold(total[:cut], more)
    lower = unfold(total[cut:], more[::-1])
    parts = [upper, lower, group_swap(upper, bits[0]), group_swap(lower, bits[0])]
    grad_w_qkv, grad_w_pos, grad_w_out, vectors = place_grads(
        scalars, parts, width, vectors.shape[0]
    )
    vectors = vectors[: 7 * width // columns].reshape(7, width)
    grad_b_out, grad_gain_one, grad_shift_one = vectors[0], vectors[1], vectors[2]
    grad_b_back, grad_gain_two, grad_shift_two = vectors[3], vectors[4], vectors[5]
    grad_b_in = vectors[6]

    ffn = after(ffn, mine[-1])
    count = ffn.shape[0] // 2
    ffn = ffn[:count] + after(swap(ffn[count:], FAR), far_mine[0])
    grad_w_in = gather(ffn[:in_rows])
    grad_w_back = gather(ffn[in_rows:])
    return (
        layer_out,
        grad_tokens,
        grad_w_qkv,
        grad_w_pos,
        grad_w_out,
        grad_b_out,
        grad_gain_one,
        grad_shift_one,
        grad_w_in,
        grad_b_in,
        grad_w_back,
        grad_b_back,
        grad_gain_two,
        grad_shift_two,
    )


def solution(mesh):
    placed = (
        P("dp", None, None),
        P("dp"),
        P("dp", None, None),
        P(None, None, "mp"),
        P(None, None, "mp"),
        P("mp", None),
        P(),
        P(),
        P(),
        P(None, "mp"),
        P("mp"),
        P("mp", None),
        P(),
        P(),
        P(),
        P("dp", None, None),
    )
    return jax.shard_map(
        partial(body, mesh.shape["dp"], mesh.shape["mp"]),
        mesh=mesh,
        in_specs=placed,
        out_specs=(
            P("dp", None, None),
            P("dp", None, None),
            P(None, None, "mp"),
            P(None, None, "mp"),
            P("mp", None),
            P(),
            P(),
            P(),
            P(None, "mp"),
            P("mp"),
            P("mp", None),
            P(),
            P(),
            P(),
        ),
        check_vma=False,
    )
```

time: 584 us -> 588 us (level)
  Pallas kernels: 25.3 us -> 61.2 us
  matrix products: 24.4 us -> 1.91 us
  local copies, waits for them, and re-layouts: 94.4 us -> 84.9 us
    pallas_call x4 -> x11, Pallas kernels: 25.3 us -> 61.2 us  [the longest x4 23.1 us: on_chunk(): pl.pallas_call(kernel, out_shape=shapes, grid_spec=pltpu.PrefetchScalarGr...]
    reduce_scatter x1, waiting for transfers between devices: 0.01 us -> 24.9 us  [body(): lax.psum_scatter(ffn.reshape(-1, units), 'dp', scatter_dimension=0, tiled...]
    dot_general x9 -> x0, matrix products: 16.1 us -> none  [the longest x6 11 us: mm_nt(): lax.dot_general(left, right, (((1,), (1,)), ((), ())), preferred_element_...]
    slice x16 -> x7, local copies, waits for them, and re-layouts: 21.4 us -> 5.46 us  [the longest x1 1.92 us: body(): blocks = arrived(gather(far_rows[:count])).reshape(dp_size, count, -1)]
    reduce_sum x9 -> x0, other arithmetic: 11 us -> none  [the longest x2 3.27 us: norm_parts(): center = values - jnp.mean(values, axis=-1, keepdims=True)]
    ppermute x10 -> x11, waiting for transfers between devices: 46.6 us -> 35.6 us  [group_swap(): return lax.ppermute(value, 'dp', pairs)]
    ppermute x17 -> x20, waiting for transfers between devices: 277 us -> 267 us  [swap(): return lax.ppermute(value, 'mp', pairs)]
    unnamed x145 -> x153, local copies, waits for them, and re-layouts: 33.7 us -> 41.3 us
  transfers between devices with their start and end apart: 31 -> 36, of which waited for: 19 -> 21; matrix products, arithmetic and copies ran while one was open for 21% -> 15% of each run, Pallas kernels for 4% -> 10%
where the time goes in v4:
time: 588 us; the launch traced here: 582 us
  waiting for transfers between devices  328 us (56%)
  local copies, waits for them, and re-layouts  84.9 us (14%)
  Pallas kernels  61.2 us (10%)
  other arithmetic  43.9 us (7%)
  starting transfers between devices  34 us (6%)
  between operations  15.4 us (3%)
  blocking collectives  12.7 us (2%)
    ppermute x20, waiting for transfers between devices, swap(): return lax.ppermute(value, 'mp', pairs)  267 us
    unnamed x153, local copies, waits for them, and re-layouts  41.3 us
    ppermute x11, waiting for transfers between devices, group_swap(): return lax.ppermute(value, 'dp', pairs)  35.6 us
    reduce_scatter x1, waiting for transfers between devices, body(): lax.psum_scatter(ffn.reshape(-1, units), 'dp', scatter_dimension=0, tiled...  24.9 us
    ppermute x20, starting transfers between devices, swap(): return lax.ppermute(value, 'mp', pairs)  24.2 us
    pallas_call x4, Pallas kernels, on_chunk(): pl.pallas_call(kernel, out_shape=shapes, grid_spec=pltpu.PrefetchScalarGr...  23.1 us
    pallas_call x1, Pallas kernels, attend_back(): pl.pallas_call(partial(attend_back_kernel, heads), out_shape=shapes, grid...  14.8 us
    all_gather x1, blocking collectives, gather(): return lax.all_gather(value, 'dp', axis=0, tiled=True)  12.7 us
  transfers between devices with their start and end apart: 36, of which 21 were waited for; matrix products, arithmetic and copies ran while one was open for 15% of the time, Pallas kernels for 10%

profile of v4, /device:TPU:0, one launch (start us, length us, event | category | flops | bytes accessed | tf_op | source)
XLA Modules:
  0.0 581.9 jit_solution(3454297195661370275)
XLA Ops:
  10.0 4.0 collective-permute-start
  18.8 4.5 attend.2
  23.3 18.2 %collective-permute-done = f32[200,768]{1,0:T(8,128)} collective-permute-done((f32[200,768]{1,0:T(8,128)}, f32[200,768]{1,0:T(8,128)}, u32[]{:S(2)}, u32[]{:S(2)}) %collective-permute-start) | collective-permute-done | bytes 614432 | tf_op jit(solution)/shard_map/ppermute | solution.py:565
  43.6 3.0 collective-permute-start.2
  46.5 2.6 pad_maximum_fusion.7
  50.7 21.3 %collective-permute-done.2 = f32[24,768]{1,0:T(8,128)S(1)} collective-permute-done((f32[24,768]{1,0:T(8,128)S(1)}, f32[24,768]{1,0:T(8,128)S(1)}, u32[]{:S(2)}, u32[]{:S(2)}) %collective-permute-start.2) | collective-permute-done | bytes 73760 | tf_op jit(solution)/shard_map/ppermute | solution.py:565
  71.9 12.7 %all_gather.15 = f32[192,768]{1,0:T(8,128)S(1)} all-gather(f32[24,768]{1,0:T(8,128)S(1)} %collective-permute-done.2), channel_id=1, replica_groups=mesh['dp'=8,'mp'=4] {'dp'}, dimensions={0}, use_global_device_ids=true | all-gather | bytes 663552 | tf_op jit(solution)/shard_map/all_gather | solution.py:576
  86.6 4.5 attend.3
  92.4 3.0 multiply_convert_fusion
  97.0 15.3 %collective-permute-done.3.other_ref = f32[256,768]{1,0:T(8,128)} collective-permute-done((f32[256,768]{1,0:T(8,128)S(1)}, f32[256,768]{1,0:T(8,128)}, u32[]{:S(2)}, u32[]{:S(2)}) %collective-permute-start.3) | collective-permute-done | bytes 786464 | tf_op jit(solution)/shard_map/ppermute | solution.py:565
  112.3 5.4 feed.2
  123.0 23.2 %collective-permute-done.10 = f32[5,96,192]{1,2,0:T(8,128)S(1)} collective-permute-done((f32[5,96,192]{1,2,0:T(8,128)S(1)}, f32[5,96,192]{1,2,0:T(8,128)S(1)}, u32[]{:S(2)}, u32[]{:S(2)}) %collective-permute-start.10) | collective-permute-done | bytes 368672 | tf_op jit(solution)/shard_map/ppermute | solution.py:565
  154.4 17.1 %collective-permute-done.5.other_ref = f32[256,768]{1,0:T(8,128)S(1)} collective-permute-done((f32[256,768]{1,0:T(8,128)}, f32[256,768]{1,0:T(8,128)S(1)}, u32[]{:S(2)}, u32[]{:S(2)}) %collective-permute-start.5) | collective-permute-done | bytes 786464 | tf_op jit(solution)/shard_map/ppermute | solution.py:565
  172.9 5.1 feed.3
  180.0 5.9 %feed_back.2 = (f32[256,768]{1,0:T(8,128)S(1)}, f32[256,768]{1,0:T(8,128)S(1)}, bf16[256,768]{1,0:T(8,128)(2,1)S(1)}, bf16[256,1536]{1,0:T(8,128)(2,1)S(1)}, f32...) custom-call(s32[3]{0:T(128)S(1)} %add_add_fusion.scalars_ref, bf16[2,512,768]{2,1,0:T(8,128)(2,1)} %cot_ref.3, ...), custom_call_target="tpu_custom_call" | custom-call | flops 2415919104 | bytes 7864320 | tf_op jit(solution)/shard_map/feed_back/pallas_call | solution.py:216
  187.3 11.8 %collective-permute-done.6.other_ref = f32[256,768]{1,0:T(8,128)S(1)} collective-permute-done((f32[256,768]{1,0:T(8,128)S(1)}, f32[256,768]{1,0:T(8,128)S(1)}, u32[]{:S(2)}, u32[]{:S(2)}) %collective-permute-start.6) | collective-permute-done | bytes 786464 | tf_op jit(solution)/shard_map/ppermute | solution.py:565
  199.2 6.7 %feed_back.3 = (f32[256,768]{1,0:T(8,128)}, f32[256,768]{1,0:T(8,128)S(1)}, bf16[256,768]{1,0:T(8,128)(2,1)S(1)}, bf16[256,1536]{1,0:T(8,128)(2,1)S(1)}, f32[256...) custom-call(s32[3]{0:T(128)S(1)} %add_add_fusion.scalars_ref, bf16[2,512,768]{2,1,0:T(8,128)(2,1)} %cot_ref.3, ...), custom_call_target="tpu_custom_call" | custom-call | flops 2415919104 | bytes 7864320 | tf_op jit(solution)/shard_map/feed_back/pallas_call | solution.py:216
  207.1 5.8 %collective-permute-done.9.other_a = f32[256,768]{1,0:T(8,128)S(1)} collective-permute-done((f32[256,768]{1,0:T(8,128)S(1)}, f32[256,768]{1,0:T(8,128)S(1)}, u32[]{:S(2)}, u32[]{:S(2)}) %collective-permute-start.9) | collective-permute-done | bytes 786464 | tf_op jit(solution)/shard_map/ppermute | solution.py:565
  212.9 4.3 feed_grads.1
  217.2 3.7 copy-done
  223.5 5.0 copy.60
  228.5 3.0 copy-done.1
  234.8 3.9 collective-permute-done.7.other_b
  238.7 14.8 %attend_back.1 = (f32[256,768]{1,0:T(8,128)S(1)}, f32[256,768]{1,0:T(8,128)S(1)}, bf16[5,512,384]{2,1,0:T(8,128)(2,1)}, bf16[512,768]{1,0:T(8,128)(2,1)S(1)}, f32[3,768]{1,0:T(4,128)S(1)}) custom-call(s32[3]{0:T(128)S(1)} %add_add_fusion.scalars_ref, f32[256,768]{1,0:T(8,128)S(1)} %copy-done.37, f32[256,768]{1,0:T(8,128)} %get-tuple-element.81.part_b, ...), custom_call_target="tpu_custom_call" | custom-call | flops 3321888768 | bytes 15728640 | tf_op jit(solution)/shard_map/attend_back/pallas_call | solution.py:384
  259.4 7.5 %weight_grads.1 = (f32[4,608,384]{2,1,0:T(8,128)}, f32[4,608,384]{2,1,0:T(8,128)}) custom-call(s32[1]{0:T(128)} %bitcast.25.scalars_ref, bf16[512,768]{1,0:T(8,128)(2,1)S(1)} %dynamic-slice_bitcast_fusion.x_ref, bf16[512,768]{1,0:T(8,128)(2,1)S(1)} %copy-done.30, bf16[5,512,384]{2,1,0:T(8,128)(2,1)S(1)} %copy-done.42, bf16[512,768]{1,0:T(8,128)(2,1)S(1)} %copy-done.45, ...), custom_call_target="tpu_custom_call" | custom-call | flops 1811939328 | bytes 11796480 | tf_op jit(solution)/shard_map/weight_grads/pallas_call | solution.py:448
  266.9 4.2 collective-permute-done.11
  272.0 24.9 %reduce-scatter.2.cloned.1.call-done = f32[384,768]{1,0:T(8,128)} async-done(((f32[3072,768]{1,0:T(8,128)}), f32[384,768]{1,0:T(8,128)}) %reduce-scatter.2.cloned.1.call-update) | async-done | bytes 1179664 | tf_op jit(solution)/shard_map/reduce_scatter | solution.py:653
  298.0 2.5 collective-permute-start.30
  301.0 42.6 %collective-permute-done.15 = f32[128,768]{1,0:T(8,128)S(1)} collective-permute-done((f32[128,768]{1,0:T(8,128)S(1)}, f32[128,768]{1,0:T(8,128)S(1)}, u32[]{:S(2)}, u32[]{:S(2)}) %collective-permute-start.15) | collective-permute-done | bytes 393248 | tf_op jit(solution)/shard_map/ppermute | solution.py:565
  345.4 3.6 add.71
  352.7 28.8 %collective-permute-done.21 = f32[2,304,384]{2,1,0:T(8,128)} collective-permute-done((f32[2,304,384]{2,1,0:T(8,128)}, f32[2,304,384]{2,1,0:T(8,128)}, u32[]{:S(2)}, u32[]{:S(2)}) %collective-permute-start.21) | collective-permute-done | bytes 933920 | tf_op jit(solution)/shard_map/ppermute | solution.py:569
  389.1 2.9 collective-permute-start.13
  394.8 2.4 collective-permute-done.20
  398.8 46.4 %collective-permute-done.8 = f32[256,768]{1,0:T(8,128)} collective-permute-done((f32[256,768]{1,0:T(8,128)S(1)}, f32[256,768]{1,0:T(8,128)}, u32[]{:S(2)}, u32[]{:S(2)}) %collective-permute-start.8) | collective-permute-done | bytes 786464 | tf_op jit(solution)/shard_map/ppermute | solution.py:565
  445.2 2.5 pad_maximum_fusion.2
  450.6 3.0 collective-permute-done.13
  455.7 4.0 collective-permute-done.23
  465.3 2.8 collective-permute-done.26
  469.6 2.1 copy.71
  475.2 2.1 copy.69
  477.7 32.5 %collective-permute-done.16 = f32[2,128,768]{2,1,0:T(8,128)} collective-permute-done((f32[2,128,768]{2,1,0:T(8,128)}, f32[2,128,768]{2,1,0:T(8,128)}, u32[]{:S(2)}, u32[]{:S(2)}) %collective-permute-start.16) | collective-permute-done | bytes 786464 | tf_op jit(solution)/shard_map/ppermute | solution.py:565
  510.2 16.8 %collective-permute-done.17 = f32[2,128,768]{2,1,0:T(8,128)} collective-permute-done((f32[2,128,768]{2,1,0:T(8,128)}, f32[2,128,768]{2,1,0:T(8,128)}, u32[]{:S(2)}, u32[]{:S(2)}) %collective-permute-start.17) | collective-permute-done | bytes 786464 | tf_op jit(solution)/shard_map/ppermute | solution.py:565
  534.7 2.1 copy.70
  540.1 4.9 reverse_select_fusion
  549.2 2.8 copy.75.high_a_ref
  551.9 2.8 copy.76.high_b_ref
  561.2 3.0 copy.77
  570.4 3.4 copy.83
  (292 shorter events, 111.5 us)
Async XLA Ops:
  7.2 85.2 %all-gather.6.cloned.1.call-start = ((), (), s32[]{:S(2)}) async-start(), calls=%async_computation.1 | async-start | bytes 5308416 | tf_op jit(solution)/shard_map/all_gather | solution.py:576
  10.0 31.4 %collective-permute-start = (f32[200,768]{1,0:T(8,128)}, f32[200,768]{1,0:T(8,128)}, u32[]{:S(2)}, u32[]{:S(2)}) collective-permute-start(f32[200,768]{1,0:T(8,128)} %maximum_maximum_fusion), channel_id=1, source_target_pairs={{0,2},{1,3},{2,0},{3,1},{4,6},{5,7},{6,4},{7,5},{8,10},{9,11},{10,... | collective-permute-start | bytes 1843208 | tf_op jit(solution)/shard_map/ppermute | solution.py:565
  15.9 70.7 %copy-start.5 = (bf16[3,768,192]{2,1,0:T(8,128)(2,1)}, bf16[3,768,192]{2,1,0:T(8,128)(2,1)S(1)}, u32[]{:S(2)}) copy-start(bf16[3,768,192]{2,1,0:T(8,128)(2,1)S(1)} %copy.54.wqkv_ref) | copy-start | bytes 2654212
  43.4 180.1 %all-gather.12.cloned.1.call-start = ((), (), s32[]{:S(2)}) async-start(), calls=%async_computation.5 | async-start | bytes 3538944 | tf_op jit(solution)/shard_map/all_gather | solution.py:576
  43.4 41.2 %collective-permute-start.1 = (f32[512,192]{1,0:T(8,128)S(1)}, f32[512,192]{1,0:T(8,128)}, u32[]{:S(2)}, u32[]{:S(2)}) collective-permute-start(f32[512,192]{1,0:T(8,128)S(1)} %attend.2), channel_id=1, source_target_pairs={{0,2},{1,3},{2,0},{3,1},{4,6},{5,7},{6,4},{7,5},{8,10},{9,11},{10,... | collective-permute-start | bytes 1179656 | tf_op jit(solution)/shard_map/ppermute | solution.py:565
  43.6 28.4 %collective-permute-start.2 = (f32[24,768]{1,0:T(8,128)S(1)}, f32[24,768]{1,0:T(8,128)S(1)}, u32[]{:S(2)}, u32[]{:S(2)}) collective-permute-start(f32[24,768]{1,0:T(8,128)S(1)} %dynamic-slice_convert_fusion.1), channel_id=1, source_target_pairs={{0,2},{1,3},{2,0},{3,1},{4,6},{5,7},{6,4},{7,5},{8,10},{9,11},{10,... | collective-permute-start | bytes 221192 | tf_op jit(solution)/shard_map/ppermute | solution.py:565
  49.1 37.5 %copy-start.7 = (bf16[2,512,768]{2,1,0:T(8,128)(2,1)S(1)}, bf16[2,512,768]{2,1,0:T(8,128)(2,1)}, u32[]{:S(2)}) copy-start(bf16[2,512,768]{2,1,0:T(8,128)(2,1)} %x_ref.6) | copy-start | bytes 4718596
  49.1 37.5 %copy-start.32 = (bf16[192,768]{1,0:T(8,128)(2,1)S(1)}, bf16[192,768]{1,0:T(8,128)(2,1)}, u32[]{:S(2)}) copy-start(bf16[192,768]{1,0:T(8,128)(2,1)} %constant.47.clone.table_ref) | copy-start | bytes 884740
  92.4 19.9 %collective-permute-start.3 = (f32[256,768]{1,0:T(8,128)S(1)}, f32[256,768]{1,0:T(8,128)}, u32[]{:S(2)}, u32[]{:S(2)}) collective-permute-start(f32[256,768]{1,0:T(8,128)S(1)} %convolution_add_fusion.1.part_ref), channel_id=1, source_target_pairs={{0,1},{1,0},{2,3},{3,2},{4,5},{5,4},{6,7},{7,6},{8,9},{9,8},{10,11... | collective-permute-start | bytes 2359304 | tf_op jit(solution)/shard_map/ppermute | solution.py:565
  118.5 61.4 %copy-start.17 = (f32[256,768]{1,0:T(8,128)}, f32[256,768]{1,0:T(8,128)S(1)}, u32[]{:S(2)}) copy-start(f32[256,768]{1,0:T(8,128)S(1)} %get-tuple-element.74.xhat_ref.xhat_a) | copy-start | bytes 2359300
  118.5 29.5 %collective-permute-start.4 = (f32[256,768]{1,0:T(8,128)S(1)}, f32[256,768]{1,0:T(8,128)S(1)}, u32[]{:S(2)}, u32[]{:S(2)}) collective-permute-start(f32[256,768]{1,0:T(8,128)S(1)} %get-tuple-element.73.part_ref), channel_id=1, source_target_pairs={{0,1},{1,0},{2,3},{3,2},{4,5},{5,4},{6,7},{7,6},{8,9},{9,8},{10,11... | collective-permute-start | bytes 2359304 | tf_op jit(solution)/shard_map/ppermute | solution.py:565
  121.4 24.7 %collective-permute-start.10 = (f32[5,96,192]{1,2,0:T(8,128)S(1)}, f32[5,96,192]{1,2,0:T(8,128)S(1)}, u32[]{:S(2)}, u32[]{:S(2)}) collective-permute-start(f32[5,96,192]{1,2,0:T(8,128)S(1)} %dynamic-slice_convert_fusion), channel_id=1, source_target_pairs={{0,2},{1,3},{2,0},{3,1},{4,6},{5,7},{6,4},{7,5},{8,10},{9,11},{10,... | collective-permute-start | bytes 1105928 | tf_op jit(solution)/shard_map/ppermute | solution.py:565
  152.9 27.0 %copy-start.70 = (f32[768]{0:T(1024)S(1)}, f32[768]{0:T(1024)}, u32[]{:S(2)}) copy-start(f32[768]{0:T(1024)} %param.29) | copy-start | bytes 9220
  152.9 27.0 %copy-start.71 = (f32[768]{0:T(1024)S(1)}, f32[768]{0:T(1024)}, u32[]{:S(2)}) copy-start(f32[768]{0:T(1024)} %param.30) | copy-start | bytes 9220
  152.9 27.0 %copy-start.72 = (f32[768]{0:T(1024)S(1)}, f32[768]{0:T(1024)}, u32[]{:S(2)}) copy-start(f32[768]{0:T(1024)} %param.31) | copy-start | bytes 9220
  153.0 143.9 %reduce-scatter.2.cloned.1.call-start = ((), (), s32[]{:S(2)}) async-start(), calls=%async_computation.2 | async-start | bytes 10616832 | tf_op jit(solution)/shard_map/reduce_scatter | solution.py:653
  153.2 26.8 %copy-start.20 = (f32[256,768]{1,0:T(8,128)S(1)}, f32[256,768]{1,0:T(8,128)}, u32[]{:S(2)}) copy-start(f32[256,768]{1,0:T(8,128)} %copy-done.19) | copy-start | bytes 2359300
  153.2 26.8 %copy-start.22 = (f32[256,768]{1,0:T(8,128)S(1)}, f32[256,768]{1,0:T(8,128)}, u32[]{:S(2)}) copy-start(f32[256,768]{1,0:T(8,128)} %copy-done.21) | copy-start | bytes 2359300
  153.2 18.3 %collective-permute-start.5 = (f32[256,768]{1,0:T(8,128)}, f32[256,768]{1,0:T(8,128)S(1)}, u32[]{:S(2)}, u32[]{:S(2)}) collective-permute-start(f32[256,768]{1,0:T(8,128)} %convolution_add_fusion.part_ref), channel_id=1, source_target_pairs={{0,1},{1,0},{2,3},{3,2},{4,5},{5,4},{6,7},{7,6},{8,9},{9,8},{10,11... | collective-permute-start | bytes 2359304 | tf_op jit(solution)/shard_map/ppermute | solution.py:565
  178.7 20.5 %copy-start.18 = (f32[256,768]{1,0:T(8,128)}, f32[256,768]{1,0:T(8,128)S(1)}, u32[]{:S(2)}) copy-start(f32[256,768]{1,0:T(8,128)S(1)} %get-tuple-element.78.xhat_ref.xhat_b) | copy-start | bytes 2359300
  178.7 20.5 %collective-permute-start.6 = (f32[256,768]{1,0:T(8,128)S(1)}, f32[256,768]{1,0:T(8,128)S(1)}, u32[]{:S(2)}, u32[]{:S(2)}) collective-permute-start(f32[256,768]{1,0:T(8,128)S(1)} %get-tuple-element.77.part_ref), channel_id=1, source_target_pairs={{0,1},{1,0},{2,3},{3,2},{4,5},{5,4},{6,7},{7,6},{8,9},{9,8},{10,11... | collective-permute-start | bytes 2359304 | tf_op jit(solution)/shard_map/ppermute | solution.py:565
  185.9 27.0 %collective-permute-start.9 = (f32[256,768]{1,0:T(8,128)S(1)}, f32[256,768]{1,0:T(8,128)S(1)}, u32[]{:S(2)}, u32[]{:S(2)}) collective-permute-start(f32[256,768]{1,0:T(8,128)S(1)} %get-tuple-element.83.part_a), channel_id=1, source_target_pairs={{0,1},{1,0},{2,3},{3,2},{4,5},{5,4},{6,7},{7,6},{8,9},{9,8},{10,11... | collective-permute-start | bytes 2359304 | tf_op jit(solution)/shard_map/ppermute | solution.py:565
  221.0 349.4 %all-gather.10.cloned.1.call-start = ((), (), s32[]{:S(2)}) async-start(), calls=%async_computation.4 | async-start | bytes 2654208 | tf_op jit(solution)/shard_map/all_gather | solution.py:576
  221.4 17.3 %collective-permute-start.7 = (f32[256,768]{1,0:T(8,128)}, f32[256,768]{1,0:T(8,128)}, u32[]{:S(2)}, u32[]{:S(2)}) collective-permute-start(f32[256,768]{1,0:T(8,128)} %get-tuple-element.81.part_b), channel_id=1, source_target_pairs={{0,1},{1,0},{2,3},{3,2},{4,5},{5,4},{6,7},{7,6},{8,9},{9,8},{10,11... | collective-permute-start | bytes 2359304 | tf_op jit(solution)/shard_map/ppermute | solution.py:565
  254.6 12.4 %collective-permute-start.14 = (f32[128,768]{1,0:T(8,128)S(1)}, f32[128,768]{1,0:T(8,128)S(1)}, u32[]{:S(2)}, u32[]{:S(2)}) collective-permute-start(f32[128,768]{1,0:T(8,128)S(1)} %get-tuple-element.176), channel_id=1, source_target_pairs={{0,1},{1,0},{2,3},{3,2},{4,5},{5,4},{6,7},{7,6},{8,9},{9,8},{10,11... | collective-permute-start | bytes 1179656 | tf_op jit(solution)/shard_map/ppermute | solution.py:565
  256.4 14.7 %collective-permute-start.11 = (f32[128,768]{1,0:T(8,128)S(1)}, f32[128,768]{1,0:T(8,128)S(1)}, u32[]{:S(2)}, u32[]{:S(2)}) collective-permute-start(f32[128,768]{1,0:T(8,128)S(1)} %get-tuple-element.177), channel_id=1, source_target_pairs={{0,1},{1,0},{2,3},{3,2},{4,5},{5,4},{6,7},{7,6},{8,9},{9,8},{10,11... | collective-permute-start | bytes 1179656 | tf_op jit(solution)/shard_map/ppermute | solution.py:565
  266.9 78.4 %collective-permute-start.18 = (f32[4,608,384]{2,1,0:T(8,128)}, f32[4,608,384]{2,1,0:T(8,128)}, u32[]{:S(2)}, u32[]{:S(2)}) collective-permute-start(f32[4,608,384]{2,1,0:T(8,128)} %get-tuple-element.108), channel_id=1, source_target_pairs={{0,4},{4,0},{8,12},{12,8},{16,20},{20,16},{24,28},{28,24},{1,5},{5... | collective-permute-start | bytes 11206664 | tf_op jit(solution)/shard_map/ppermute | solution.py:569
  272.0 73.3 %copy-start.55 = (f32[128,768]{1,0:T(8,128)}, f32[128,768]{1,0:T(8,128)S(1)}, u32[]{:S(2)}) copy-start(f32[128,768]{1,0:T(8,128)S(1)} %get-tuple-element.174) | copy-start | bytes 1179652
  296.8 47.5 %copy-start.64 = (f32[384,768]{1,0:T(8,128)S(1)}, f32[384,768]{1,0:T(8,128)}, u32[]{:S(2)}) copy-start(f32[384,768]{1,0:T(8,128)} %reduce-scatter.2.cloned.1.call-done) | copy-start | bytes 3538948
  298.0 46.3 %collective-permute-start.30 = (f32[192,768]{1,0:T(8,128)S(1)}, f32[192,768]{1,0:T(8,128)S(1)}, u32[]{:S(2)}, u32[]{:S(2)}) collective-permute-start(f32[192,768]{1,0:T(8,128)S(1)} %slice.175), channel_id=1, source_target_pairs={{0,2},{1,3},{2,0},{3,1},{4,6},{5,7},{6,4},{7,5},{8,10},{9,11},{10,... | collective-permute-start | bytes 1769480 | tf_op jit(solution)/shard_map/ppermute | solution.py:565
  300.5 43.1 %collective-permute-start.15 = (f32[128,768]{1,0:T(8,128)S(1)}, f32[128,768]{1,0:T(8,128)S(1)}, u32[]{:S(2)}, u32[]{:S(2)}) collective-permute-start(f32[128,768]{1,0:T(8,128)S(1)} %get-tuple-element.174), channel_id=1, source_target_pairs={{0,2},{1,3},{2,0},{3,1},{4,6},{5,7},{6,4},{7,5},{8,10},{9,11},{10,... | collective-permute-start | bytes 1179656 | tf_op jit(solution)/shard_map/ppermute | solution.py:565
  345.3 225.1 %all-gather.8.cloned.1.call-start = ((), (), s32[]{:S(2)}) async-start(), calls=%async_computation.3 | async-start | bytes 2654208 | tf_op jit(solution)/shard_map/all_gather | solution.py:576
  350.0 31.5 %collective-permute-start.21 = (f32[2,304,384]{2,1,0:T(8,128)}, f32[2,304,384]{2,1,0:T(8,128)}, u32[]{:S(2)}, u32[]{:S(2)}) collective-permute-start(f32[2,304,384]{2,1,0:T(8,128)} %slice.194), channel_id=1, source_target_pairs={{0,16},{4,20},{8,24},{12,28},{16,0},{20,4},{24,8},{28,12},{1,17},{... | collective-permute-start | bytes 2801672 | tf_op jit(solution)/shard_map/ppermute | solution.py:569
  351.6 34.6 %collective-permute-start.19 = (f32[2,304,384]{2,1,0:T(8,128)S(1)}, f32[2,304,384]{2,1,0:T(8,128)}, u32[]{:S(2)}, u32[]{:S(2)}) collective-permute-start(f32[2,304,384]{2,1,0:T(8,128)S(1)} %slice_bitcast_fusion), channel_id=1, source_target_pairs={{0,8},{4,12},{8,0},{12,4},{16,24},{20,28},{24,16},{28,20},{1,9},{5... | collective-permute-start | bytes 2801672 | tf_op jit(solution)/shard_map/ppermute | solution.py:569
  384.8 8.9 %collective-permute-start.22 = (f32[1,304,384]{2,1,0:T(8,128)}, f32[1,304,384]{2,1,0:T(8,128)}, u32[]{:S(2)}, u32[]{:S(2)}) collective-permute-start(f32[1,304,384]{2,1,0:T(8,128)} %slice.196), channel_id=1, source_target_pairs={{0,8},{4,12},{8,0},{12,4},{16,24},{20,28},{24,16},{28,20},{1,9},{5... | collective-permute-start | bytes 1400840 | tf_op jit(solution)/shard_map/ppermute | solution.py:569
  388.3 8.9 %collective-permute-start.20 = (f32[1,304,384]{2,1,0:T(8,128)}, f32[1,304,384]{2,1,0:T(8,128)}, u32[]{:S(2)}, u32[]{:S(2)}) collective-permute-start(f32[1,304,384]{2,1,0:T(8,128)} %slice_bitcast_fusion.2), channel_id=1, source_target_pairs={{0,16},{4,20},{8,24},{12,28},{16,0},{20,4},{24,8},{28,12},{1,17},{... | collective-permute-start | bytes 1400840 | tf_op jit(solution)/shard_map/ppermute | solution.py:569
  389.0 56.2 %collective-permute-start.8 = (f32[256,768]{1,0:T(8,128)S(1)}, f32[256,768]{1,0:T(8,128)}, u32[]{:S(2)}, u32[]{:S(2)}) collective-permute-start(f32[256,768]{1,0:T(8,128)S(1)} %broadcast_select_fusion), channel_id=1, source_target_pairs={{0,2},{1,3},{2,0},{3,1},{4,6},{5,7},{6,4},{7,5},{8,10},{9,11},{10,... | collective-permute-start | bytes 2359304 | tf_op jit(solution)/shard_map/ppermute | solution.py:565
  389.1 64.5 %collective-permute-start.13 = (f32[128,768]{1,0:T(8,128)}, f32[128,768]{1,0:T(8,128)}, u32[]{:S(2)}, u32[]{:S(2)}) collective-permute-start(f32[128,768]{1,0:T(8,128)} %get-tuple-element.175), channel_id=1, source_target_pairs={{0,2},{1,3},{2,0},{3,1},{4,6},{5,7},{6,4},{7,5},{8,10},{9,11},{10,... | collective-permute-start | bytes 1179656 | tf_op jit(solution)/shard_map/ppermute | solution.py:565
  398.7 60.9 %collective-permute-start.23 = (f32[608,192]{0,1:T(8,128)S(1)}, f32[608,192]{0,1:T(8,128)}, u32[]{:S(2)}, u32[]{:S(2)}) collective-permute-start(f32[608,192]{0,1:T(8,128)S(1)} %copy.67), channel_id=1, source_target_pairs={{0,2},{1,3},{2,0},{3,1},{4,6},{5,7},{6,4},{7,5},{8,10},{9,11},{10,... | collective-permute-start | bytes 1400840 | tf_op jit(solution)/shard_map/ppermute | solution.py:565
  447.6 97.4 %collective-permute-start.12 = (f32[2,256,768]{2,1,0:T(8,128)}, f32[2,256,768]{2,1,0:T(8,128)}, u32[]{:S(2)}, u32[]{:S(2)}) collective-permute-start(f32[2,256,768]{2,1,0:T(8,128)} %pad_maximum_fusion.2), channel_id=1, source_target_pairs={{0,1},{1,0},{2,3},{3,2},{4,5},{5,4},{6,7},{7,6},{8,9},{9,8},{10,11... | collective-permute-start | bytes 4718600 | tf_op jit(solution)/shard_map/ppermute | solution.py:565
  448.6 61.6 %collective-permute-start.16 = (f32[2,128,768]{2,1,0:T(8,128)}, f32[2,128,768]{2,1,0:T(8,128)}, u32[]{:S(2)}, u32[]{:S(2)}) collective-permute-start(f32[2,128,768]{2,1,0:T(8,128)} %pad_maximum_fusion.10), channel_id=1, source_target_pairs={{0,1},{1,0},{2,3},{3,2},{4,5},{5,4},{6,7},{7,6},{8,9},{9,8},{10,11... | collective-permute-start | bytes 2359304 | tf_op jit(solution)/shard_map/ppermute | solution.py:565
  455.7 71.3 %collective-permute-start.17 = (f32[2,128,768]{2,1,0:T(8,128)}, f32[2,128,768]{2,1,0:T(8,128)}, u32[]{:S(2)}, u32[]{:S(2)}) collective-permute-start(f32[2,128,768]{2,1,0:T(8,128)} %pad_maximum_fusion.11), channel_id=1, source_target_pairs={{0,1},{1,0},{2,3},{3,2},{4,5},{5,4},{6,7},{7,6},{8,9},{9,8},{10,11... | collective-permute-start | bytes 2359304 | tf_op jit(solution)/shard_map/ppermute | solution.py:565
  461.1 7.0 %collective-permute-start.26 = (f32[1,304,192]{2,1,0:T(8,128)S(1)}, f32[1,304,192]{2,1,0:T(8,128)S(1)}, u32[]{:S(2)}, u32[]{:S(2)}) collective-permute-start(f32[1,304,192]{2,1,0:T(8,128)S(1)} %get-tuple-element.178), channel_id=1, source_target_pairs={{0,16},{4,20},{8,24},{12,28},{16,0},{20,4},{24,8},{28,12},{1,17},{... | collective-permute-start | bytes 700424 | tf_op jit(solution)/shard_map/ppermute | solution.py:569
  462.7 10.7 %collective-permute-start.24 = (f32[1,304,192]{2,1,0:T(8,128)S(1)}, f32[1,304,192]{2,1,0:T(8,128)}, u32[]{:S(2)}, u32[]{:S(2)}) collective-permute-start(f32[1,304,192]{2,1,0:T(8,128)S(1)} %get-tuple-element.179), channel_id=1, source_target_pairs={{0,8},{4,12},{8,0},{12,4},{16,24},{20,28},{24,16},{28,20},{1,9},{5... | collective-permute-start | bytes 700424 | tf_op jit(solution)/shard_map/ppermute | solution.py:569
  471.7 59.1 %collective-permute-start.27 = (f32[2,304,192]{1,2,0:T(8,128)}, f32[2,304,192]{1,2,0:T(8,128)}, u32[]{:S(2)}, u32[]{:S(2)}) collective-permute-start(f32[2,304,192]{1,2,0:T(8,128)} %copy.71), channel_id=1, source_target_pairs={{0,8},{4,12},{8,0},{12,4},{16,24},{20,28},{24,16},{28,20},{1,9},{5... | collective-permute-start | bytes 1400840 | tf_op jit(solution)/shard_map/ppermute | solution.py:569
  477.3 57.3 %collective-permute-start.25 = (f32[2,304,192]{1,2,0:T(8,128)}, f32[2,304,192]{1,2,0:T(8,128)}, u32[]{:S(2)}, u32[]{:S(2)}) collective-permute-start(f32[2,304,192]{1,2,0:T(8,128)} %copy.69), channel_id=1, source_target_pairs={{0,16},{4,20},{8,24},{12,28},{16,0},{20,4},{24,8},{28,12},{1,17},{... | collective-permute-start | bytes 1400840 | tf_op jit(solution)/shard_map/ppermute | solution.py:569
  539.6 9.5 %collective-permute-start.28 = (f32[4,304,192]{1,2,0:T(8,128)}, f32[4,304,192]{1,2,0:T(8,128)}, u32[]{:S(2)}, u32[]{:S(2)}) collective-permute-start(f32[4,304,192]{1,2,0:T(8,128)} %copy.73), channel_id=1, source_target_pairs={{0,4},{4,0},{8,12},{12,8},{16,20},{20,16},{24,28},{28,24},{1,5},{5... | collective-permute-start | bytes 2801672 | tf_op jit(solution)/shard_map/ppermute | solution.py:569
  539.6 12.3 %collective-permute-start.29 = (f32[4,304,192]{1,2,0:T(8,128)}, f32[4,304,192]{1,2,0:T(8,128)}, u32[]{:S(2)}, u32[]{:S(2)}) collective-permute-start(f32[4,304,192]{1,2,0:T(8,128)} %copy.74), channel_id=1, source_target_pairs={{0,4},{4,0},{8,12},{12,8},{16,20},{20,16},{24,28},{28,24},{1,5},{5... | collective-permute-start | bytes 2801672 | tf_op jit(solution)/shard_map/ppermute | solution.py:569
  (61 other events, 236.7 us)
Sparse Core Ops, SparseCore 0:
  43.5 42.4 all-gather.5
  153.1 31.2 all-gather.11
  221.1 75.7 reduce-scatter.1
  345.4 37.5 all-gather.9
  392.1 29.9 all-gather.7

commit v5 on v4

v5 whole, which is shorter than its diff:
```python
from functools import partial
import math

import jax
import jax.numpy as jnp
import numpy as np
from jax import lax
from jax.experimental import pallas as pl
from jax.experimental.pallas import tpu as pltpu
from jax.sharding import PartitionSpec as P

HEAD_DIM = 64
STEP_BITS = 5
STEP = 1 << STEP_BITS
NEAR = 1
FAR = 2
MASKED = -1e30


def mm(left, right):
    return jnp.dot(left, right, preferred_element_type=jnp.float32)


def mm_nt(left, right):
    return lax.dot_general(
        left, right, (((1,), (1,)), ((), ())), preferred_element_type=jnp.float32
    )


def mm_tn(left, right):
    return lax.dot_general(
        left, right, (((0,), (0,)), ((), ())), preferred_element_type=jnp.float32
    )


def angle_tables(model_width):
    quarter = model_width // 4
    rate = np.exp(np.arange(quarter) * (-math.log(10000.0) / quarter))
    fine = np.arange(STEP)[:, None] * rate
    coarse = fine * STEP
    zero = np.zeros((STEP, 2 * quarter))
    table = np.concatenate(
        [
            np.concatenate([np.sin(coarse), np.cos(coarse), zero], axis=1),
            np.concatenate([zero, np.sin(fine), np.cos(fine)], axis=1),
        ],
        axis=0,
    )
    parts = []
    rest = table
    for _ in range(3):
        part = rest.astype(jnp.bfloat16)
        parts.append(part)
        rest = rest - part.astype(np.float64)
    return np.concatenate(parts, axis=0)


def sinusoid(coord, table_ref):
    quarter = table_ref.shape[1] // 4
    slot = lax.broadcasted_iota(jnp.int32, (2 * STEP, coord.shape[1]), 0)
    coarse = coord >> STEP_BITS
    fine = (coord & (STEP - 1)) + STEP
    hit = ((slot == coarse) | (slot == fine)).astype(jnp.float32).astype(jnp.bfloat16)
    looked = mm_tn(jnp.concatenate([hit, hit, hit], axis=0), table_ref[...])
    sin_a, cos_a, sin_b, cos_b = [looked[:, k * quarter : (k + 1) * quarter] for k in range(4)]
    return jnp.concatenate([sin_a * cos_b + cos_a * sin_b, cos_a * cos_b - sin_a * sin_b], axis=1)


def probs_t(q, k, pq, pk, length, factor):
    left = jnp.concatenate([k, pk, k], axis=0)
    right = jnp.concatenate([q, q, pq], axis=0)
    scores = mm_tn(left, right) * factor
    visible = lax.broadcasted_iota(jnp.int32, scores.shape, 0) < length
    scores = jnp.where(visible, scores, MASKED)
    raised = jnp.exp(scores - jnp.max(scores, axis=0, keepdims=True))
    return raised * (1.0 / jnp.sum(raised, axis=0, keepdims=True))


def rows_at(head):
    return pl.ds(pl.multiple_of(head * HEAD_DIM, HEAD_DIM), HEAD_DIM)


def attend_kernel(
    heads, scalars_ref, lengths_ref, x_ref, coords_ref, table_ref, wqkv_ref, wpos_ref,
    send_ref, own_ref, proj_ref, pos_ref,
):
    step = pl.program_id(0)
    length = lengths_ref[scalars_ref[0] ^ (1 - step)]
    factor = 1.0 / math.sqrt(3.0 * HEAD_DIM)
    rows = x_ref[0]
    for part in range(3):
        proj_ref[part] = mm_nt(wqkv_ref[part], rows).astype(jnp.bfloat16)
    sides = [sinusoid(coords_ref[0, axis : axis + 1], table_ref) for axis in range(2)]
    position = jnp.concatenate(sides, axis=1).astype(jnp.bfloat16)
    pos_ref[...] = position
    for part in range(2):
        proj_ref[3 + part] = mm_nt(wpos_ref[part], position).astype(jnp.bfloat16)

    def one_head(head, _):
        at = rows_at(head)
        q, k, v, pq, pk = [proj_ref[part, at] for part in range(5)]
        weights = probs_t(q, k, pq, pk, length, factor).astype(jnp.bfloat16)
        mixed = mm(v, weights).astype(jnp.bfloat16)

        @pl.when(step == 0)
        def _():
            send_ref[at] = mixed.astype(jnp.float32)

        @pl.when(step == 1)
        def _():
            own_ref[at] = mixed

        return 0

    lax.fori_loop(0, heads, one_head, 0, unroll=True)


def attend(scalars, lengths, tokens, coords, table, w_qkv, w_pos):
    pages, length, width = tokens.shape
    columns = w_qkv.shape[1]
    whole = lambda shape: pl.BlockSpec(shape, lambda i, s, n: (0,) * len(shape))
    shapes = (
        jax.ShapeDtypeStruct((columns, length), jnp.float32),
        jax.ShapeDtypeStruct((columns, length), jnp.bfloat16),
        jax.ShapeDtypeStruct((5, columns, length), jnp.bfloat16),
        jax.ShapeDtypeStruct((length, width), jnp.bfloat16),
    )
    page = lambda i, s, n: (s[0] ^ (1 - i), 0, 0)
    return pl.pallas_call(
        partial(attend_kernel, columns // HEAD_DIM),
        out_shape=shapes,
        grid_spec=pltpu.PrefetchScalarGridSpec(
            num_scalar_prefetch=2,
            grid=(pages,),
            in_specs=[
                pl.BlockSpec((1, length, width), page),
                pl.BlockSpec((1,) + coords.shape[1:], page),
                whole(table.shape),
                whole(w_qkv.shape),
                whole(w_pos.shape),
            ],
            out_specs=[whole(shape.shape) for shape in shapes],
        ),
        compiler_params=pltpu.CompilerParams(vmem_limit_bytes=40 << 20),
        cost_estimate=pl.CostEstimate(
            flops=2 * pages * length * columns * (5 * width + 4 * length),
            transcendentals=pages * length * length * columns // HEAD_DIM,
            bytes_accessed=pages * length * (4 * width + 14 * columns),
        ),
        name="attend",
    )(scalars, lengths, tokens, coords, table, w_qkv, w_pos)


def norm_parts(values):
    center = values - jnp.mean(values, axis=-1, keepdims=True)
    spread = jnp.mean(center * center, axis=-1, keepdims=True)
    scale = lax.rsqrt(spread + 1e-05)
    return center * scale, scale


def norm_back(grad, gain, xhat, scale):
    up = grad * gain
    mean = jnp.mean(up, axis=-1, keepdims=True)
    along = jnp.mean(up * xhat, axis=-1, keepdims=True)
    return scale * (up - mean - xhat * along)


def column_sum(values):
    return jnp.sum(values.astype(jnp.float32), axis=0, keepdims=True)


def feed_kernel(
    scalars_ref, x_ref, part_ref, other_ref, b_out_ref, gain_ref, shift_ref, w_in_ref, w_in_far_ref, b_in_ref,
    w_back_ref, w_back_far_ref, next_ref, xhat_ref, scale_ref, low_ref, hidden_ref, slope_ref,
):
    first = x_ref[0].astype(jnp.float32) + (part_ref[...] + other_ref[...] + b_out_ref[...])
    xhat, scale = norm_parts(first)
    low = (xhat * gain_ref[...] + shift_ref[...]).astype(jnp.bfloat16)
    xhat_ref[...] = xhat
    scale_ref[...] = scale
    low_ref[...] = low
    units = w_in_ref.shape[1]
    total = None
    for side, (into, back) in enumerate(((w_in_ref, w_back_ref), (w_in_far_ref, w_back_far_ref))):
        at = slice(side * units, (side + 1) * units)
        pre = mm(low, into[...]) + b_in_ref[side : side + 1]
        cdf = 0.5 * (1.0 + lax.erf(pre * math.sqrt(0.5)))
        hidden = (pre * cdf).astype(jnp.bfloat16)
        hidden_ref[:, at] = hidden
        slope_ref[:, at] = cdf + pre * (jnp.exp(-0.5 * pre * pre) * (1.0 / math.sqrt(2.0 * math.pi)))
        product = mm(hidden, back[...])
        total = product if total is None else total + product
    next_ref[...] = total


def feed_back_kernel(
    scalars_ref, cot_ref, part_ref, other_ref, xhat_ref, slope_ref, gain_one_ref, shift_one_ref, b_back_ref,
    gain_ref, shift_ref, w_in_ref, w_in_far_ref, w_back_ref, w_back_far_ref,
    next_ref, second_ref, feed_ref, pre_ref, out_ref, sums_ref, sums_in_ref,
):
    normed = xhat_ref[...] * gain_one_ref[...] + shift_one_ref[...]
    second = normed + (part_ref[...] + other_ref[...] + b_back_ref[...])
    xhat, scale = norm_parts(second)
    out_ref[...] = xhat * gain_ref[...] + shift_ref[...]
    grad = cot_ref[0].astype(jnp.float32)
    d_second = norm_back(grad, gain_ref[...], xhat, scale)
    second_ref[...] = d_second
    d_feed = d_second.astype(jnp.bfloat16)
    feed_ref[...] = d_feed
    sums_ref[0:1] = column_sum(d_feed)
    sums_ref[1:2] = column_sum(grad * xhat)
    sums_ref[2:3] = column_sum(grad)
    units = w_in_ref.shape[1]
    total = None
    for side, (into, back) in enumerate(((w_in_ref, w_back_ref), (w_in_far_ref, w_back_far_ref))):
        at = slice(side * units, (side + 1) * units)
        d_pre = (mm_nt(d_feed, back[...]) * slope_ref[:, at]).astype(jnp.bfloat16)
        pre_ref[:, at] = d_pre
        sums_in_ref[side : side + 1] = column_sum(d_pre)
        product = mm_nt(d_pre, into[...])
        total = product if total is None else total + product
    next_ref[...] = total


def on_chunk(kernel, name, chunk, scalars, pages_array, rows, arrays, shapes):
    length, width = pages_array.shape[1:]
    whole = lambda shape: pl.BlockSpec(shape, lambda i, s: (0,) * len(shape))
    return pl.pallas_call(
        kernel,
        out_shape=shapes,
        grid_spec=pltpu.PrefetchScalarGridSpec(
            num_scalar_prefetch=1,
            grid=(1,),
            in_specs=[pl.BlockSpec((1, rows, width), lambda i, s: (s[0], chunk, 0))]
            + [whole(array.shape) for array in arrays],
            out_specs=[whole(shape.shape) for shape in shapes],
        ),
        compiler_params=pltpu.CompilerParams(vmem_limit_bytes=48 << 20),
        cost_estimate=pl.CostEstimate(
            flops=16 * rows * width * width, transcendentals=2 * rows * width, bytes_accessed=40 * rows * width
        ),
        name=name,
    )(scalars, pages_array, *arrays)


def feed_grads_kernel(count, low_ref, pre_ref, hidden_ref, feed_ref, out_ref):
    rows = out_ref.shape[2]

    def put(left, right):
        product = mm_tn(left[...], right[...])
        for block in range(count):
            out_ref[block, 0] = product[block * rows : (block + 1) * rows]

    @pl.when(pl.program_id(0) % 2 == 0)
    def _():
        put(low_ref, pre_ref)

    @pl.when(pl.program_id(0) % 2 == 1)
    def _():
        put(hidden_ref, feed_ref)


def feed_grads(count, low, d_pre, hidden, d_feed):
    length, width = low.shape
    units = hidden.shape[1] // 2
    return pl.pallas_call(
        partial(feed_grads_kernel, count),
        out_shape=jax.ShapeDtypeStruct((count, 4, width // count, units), jnp.float32),
        grid_spec=pl.GridSpec(
            grid=(4,),
            in_specs=[
                pl.BlockSpec((length, width), lambda i: (0, 0)),
                pl.BlockSpec((length, units), lambda i: (0, i // 2)),
                pl.BlockSpec((length, units), lambda i: (0, i // 2)),
                pl.BlockSpec((length, width), lambda i: (0, 0)),
            ],
            out_specs=pl.BlockSpec((count, 1, width // count, units), lambda i: (0, i, 0, 0)),
        ),
        compiler_params=pltpu.CompilerParams(vmem_limit_bytes=40 << 20),
        cost_estimate=pl.CostEstimate(
            flops=8 * length * width * units, transcendentals=0, bytes_accessed=16 * width * units
        ),
        name="feed_grads",
    )(low, d_pre, hidden, d_feed)


def attend_back_kernel(
    heads, scalars_ref, lengths_ref, part_a, part_b, other_a, other_b, second_a, second_b, xhat_a, xhat_b,
    scale_a, scale_b, gain_ref, w_out_ref, w_out_far_ref, own_ref, wqkv_ref, blocks_ref, x_ref, pos_ref,
    send_ref, base_ref, d_ref, branch_ref, sums_ref, dm_ref, first_ref, proj_ref, wfar_ref,
):
    page, low = scalars_ref[0], scalars_ref[1]
    length = lengths_ref[page]
    factor = 1.0 / math.sqrt(3.0 * HEAD_DIM)
    columns = heads * HEAD_DIM
    half = part_a.shape[0]
    count, _, block_rows, _ = blocks_ref.shape
    for part in range(5):
        for block in range(count):
            at = slice(block * block_rows, (block + 1) * block_rows)
            wfar_ref[part, at] = blocks_ref[block, part]
        weight = wfar_ref[part].astype(jnp.bfloat16)
        left = x_ref if part < 3 else pos_ref
        proj_ref[part, columns:] = mm_nt(weight, left[...]).astype(jnp.bfloat16)
        proj_ref[part, :columns] = own_ref[part]
    sums = None
    chunks = ((part_a, other_a, second_a, xhat_a, scale_a), (part_b, other_b, second_b, xhat_b, scale_b))
    for index, (part, other, second, xhat, scale) in enumerate(chunks):
        at = slice(index * half, (index + 1) * half)
        d_normed = second[...] + (part[...] + other[...])
        d_first = norm_back(d_normed, gain_ref[...], xhat[...], scale[...])
        first_ref[at] = d_first
        d_branch = d_first.astype(jnp.bfloat16)
        branch_ref[at] = d_branch
        some = (column_sum(d_branch), column_sum(d_normed * xhat[...]), column_sum(d_normed))
        sums = some if sums is None else tuple(x + y for x, y in zip(sums, some))
        dm_ref[:columns, at] = mm_nt(w_out_ref[...], d_branch).astype(jnp.bfloat16)
        dm_ref[columns:, at] = mm_nt(w_out_far_ref[...], d_branch).astype(jnp.bfloat16)
    for index, value in enumerate(sums):
        sums_ref[index : index + 1] = value

    def one_head(head, _):
        at = rows_at(head)
        q, k, v, pq, pk = [proj_ref[part, at] for part in range(5)]
        dm = dm_ref[at]
        probs = probs_t(q, k, pq, pk, length, factor)
        weights = probs.astype(jnp.bfloat16)
        d_values = mm(weights, dm.T)
        d_probs = mm_tn(v, dm)
        inner = jnp.sum(d_probs * probs, axis=0, keepdims=True)
        d_scores = (probs * (d_probs - inner)).astype(jnp.bfloat16)
        by_queries = mm(d_scores, jnp.concatenate([q, pq], axis=0).T).T
        by_query, by_pos_query = by_queries[:HEAD_DIM], by_queries[HEAD_DIM:]
        by_keys = mm(jnp.concatenate([k, pk], axis=0), d_scores)
        by_key, by_pos_key = by_keys[:HEAD_DIM], by_keys[HEAD_DIM:]
        grads = (
            (by_key + by_pos_key) * factor,
            (by_query + by_pos_query) * factor,
            d_values.T,
            by_key * factor,
            by_query * factor,
        )
        for part, value in enumerate(grads):
            d_ref[part, at] = value.astype(jnp.bfloat16)
        return 0

    lax.fori_loop(0, 2 * heads, one_head, 0, unroll=2)
    for part in range(3):
        for side in range(2):
            at = slice(side * columns, (side + 1) * columns)
            weight = wqkv_ref[part] if side == 0 else wfar_ref[part].astype(jnp.bfloat16)
            first_ref_part = mm_tn(d_ref[part, at], weight)
            if part == side == 0:
                total = first_ref_part
            else:
                total = total + first_ref_part
    upper, lower = total[:half], total[half:]
    send_ref[...] = jnp.where(low == 0, lower, upper)
    base_ref[...] = jnp.where(low == 0, upper + first_ref[:half], lower + first_ref[half:])


def attend_back(scalars, lengths, arrays):
    proj = arrays[13]
    parts, columns, length = proj.shape
    half, width = arrays[0].shape
    heads = columns // HEAD_DIM
    whole = lambda shape: pl.BlockSpec(shape, lambda i, s, n: (0,) * len(shape))
    shapes = (
        jax.ShapeDtypeStruct((half, width), jnp.float32),
        jax.ShapeDtypeStruct((half, width), jnp.float32),
        jax.ShapeDtypeStruct((parts, 2 * columns, length), jnp.bfloat16),
        jax.ShapeDtypeStruct((length, width), jnp.bfloat16),
        jax.ShapeDtypeStruct((3, width), jnp.float32),
    )
    return pl.pallas_call(
        partial(attend_back_kernel, heads),
        out_shape=shapes,
        grid_spec=pltpu.PrefetchScalarGridSpec(
            num_scalar_prefetch=2,
            grid=(1,),
            in_specs=[whole(array.shape) for array in arrays],
            out_specs=[whole(shape.shape) for shape in shapes],
            scratch_shapes=[
                pltpu.VMEM((2 * columns, length), jnp.bfloat16),
                pltpu.VMEM((length, width), jnp.float32),
                pltpu.VMEM((parts, 2 * columns, length), jnp.bfloat16),
                pltpu.VMEM((parts, columns, width), jnp.float32),
            ],
        ),
        compiler_params=pltpu.CompilerParams(vmem_limit_bytes=52 << 20),
        cost_estimate=pl.CostEstimate(
            flops=2 * 2 * heads * length * length * HEAD_DIM * 9 + 20 * length * width * columns,
            transcendentals=2 * heads * length * length,
            bytes_accessed=40 * length * width,
        ),
        name="attend_back",
    )(scalars, lengths, *arrays)


def weight_grads_kernel(
    count, scalars_ref, x_ref, pos_ref, d_ref, db_ref, mixed_ref, far_ref, vec_ref, keep_ref, send_ref
):
    group = scalars_ref[0]
    columns = mixed_ref.shape[0]
    rows = columns // count
    odd = group & 1
    extra = vec_ref.shape[1]
    side_rows = 6 * rows + extra
    mixed = jnp.concatenate([mixed_ref[...], far_ref[...]], axis=0)
    rights = [x_ref] * 3 + [pos_ref] * 2 + [db_ref]

    def put(block, at, value):
        place = (block ^ group) >> 1

        @pl.when(odd == (block & 1))
        def _():
            keep_ref[place, at] = value

        @pl.when(odd != (block & 1))
        def _():
            send_ref[place, at] = value

    for part, right in enumerate(rights):
        product = mm(d_ref[part] if part < 5 else mixed, right[...])
        for block in range(count):
            for side in range(2):
                start = side * columns + block * rows
                at = side * side_rows + part * rows
                put(block, slice(at, at + rows), product[start : start + rows])
    for block in range(count):
        for side in range(2):
            at = slice(side * side_rows + 6 * rows, (side + 1) * side_rows)
            put(block, at, vec_ref[side] if block == 0 else jnp.zeros(vec_ref.shape[1:], jnp.float32))


def weight_grads(count, scalars, rows, pos_rows, d_heads, d_branch, mixed, mixed_far, vectors):
    length, width = rows.shape
    columns = mixed.shape[0]
    block = 2 * (6 * (columns // count) + vectors.shape[1])
    shape = jax.ShapeDtypeStruct((count // 2, block, width), jnp.float32)
    return pl.pallas_call(
        partial(weight_grads_kernel, count),
        out_shape=(shape, shape),
        in_specs=[pl.BlockSpec(memory_space=pltpu.SMEM)] + [pl.BlockSpec(memory_space=pltpu.VMEM)] * 7,
        out_specs=[pl.BlockSpec(memory_space=pltpu.VMEM)] * 2,
        compiler_params=pltpu.CompilerParams(vmem_limit_bytes=48 << 20),
        cost_estimate=pl.CostEstimate(
            flops=24 * length * width * columns,
            transcendentals=0,
            bytes_accessed=4 * count * block * width + 20 * length * columns + 6 * length * width,
        ),
        name="weight_grads",
    )(scalars, rows, pos_rows, d_heads, d_branch, mixed, mixed_far, vectors)


def place_grads_kernel(
    order, scalars_ref, low_a_ref, low_b_ref, high_a_ref, high_b_ref, qkv_ref, pos_ref, out_ref, vec_ref
):
    group = scalars_ref[0]
    count = 2 * low_a_ref.shape[0]
    rows = qkv_ref.shape[1] // count
    cut = low_a_ref.shape[1]

    def read(place, start, stop):
        upper = (place & 1) == 1
        index = place >> 1
        pieces = []
        if start < cut:
            at = slice(start, min(stop, cut))
            pieces.append(jnp.where(upper, high_a_ref[index, at], low_a_ref[index, at]))
        if stop > cut:
            at = slice(max(start, cut) - cut, stop - cut)
            turned_index = 0
            for bit in range(len(order)):
                turned_index = turned_index | (((index >> bit) & 1) << order[bit])
            pieces.append(jnp.where(upper, high_b_ref[turned_index, at], low_b_ref[turned_index, at]))
        return jnp.concatenate(pieces, axis=0) if len(pieces) > 1 else pieces[0]

    for block in range(count):
        place = block ^ group
        at = slice(block * rows, (block + 1) * rows)
        for part in range(6):
            value = read(place, part * rows, (part + 1) * rows)
            if part < 3:
                qkv_ref[part, at] = value
            elif part < 5:
                pos_ref[part - 3, at] = value
            else:
                out_ref[at] = value
        if block == 0:
            vec_ref[...] = read(place, 6 * rows, cut + low_b_ref.shape[1])


def place_grads(scalars, parts, columns, vec_rows):
    width = parts[0].shape[2]
    bits = parts[0].shape[0].bit_length() - 1
    whole = lambda shape: pl.BlockSpec(shape, lambda i: (0,) * len(shape))
    shapes = (
        jax.ShapeDtypeStruct((3, columns, width), jnp.float32),
        jax.ShapeDtypeStruct((2, columns, width), jnp.float32),
        jax.ShapeDtypeStruct((columns, width), jnp.float32),
        jax.ShapeDtypeStruct((vec_rows, width), jnp.float32),
    )
    return pl.pallas_call(
        partial(place_grads_kernel, tuple(range(bits))[::-1]),
        out_shape=shapes,
        grid_spec=pl.GridSpec(
            grid=(1,),
            in_specs=[pl.BlockSpec(memory_space=pltpu.SMEM)] + [whole(part.shape) for part in parts],
            out_specs=[whole(shape.shape) for shape in shapes],
        ),
        compiler_params=pltpu.CompilerParams(vmem_limit_bytes=40 << 20),
        cost_estimate=pl.CostEstimate(
            flops=0, transcendentals=0, bytes_accessed=32 * width * columns * 3
        ),
        name="place_grads",
    )(scalars, *parts)


def body(
    dp_size,
    mp_size,
    tokens,
    lengths,
    coords,
    w_qkv,
    w_pos,
    w_out,
    b_out,
    gain_one,
    shift_one,
    w_in,
    b_in,
    w_back,
    b_back,
    gain_two,
    shift_two,
    cotangent,
):
    pages, length, width = tokens.shape
    columns = w_qkv.shape[2]
    units = w_in.shape[1]
    here = lax.axis_index("mp")
    low = here & 1
    page = here >> 1
    group = lax.axis_index("dp")
    f32, bf16 = jnp.float32, jnp.bfloat16
    half = length // 2
    one = jnp.where(lengths[0] > 0, 1.0, 0.0).astype(f32)

    def arrived(value):
        return value * one

    def swap(value, bit):
        pairs = [(i, i ^ bit) for i in range(mp_size)]
        return lax.ppermute(value, "mp", pairs)

    def group_swap(value, bit):
        pairs = [(i, i ^ bit) for i in range(dp_size)]
        return lax.ppermute(value, "dp", pairs)

    def my_rows(value):
        rows = value.shape[0] // dp_size
        return lax.dynamic_slice_in_dim(value, group * rows, rows, 0)

    def gather(value):
        return lax.all_gather(value, "dp", axis=0, tiled=True)

    def take(value, index):
        return lax.dynamic_index_in_dim(value, index, 0, keepdims=False)

    def after(value, *others):
        return lax.optimization_barrier((value,) + others)[0]

    def row(value):
        return value.reshape(1, -1)

    chunk_rows = lambda value: [value[:half], value[half:]]

    turn = lambda value: jnp.swapaxes(value, 1, 2)
    w_qkv, w_pos = turn(w_qkv), turn(w_pos)
    out_rows = my_rows(w_out).astype(f32)
    out_rows = jnp.pad(out_rows, ((0, max(0, 48 - out_rows.shape[0])), (0, 0)))
    out_rows = swap(out_rows, FAR)
    unit_rows = jnp.concatenate([my_rows(w_in), my_rows(w_back)], axis=0).astype(f32)
    tail = jnp.concatenate([row(b_in), jnp.zeros((7, units), f32)], axis=0)
    far_rows = swap(jnp.concatenate([unit_rows, tail], axis=0), FAR)
    count = columns // dp_size
    w_out_far = gather(out_rows).reshape(dp_size, -1, width)[:, :count].reshape(columns, width)
    w_out_far = arrived(w_out_far).astype(bf16)

    table = jnp.asarray(angle_tables(width))
    scalars = jnp.stack([page, low])
    mixed_send, mixed, proj, pos_rows = attend(scalars, lengths, tokens, coords, table, w_qkv, w_pos)
    mixed_far = swap(mixed_send, FAR)
    far_rows = after(far_rows, mixed_far)
    count = unit_rows.shape[0]
    b_in_two = jnp.stack([b_in, far_rows[count]])
    blocks = arrived(gather(far_rows[:count])).reshape(dp_size, count, -1)
    in_rows = width // dp_size
    w_in_far = blocks[:, :in_rows].reshape(width, units).astype(bf16)
    w_back_far = blocks[:, in_rows:].reshape(units, width).astype(bf16)

    mixed_far = arrived(mixed_far).astype(bf16)
    chunk_columns = lambda value: [value[:, :half], value[:, half:]]
    part = [
        mm_tn(own, w_out) + mm_tn(far, w_out_far)
        for own, far in zip(chunk_columns(mixed), chunk_columns(mixed_far))
    ]
    other = [swap(value, NEAR) for value in part]
    head_rows = jnp.concatenate([w_qkv, w_pos], axis=0)
    count = columns // dp_size
    head_rows = lax.dynamic_slice_in_dim(after(head_rows, part[1]), group * count, count, 1)
    head_rows = swap(head_rows.astype(f32), FAR)
    part[0] = after(part[0], head_rows)

    rows_of = jax.ShapeDtypeStruct((half, width), f32)
    rows_low = jax.ShapeDtypeStruct((half, width), bf16)
    units_of = jax.ShapeDtypeStruct((half, 2 * units), f32)
    units_low = jax.ShapeDtypeStruct((half, 2 * units), bf16)
    scale_of = jax.ShapeDtypeStruct((half, 1), f32)
    fed = []
    for index in range(2):
        arrays = [part[index], other[index], row(b_out), row(gain_one), row(shift_one)]
        arrays += [w_in, w_in_far, b_in_two, w_back, w_back_far]
        shapes = (rows_of, rows_of, scale_of, rows_low, units_low, units_of)
        fed.append(
            on_chunk(feed_kernel, "feed", index, scalars, tokens, half, arrays, shapes)
        )
    part = [value[0] for value in fed]
    other = [swap(value, NEAR) for value in part]
    blocks = gather(head_rows.reshape(-1, width)).reshape(dp_size, 5, count, width)
    back = []
    for index in range(2):
        arrays = [part[index], other[index], fed[index][1], fed[index][5], row(gain_one), row(shift_one)]
        arrays += [row(b_back), row(gain_two), row(shift_two), w_in, w_in_far, w_back, w_back_far]
        shapes = (rows_of, rows_of, rows_low, units_low, rows_of)
        shapes += (jax.ShapeDtypeStruct((3, width), f32), jax.ShapeDtypeStruct((2, units), f32))
        back.append(
            on_chunk(feed_back_kernel, "feed_back", index, scalars, cotangent, half, arrays, shapes)
        )
    part = [value[0] for value in back]
    other = [swap(value, NEAR) for value in part]

    both = lambda index, source: jnp.concatenate([source[0][index], source[1][index]], axis=0)
    d_feed = after(both(2, back), part[1])
    ffn = feed_grads(dp_size, both(3, fed), both(3, back), both(4, fed), d_feed)
    ffn = lax.psum_scatter(ffn.reshape(-1, units), "dp", scatter_dimension=0, tiled=True)

    rows = take(tokens, page)
    arrays = part + other + [back[0][1], back[1][1], fed[0][1], fed[1][1], fed[0][2], fed[1][2]]
    arrays += [row(gain_one), w_out, w_out_far]
    arrays += [proj, w_qkv, blocks, rows, pos_rows]
    send, base, d_heads, d_branch, sums = attend_back(scalars, lengths, arrays)

    def spread(mine, far, rest):
        both = jnp.stack([mine, far])
        out = jnp.stack([jnp.where(low == 0, both, rest), jnp.where(low == 0, rest, both)], axis=1)
        out = out.reshape(pages, length, width)
        return jnp.where(page == 0, out, out[::-1])

    out_mine = jnp.where(low == 0, back[0][4], back[1][4])
    out_far = swap(after(out_mine, other[1]), FAR)

    bits = [1 << k for k in range(dp_size.bit_length() - 1)]
    near_sum = swap(send, NEAR)
    vectors = jnp.concatenate([sums, back[0][5] + back[1][5]], axis=0)
    d_b_in = back[0][6] + back[1][6]
    spare = jnp.zeros((8 - vectors.shape[0] - 1, width), f32)
    vectors = jnp.stack(
        [jnp.concatenate([vectors, d_b_in[side : side + 1], spare], axis=0) for side in range(2)]
    )
    scalars = jnp.reshape(group, (1,))
    keep, give = weight_grads(
        dp_size, scalars, rows, pos_rows, d_heads, d_branch, mixed, mixed_far, vectors
    )
    total = keep + group_swap(give, bits[0])

    mine = base + near_sum
    mine = after(mine, out_far)
    far_mine = swap(mine, FAR)
    more = bits[1:]

    def fold_two(upper, lower):
        for step in range(len(more)):
            upper = upper.reshape((-1, 2) + upper.shape[1:])
            lower = lower.reshape((2, -1) + lower.shape[1:])
            give_upper, give_lower = after_all(upper[:, 1], lower[1])
            upper = upper[:, 0] + group_swap(give_upper, more[step])
            lower = lower[0] + group_swap(give_lower, more[-1 - step])
        return upper[0], lower[0]

    def after_all(*values):
        return lax.optimization_barrier(values)

    cut = total.shape[1] // 2
    upper, lower = fold_two(total[:, :cut], total[:, cut:])
    far_sum = swap(lower, FAR)

    rest = swap(jnp.stack([mine, far_mine, out_far]), NEAR)
    grad_tokens = spread(mine, far_mine, rest[:2])
    out_rest = jnp.where(low == 0, back[1][4], back[0][4])
    layer_out = spread(out_mine, arrived(out_far), jnp.stack([out_rest, arrived(rest[2])])).astype(bf16)
    total = upper + far_sum
    cut = total.shape[0] // 16 * 8
    upper, lower = total[None, :cut], total[None, cut:]
    for step in range(len(more)):
        got_upper = group_swap(upper, more[step])
        got_lower = group_swap(lower, more[-1 - step])
        upper = jnp.concatenate([upper, got_upper], axis=0)
        lower = jnp.concatenate([lower, got_lower], axis=0)
    parts = [upper, lower, group_swap(upper, bits[0]), group_swap(lower, bits[0])]
    grad_w_qkv, grad_w_pos, grad_w_out, vectors = place_grads(scalars, parts, columns, 8)
    grad_w_qkv, grad_w_pos = turn(grad_w_qkv), turn(grad_w_pos)
    grad_b_out, grad_gain_one, grad_shift_one = vectors[0], vectors[1], vectors[2]
    grad_b_back, grad_gain_two, grad_shift_two = vectors[3], vectors[4], vectors[5]
    grad_b_in = vectors[6]

    ffn = after(ffn, mine)
    count = ffn.shape[0] // 2
    ffn = ffn[:count] + swap(ffn[count:], FAR)
    grad_w_in = gather(ffn[:in_rows])
    grad_w_back = gather(ffn[in_rows:])
    return (
        layer_out,
        grad_tokens,
        grad_w_qkv,
        grad_w_pos,
        grad_w_out,
        grad_b_out,
        grad_gain_one,
        grad_shift_one,
        grad_w_in,
        grad_b_in,
        grad_w_back,
        grad_b_back,
        grad_gain_two,
        grad_shift_two,
    )


def solution(mesh):
    placed = (
        P("dp", None, None),
        P("dp"),
        P("dp", None, None),
        P(None, None, "mp"),
        P(None, None, "mp"),
        P("mp", None),
        P(),
        P(),
        P(),
        P(None, "mp"),
        P("mp"),
        P("mp", None),
        P(),
        P(),
        P(),
        P("dp", None, None),
    )
    return jax.shard_map(
        partial(body, mesh.shape["dp"], mesh.shape["mp"]),
        mesh=mesh,
        in_specs=placed,
        out_specs=(
            P("dp", None, None),
            P("dp", None, None),
            P(None, None, "mp"),
            P(None, None, "mp"),
            P("mp", None),
            P(),
            P(),
            P(),
            P(None, "mp"),
            P("mp"),
            P("mp", None),
            P(),
            P(),
            P(),
        ),
        check_vma=False,
    )
```

time: 588 us -> 451 us (0.77)
  local copies, waits for them, and re-layouts: 84.9 us -> 35.5 us
  waiting for transfers between devices: 328 us -> 288 us
  other arithmetic: 43.9 us -> 21.8 us
  blocking collectives: 12.7 us -> 0 us
  starting transfers between devices: 34 us -> 25 us
    reduce_scatter x1, waiting for transfers between devices: 24.9 us -> 0.01 us  [body(): lax.psum_scatter(ffn.reshape(-1, units), 'dp', scatter_dimension=0, tiled...]
    unnamed x153 -> x90, local copies, waits for them, and re-layouts: 41.3 us -> 20.8 us
    ppermute x20 -> x16, waiting for transfers between devices: 267 us -> 251 us  [swap(): return lax.ppermute(value, 'mp', pairs)]
    all_gather x1 -> x0, blocking collectives: 12.7 us -> none  [gather(): return lax.all_gather(value, 'dp', axis=0, tiled=True)]
    all_gather x4 -> x5, waiting for transfers between devices: 0.04 us -> 11.3 us  [gather(): return lax.all_gather(value, 'dp', axis=0, tiled=True)]
    ppermute x11, waiting for transfers between devices: 35.6 us -> 25.3 us  [group_swap(): return lax.ppermute(value, 'dp', pairs)]
    ppermute x5 -> x0, local copies, waits for them, and re-layouts: 10.2 us -> none  [the longest x4 8.95 us: group_swap(): return lax.ppermute(value, 'dp', pairs)]
    ppermute x20 -> x16, starting transfers between devices: 24.2 us -> 15.8 us  [swap(): return lax.ppermute(value, 'mp', pairs)]
  transfers between devices with their start and end apart: 36 -> 33, of which waited for: 21 -> 20; matrix products, arithmetic and copies ran while one was open for 15% -> 8% of each run, Pallas kernels for 10% -> 14%
where the time goes in v5:
time: 451 us; the launch traced here: 450 us
  waiting for transfers between devices  288 us (64%)
  Pallas kernels  63.4 us (14%)
  local copies, waits for them, and re-layouts  35.5 us (8%)
  starting transfers between devices  25 us (6%)
  other arithmetic  21.8 us (5%)
  between operations  14.9 us (3%)
    ppermute x16, waiting for transfers between devices, swap(): return lax.ppermute(value, 'mp', pairs)  251 us
    ppermute x11, waiting for transfers between devices, group_swap(): return lax.ppermute(value, 'dp', pairs)  25.3 us
    pallas_call x4, Pallas kernels, on_chunk(): pl.pallas_call(kernel, out_shape=shapes, grid_spec=pltpu.PrefetchScalarGr...  22.2 us
    unnamed x90, local copies, waits for them, and re-layouts  20.8 us
    pallas_call x1, Pallas kernels, attend_back(): pl.pallas_call(partial(attend_back_kernel, heads), out_shape=shapes, grid...  17.4 us
    ppermute x16, starting transfers between devices, swap(): return lax.ppermute(value, 'mp', pairs)  15.8 us
    all_gather x5, waiting for transfers between devices, gather(): return lax.all_gather(value, 'dp', axis=0, tiled=True)  11.3 us
    pallas_call x1, Pallas kernels, attend(): pl.pallas_call(partial(attend_kernel, columns // HEAD_DIM), out_shape=sha...  9.81 us
  transfers between devices with their start and end apart: 33, of which 20 were waited for; matrix products, arithmetic and copies ran while one was open for 8% of the time, Pallas kernels for 14%

profile of v5, /device:TPU:0, one launch (start us, length us, event | category | flops | bytes accessed | tf_op | source)
XLA Modules:
  0.0 450.0 jit_solution(8751947459078116590)
XLA Ops:
  8.2 4.1 collective-permute-start.1
  12.3 7.0 %collective-permute-done.1 = f32[48,768]{1,0:T(8,128)S(1)} collective-permute-done((f32[48,768]{1,0:T(8,128)S(1)}, f32[48,768]{1,0:T(8,128)S(1)}, u32[]{:S(2)}, u32[]{:S(2)}) %collective-permute-start.1) | collective-permute-done | bytes 147488 | tf_op jit(solution)/shard_map/ppermute | solution.py:556
  23.9 9.8 %attend.1 = (f32[192,512]{1,0:T(8,128)S(1)}, bf16[192,512]{1,0:T(8,128)(2,1)S(1)}, bf16[5,192,512]{2,1,0:T(8,128)(2,1)S(1)}, bf16[512,768]{1,0:T(8,128)(2,1)S(1)}) custom-call(s32[2]{0:T(128)S(1)} %pad_add_fusion.scalars_ref, s32[2]{0:T(128)S(1)} %copy-done.19, bf16[2,512,768]{2,1,0:T(8,128)(2,1)S(1)} %copy-done.16, s32[2,2,512]{2,1,0:T(2,128)S(1)} %copy-done.24, ...), custom_call_target="tpu_custom_call" | custom-call | flops 2315255808 | bytes 5898240 | tf_op jit(solution)/shard_map/attend/pallas_call | solution.py:129
  35.6 2.9 collective-permute-start
  38.5 30.5 %collective-permute-done = f32[192,512]{1,0:T(8,128)S(1)} collective-permute-done((f32[192,512]{1,0:T(8,128)S(1)}, f32[192,512]{1,0:T(8,128)S(1)}, u32[]{:S(2)}, u32[]{:S(2)}) %collective-permute-start) | collective-permute-done | bytes 393248 | tf_op jit(solution)/shard_map/ppermute | solution.py:556
  69.0 1.9 slice.123
  75.1 17.6 %collective-permute-done.2 = f32[5,24,768]{2,1,0:T(8,128)S(1)} collective-permute-done((f32[5,24,768]{2,1,0:T(8,128)S(1)}, f32[5,24,768]{2,1,0:T(8,128)S(1)}, u32[]{:S(2)}, u32[]{:S(2)}) %collective-permute-start.2) | collective-permute-done | bytes 368672 | tf_op jit(solution)/shard_map/ppermute | solution.py:556
  95.3 2.1 collective-permute-start.3
  97.4 11.2 %all-gather.8.cloned.1.call-done = f32[1536,768]{1,0:T(8,128)} async-done(((f32[192,768]{1,0:T(8,128)}), f32[1536,768]{1,0:T(8,128)}) %all-gather.8.cloned.1.call-update) | async-done | bytes 4718608 | tf_op jit(solution)/shard_map/all_gather | solution.py:567
  108.6 2.7 multiply_convert_fusion
  111.3 1.6 fusion.17
  112.9 2.5 collective-permute-done.6.other_ref
  117.5 5.2 %feed.3 = (f32[256,768]{1,0:T(8,128)S(1)}, f32[256,768]{1,0:T(8,128)S(1)}, f32[256,1]{1,0:T(8,128)S(1)}, bf16[256,768]{1,0:T(8,128)(2,1)S(1)}, bf16[256,1536]{1,0:T(8,128)(2,1)S(1)}, /*index=5*/f32[256,1536]{1,0:T(8,128)}) custom-call(s32[2]{0:T(128)S(1)} %pad_add_fusion.scalars_ref, bf16[2,512,768]{2,1,0:T(8,128)(2,1)} %x_ref.5, ...), custom_call_target="tpu_custom_call" | custom-call | flops 2415919104 | bytes 7864320 | tf_op jit(solution)/shard_map/feed/pallas_call | solution.py:228
  122.8 9.6 %collective-permute-done.3.other_ref = f32[256,768]{1,0:T(8,128)} collective-permute-done((f32[256,768]{1,0:T(8,128)S(1)}, f32[256,768]{1,0:T(8,128)}, u32[]{:S(2)}, u32[]{:S(2)}) %collective-permute-start.3) | collective-permute-done | bytes 786464 | tf_op jit(solution)/shard_map/ppermute | solution.py:556
  132.4 5.4 %feed.2 = (f32[256,768]{1,0:T(8,128)S(1)}, f32[256,768]{1,0:T(8,128)S(1)}, f32[256,1]{1,0:T(8,128)S(1)}, bf16[256,768]{1,0:T(8,128)(2,1)S(1)}, bf16[256,1536]{1,0:T(8,128)(2,1)S(1)}, /*index=5*/f32[256,1536]{1,0:T(8,128)}) custom-call(s32[2]{0:T(128)S(1)} %pad_add_fusion.scalars_ref, bf16[2,512,768]{2,1,0:T(8,128)(2,1)} %x_ref.5, ...), custom_call_target="tpu_custom_call" | custom-call | flops 2415919104 | bytes 7864320 | tf_op jit(solution)/shard_map/feed/pallas_call | solution.py:228
  138.5 10.6 %collective-permute-done.7.other_ref = f32[256,768]{1,0:T(8,128)S(1)} collective-permute-done((f32[256,768]{1,0:T(8,128)S(1)}, f32[256,768]{1,0:T(8,128)S(1)}, u32[]{:S(2)}, u32[]{:S(2)}) %collective-permute-start.7) | collective-permute-done | bytes 786464 | tf_op jit(solution)/shard_map/ppermute | solution.py:556
  149.1 5.8 %feed_back.3 = (f32[256,768]{1,0:T(8,128)S(1)}, f32[256,768]{1,0:T(8,128)S(1)}, bf16[256,768]{1,0:T(8,128)(2,1)S(1)}, bf16[256,1536]{1,0:T(8,128)(2,1)S(1)}, f32...) custom-call(s32[2]{0:T(128)S(1)} %pad_add_fusion.scalars_ref, bf16[2,512,768]{2,1,0:T(8,128)(2,1)} %cot_ref.3, ...), custom_call_target="tpu_custom_call" | custom-call | flops 2415919104 | bytes 7864320 | tf_op jit(solution)/shard_map/feed_back/pallas_call | solution.py:228
  155.0 9.8 %collective-permute-done.5.other_ref = f32[256,768]{1,0:T(8,128)S(1)} collective-permute-done((f32[256,768]{1,0:T(8,128)S(1)}, f32[256,768]{1,0:T(8,128)S(1)}, u32[]{:S(2)}, u32[]{:S(2)}) %collective-permute-start.5) | collective-permute-done | bytes 786464 | tf_op jit(solution)/shard_map/ppermute | solution.py:556
  164.8 5.8 %feed_back.2 = (f32[256,768]{1,0:T(8,128)S(1)}, f32[256,768]{1,0:T(8,128)S(1)}, bf16[256,768]{1,0:T(8,128)(2,1)S(1)}, bf16[256,1536]{1,0:T(8,128)(2,1)S(1)}, f32...) custom-call(s32[2]{0:T(128)S(1)} %pad_add_fusion.scalars_ref, bf16[2,512,768]{2,1,0:T(8,128)(2,1)} %cot_ref.3, ...), custom_call_target="tpu_custom_call" | custom-call | flops 2415919104 | bytes 7864320 | tf_op jit(solution)/shard_map/feed_back/pallas_call | solution.py:228
  171.9 4.3 feed_grads.1
  176.2 3.7 copy-done
  181.3 1.7 collective-permute-start.10
  183.1 2.3 dynamic-slice_bitcast_fusion.x_ref
  185.5 16.1 %collective-permute-done.8.other_b = f32[256,768]{1,0:T(8,128)} collective-permute-done((f32[256,768]{1,0:T(8,128)S(1)}, f32[256,768]{1,0:T(8,128)}, u32[]{:S(2)}, u32[]{:S(2)}) %collective-permute-start.8) | collective-permute-done | bytes 786464 | tf_op jit(solution)/shard_map/ppermute | solution.py:556
  201.6 14.8 %collective-permute-done.10.other_a = f32[256,768]{1,0:T(8,128)} collective-permute-done((f32[256,768]{1,0:T(8,128)}, f32[256,768]{1,0:T(8,128)}, u32[]{:S(2)}, u32[]{:S(2)}) %collective-permute-start.10) | collective-permute-done | bytes 786464 | tf_op jit(solution)/shard_map/ppermute | solution.py:556
  217.3 17.4 %attend_back.1 = (f32[256,768]{1,0:T(8,128)S(1)}, f32[256,768]{1,0:T(8,128)}, bf16[5,384,512]{2,1,0:T(8,128)(2,1)}, bf16[512,768]{1,0:T(8,128)(2,1)}, f32[3,768]{1,0:T(4,128)S(1)}) custom-call(s32[2]{0:T(128)S(1)} %pad_add_fusion.scalars_ref, s32[2]{0:T(128)S(1)} %copy-done.19, f32[256,768]{1,0:T(8,128)} %copy-done.13, f32[256,768]{1,0:T(8,128)} %copy-done.10, ...), custom_call_target="tpu_custom_call" | custom-call | flops 3321888768 | bytes 15728640 | tf_op jit(solution)/shard_map/attend_back/pallas_call | solution.py:375
  234.8 1.5 copy-done.20
  237.4 7.5 %weight_grads.1 = (f32[4,304,768]{2,1,0:T(8,128)}, f32[4,304,768]{2,1,0:T(8,128)}) custom-call(s32[1]{0:T(128)} %bitcast.24.scalars_ref, bf16[512,768]{1,0:T(8,128)(2,1)S(1)} %copy-done.5, bf16[512,768]{1,0:T(8,128)(2,1)S(1)} %copy-done.9, bf16[5,384,512]{2,1,0:T(8,128)(2,1)S(1)} %copy-done.20, bf16[512,768]{1,0:T(8,128)(2,1)S(1)} %copy-done.21, ...), custom_call_target="tpu_custom_call" | custom-call | flops 1811939328 | bytes 11796480 | tf_op jit(solution)/shard_map/weight_grads/pallas_call | solution.py:441
  247.3 33.5 %collective-permute-done.11 = f32[256,768]{1,0:T(8,128)S(1)} collective-permute-done((f32[256,768]{1,0:T(8,128)S(1)}, f32[256,768]{1,0:T(8,128)S(1)}, u32[]{:S(2)}, u32[]{:S(2)}) %collective-permute-start.11) | collective-permute-done | bytes 786464 | tf_op jit(solution)/shard_map/ppermute | solution.py:556
  280.9 2.5 collective-permute-done.9
  283.4 1.4 slice.146
  285.2 26.9 %collective-permute-done.26 = f32[192,768]{1,0:T(8,128)S(1)} collective-permute-done((f32[192,768]{1,0:T(8,128)S(1)}, f32[192,768]{1,0:T(8,128)S(1)}, u32[]{:S(2)}, u32[]{:S(2)}) %collective-permute-start.26) | collective-permute-done | bytes 589856 | tf_op jit(solution)/shard_map/ppermute | solution.py:556
  313.6 3.7 add.60
  319.1 29.2 %collective-permute-done.12 = f32[256,768]{1,0:T(8,128)S(1)} collective-permute-done((f32[256,768]{1,0:T(8,128)S(1)}, f32[256,768]{1,0:T(8,128)S(1)}, u32[]{:S(2)}, u32[]{:S(2)}) %collective-permute-start.12) | collective-permute-done | bytes 786464 | tf_op jit(solution)/shard_map/ppermute | solution.py:556
  348.3 1.7 pad_maximum_fusion.2
  352.0 1.5 collective-permute-start.18
  354.9 12.9 %collective-permute-done.18 = f32[1,152,768]{2,1,0:T(8,128)} collective-permute-done((f32[1,152,768]{2,1,0:T(8,128)}, f32[1,152,768]{2,1,0:T(8,128)}, u32[]{:S(2)}, u32[]{:S(2)}) %collective-permute-start.18) | collective-permute-done | bytes 466976 | tf_op jit(solution)/shard_map/ppermute | solution.py:560
  369.0 1.7 collective-permute-start.19
  370.9 40.3 %collective-permute-done.19 = f32[152,768]{1,0:T(8,128)S(1)} collective-permute-done((f32[152,768]{1,0:T(8,128)S(1)}, f32[152,768]{1,0:T(8,128)S(1)}, u32[]{:S(2)}, u32[]{:S(2)}) %collective-permute-start.19) | collective-permute-done | bytes 466976 | tf_op jit(solution)/shard_map/ppermute | solution.py:556
  413.5 1.7 select_bitcast_fusion.1
  415.1 3.1 collective-permute-done.20
  418.3 1.8 collective-permute-start.21
  422.0 6.7 %collective-permute-done.21 = f32[2,72,768]{2,1,0:T(8,128)S(1)} collective-permute-done((f32[2,72,768]{2,1,0:T(8,128)S(1)}, f32[2,72,768]{2,1,0:T(8,128)S(1)}, u32[]{:S(2)}, u32[]{:S(2)}) %collective-permute-start.21) | collective-permute-done | bytes 442400 | tf_op jit(solution)/shard_map/ppermute | solution.py:560
  428.9 2.5 collective-permute-done.23
  432.2 1.4 fusion
  433.7 1.9 reverse_select_fusion
  435.6 2.2 place_grads.1
  438.4 3.4 copy.40
  (195 shorter events, 39.6 us)
Async XLA Ops:
  7.2 65.5 %all-gather.6.cloned.1.call-start = ((), (), s32[]{:S(2)}) async-start(), calls=%async_computation.1 | async-start | bytes 1327104 | tf_op jit(solution)/shard_map/all_gather | solution.py:567
  8.2 11.1 %collective-permute-start.1 = (f32[48,768]{1,0:T(8,128)S(1)}, f32[48,768]{1,0:T(8,128)S(1)}, u32[]{:S(2)}, u32[]{:S(2)}) collective-permute-start(f32[48,768]{1,0:T(8,128)S(1)} %pad_convert_fusion), channel_id=1, source_target_pairs={{0,2},{1,3},{2,0},{3,1},{4,6},{5,7},{6,4},{7,5},{8,10},{9,11},{10,... | collective-permute-start | bytes 442376 | tf_op jit(solution)/shard_map/ppermute | solution.py:556
  20.0 88.6 %all-gather.8.cloned.1.call-start = ((), (), s32[]{:S(2)}) async-start(), calls=%async_computation.2 | async-start | bytes 5308416 | tf_op jit(solution)/shard_map/all_gather | solution.py:567
  22.8 46.2 %collective-permute-start.4 = (f32[200,768]{1,0:T(8,128)}, f32[200,768]{1,0:T(8,128)}, u32[]{:S(2)}, u32[]{:S(2)}) collective-permute-start(f32[200,768]{1,0:T(8,128)} %maximum_maximum_fusion), channel_id=1, source_target_pairs={{0,2},{1,3},{2,0},{3,1},{4,6},{5,7},{6,4},{7,5},{8,10},{9,11},{10,... | collective-permute-start | bytes 1843208 | tf_op jit(solution)/shard_map/ppermute | solution.py:556
  35.6 33.4 %collective-permute-start = (f32[192,512]{1,0:T(8,128)S(1)}, f32[192,512]{1,0:T(8,128)S(1)}, u32[]{:S(2)}, u32[]{:S(2)}) collective-permute-start(f32[192,512]{1,0:T(8,128)S(1)} %get-tuple-element.67), channel_id=1, source_target_pairs={{0,2},{1,3},{2,0},{3,1},{4,6},{5,7},{6,4},{7,5},{8,10},{9,11},{10,... | collective-permute-start | bytes 1179656 | tf_op jit(solution)/shard_map/ppermute | solution.py:556
  71.0 114.5 %all-gather.10.cloned.1.call-start = ((), (), s32[]{:S(2)}) async-start(), calls=%async_computation.3 | async-start | bytes 3317760 | tf_op jit(solution)/shard_map/all_gather | solution.py:567
  73.8 20.0 %copy-start.38 = (f32[768]{0:T(1024)S(1)}, f32[768]{0:T(1024)}, u32[]{:S(2)}) copy-start(f32[768]{0:T(1024)} %param.24) | copy-start | bytes 9220
  73.8 20.0 %copy-start.39 = (f32[768]{0:T(1024)S(1)}, f32[768]{0:T(1024)}, u32[]{:S(2)}) copy-start(f32[768]{0:T(1024)} %param.25) | copy-start | bytes 9220
  73.8 20.0 %copy-start.40 = (f32[768]{0:T(1024)S(1)}, f32[768]{0:T(1024)}, u32[]{:S(2)}) copy-start(f32[768]{0:T(1024)} %param.23) | copy-start | bytes 9220
  75.1 17.7 %collective-permute-start.2 = (f32[5,24,768]{2,1,0:T(8,128)S(1)}, f32[5,24,768]{2,1,0:T(8,128)S(1)}, u32[]{:S(2)}, u32[]{:S(2)}) collective-permute-start(f32[5,24,768]{2,1,0:T(8,128)S(1)} %dynamic-slice_convert_fusion), channel_id=1, source_target_pairs={{0,2},{1,3},{2,0},{3,1},{4,6},{5,7},{6,4},{7,5},{8,10},{9,11},{10,... | collective-permute-start | bytes 1105928 | tf_op jit(solution)/shard_map/ppermute | solution.py:556
  93.6 189.8 %reduce-scatter.2.cloned.1.call-start = ((), (), s32[]{:S(2)}) async-start(), calls=%async_computation.4 | async-start | bytes 10616832 | tf_op jit(solution)/shard_map/reduce_scatter | solution.py:648
  94.9 20.5 %collective-permute-start.6 = (f32[256,768]{1,0:T(8,128)S(1)}, f32[256,768]{1,0:T(8,128)S(1)}, u32[]{:S(2)}, u32[]{:S(2)}) collective-permute-start(f32[256,768]{1,0:T(8,128)S(1)} %convolution_add_fusion.part_ref), channel_id=1, source_target_pairs={{0,1},{1,0},{2,3},{3,2},{4,5},{5,4},{6,7},{7,6},{8,9},{9,8},{10,11... | collective-permute-start | bytes 2359304 | tf_op jit(solution)/shard_map/ppermute | solution.py:556
  95.3 37.1 %collective-permute-start.3 = (f32[256,768]{1,0:T(8,128)S(1)}, f32[256,768]{1,0:T(8,128)}, u32[]{:S(2)}, u32[]{:S(2)}) collective-permute-start(f32[256,768]{1,0:T(8,128)S(1)} %convolution_add_fusion.1.part_ref), channel_id=1, source_target_pairs={{0,1},{1,0},{2,3},{3,2},{4,5},{5,4},{6,7},{7,6},{8,9},{9,8},{10,11... | collective-permute-start | bytes 2359304 | tf_op jit(solution)/shard_map/ppermute | solution.py:556
  122.7 26.4 %copy-start.3 = (f32[256,768]{1,0:T(8,128)}, f32[256,768]{1,0:T(8,128)S(1)}, u32[]{:S(2)}) copy-start(f32[256,768]{1,0:T(8,128)S(1)} %get-tuple-element.76.xhat_ref.xhat_b) | copy-start | bytes 2359300
  122.7 26.4 %collective-permute-start.7 = (f32[256,768]{1,0:T(8,128)S(1)}, f32[256,768]{1,0:T(8,128)S(1)}, u32[]{:S(2)}, u32[]{:S(2)}) collective-permute-start(f32[256,768]{1,0:T(8,128)S(1)} %get-tuple-element.75.part_ref), channel_id=1, source_target_pairs={{0,1},{1,0},{2,3},{3,2},{4,5},{5,4},{6,7},{7,6},{8,9},{9,8},{10,11... | collective-permute-start | bytes 2359304 | tf_op jit(solution)/shard_map/ppermute | solution.py:556
  137.7 27.1 %copy-start.4 = (f32[256,768]{1,0:T(8,128)}, f32[256,768]{1,0:T(8,128)S(1)}, u32[]{:S(2)}) copy-start(f32[256,768]{1,0:T(8,128)S(1)} %get-tuple-element.72.xhat_ref.xhat_a) | copy-start | bytes 2359300
  137.7 27.1 %collective-permute-start.5 = (f32[256,768]{1,0:T(8,128)S(1)}, f32[256,768]{1,0:T(8,128)S(1)}, u32[]{:S(2)}, u32[]{:S(2)}) collective-permute-start(f32[256,768]{1,0:T(8,128)S(1)} %get-tuple-element.71.part_ref), channel_id=1, source_target_pairs={{0,1},{1,0},{2,3},{3,2},{4,5},{5,4},{6,7},{7,6},{8,9},{9,8},{10,11... | collective-permute-start | bytes 2359304 | tf_op jit(solution)/shard_map/ppermute | solution.py:556
  154.9 15.7 %copy-start.10 = (f32[256,768]{1,0:T(8,128)}, f32[256,768]{1,0:T(8,128)S(1)}, u32[]{:S(2)}) copy-start(f32[256,768]{1,0:T(8,128)S(1)} %get-tuple-element.79.part_b) | copy-start | bytes 2359300
  155.0 15.7 %copy-start.12 = (f32[256,768]{1,0:T(8,128)}, f32[256,768]{1,0:T(8,128)S(1)}, u32[]{:S(2)}) copy-start(f32[256,768]{1,0:T(8,128)S(1)} %get-tuple-element.83.second_b) | copy-start | bytes 2359300
  179.9 258.4 %all-gather.12.cloned.1.call-start = ((), (), s32[]{:S(2)}) async-start(), calls=%async_computation.5 | async-start | bytes 2654208 | tf_op jit(solution)/shard_map/all_gather | solution.py:567
  181.0 20.6 %collective-permute-start.8 = (f32[256,768]{1,0:T(8,128)S(1)}, f32[256,768]{1,0:T(8,128)}, u32[]{:S(2)}, u32[]{:S(2)}) collective-permute-start(f32[256,768]{1,0:T(8,128)S(1)} %copy-done.11), channel_id=1, source_target_pairs={{0,1},{1,0},{2,3},{3,2},{4,5},{5,4},{6,7},{7,6},{8,9},{9,8},{10,11... | collective-permute-start | bytes 2359304 | tf_op jit(solution)/shard_map/ppermute | solution.py:556
  181.3 35.1 %collective-permute-start.10 = (f32[256,768]{1,0:T(8,128)}, f32[256,768]{1,0:T(8,128)}, u32[]{:S(2)}, u32[]{:S(2)}) collective-permute-start(f32[256,768]{1,0:T(8,128)} %copy-done.13), channel_id=1, source_target_pairs={{0,1},{1,0},{2,3},{3,2},{4,5},{5,4},{6,7},{7,6},{8,9},{9,8},{10,11... | collective-permute-start | bytes 2359304 | tf_op jit(solution)/shard_map/ppermute | solution.py:556
  217.3 17.4 %copy-start.5 = (bf16[512,768]{1,0:T(8,128)(2,1)S(1)}, bf16[512,768]{1,0:T(8,128)(2,1)}, u32[]{:S(2)}) copy-start(bf16[512,768]{1,0:T(8,128)(2,1)} %dynamic-slice_bitcast_fusion.x_ref) | copy-start | bytes 2359300
  217.3 17.4 %copy-start.9 = (bf16[512,768]{1,0:T(8,128)(2,1)S(1)}, bf16[512,768]{1,0:T(8,128)(2,1)}, u32[]{:S(2)}) copy-start(bf16[512,768]{1,0:T(8,128)(2,1)} %copy-done.8) | copy-start | bytes 2359300
  245.0 35.8 %copy-start.35 = (f32[256,768]{1,0:T(8,128)S(1)}, f32[256,768]{1,0:T(8,128)}, u32[]{:S(2)}) copy-start(f32[256,768]{1,0:T(8,128)} %get-tuple-element.88) | copy-start | bytes 2359300
  245.0 68.6 %collective-permute-start.14 = (f32[4,304,768]{2,1,0:T(8,128)}, f32[4,304,768]{2,1,0:T(8,128)}, u32[]{:S(2)}, u32[]{:S(2)}) collective-permute-start(f32[4,304,768]{2,1,0:T(8,128)} %get-tuple-element.99), channel_id=1, source_target_pairs={{0,4},{4,0},{8,12},{12,8},{16,20},{20,16},{24,28},{28,24},{1,5},{5... | collective-permute-start | bytes 11206664 | tf_op jit(solution)/shard_map/ppermute | solution.py:560
  245.1 35.7 %copy-start.31 = (f32[256,768]{1,0:T(8,128)}, f32[256,768]{1,0:T(8,128)S(1)}, u32[]{:S(2)}) copy-start(f32[256,768]{1,0:T(8,128)S(1)} %broadcast_select_fusion) | copy-start | bytes 2359300
  245.1 35.7 %collective-permute-start.11 = (f32[256,768]{1,0:T(8,128)S(1)}, f32[256,768]{1,0:T(8,128)S(1)}, u32[]{:S(2)}, u32[]{:S(2)}) collective-permute-start(f32[256,768]{1,0:T(8,128)S(1)} %get-tuple-element.89), channel_id=1, source_target_pairs={{0,1},{1,0},{2,3},{3,2},{4,5},{5,4},{6,7},{7,6},{8,9},{9,8},{10,11... | collective-permute-start | bytes 2359304 | tf_op jit(solution)/shard_map/ppermute | solution.py:556
  245.9 37.5 %collective-permute-start.9 = (f32[256,768]{1,0:T(8,128)S(1)}, f32[256,768]{1,0:T(8,128)S(1)}, u32[]{:S(2)}, u32[]{:S(2)}) collective-permute-start(f32[256,768]{1,0:T(8,128)S(1)} %broadcast_select_fusion), channel_id=1, source_target_pairs={{0,2},{1,3},{2,0},{3,1},{4,6},{5,7},{6,4},{7,5},{8,10},{9,11},{10,... | collective-permute-start | bytes 2359304 | tf_op jit(solution)/shard_map/ppermute | solution.py:556
  283.4 64.9 %copy-start.29 = (f32[256,768]{1,0:T(8,128)}, f32[256,768]{1,0:T(8,128)S(1)}, u32[]{:S(2)}) copy-start(f32[256,768]{1,0:T(8,128)S(1)} %collective-permute-done.9) | copy-start | bytes 2359300
  283.4 28.8 %copy-start.34 = (f32[384,768]{1,0:T(8,128)S(1)}, f32[384,768]{1,0:T(8,128)}, u32[]{:S(2)}) copy-start(f32[384,768]{1,0:T(8,128)} %reduce-scatter.2.cloned.1.call-done) | copy-start | bytes 3538948
  284.8 27.4 %collective-permute-start.26 = (f32[192,768]{1,0:T(8,128)S(1)}, f32[192,768]{1,0:T(8,128)S(1)}, u32[]{:S(2)}, u32[]{:S(2)}) collective-permute-start(f32[192,768]{1,0:T(8,128)S(1)} %slice.146), channel_id=1, source_target_pairs={{0,2},{1,3},{2,0},{3,1},{4,6},{5,7},{6,4},{7,5},{8,10},{9,11},{10,... | collective-permute-start | bytes 1769480 | tf_op jit(solution)/shard_map/ppermute | solution.py:556
  313.2 125.2 %all-gather.14.cloned.1.call-start = ((), (), s32[]{:S(2)}) async-start(), calls=%async_computation.6 | async-start | bytes 2654208 | tf_op jit(solution)/shard_map/all_gather | solution.py:567
  313.5 34.8 %collective-permute-start.12 = (f32[256,768]{1,0:T(8,128)S(1)}, f32[256,768]{1,0:T(8,128)S(1)}, u32[]{:S(2)}, u32[]{:S(2)}) collective-permute-start(f32[256,768]{1,0:T(8,128)S(1)} %add.57), channel_id=1, source_target_pairs={{0,2},{1,3},{2,0},{3,1},{4,6},{5,7},{6,4},{7,5},{8,10},{9,11},{10,... | collective-permute-start | bytes 2359304 | tf_op jit(solution)/shard_map/ppermute | solution.py:556
  317.6 32.4 %collective-permute-start.16 = (f32[2,152,768]{2,1,0:T(8,128)S(1)}, f32[2,152,768]{2,1,0:T(8,128)S(1)}, u32[]{:S(2)}, u32[]{:S(2)}) collective-permute-start(f32[2,152,768]{2,1,0:T(8,128)S(1)} %slice.165), channel_id=1, source_target_pairs={{0,16},{4,20},{8,24},{12,28},{16,0},{20,4},{24,8},{28,12},{1,17},{... | collective-permute-start | bytes 2801672 | tf_op jit(solution)/shard_map/ppermute | solution.py:560
  317.7 32.4 %collective-permute-start.15 = (f32[2,152,768]{2,1,0:T(8,128)S(1)}, f32[2,152,768]{2,1,0:T(8,128)S(1)}, u32[]{:S(2)}, u32[]{:S(2)}) collective-permute-start(f32[2,152,768]{2,1,0:T(8,128)S(1)} %slice_bitcast_fusion), channel_id=1, source_target_pairs={{0,8},{4,12},{8,0},{12,4},{16,24},{20,28},{24,16},{28,20},{1,9},{5... | collective-permute-start | bytes 2801672 | tf_op jit(solution)/shard_map/ppermute | solution.py:560
  350.0 63.5 %collective-permute-start.13 = (f32[3,256,768]{2,1,0:T(8,128)}, f32[3,256,768]{2,1,0:T(8,128)}, u32[]{:S(2)}, u32[]{:S(2)}) collective-permute-start(f32[3,256,768]{2,1,0:T(8,128)} %pad_maximum_fusion.2), channel_id=1, source_target_pairs={{0,1},{1,0},{2,3},{3,2},{4,5},{5,4},{6,7},{7,6},{8,9},{9,8},{10,11... | collective-permute-start | bytes 7077896 | tf_op jit(solution)/shard_map/ppermute | solution.py:556
  352.0 15.8 %collective-permute-start.18 = (f32[1,152,768]{2,1,0:T(8,128)}, f32[1,152,768]{2,1,0:T(8,128)}, u32[]{:S(2)}, u32[]{:S(2)}) collective-permute-start(f32[1,152,768]{2,1,0:T(8,128)} %slice.169), channel_id=1, source_target_pairs={{0,8},{4,12},{8,0},{12,4},{16,24},{20,28},{24,16},{28,20},{1,9},{5... | collective-permute-start | bytes 1400840 | tf_op jit(solution)/shard_map/ppermute | solution.py:560
  353.5 17.3 %copy-start.30 = (f32[256,768]{1,0:T(8,128)S(1)}, f32[256,768]{1,0:T(8,128)}, u32[]{:S(2)}) copy-start(f32[256,768]{1,0:T(8,128)} %copy-done.29) | copy-start | bytes 2359300
  353.6 17.3 %collective-permute-start.17 = (f32[1,152,768]{2,1,0:T(8,128)}, f32[1,152,768]{2,1,0:T(8,128)S(1)}, u32[]{:S(2)}, u32[]{:S(2)}) collective-permute-start(f32[1,152,768]{2,1,0:T(8,128)} %slice_bitcast_fusion.2), channel_id=1, source_target_pairs={{0,16},{4,20},{8,24},{12,28},{16,0},{20,4},{24,8},{28,12},{1,17},{... | collective-permute-start | bytes 1400840 | tf_op jit(solution)/shard_map/ppermute | solution.py:560
  369.0 42.2 %collective-permute-start.19 = (f32[152,768]{1,0:T(8,128)S(1)}, f32[152,768]{1,0:T(8,128)S(1)}, u32[]{:S(2)}, u32[]{:S(2)}) collective-permute-start(f32[152,768]{1,0:T(8,128)S(1)} %fusion.7), channel_id=1, source_target_pairs={{0,2},{1,3},{2,0},{3,1},{4,6},{5,7},{6,4},{7,5},{8,10},{9,11},{10,... | collective-permute-start | bytes 1400840 | tf_op jit(solution)/shard_map/ppermute | solution.py:556
  370.9 42.6 %copy-start.28 = (f32[256,768]{1,0:T(8,128)S(1)}, f32[256,768]{1,0:T(8,128)}, u32[]{:S(2)}) copy-start(f32[256,768]{1,0:T(8,128)} %copy-done.27) | copy-start | bytes 2359300
  411.3 8.8 %collective-permute-start.22 = (f32[1,80,768]{2,1,0:T(8,128)S(1)}, f32[1,80,768]{2,1,0:T(8,128)S(1)}, u32[]{:S(2)}, u32[]{:S(2)}) collective-permute-start(f32[1,80,768]{2,1,0:T(8,128)S(1)} %slice_bitcast_fusion.4), channel_id=1, source_target_pairs={{0,16},{4,20},{8,24},{12,28},{16,0},{20,4},{24,8},{28,12},{1,17},{... | collective-permute-start | bytes 737288 | tf_op jit(solution)/shard_map/ppermute | solution.py:560
  412.2 6.1 %collective-permute-start.20 = (f32[1,72,768]{2,1,0:T(8,128)S(1)}, f32[1,72,768]{2,1,0:T(8,128)S(1)}, u32[]{:S(2)}, u32[]{:S(2)}) collective-permute-start(f32[1,72,768]{2,1,0:T(8,128)S(1)} %slice_bitcast_fusion.5), channel_id=1, source_target_pairs={{0,8},{4,12},{8,0},{12,4},{16,24},{20,28},{24,16},{28,20},{1,9},{5... | collective-permute-start | bytes 663560 | tf_op jit(solution)/shard_map/ppermute | solution.py:560
  418.3 10.4 %collective-permute-start.21 = (f32[2,72,768]{2,1,0:T(8,128)S(1)}, f32[2,72,768]{2,1,0:T(8,128)S(1)}, u32[]{:S(2)}, u32[]{:S(2)}) collective-permute-start(f32[2,72,768]{2,1,0:T(8,128)S(1)} %pad_maximum_fusion.14), channel_id=1, source_target_pairs={{0,16},{4,20},{8,24},{12,28},{16,0},{20,4},{24,8},{28,12},{1,17},{... | collective-permute-start | bytes 1327112 | tf_op jit(solution)/shard_map/ppermute | solution.py:560
  420.2 11.2 %collective-permute-start.23 = (f32[2,80,768]{2,1,0:T(8,128)S(1)}, f32[2,80,768]{2,1,0:T(8,128)S(1)}, u32[]{:S(2)}, u32[]{:S(2)}) collective-permute-start(f32[2,80,768]{2,1,0:T(8,128)S(1)} %pad_maximum_fusion.13), channel_id=1, source_target_pairs={{0,8},{4,12},{8,0},{12,4},{16,24},{20,28},{24,16},{28,20},{1,9},{5... | collective-permute-start | bytes 1474568 | tf_op jit(solution)/shard_map/ppermute | solution.py:560
  428.8 6.7 %collective-permute-start.24 = (f32[4,72,768]{2,1,0:T(8,128)S(1)}, f32[4,72,768]{2,1,0:T(8,128)S(1)}, u32[]{:S(2)}, u32[]{:S(2)}) collective-permute-start(f32[4,72,768]{2,1,0:T(8,128)S(1)} %pad_maximum_fusion.10.low_a_ref), channel_id=1, source_target_pairs={{0,4},{4,0},{8,12},{12,8},{16,20},{20,16},{24,28},{28,24},{1,5},{5... | collective-permute-start | bytes 2654216 | tf_op jit(solution)/shard_map/ppermute | solution.py:560
  431.5 4.1 collective-permute-start.25
  (29 other events, 162.8 us)
Sparse Core Ops, SparseCore 0:
  20.1 25.3 all-gather.5
  71.1 37.4 all-gather.7
  110.5 31.4 all-gather.9
  180.1 74.9 reduce-scatter.1
  313.3 37.2 all-gather.11
  353.7 29.1 all-gather.13

commit v6 on v5

--- a/solution.py
+++ b/solution.py
@@ -13,6 +13,7 @@
 STEP_BITS = 5
 STEP = 1 << STEP_BITS
 NEAR = 1
+MP = ("far", "near")
 FAR = 2
 MASKED = -1e30
 
@@ -171,7 +172,7 @@
 
 def feed_kernel(
     scalars_ref, x_ref, part_ref, other_ref, b_out_ref, gain_ref, shift_ref, w_in_ref, w_in_far_ref, b_in_ref,
-    w_back_ref, w_back_far_ref, next_ref, xhat_ref, scale_ref, low_ref, hidden_ref, slope_ref,
+    w_back_ref, w_back_far_ref, xhat_ref, scale_ref, low_ref, hidden_ref, slope_ref, next_ref,
 ):
     first = x_ref[0].astype(jnp.float32) + (part_ref[...] + other_ref[...] + b_out_ref[...])
     xhat, scale = norm_parts(first)
@@ -222,25 +223,40 @@
     next_ref[...] = total
 
 
-def on_chunk(kernel, name, chunk, scalars, pages_array, rows, arrays, shapes):
+def without(kernel, first, count):
+    def call(*refs):
+        return kernel(*refs[:first], *refs[first + count :])
+
+    return call
+
+
+def on_chunk(kernel, name, chunk, scalars, pages_array, rows, arrays, shapes, before=()):
     length, width = pages_array.shape[1:]
-    whole = lambda shape: pl.BlockSpec(shape, lambda i, s: (0,) * len(shape))
+
+    def rows_of(array):
+        if array.shape[0] == length and len(array.shape) == 2:
+            return pl.BlockSpec((rows, array.shape[1]), lambda i, s: (chunk, 0))
+        return pl.BlockSpec(array.shape, lambda i, s: (0,) * len(array.shape))
+
+    inputs = 2 + len(arrays)
     return pl.pallas_call(
-        kernel,
+        without(kernel, inputs, len(before)),
         out_shape=shapes,
         grid_spec=pltpu.PrefetchScalarGridSpec(
             num_scalar_prefetch=1,
             grid=(1,),
             in_specs=[pl.BlockSpec((1, rows, width), lambda i, s: (s[0], chunk, 0))]
-            + [whole(array.shape) for array in arrays],
-            out_specs=[whole(shape.shape) for shape in shapes],
-        ),
+            + [rows_of(array) for array in arrays]
+            + [pl.BlockSpec(memory_space=pl.ANY)] * len(before),
+            out_specs=[rows_of(shape) for shape in shapes],
+        ),
+        input_output_aliases={inputs + index: index for index in range(len(before))},
         compiler_params=pltpu.CompilerParams(vmem_limit_bytes=48 << 20),
         cost_estimate=pl.CostEstimate(
             flops=16 * rows * width * width, transcendentals=2 * rows * width, bytes_accessed=40 * rows * width
         ),
         name=name,
-    )(scalars, pages_array, *arrays)
+    )(scalars, pages_array, *arrays, *before)
 
 
 def feed_grads_kernel(count, low_ref, pre_ref, hidden_ref, feed_ref, out_ref):
@@ -265,7 +281,7 @@
     units = hidden.shape[1] // 2
     return pl.pallas_call(
         partial(feed_grads_kernel, count),
-        out_shape=jax.ShapeDtypeStruct((count, 4, width // count, units), jnp.float32),
+        out_shape=pltpu.HBM((count, 4, width // count, units), jnp.float32),
         grid_spec=pl.GridSpec(
             grid=(4,),
             in_specs=[
@@ -284,40 +300,74 @@
     )(low, d_pre, hidden, d_feed)
 
 
+def weight_grads(count, group, x_ref, pos_ref, d_ref, db_ref, mixed_ref, far_ref, vec_ref, keep_ref, send_ref):
+    columns = mixed_ref.shape[0]
+    rows = columns // count
+    odd = group & 1
+    extra = vec_ref.shape[1]
+    side_rows = 6 * rows + extra
+    mixed = jnp.concatenate([mixed_ref[...], far_ref[...]], axis=0)
+    rights = [x_ref] * 3 + [pos_ref] * 2 + [db_ref]
+
+    def put(block, at, value):
+        place = (block ^ group) >> 1
+
+        @pl.when(odd == (block & 1))
+        def _():
+            keep_ref[place, at] = value
+
+        @pl.when(odd != (block & 1))
+        def _():
+            send_ref[place, at] = value
+
+    for part, right in enumerate(rights):
+        product = mm(d_ref[part] if part < 5 else mixed, right[...])
+        for block in range(count):
+            for side in range(2):
+                start = side * columns + block * rows
+                at = side * side_rows + part * rows
+                put(block, slice(at, at + rows), product[start : start + rows])
+    for block in range(count):
+        for side in range(2):
+            at = slice(side * side_rows + 6 * rows, (side + 1) * side_rows)
+            put(block, at, vec_ref[side] if block == 0 else jnp.zeros(vec_ref.shape[1:], jnp.float32))
+
+
 def attend_back_kernel(
-    heads, scalars_ref, lengths_ref, part_a, part_b, other_a, other_b, second_a, second_b, xhat_a, xhat_b,
-    scale_a, scale_b, gain_ref, w_out_ref, w_out_far_ref, own_ref, wqkv_ref, blocks_ref, x_ref, pos_ref,
-    send_ref, base_ref, d_ref, branch_ref, sums_ref, dm_ref, first_ref, proj_ref, wfar_ref,
+    heads, count, scalars_ref, lengths_ref, part_ref, other_ref, second_ref, xhat_ref, scale_ref, gain_ref, w_out_ref, w_out_far_ref, own_ref, wqkv_ref, blocks_ref, x_ref, pos_ref, mixed_ref, mixed_far_ref, more_ref,
+    send_ref, base_ref, keep_ref, give_ref, d_ref, branch_ref, dm_ref, first_ref, proj_ref, wfar_ref, vec_ref,
 ):
     page, low = scalars_ref[0], scalars_ref[1]
     length = lengths_ref[page]
     factor = 1.0 / math.sqrt(3.0 * HEAD_DIM)
     columns = heads * HEAD_DIM
-    half = part_a.shape[0]
-    count, _, block_rows, _ = blocks_ref.shape
+    half = part_ref.shape[0] // 2
+    block_rows = blocks_ref.shape[3]
     for part in range(5):
         for block in range(count):
             at = slice(block * block_rows, (block + 1) * block_rows)
-            wfar_ref[part, at] = blocks_ref[block, part]
+            wfar_ref[part, at] = blocks_ref[0, block, part]
         weight = wfar_ref[part].astype(jnp.bfloat16)
         left = x_ref if part < 3 else pos_ref
         proj_ref[part, columns:] = mm_nt(weight, left[...]).astype(jnp.bfloat16)
         proj_ref[part, :columns] = own_ref[part]
     sums = None
-    chunks = ((part_a, other_a, second_a, xhat_a, scale_a), (part_b, other_b, second_b, xhat_b, scale_b))
-    for index, (part, other, second, xhat, scale) in enumerate(chunks):
+    for index in range(2):
         at = slice(index * half, (index + 1) * half)
-        d_normed = second[...] + (part[...] + other[...])
-        d_first = norm_back(d_normed, gain_ref[...], xhat[...], scale[...])
+        xhat = xhat_ref[at]
+        d_normed = second_ref[at] + (part_ref[at] + other_ref[at])
+        d_first = norm_back(d_normed, gain_ref[...], xhat, scale_ref[at])
         first_ref[at] = d_first
         d_branch = d_first.astype(jnp.bfloat16)
         branch_ref[at] = d_branch
-        some = (column_sum(d_branch), column_sum(d_normed * xhat[...]), column_sum(d_normed))
+        some = (column_sum(d_branch), column_sum(d_normed * xhat), column_sum(d_normed))
         sums = some if sums is None else tuple(x + y for x, y in zip(sums, some))
         dm_ref[:columns, at] = mm_nt(w_out_ref[...], d_branch).astype(jnp.bfloat16)
         dm_ref[columns:, at] = mm_nt(w_out_far_ref[...], d_branch).astype(jnp.bfloat16)
-    for index, value in enumerate(sums):
-        sums_ref[index : index + 1] = value
+    for side in range(2):
+        for index, value in enumerate(sums):
+            vec_ref[side, index : index + 1] = value
+        vec_ref[side, len(sums) :] = more_ref[side]
 
     def one_head(head, _):
         at = rows_at(head)
@@ -357,37 +407,45 @@
     upper, lower = total[:half], total[half:]
     send_ref[...] = jnp.where(low == 0, lower, upper)
     base_ref[...] = jnp.where(low == 0, upper + first_ref[:half], lower + first_ref[half:])
-
-
-def attend_back(scalars, lengths, arrays):
-    proj = arrays[13]
+    weight_grads(
+        count, scalars_ref[2], x_ref, pos_ref, d_ref, branch_ref, mixed_ref, mixed_far_ref, vec_ref, keep_ref, give_ref
+    )
+
+
+def attend_back(count, scalars, lengths, arrays):
+    proj = arrays[8]
     parts, columns, length = proj.shape
-    half, width = arrays[0].shape
+    half, width = length // 2, arrays[0].shape[1]
     heads = columns // HEAD_DIM
     whole = lambda shape: pl.BlockSpec(shape, lambda i, s, n: (0,) * len(shape))
     shapes = (
         jax.ShapeDtypeStruct((half, width), jnp.float32),
         jax.ShapeDtypeStruct((half, width), jnp.float32),
-        jax.ShapeDtypeStruct((parts, 2 * columns, length), jnp.bfloat16),
-        jax.ShapeDtypeStruct((length, width), jnp.bfloat16),
-        jax.ShapeDtypeStruct((3, width), jnp.float32),
-    )
+    ) + 2 * (jax.ShapeDtypeStruct((count // 2, 2 * (6 * (columns // count) + 8), width), jnp.float32),)
     return pl.pallas_call(
-        partial(attend_back_kernel, heads),
+        partial(attend_back_kernel, heads, count),
         out_shape=shapes,
         grid_spec=pltpu.PrefetchScalarGridSpec(
             num_scalar_prefetch=2,
             grid=(1,),
-            in_specs=[whole(array.shape) for array in arrays],
+            in_specs=[
+                whole(array.shape)
+                if len(array.shape) < 5
+                else pl.BlockSpec((1,) + array.shape[1:], lambda i, s, n: (0, 0, 0, 0, 0))
+                for array in arrays
+            ],
             out_specs=[whole(shape.shape) for shape in shapes],
             scratch_shapes=[
+                pltpu.VMEM((parts, 2 * columns, length), jnp.bfloat16),
+                pltpu.VMEM((length, width), jnp.bfloat16),
                 pltpu.VMEM((2 * columns, length), jnp.bfloat16),
                 pltpu.VMEM((length, width), jnp.float32),
                 pltpu.VMEM((parts, 2 * columns, length), jnp.bfloat16),
                 pltpu.VMEM((parts, columns, width), jnp.float32),
+                pltpu.VMEM((2, 8, width), jnp.float32),
             ],
         ),
-        compiler_params=pltpu.CompilerParams(vmem_limit_bytes=52 << 20),
+        compiler_params=pltpu.CompilerParams(vmem_limit_bytes=58 << 20),
         cost_estimate=pl.CostEstimate(
             flops=2 * 2 * heads * length * length * HEAD_DIM * 9 + 20 * length * width * columns,
             transcendentals=2 * heads * length * length,
@@ -395,62 +453,6 @@
         ),
         name="attend_back",
     )(scalars, lengths, *arrays)
-
-
-def weight_grads_kernel(
-    count, scalars_ref, x_ref, pos_ref, d_ref, db_ref, mixed_ref, far_ref, vec_ref, keep_ref, send_ref
-):
-    group = scalars_ref[0]
-    columns = mixed_ref.shape[0]
-    rows = columns // count
-    odd = group & 1
-    extra = vec_ref.shape[1]
-    side_rows = 6 * rows + extra
-    mixed = jnp.concatenate([mixed_ref[...], far_ref[...]], axis=0)
-    rights = [x_ref] * 3 + [pos_ref] * 2 + [db_ref]
-
-    def put(block, at, value):
-        place = (block ^ group) >> 1
-
-        @pl.when(odd == (block & 1))
-        def _():
-            keep_ref[place, at] = value
-
-        @pl.when(odd != (block & 1))
-        def _():
-            send_ref[place, at] = value
-
-    for part, right in enumerate(rights):
-        product = mm(d_ref[part] if part < 5 else mixed, right[...])
-        for block in range(count):
-            for side in range(2):
-                start = side * columns + block * rows
-                at = side * side_rows + part * rows
-                put(block, slice(at, at + rows), product[start : start + rows])
-    for block in range(count):
-        for side in range(2):
-            at = slice(side * side_rows + 6 * rows, (side + 1) * side_rows)
-            put(block, at, vec_ref[side] if block == 0 else jnp.zeros(vec_ref.shape[1:], jnp.float32))
-
-
-def weight_grads(count, scalars, rows, pos_rows, d_heads, d_branch, mixed, mixed_far, vectors):
-    length, width = rows.shape
-    columns = mixed.shape[0]
-    block = 2 * (6 * (columns // count) + vectors.shape[1])
-    shape = jax.ShapeDtypeStruct((count // 2, block, width), jnp.float32)
-    return pl.pallas_call(
-        partial(weight_grads_kernel, count),
-        out_shape=(shape, shape),
-        in_specs=[pl.BlockSpec(memory_space=pltpu.SMEM)] + [pl.BlockSpec(memory_space=pltpu.VMEM)] * 7,
-        out_specs=[pl.BlockSpec(memory_space=pltpu.VMEM)] * 2,
-        compiler_params=pltpu.CompilerParams(vmem_limit_bytes=48 << 20),
-        cost_estimate=pl.CostEstimate(
-            flops=24 * length * width * columns,
-            transcendentals=0,
-            bytes_accessed=4 * count * block * width + 20 * length * columns + 6 * length * width,
-        ),
-        name="weight_grads",
-    )(scalars, rows, pos_rows, d_heads, d_branch, mixed, mixed_far, vectors)
 
 
 def place_grads_kernel(
@@ -540,7 +542,7 @@
     pages, length, width = tokens.shape
     columns = w_qkv.shape[2]
     units = w_in.shape[1]
-    here = lax.axis_index("mp")
+    here = lax.axis_index(MP)
     low = here & 1
     page = here >> 1
     group = lax.axis_index("dp")
@@ -553,7 +555,7 @@
 
     def swap(value, bit):
         pairs = [(i, i ^ bit) for i in range(mp_size)]
-        return lax.ppermute(value, "mp", pairs)
+        return lax.ppermute(value, MP, pairs)
 
     def group_swap(value, bit):
         pairs = [(i, i ^ bit) for i in range(dp_size)]
@@ -579,19 +581,18 @@
 
     turn = lambda value: jnp.swapaxes(value, 1, 2)
     w_qkv, w_pos = turn(w_qkv), turn(w_pos)
-    out_rows = my_rows(w_out).astype(f32)
+    out_rows = swap(my_rows(w_out).astype(f32), FAR)
     out_rows = jnp.pad(out_rows, ((0, max(0, 48 - out_rows.shape[0])), (0, 0)))
-    out_rows = swap(out_rows, FAR)
     unit_rows = jnp.concatenate([my_rows(w_in), my_rows(w_back)], axis=0).astype(f32)
     tail = jnp.concatenate([row(b_in), jnp.zeros((7, units), f32)], axis=0)
     far_rows = swap(jnp.concatenate([unit_rows, tail], axis=0), FAR)
     count = columns // dp_size
-    w_out_far = gather(out_rows).reshape(dp_size, -1, width)[:, :count].reshape(columns, width)
-    w_out_far = arrived(w_out_far).astype(bf16)
 
     table = jnp.asarray(angle_tables(width))
     scalars = jnp.stack([page, low])
     mixed_send, mixed, proj, pos_rows = attend(scalars, lengths, tokens, coords, table, w_qkv, w_pos)
+    w_out_far = gather(out_rows).reshape(dp_size, -1, width)[:, : columns // dp_size]
+    w_out_far = arrived(w_out_far.reshape(columns, width)).astype(bf16)
     mixed_far = swap(mixed_send, FAR)
     far_rows = after(far_rows, mixed_far)
     count = unit_rows.shape[0]
@@ -602,56 +603,60 @@
     w_back_far = blocks[:, in_rows:].reshape(units, width).astype(bf16)
 
     mixed_far = arrived(mixed_far).astype(bf16)
-    chunk_columns = lambda value: [value[:, :half], value[:, half:]]
-    part = [
-        mm_tn(own, w_out) + mm_tn(far, w_out_far)
-        for own, far in zip(chunk_columns(mixed), chunk_columns(mixed_far))
-    ]
-    other = [swap(value, NEAR) for value in part]
+    part = mm_tn(jnp.concatenate([mixed, mixed_far], axis=0), jnp.concatenate([w_out, w_out_far], axis=0))
+    other = swap(part, NEAR)
     head_rows = jnp.concatenate([w_qkv, w_pos], axis=0)
     count = columns // dp_size
-    head_rows = lax.dynamic_slice_in_dim(after(head_rows, part[1]), group * count, count, 1)
-    head_rows = swap(head_rows.astype(f32), FAR)
-    part[0] = after(part[0], head_rows)
-
-    rows_of = jax.ShapeDtypeStruct((half, width), f32)
-    rows_low = jax.ShapeDtypeStruct((half, width), bf16)
-    units_of = jax.ShapeDtypeStruct((half, 2 * units), f32)
-    units_low = jax.ShapeDtypeStruct((half, 2 * units), bf16)
-    scale_of = jax.ShapeDtypeStruct((half, 1), f32)
-    fed = []
+    head_rows = lax.dynamic_slice_in_dim(after(head_rows, part), group * count, count, 1)
+    blocks = gather(swap(head_rows.astype(f32), FAR).reshape(-1, width))
+    blocks = blocks.reshape(1, dp_size, 5, count, width)
+
+    rows_f32 = jax.ShapeDtypeStruct((length, width), f32)
+    rows_low = jax.ShapeDtypeStruct((length, width), bf16)
+    units_f32 = jax.ShapeDtypeStruct((length, 2 * units), f32)
+    units_low = jax.ShapeDtypeStruct((length, 2 * units), bf16)
+    chunk_f32 = jax.ShapeDtypeStruct((half, width), f32)
+    scale_of = jax.ShapeDtypeStruct((length, 1), f32)
+    shapes = (rows_f32, scale_of, rows_low, units_low, units_f32, chunk_f32)
+    arrays = [part, other, row(b_out), row(gain_one), row(shift_one)]
+    arrays += [w_in, w_in_far, b_in_two, w_back, w_back_far]
+    part, other = [], []
+    fed = ()
     for index in range(2):
-        arrays = [part[index], other[index], row(b_out), row(gain_one), row(shift_one)]
-        arrays += [w_in, w_in_far, b_in_two, w_back, w_back_far]
-        shapes = (rows_of, rows_of, scale_of, rows_low, units_low, units_of)
-        fed.append(
-            on_chunk(feed_kernel, "feed", index, scalars, tokens, half, arrays, shapes)
+        *fed, product = on_chunk(
+            feed_kernel, "feed", index, scalars, tokens, half, arrays, shapes, tuple(fed)
         )
-    part = [value[0] for value in fed]
-    other = [swap(value, NEAR) for value in part]
-    blocks = gather(head_rows.reshape(-1, width)).reshape(dp_size, 5, count, width)
-    back = []
+        part.append(product)
+        other.append(swap(product, NEAR))
+    xhat_one, scale_one, normed_low, hidden, slope = fed
+    shapes = (rows_f32, rows_f32, rows_low, units_low, rows_f32)
+    shapes += (jax.ShapeDtypeStruct((3, width), f32), jax.ShapeDtypeStruct((2, units), f32))
+    back, sums_two, sums_in = (), [], []
     for index in range(2):
-        arrays = [part[index], other[index], fed[index][1], fed[index][5], row(gain_one), row(shift_one)]
+        arrays = [part[index], other[index], xhat_one, slope, row(gain_one), row(shift_one)]
         arrays += [row(b_back), row(gain_two), row(shift_two), w_in, w_in_far, w_back, w_back_far]
-        shapes = (rows_of, rows_of, rows_low, units_low, rows_of)
-        shapes += (jax.ShapeDtypeStruct((3, width), f32), jax.ShapeDtypeStruct((2, units), f32))
-        back.append(
-            on_chunk(feed_back_kernel, "feed_back", index, scalars, cotangent, half, arrays, shapes)
+        *back, some, some_in = on_chunk(
+            feed_back_kernel, "feed_back", index, scalars, cotangent, half, arrays, shapes, tuple(back)
         )
-    part = [value[0] for value in back]
-    other = [swap(value, NEAR) for value in part]
-
-    both = lambda index, source: jnp.concatenate([source[0][index], source[1][index]], axis=0)
-    d_feed = after(both(2, back), part[1])
-    ffn = feed_grads(dp_size, both(3, fed), both(3, back), both(4, fed), d_feed)
+        sums_two.append(some)
+        sums_in.append(some_in)
+    part, d_second, d_feed, d_pre, output = back
+    other = swap(part, NEAR)
+
+    ffn = feed_grads(dp_size, normed_low, d_pre, hidden, d_feed)
     ffn = lax.psum_scatter(ffn.reshape(-1, units), "dp", scatter_dimension=0, tiled=True)
 
     rows = take(tokens, page)
-    arrays = part + other + [back[0][1], back[1][1], fed[0][1], fed[1][1], fed[0][2], fed[1][2]]
+    arrays = [part, other, d_second, xhat_one, scale_one]
     arrays += [row(gain_one), w_out, w_out_far]
-    arrays += [proj, w_qkv, blocks, rows, pos_rows]
-    send, base, d_heads, d_branch, sums = attend_back(scalars, lengths, arrays)
+    vectors = sums_two[0] + sums_two[1]
+    d_b_in = sums_in[0] + sums_in[1]
+    spare = jnp.zeros((1, width), f32)
+    vectors = jnp.stack(
+        [jnp.concatenate([vectors, d_b_in[side : side + 1], spare], axis=0) for side in range(2)]
+    )
+    arrays += [proj, w_qkv, blocks, rows, pos_rows, mixed, mixed_far, vectors]
+    send, base, keep, give = attend_back(dp_size, jnp.stack([page, low, group]), lengths, arrays)
 
     def spread(mine, far, rest):
         both = jnp.stack([mine, far])
@@ -659,48 +664,48 @@
         out = out.reshape(pages, length, width)
         return jnp.where(page == 0, out, out[::-1])
 
-    out_mine = jnp.where(low == 0, back[0][4], back[1][4])
-    out_far = swap(after(out_mine, other[1]), FAR)
+    half_of = lambda value, index: lax.dynamic_slice_in_dim(value, index * half, half, 0)
+    quarter = half // 2
+    out_mine = half_of(output, low)
+    out_far = [swap(after(out_mine[:quarter], other), FAR)]
 
     bits = [1 << k for k in range(dp_size.bit_length() - 1)]
+    send, give, _ = lax.optimization_barrier((send, give, out_far[0]))
     near_sum = swap(send, NEAR)
-    vectors = jnp.concatenate([sums, back[0][5] + back[1][5]], axis=0)
-    d_b_in = back[0][6] + back[1][6]
-    spare = jnp.zeros((8 - vectors.shape[0] - 1, width), f32)
-    vectors = jnp.stack(
-        [jnp.concatenate([vectors, d_b_in[side : side + 1], spare], axis=0) for side in range(2)]
-    )
-    scalars = jnp.reshape(group, (1,))
-    keep, give = weight_grads(
-        dp_size, scalars, rows, pos_rows, d_heads, d_branch, mixed, mixed_far, vectors
-    )
-    total = keep + group_swap(give, bits[0])
-
+    out_far.append(swap(after(out_mine[quarter:], send), FAR))
+    out_far = jnp.concatenate(out_far, axis=0)
     mine = base + near_sum
-    mine = after(mine, out_far)
-    far_mine = swap(mine, FAR)
+
+    group_scalar = jnp.reshape(group, (1,))
+    out_turned = swap(out_far, NEAR)
+    ffn_rows = ffn.shape[0] // 2
+    crossed = swap(jnp.concatenate([mine, ffn[ffn_rows:]], axis=0), FAR)
+    ffn = ffn[:ffn_rows] + crossed[half:]
+    far_mine = crossed[:half]
+    total = after(keep + group_swap(give, bits[0]), near_sum, out_far)
     more = bits[1:]
-
-    def fold_two(upper, lower):
-        for step in range(len(more)):
-            upper = upper.reshape((-1, 2) + upper.shape[1:])
-            lower = lower.reshape((2, -1) + lower.shape[1:])
-            give_upper, give_lower = after_all(upper[:, 1], lower[1])
-            upper = upper[:, 0] + group_swap(give_upper, more[step])
-            lower = lower[0] + group_swap(give_lower, more[-1 - step])
-        return upper[0], lower[0]
 
     def after_all(*values):
         return lax.optimization_barrier(values)
 
     cut = total.shape[1] // 2
-    upper, lower = fold_two(total[:, :cut], total[:, cut:])
-    far_sum = swap(lower, FAR)
-
-    rest = swap(jnp.stack([mine, far_mine, out_far]), NEAR)
-    grad_tokens = spread(mine, far_mine, rest[:2])
-    out_rest = jnp.where(low == 0, back[1][4], back[0][4])
-    layer_out = spread(out_mine, arrived(out_far), jnp.stack([out_rest, arrived(rest[2])])).astype(bf16)
+    upper, lower = total[:, :cut], total[:, cut:]
+    for step in range(len(more)):
+        upper = upper.reshape((-1, 2) + upper.shape[1:])
+        lower = lower.reshape((2, -1) + lower.shape[1:])
+        give_upper, give_lower = after_all(upper[:, 1], lower[1], *([out_turned] if step else []))[:2]
+        got_upper = group_swap(give_upper, more[step])
+        got_lower = group_swap(give_lower, more[-1 - step])
+        upper = upper[:, 0] + got_upper
+        lower = lower[0] + got_lower
+    upper, lower = upper[0], lower[0]
+    far_sum = swap(after(lower, crossed), FAR)
+    ffn = after(ffn, got_upper, got_lower)
+
+    rest = swap(after(jnp.stack([mine, far_mine]), far_sum), NEAR)
+    grad_tokens = spread(mine, far_mine, rest)
+    out_rest = half_of(output, 1 - low)
+    layer_out = spread(out_mine, arrived(out_far), jnp.stack([out_rest, arrived(out_turned)])).astype(bf16)
     total = upper + far_sum
     cut = total.shape[0] // 16 * 8
     upper, lower = total[None, :cut], total[None, cut:]
@@ -709,18 +714,17 @@
         got_lower = group_swap(lower, more[-1 - step])
         upper = jnp.concatenate([upper, got_upper], axis=0)
         lower = jnp.concatenate([lower, got_lower], axis=0)
+    upper, lower, _ = lax.optimization_barrier((upper, lower, rest))
     parts = [upper, lower, group_swap(upper, bits[0]), group_swap(lower, bits[0])]
-    grad_w_qkv, grad_w_pos, grad_w_out, vectors = place_grads(scalars, parts, columns, 8)
+    grad_w_qkv, grad_w_pos, grad_w_out, vectors = place_grads(group_scalar, parts, columns, 8)
     grad_w_qkv, grad_w_pos = turn(grad_w_qkv), turn(grad_w_pos)
     grad_b_out, grad_gain_one, grad_shift_one = vectors[0], vectors[1], vectors[2]
     grad_b_back, grad_gain_two, grad_shift_two = vectors[3], vectors[4], vectors[5]
     grad_b_in = vectors[6]
 
-    ffn = after(ffn, mine)
-    count = ffn.shape[0] // 2
-    ffn = ffn[:count] + swap(ffn[count:], FAR)
-    grad_w_in = gather(ffn[:in_rows])
-    grad_w_back = gather(ffn[in_rows:])
+    ffn = gather(ffn).reshape(dp_size, ffn_rows, units)
+    grad_w_in = ffn[:, :in_rows].reshape(width, units)
+    grad_w_back = ffn[:, in_rows:].reshape(units, width)
     return (
         layer_out,
         grad_tokens,
@@ -740,40 +744,43 @@
 
 
 def solution(mesh):
+    mp_size = mesh.shape["mp"]
+    dp_size = mesh.devices.size // mp_size
+    split = jax.sharding.Mesh(mesh.devices.reshape(dp_size, mp_size // 2, 2), ("dp",) + MP)
     placed = (
         P("dp", None, None),
         P("dp"),
         P("dp", None, None),
-        P(None, None, "mp"),
-        P(None, None, "mp"),
-        P("mp", None),
+        P(None, None, MP),
+        P(None, None, MP),
+        P(MP, None),
         P(),
         P(),
         P(),
-        P(None, "mp"),
-        P("mp"),
-        P("mp", None),
+        P(None, MP),
+        P(MP),
+        P(MP, None),
         P(),
         P(),
         P(),
         P("dp", None, None),
     )
     return jax.shard_map(
-        partial(body, mesh.shape["dp"], mesh.shape["mp"]),
-        mesh=mesh,
+        partial(body, dp_size, mp_size),
+        mesh=split,
         in_specs=placed,
         out_specs=(
             P("dp", None, None),
             P("dp", None, None),
-            P(None, None, "mp"),
-            P(None, None, "mp"),
-            P("mp", None),
+            P(None, None, MP),
+            P(None, None, MP),
+            P(MP, None),
             P(),
             P(),
             P(),
-            P(None, "mp"),
-            P("mp"),
-            P("mp", None),
+            P(None, MP),
+            P(MP),
+            P(MP, None),
             P(),
             P(),
             P(),

time: 451 us -> 421 us (0.933)
  waiting for transfers between devices: 288 us -> 255 us
  starting transfers between devices: 25 us -> 32.5 us
  local copies, waits for them, and re-layouts: 35.5 us -> 29 us
    ppermute x16 -> x15, waiting for transfers between devices: 251 us -> 199 us  [swap(): return lax.ppermute(value, MP, pairs)]
    ppermute x11, waiting for transfers between devices: 25.3 us -> 38 us  [group_swap(): return lax.ppermute(value, 'dp', pairs)]
    unnamed x90 -> x93, local copies, waits for them, and re-layouts: 20.8 us -> 10.2 us
    ppermute x16 -> x15, starting transfers between devices: 15.8 us -> 24.1 us  [swap(): return lax.ppermute(value, MP, pairs)]
    all_gather x5 -> x4, waiting for transfers between devices: 11.3 us -> 17.5 us  [gather(): return lax.all_gather(value, 'dp', axis=0, tiled=True)]
    slice x5 -> x7, local copies, waits for them, and re-layouts: 3.5 us -> 8.12 us  [the longest x1 4.98 us: body(): grad_w_back = ffn[:, in_rows:].reshape(units, width)]
    pallas_call x7 -> x6, Pallas kernels: 51.4 us -> 53.2 us  [the longest x1 24.8 us: attend_back(): pl.pallas_call(partial(attend_back_kernel, heads, count), out_shape=shape...]
  transfers between devices with their start and end apart: 33 -> 31, of which waited for: 20 -> 17; matrix products, arithmetic and copies ran while one was open for 8% -> 8% of each run, Pallas kernels for 14% -> 16%
where the time goes in v6:
time: 421 us; the launch traced here: 420 us
  waiting for transfers between devices  255 us (61%)
  Pallas kernels  65.1 us (15%)
  starting transfers between devices  32.5 us (8%)
  local copies, waits for them, and re-layouts  29 us (7%)
  other arithmetic  23.7 us (6%)
  between operations  14.5 us (3%)
    ppermute x15, waiting for transfers between devices, swap(): return lax.ppermute(value, MP, pairs)  199 us
    ppermute x11, waiting for transfers between devices, group_swap(): return lax.ppermute(value, 'dp', pairs)  38 us
    pallas_call x1, Pallas kernels, attend_back(): pl.pallas_call(partial(attend_back_kernel, heads, count), out_shape=shape...  24.8 us
    ppermute x15, starting transfers between devices, swap(): return lax.ppermute(value, MP, pairs)  24.1 us
    pallas_call x4, Pallas kernels, on_chunk(): pl.pallas_call(without(kernel, inputs, len(before)), out_shape=shapes, gr...  22.8 us
    all_gather x4, waiting for transfers between devices, gather(): return lax.all_gather(value, 'dp', axis=0, tiled=True)  17.5 us
    unnamed x93, local copies, waits for them, and re-layouts  10.2 us
    pallas_call x1, Pallas kernels, attend(): pl.pallas_call(partial(attend_kernel, columns // HEAD_DIM), out_shape=sha...  9.81 us
  transfers between devices with their start and end apart: 31, of which 17 were waited for; matrix products, arithmetic and copies ran while one was open for 8% of the time, Pallas kernels for 16%

profile of v6, /device:TPU:0, one launch (start us, length us, event | category | flops | bytes accessed | tf_op | source)
XLA Modules:
  0.0 420.2 jit_solution(2302731908630949628)
XLA Ops:
  8.1 4.1 collective-permute-start.1
  12.2 3.9 collective-permute-done.1
  19.6 1.3 collective-permute-start.3
  22.0 9.8 %attend.1 = (f32[192,512]{1,0:T(8,128)S(1)}, bf16[192,512]{1,0:T(8,128)(2,1)S(1)}, bf16[5,192,512]{2,1,0:T(8,128)(2,1)S(1)}, bf16[512,768]{1,0:T(8,128)(2,1)S(1)}) custom-call(s32[2]{0:T(128)S(1)} %pad_add_fusion.scalars_ref.refs_0_, s32[2]{0:T(128)S(1)} %copy-done.13, bf16[2,512,768]{2,1,0:T(8,128)(2,1)S(1)} %copy-done.2, s32[2,2,512]{2,1,0:T(2,128)S(1)} %copy-done.14, ...), custom_call_target="tpu_custom_call" | custom-call | flops 2315255808 | bytes 5898240 | tf_op jit(solution)/shard_map/attend/pallas_call | solution.py:130
  33.7 1.6 collective-permute-start
  35.3 28.6 %collective-permute-done = f32[192,512]{1,0:T(8,128)S(1)} collective-permute-done((f32[192,512]{1,0:T(8,128)S(1)}, f32[192,512]{1,0:T(8,128)S(1)}, u32[]{:S(2)}, u32[]{:S(2)}) %collective-permute-start) | collective-permute-done | bytes 393248 | tf_op jit(solution)/shard_map/ppermute | solution.py:558
  63.9 1.9 slice.113
  66.0 1.2 pad_maximum_fusion.5
  69.2 1.2 dynamic-slice_convert_fusion
  70.4 16.2 %collective-permute-done.8 = f32[5,24,768]{2,1,0:T(8,128)S(1)} collective-permute-done((f32[5,24,768]{2,1,0:T(8,128)S(1)}, f32[5,24,768]{2,1,0:T(8,128)S(1)}, u32[]{:S(2)}, u32[]{:S(2)}) %collective-permute-start.8) | collective-permute-done | bytes 368672 | tf_op jit(solution)/shard_map/ppermute | solution.py:558
  88.6 17.5 %all-gather.7.cloned.1.call-done = f32[1536,768]{1,0:T(8,128)} async-done(((f32[192,768]{1,0:T(8,128)}), f32[1536,768]{1,0:T(8,128)}) %all-gather.7.cloned.1.call-update) | async-done | bytes 4718608 | tf_op jit(solution)/shard_map/all_gather | solution.py:569
  106.1 2.7 multiply_convert_fusion
  110.0 10.6 %collective-permute-done.2.refs_3_ = f32[512,768]{1,0:T(8,128)} collective-permute-done((f32[512,768]{1,0:T(8,128)S(1)}, f32[512,768]{1,0:T(8,128)}, u32[]{:S(2)}, u32[]{:S(2)}) %collective-permute-start.2) | collective-permute-done | bytes 1572896 | tf_op jit(solution)/shard_map/ppermute | solution.py:558
  120.7 5.2 %feed.2 = (f32[512,768]{1,0:T(8,128)}, f32[512,1]{1,0:T(8,128)S(1)}, bf16[512,768]{1,0:T(8,128)(2,1)S(1)}, bf16[512,1536]{1,0:T(8,128)(2,1)}, f32[512,1536]{1,0:T(8,128)}, /*index=5*/f32[256,768]{1,0:T(8,128)S(1)}) custom-call(s32[2]{0:T(128)S(1)} %pad_add_fusion.scalars_ref.refs_0_, bf16[2,512,768]{2,1,0:T(8,128)(2,1)} %refs_1_.5, f32[512,768]{1,0:T(8,128)} %copy-done.17, ...), custom_call_target="tpu_custom_call" | custom-call | flops 2415919104 | bytes 7864320 | tf_op jit(solution)/shard_map/feed/pallas_call | solution.py:242
  125.8 1.7 collective-permute-start.5
  127.6 5.4 %feed.3 = (f32[512,768]{1,0:T(8,128)}, f32[512,1]{1,0:T(8,128)S(1)}, bf16[512,768]{1,0:T(8,128)(2,1)S(1)}, bf16[512,1536]{1,0:T(8,128)(2,1)}, f32[512,1536]{1,0:T(8,128)}, /*index=5*/f32[256,768]{1,0:T(8,128)S(1)}) custom-call(s32[2]{0:T(128)S(1)} %pad_add_fusion.scalars_ref.refs_0_, ...), custom_call_target="tpu_custom_call", output_to_operand_aliasing={{0}: (12, {}), {1}: (13, {}), {2}: (14, {}), {3}: (15, {}),... | custom-call | flops 2415919104 | bytes 7864320 | tf_op jit(solution)/shard_map/feed/pallas_call | solution.py:242
  133.7 12.6 %collective-permute-done.5.refs_3_ = f32[256,768]{1,0:T(8,128)S(1)} collective-permute-done((f32[256,768]{1,0:T(8,128)S(1)}, f32[256,768]{1,0:T(8,128)S(1)}, u32[]{:S(2)}, u32[]{:S(2)}) %collective-permute-start.5) | collective-permute-done | bytes 786464 | tf_op jit(solution)/shard_map/ppermute | solution.py:558
  146.3 6.3 %feed_back.2 = (f32[512,768]{1,0:T(8,128)}, f32[512,768]{1,0:T(8,128)}, bf16[512,768]{1,0:T(8,128)(2,1)S(1)}, bf16[512,1536]{1,0:T(8,128)(2,1)}, f32[512,768]{1,...) custom-call(s32[2]{0:T(128)S(1)} %pad_add_fusion.scalars_ref.refs_0_, bf16[2,512,768]{2,1,0:T(8,128)(2,1)} %refs_1_.7, ...), custom_call_target="tpu_custom_call" | custom-call | flops 2415919104 | bytes 7864320 | tf_op jit(solution)/shard_map/feed_back/pallas_call | solution.py:242
  152.6 6.8 %collective-permute-done.4.refs_3_ = f32[256,768]{1,0:T(8,128)S(1)} collective-permute-done((f32[256,768]{1,0:T(8,128)S(1)}, f32[256,768]{1,0:T(8,128)S(1)}, u32[]{:S(2)}, u32[]{:S(2)}) %collective-permute-start.4) | collective-permute-done | bytes 786464 | tf_op jit(solution)/shard_map/ppermute | solution.py:558
  159.4 5.9 %feed_back.3 = (f32[512,768]{1,0:T(8,128)}, f32[512,768]{1,0:T(8,128)}, bf16[512,768]{1,0:T(8,128)(2,1)S(1)}, bf16[512,1536]{1,0:T(8,128)(2,1)}, f32[512,768]{1,...) custom-call(s32[2]{0:T(128)S(1)} %pad_add_fusion.scalars_ref.refs_0_, ...), custom_call_target="tpu_custom_call", output_to_operand_aliasing={{0}: (15, {}), {1}: (16, {}), {2}: (17, {}), {3}: (18, {}),... | custom-call | flops 2415919104 | bytes 7864320 | tf_op jit(solution)/shard_map/feed_back/pallas_call | solution.py:242
  165.3 1.4 copy-done.4
  166.7 5.6 %feed_grads.1 = f32[8,4,96,768]{3,2,1,0:T(8,128)} custom-call(bf16[512,768]{1,0:T(8,128)(2,1)S(1)} %get-tuple-element.102.low_ref, bf16[512,1536]{1,0:T(8,128)(2,1)S(1)} %copy-done.4, bf16[512,1536]{1,0:T(8,128)(2,1)S(1)} %copy-done.5, bf16[512,768]{1,0:T(8,128)(2,1)S(1)} %get-tuple-element.105.feed_ref), custom_call_target="tpu_custom_call" | custom-call | flops 2415919104 | bytes 9437184 | tf_op jit(solution)/shard_map/feed_grads/pallas_call | solution.py:282
  173.7 1.7 collective-permute-start.6
  177.3 29.3 %collective-permute-done.6.other_ref = f32[512,768]{1,0:T(8,128)} collective-permute-done((f32[512,768]{1,0:T(8,128)S(1)}, f32[512,768]{1,0:T(8,128)}, u32[]{:S(2)}, u32[]{:S(2)}) %collective-permute-start.6) | collective-permute-done | bytes 1572896 | tf_op jit(solution)/shard_map/ppermute | solution.py:558
  206.5 8.3 %collective-permute-start.7 = (f32[128,768]{1,0:T(8,128)S(1)}, f32[128,768]{1,0:T(8,128)S(1)}, u32[]{:S(2)}, u32[]{:S(2)}) collective-permute-start(f32[128,768]{1,0:T(8,128)S(1)} %get-tuple-element.87), channel_id=1, source_target_pairs={{0,2},{1,3},{2,0},{3,1},{4,6},{5,7},{6,4},{7,5},{8,10},{9,11},{10,... | collective-permute-start | bytes 1179656 | tf_op jit(solution)/shard_map/ppermute | solution.py:558
  215.4 24.8 %attend_back.1 = (f32[256,768]{1,0:T(8,128)}, f32[256,768]{1,0:T(8,128)}, f32[4,304,768]{2,1,0:T(8,128)}, f32[4,304,768]{2,1,0:T(8,128)}) custom-call(s32[3]{0:T(128)} %pad_add_fusion.1.scalars_ref, s32[2]{0:T(128)} %lengths_ref.3, f32[512,768]{1,0:T(8,128)} %get-tuple-element.86.part_ref, f32[512,768]{1,0:T(8,128)} %collective-permute-done.6.other_ref, ...), custom_call_target="tpu_custom_call" | custom-call | flops 3321888768 | bytes 15728640 | tf_op jit(solution)/shard_map/attend_back/pallas_call | solution.py:425
  241.3 26.0 %collective-permute-done.9 = f32[128,768]{1,0:T(8,128)S(1)} collective-permute-done((f32[128,768]{1,0:T(8,128)S(1)}, f32[128,768]{1,0:T(8,128)S(1)}, u32[]{:S(2)}, u32[]{:S(2)}) %collective-permute-start.9) | collective-permute-done | bytes 393248 | tf_op jit(solution)/shard_map/ppermute | solution.py:558
  267.4 3.1 add.64
  270.7 1.7 copy-done.16
  274.4 1.5 collective-permute-start.14
  275.9 1.3 collective-permute-start.15
  278.6 3.4 collective-permute-start.12
  282.0 15.0 %collective-permute-done.14 = f32[2,152,768]{2,1,0:T(8,128)} collective-permute-done((f32[2,152,768]{2,1,0:T(8,128)}, f32[2,152,768]{2,1,0:T(8,128)}, u32[]{:S(2)}, u32[]{:S(2)}) %collective-permute-start.14) | collective-permute-done | bytes 933920 | tf_op jit(solution)/shard_map/ppermute | solution.py:562
  297.0 1.6 slice_add_fusion
  299.7 1.4 fusion.4
  302.0 25.6 %collective-permute-done.10 = f32[256,768]{1,0:T(8,128)S(1)} collective-permute-done((f32[256,768]{1,0:T(8,128)S(1)}, f32[256,768]{1,0:T(8,128)S(1)}, u32[]{:S(2)}, u32[]{:S(2)}) %collective-permute-start.10) | collective-permute-done | bytes 786464 | tf_op jit(solution)/shard_map/ppermute | solution.py:558
  328.9 12.1 %collective-permute-done.12 = f32[448,768]{1,0:T(8,128)S(1)} collective-permute-done((f32[448,768]{1,0:T(8,128)S(1)}, f32[448,768]{1,0:T(8,128)S(1)}, u32[]{:S(2)}, u32[]{:S(2)}) %collective-permute-start.12) | collective-permute-done | bytes 1376288 | tf_op jit(solution)/shard_map/ppermute | solution.py:558
  343.0 1.2 fusion.14
  344.3 1.2 slice_bitcast_fusion.2
  345.7 19.2 %collective-permute-done.17 = f32[152,768]{1,0:T(8,128)} collective-permute-done((f32[152,768]{1,0:T(8,128)S(1)}, f32[152,768]{1,0:T(8,128)}, u32[]{:S(2)}, u32[]{:S(2)}) %collective-permute-start.17) | collective-permute-done | bytes 466976 | tf_op jit(solution)/shard_map/ppermute | solution.py:558
  367.2 11.9 %collective-permute-done.20 = f32[1,72,768]{2,1,0:T(8,128)S(1)} collective-permute-done((f32[1,72,768]{2,1,0:T(8,128)S(1)}, f32[1,72,768]{2,1,0:T(8,128)S(1)}, u32[]{:S(2)}, u32[]{:S(2)}) %collective-permute-start.20) | collective-permute-done | bytes 221216 | tf_op jit(solution)/shard_map/ppermute | solution.py:562
  379.1 1.8 collective-permute-start.21
  381.7 10.3 %collective-permute-done.21 = f32[2,72,768]{2,1,0:T(8,128)S(1)} collective-permute-done((f32[2,72,768]{2,1,0:T(8,128)S(1)}, f32[2,72,768]{2,1,0:T(8,128)S(1)}, u32[]{:S(2)}, u32[]{:S(2)}) %collective-permute-start.21) | collective-permute-done | bytes 442400 | tf_op jit(solution)/shard_map/ppermute | solution.py:562
  392.9 8.2 %collective-permute-done.18 = f32[2,256,768]{2,1,0:T(8,128)S(1)} collective-permute-done((f32[2,256,768]{2,1,0:T(8,128)S(1)}, f32[2,256,768]{2,1,0:T(8,128)S(1)}, u32[]{:S(2)}, u32[]{:S(2)}) %collective-permute-start.18) | collective-permute-done | bytes 1572896 | tf_op jit(solution)/shard_map/ppermute | solution.py:558
  401.2 1.4 fusion
  404.0 1.9 reverse_select_fusion
  405.9 2.2 place_grads.1
  408.7 5.0 %fusion.23 = (f32[8,96,768]{2,1,0:T(8,128)}, f32[8,96,768]{2,1,0:T(8,128)}) fusion(f32[8,192,768]{2,1,0:T(8,128)} %bitcast.103), kind=kLoop, calls=%fused_computation.79 | loop fusion | bytes 9437184 | tf_op jit(solution)/shard_map/slice | solution.py:727
  (190 shorter events, 32.9 us)
Async XLA Ops:
  7.2 60.1 %all-gather.5.cloned.1.call-start = ((), (), s32[]{:S(2)}) async-start(), calls=%async_computation.1 | async-start | bytes 1327104 | tf_op jit(solution)/shard_map/all_gather | solution.py:569
  8.0 13.0 %copy-start.6 = (bf16[3,768,192]{1,2,0:T(8,128)(2,1)S(1)}, bf16[3,768,192]{1,2,0:T(8,128)(2,1)}, u32[]{:S(2)}) copy-start(bf16[3,768,192]{1,2,0:T(8,128)(2,1)} %param.20) | copy-start | bytes 2654212
  8.1 8.0 %collective-permute-start.1 = (f32[24,768]{1,0:T(8,128)S(1)}, f32[24,768]{1,0:T(8,128)S(1)}, u32[]{:S(2)}, u32[]{:S(2)}) collective-permute-start(f32[24,768]{1,0:T(8,128)S(1)} %dynamic-slice_convert_fusion.1), channel_id=1, source_target_pairs={{0,2},{1,3},{2,0},{3,1},{4,6},{5,7},{6,4},{7,5},{8,10},{9,11},{10,... | collective-permute-start | bytes 221192 | tf_op jit(solution)/shard_map/ppermute | solution.py:558
  16.8 89.4 %all-gather.7.cloned.1.call-start = ((), (), s32[]{:S(2)}) async-start(), calls=%async_computation.2 | async-start | bytes 5308416 | tf_op jit(solution)/shard_map/all_gather | solution.py:569
  19.6 44.3 %collective-permute-start.3 = (f32[200,768]{1,0:T(8,128)}, f32[200,768]{1,0:T(8,128)}, u32[]{:S(2)}, u32[]{:S(2)}) collective-permute-start(f32[200,768]{1,0:T(8,128)} %maximum_maximum_fusion), channel_id=1, source_target_pairs={{0,2},{1,3},{2,0},{3,1},{4,6},{5,7},{6,4},{7,5},{8,10},{9,11},{10,... | collective-permute-start | bytes 1843208 | tf_op jit(solution)/shard_map/ppermute | solution.py:558
  33.7 34.8 %copy-start.10 = (bf16[192,512]{1,0:T(8,128)(2,1)}, bf16[192,512]{1,0:T(8,128)(2,1)S(1)}, u32[]{:S(2)}) copy-start(bf16[192,512]{1,0:T(8,128)(2,1)S(1)} %get-tuple-element.68.mixed_ref) | copy-start | bytes 589828
  33.7 30.2 %collective-permute-start = (f32[192,512]{1,0:T(8,128)S(1)}, f32[192,512]{1,0:T(8,128)S(1)}, u32[]{:S(2)}, u32[]{:S(2)}) collective-permute-start(f32[192,512]{1,0:T(8,128)S(1)} %get-tuple-element.69), channel_id=1, source_target_pairs={{0,2},{1,3},{2,0},{3,1},{4,6},{5,7},{6,4},{7,5},{8,10},{9,11},{10,... | collective-permute-start | bytes 1179656 | tf_op jit(solution)/shard_map/ppermute | solution.py:558
  65.9 149.6 %all-gather.9.cloned.1.call-start = ((), (), s32[]{:S(2)}) async-start(), calls=%async_computation.3 | async-start | bytes 3317760 | tf_op jit(solution)/shard_map/all_gather | solution.py:569
  68.5 19.0 %copy-start.25 = (bf16[8,24,768]{2,1,0:T(8,128)(2,1)}, bf16[8,24,768]{2,1,0:T(8,128)(2,1)S(1)}, u32[]{:S(2)}) copy-start(bf16[8,24,768]{2,1,0:T(8,128)(2,1)S(1)} %fusion.6) | copy-start | bytes 884740
  68.5 19.3 %copy-start.40 = (f32[768]{0:T(1024)S(1)}, f32[768]{0:T(1024)}, u32[]{:S(2)}) copy-start(f32[768]{0:T(1024)} %param.24) | copy-start | bytes 9220
  68.5 19.3 %copy-start.41 = (f32[768]{0:T(1024)S(1)}, f32[768]{0:T(1024)}, u32[]{:S(2)}) copy-start(f32[768]{0:T(1024)} %param.25) | copy-start | bytes 9220
  68.5 19.3 %copy-start.42 = (f32[768]{0:T(1024)S(1)}, f32[768]{0:T(1024)}, u32[]{:S(2)}) copy-start(f32[768]{0:T(1024)} %param.23) | copy-start | bytes 9220
  68.5 20.1 %copy-start.39 = (f32[1,768]{1,0:T(1,128)S(1)}, f32[1,768]{1,0:T(1,128)}, u32[]{:S(2)}) copy-start(f32[1,768]{1,0:T(1,128)} %copy-done.38) | copy-start | bytes 9220
  69.1 39.7 %copy-start.17 = (f32[512,768]{1,0:T(8,128)}, f32[512,768]{1,0:T(8,128)S(1)}, u32[]{:S(2)}) copy-start(f32[512,768]{1,0:T(8,128)S(1)} %fusion.7.refs_2_) | copy-start | bytes 4718596
  70.4 16.3 %collective-permute-start.8 = (f32[5,24,768]{2,1,0:T(8,128)S(1)}, f32[5,24,768]{2,1,0:T(8,128)S(1)}, u32[]{:S(2)}, u32[]{:S(2)}) collective-permute-start(f32[5,24,768]{2,1,0:T(8,128)S(1)} %dynamic-slice_convert_fusion), channel_id=1, source_target_pairs={{0,2},{1,3},{2,0},{3,1},{4,6},{5,7},{6,4},{7,5},{8,10},{9,11},{10,... | collective-permute-start | bytes 1105928 | tf_op jit(solution)/shard_map/ppermute | solution.py:558
  87.5 189.9 %reduce-scatter.2.cloned.1.call-start = ((), (), s32[]{:S(2)}) async-start(), calls=%async_computation.4 | async-start | bytes 10616832 | tf_op jit(solution)/shard_map/reduce_scatter | solution.py:647
  87.7 33.0 %collective-permute-start.2 = (f32[512,768]{1,0:T(8,128)S(1)}, f32[512,768]{1,0:T(8,128)}, u32[]{:S(2)}, u32[]{:S(2)}) collective-permute-start(f32[512,768]{1,0:T(8,128)S(1)} %fusion.7.refs_2_), channel_id=1, source_target_pairs={{0,1},{1,0},{2,3},{3,2},{4,5},{5,4},{6,7},{7,6},{8,9},{9,8},{10,11... | collective-permute-start | bytes 4718600 | tf_op jit(solution)/shard_map/ppermute | solution.py:558
  87.8 71.6 %copy-start.12 = (f32[1,768]{1,0:T(1,128)}, f32[1,768]{1,0:T(1,128)S(1)}, u32[]{:S(2)}) copy-start(f32[1,768]{1,0:T(1,128)S(1)} %reshape.288.refs_5_.refs_6_.gain_ref) | copy-start | bytes 9220
  125.8 20.5 %collective-permute-start.5 = (f32[256,768]{1,0:T(8,128)S(1)}, f32[256,768]{1,0:T(8,128)S(1)}, u32[]{:S(2)}, u32[]{:S(2)}) collective-permute-start(f32[256,768]{1,0:T(8,128)S(1)} %get-tuple-element.79.refs_2_), channel_id=1, source_target_pairs={{0,1},{1,0},{2,3},{3,2},{4,5},{5,4},{6,7},{7,6},{8,9},{9,8},{10,11... | collective-permute-start | bytes 2359304 | tf_op jit(solution)/shard_map/ppermute | solution.py:558
  133.0 19.6 %copy-start.7 = (f32[512,1]{1,0:T(8,128)}, f32[512,1]{1,0:T(8,128)S(1)}, u32[]{:S(2)}) copy-start(f32[512,1]{1,0:T(8,128)S(1)} %get-tuple-element.89.scale_ref) | copy-start | bytes 6148
  133.0 26.4 %collective-permute-start.4 = (f32[256,768]{1,0:T(8,128)S(1)}, f32[256,768]{1,0:T(8,128)S(1)}, u32[]{:S(2)}, u32[]{:S(2)}) collective-permute-start(f32[256,768]{1,0:T(8,128)S(1)} %get-tuple-element.76.refs_2_), channel_id=1, source_target_pairs={{0,1},{1,0},{2,3},{3,2},{4,5},{5,4},{6,7},{7,6},{8,9},{9,8},{10,11... | collective-permute-start | bytes 2359304 | tf_op jit(solution)/shard_map/ppermute | solution.py:558
  172.4 236.4 %all-gather.11.cloned.1.call-start = ((), (), s32[]{:S(2)}) async-start(), calls=%async_computation.5 | async-start | bytes 5308416 | tf_op jit(solution)/shard_map/all_gather | solution.py:569
  173.7 32.8 %collective-permute-start.6 = (f32[512,768]{1,0:T(8,128)S(1)}, f32[512,768]{1,0:T(8,128)}, u32[]{:S(2)}, u32[]{:S(2)}) collective-permute-start(f32[512,768]{1,0:T(8,128)S(1)} %copy-done.18), channel_id=1, source_target_pairs={{0,1},{1,0},{2,3},{3,2},{4,5},{5,4},{6,7},{7,6},{8,9},{9,8},{10,11... | collective-permute-start | bytes 4718600 | tf_op jit(solution)/shard_map/ppermute | solution.py:558
  206.5 33.8 %collective-permute-start.7 = (f32[128,768]{1,0:T(8,128)S(1)}, f32[128,768]{1,0:T(8,128)S(1)}, u32[]{:S(2)}, u32[]{:S(2)}) collective-permute-start(f32[128,768]{1,0:T(8,128)S(1)} %get-tuple-element.87), channel_id=1, source_target_pairs={{0,2},{1,3},{2,0},{3,1},{4,6},{5,7},{6,4},{7,5},{8,10},{9,11},{10,... | collective-permute-start | bytes 1179656 | tf_op jit(solution)/shard_map/ppermute | solution.py:558
  240.3 27.1 %collective-permute-start.13 = (f32[4,304,768]{2,1,0:T(8,128)}, f32[4,304,768]{2,1,0:T(8,128)S(1)}, u32[]{:S(2)}, u32[]{:S(2)}) collective-permute-start(f32[4,304,768]{2,1,0:T(8,128)} %get-tuple-element.107), channel_id=1, source_target_pairs={{0,4},{4,0},{8,12},{12,8},{16,20},{20,16},{24,28},{28,24},{1,5},{5... | collective-permute-start | bytes 11206664 | tf_op jit(solution)/shard_map/ppermute | solution.py:562
  240.3 30.2 %collective-permute-start.11 = (f32[256,768]{1,0:T(8,128)}, f32[256,768]{1,0:T(8,128)S(1)}, u32[]{:S(2)}, u32[]{:S(2)}) collective-permute-start(f32[256,768]{1,0:T(8,128)} %get-tuple-element.99), channel_id=1, source_target_pairs={{0,1},{1,0},{2,3},{3,2},{4,5},{5,4},{6,7},{7,6},{8,9},{9,8},{10,11... | collective-permute-start | bytes 2359304 | tf_op jit(solution)/shard_map/ppermute | solution.py:558
  241.3 26.0 %collective-permute-start.9 = (f32[128,768]{1,0:T(8,128)S(1)}, f32[128,768]{1,0:T(8,128)S(1)}, u32[]{:S(2)}, u32[]{:S(2)}) collective-permute-start(f32[128,768]{1,0:T(8,128)S(1)} %get-tuple-element.100), channel_id=1, source_target_pairs={{0,2},{1,3},{2,0},{3,1},{4,6},{5,7},{6,4},{7,5},{8,10},{9,11},{10,... | collective-permute-start | bytes 1179656 | tf_op jit(solution)/shard_map/ppermute | solution.py:558
  274.4 22.6 %collective-permute-start.14 = (f32[2,152,768]{2,1,0:T(8,128)}, f32[2,152,768]{2,1,0:T(8,128)}, u32[]{:S(2)}, u32[]{:S(2)}) collective-permute-start(f32[2,152,768]{2,1,0:T(8,128)} %slice.126), channel_id=1, source_target_pairs={{0,16},{4,20},{8,24},{12,28},{16,0},{20,4},{24,8},{28,12},{1,17},{... | collective-permute-start | bytes 2801672 | tf_op jit(solution)/shard_map/ppermute | solution.py:562
  275.9 23.8 %collective-permute-start.15 = (f32[2,152,768]{2,1,0:T(8,128)}, f32[2,152,768]{2,1,0:T(8,128)}, u32[]{:S(2)}, u32[]{:S(2)}) collective-permute-start(f32[2,152,768]{2,1,0:T(8,128)} %slice_bitcast_fusion.1), channel_id=1, source_target_pairs={{0,8},{4,12},{8,0},{12,4},{16,24},{20,28},{24,16},{28,20},{1,9},{5... | collective-permute-start | bytes 2801672 | tf_op jit(solution)/shard_map/ppermute | solution.py:562
  278.6 62.4 %collective-permute-start.12 = (f32[448,768]{1,0:T(8,128)S(1)}, f32[448,768]{1,0:T(8,128)S(1)}, u32[]{:S(2)}, u32[]{:S(2)}) collective-permute-start(f32[448,768]{1,0:T(8,128)S(1)} %pad_maximum_fusion.6), channel_id=1, source_target_pairs={{0,2},{1,3},{2,0},{3,1},{4,6},{5,7},{6,4},{7,5},{8,10},{9,11},{10,... | collective-permute-start | bytes 4128776 | tf_op jit(solution)/shard_map/ppermute | solution.py:558
  282.0 45.6 %collective-permute-start.10 = (f32[256,768]{1,0:T(8,128)S(1)}, f32[256,768]{1,0:T(8,128)S(1)}, u32[]{:S(2)}, u32[]{:S(2)}) collective-permute-start(f32[256,768]{1,0:T(8,128)S(1)} %copy-done.37), channel_id=1, source_target_pairs={{0,1},{1,0},{2,3},{3,2},{4,5},{5,4},{6,7},{7,6},{8,9},{9,8},{10,11... | collective-permute-start | bytes 2359304 | tf_op jit(solution)/shard_map/ppermute | solution.py:558
  299.7 42.3 %copy-start.26 = (f32[384,768]{1,0:T(8,128)S(1)}, f32[384,768]{1,0:T(8,128)}, u32[]{:S(2)}) copy-start(f32[384,768]{1,0:T(8,128)} %reduce-scatter.2.cloned.1.call-done) | copy-start | bytes 3538948
  302.0 40.9 %copy-start.24 = (f32[2,152,768]{2,1,0:T(8,128)S(1)}, f32[2,152,768]{2,1,0:T(8,128)}, u32[]{:S(2)}) copy-start(f32[2,152,768]{2,1,0:T(8,128)} %copy-done.23) | copy-start | bytes 2801668
  327.6 13.3 %copy-start.30 = (f32[256,768]{1,0:T(8,128)}, f32[256,768]{1,0:T(8,128)S(1)}, u32[]{:S(2)}) copy-start(f32[256,768]{1,0:T(8,128)S(1)} %collective-permute-done.10) | copy-start | bytes 2359300
  327.6 15.3 %collective-permute-start.16 = (f32[1,152,768]{2,1,0:T(8,128)}, f32[1,152,768]{2,1,0:T(8,128)}, u32[]{:S(2)}, u32[]{:S(2)}) collective-permute-start(f32[1,152,768]{2,1,0:T(8,128)} %slice.156), channel_id=1, source_target_pairs={{0,8},{4,12},{8,0},{12,4},{16,24},{20,28},{24,16},{28,20},{1,9},{5... | collective-permute-start | bytes 1400840 | tf_op jit(solution)/shard_map/ppermute | solution.py:562
  328.3 14.6 %collective-permute-start.19 = (f32[1,152,768]{2,1,0:T(8,128)S(1)}, f32[1,152,768]{2,1,0:T(8,128)S(1)}, u32[]{:S(2)}, u32[]{:S(2)}) collective-permute-start(f32[1,152,768]{2,1,0:T(8,128)S(1)} %slice_bitcast_fusion.4), channel_id=1, source_target_pairs={{0,16},{4,20},{8,24},{12,28},{16,0},{20,4},{24,8},{28,12},{1,17},{... | collective-permute-start | bytes 1400840 | tf_op jit(solution)/shard_map/ppermute | solution.py:562
  344.2 20.7 %collective-permute-start.17 = (f32[152,768]{1,0:T(8,128)S(1)}, f32[152,768]{1,0:T(8,128)}, u32[]{:S(2)}, u32[]{:S(2)}) collective-permute-start(f32[152,768]{1,0:T(8,128)S(1)} %fusion.14), channel_id=1, source_target_pairs={{0,2},{1,3},{2,0},{3,1},{4,6},{5,7},{6,4},{7,5},{8,10},{9,11},{10,... | collective-permute-start | bytes 1400840 | tf_op jit(solution)/shard_map/ppermute | solution.py:558
  345.5 19.4 %copy-start.22 = (f32[1,2,152,768]{3,2,1,0:T(8,128)S(1)}, f32[1,2,152,768]{3,2,1,0:T(8,128)}, u32[]{:S(2)}) copy-start(f32[1,2,152,768]{3,2,1,0:T(8,128)} %copy-done.21) | copy-start | bytes 2801668
  345.5 19.4 %copy-start.34 = (f32[1,152,768]{2,1,0:T(8,128)S(1)}, f32[1,152,768]{2,1,0:T(8,128)}, u32[]{:S(2)}) copy-start(f32[1,152,768]{2,1,0:T(8,128)} %copy-done.33) | copy-start | bytes 1400836
  345.7 21.4 %copy-start.20 = (f32[512,768]{1,0:T(8,128)S(1)}, f32[512,768]{1,0:T(8,128)}, u32[]{:S(2)}) copy-start(f32[512,768]{1,0:T(8,128)} %get-tuple-element.85) | copy-start | bytes 4718596
  364.9 36.3 %collective-permute-start.18 = (f32[2,256,768]{2,1,0:T(8,128)S(1)}, f32[2,256,768]{2,1,0:T(8,128)S(1)}, u32[]{:S(2)}, u32[]{:S(2)}) collective-permute-start(f32[2,256,768]{2,1,0:T(8,128)S(1)} %pad_maximum_fusion.4), channel_id=1, source_target_pairs={{0,1},{1,0},{2,3},{3,2},{4,5},{5,4},{6,7},{7,6},{8,9},{9,8},{10,11... | collective-permute-start | bytes 4718600 | tf_op jit(solution)/shard_map/ppermute | solution.py:558
  366.0 14.9 %collective-permute-start.22 = (f32[1,80,768]{2,1,0:T(8,128)S(1)}, f32[1,80,768]{2,1,0:T(8,128)S(1)}, u32[]{:S(2)}, u32[]{:S(2)}) collective-permute-start(f32[1,80,768]{2,1,0:T(8,128)S(1)} %slice_bitcast_fusion.5), channel_id=1, source_target_pairs={{0,16},{4,20},{8,24},{12,28},{16,0},{20,4},{24,8},{28,12},{1,17},{... | collective-permute-start | bytes 737288 | tf_op jit(solution)/shard_map/ppermute | solution.py:562
  366.4 12.7 %collective-permute-start.20 = (f32[1,72,768]{2,1,0:T(8,128)S(1)}, f32[1,72,768]{2,1,0:T(8,128)S(1)}, u32[]{:S(2)}, u32[]{:S(2)}) collective-permute-start(f32[1,72,768]{2,1,0:T(8,128)S(1)} %slice_bitcast_fusion.6), channel_id=1, source_target_pairs={{0,8},{4,12},{8,0},{12,4},{16,24},{20,28},{24,16},{28,20},{1,9},{5... | collective-permute-start | bytes 663560 | tf_op jit(solution)/shard_map/ppermute | solution.py:562
  367.1 14.2 %copy-start.31 = (f32[256,768]{1,0:T(8,128)S(1)}, f32[256,768]{1,0:T(8,128)}, u32[]{:S(2)}) copy-start(f32[256,768]{1,0:T(8,128)} %copy-done.30) | copy-start | bytes 2359300
  379.1 12.8 %collective-permute-start.21 = (f32[2,72,768]{2,1,0:T(8,128)S(1)}, f32[2,72,768]{2,1,0:T(8,128)S(1)}, u32[]{:S(2)}, u32[]{:S(2)}) collective-permute-start(f32[2,72,768]{2,1,0:T(8,128)S(1)} %pad_maximum_fusion.10), channel_id=1, source_target_pairs={{0,16},{4,20},{8,24},{12,28},{16,0},{20,4},{24,8},{28,12},{1,17},{... | collective-permute-start | bytes 1327112 | tf_op jit(solution)/shard_map/ppermute | solution.py:562
  380.9 11.9 %collective-permute-start.23 = (f32[2,80,768]{2,1,0:T(8,128)S(1)}, f32[2,80,768]{2,1,0:T(8,128)S(1)}, u32[]{:S(2)}, u32[]{:S(2)}) collective-permute-start(f32[2,80,768]{2,1,0:T(8,128)S(1)} %pad_maximum_fusion.9), channel_id=1, source_target_pairs={{0,8},{4,12},{8,0},{12,4},{16,24},{20,28},{24,16},{28,20},{1,9},{5... | collective-permute-start | bytes 1474568 | tf_op jit(solution)/shard_map/ppermute | solution.py:562
  401.2 4.7 %collective-permute-start.25 = (f32[4,80,768]{2,1,0:T(8,128)S(1)}, f32[4,80,768]{2,1,0:T(8,128)S(1)}, u32[]{:S(2)}, u32[]{:S(2)}) collective-permute-start(f32[4,80,768]{2,1,0:T(8,128)S(1)} %pad_maximum_fusion.7.low_b_ref), channel_id=1, source_target_pairs={{0,4},{4,0},{8,12},{12,8},{16,20},{20,16},{24,28},{28,24},{1,5},{5... | collective-permute-start | bytes 2949128 | tf_op jit(solution)/shard_map/ppermute | solution.py:562
  402.6 3.3 collective-permute-start.24
  (30 other events, 138.1 us)
Sparse Core Ops, SparseCore 0:
  16.9 25.1 all-gather.4
  66.0 40.0 all-gather.6
  108.0 31.4 all-gather.8
  172.5 80.5 reduce-scatter.1
  343.1 42.4 all-gather.10

commit v7 on v6

--- a/solution.py
+++ b/solution.py
@@ -113,7 +113,7 @@
 
         return 0
 
-    lax.fori_loop(0, heads, one_head, 0, unroll=True)
+    lax.fori_loop(0, heads, one_head, 0)
 
 
 def attend(scalars, lengths, tokens, coords, table, w_qkv, w_pos):
@@ -394,7 +394,7 @@
             d_ref[part, at] = value.astype(jnp.bfloat16)
         return 0
 
-    lax.fori_loop(0, 2 * heads, one_head, 0, unroll=2)
+    lax.fori_loop(0, 2 * heads, one_head, 0)
     for part in range(3):
         for side in range(2):
             at = slice(side * columns, (side + 1) * columns)
@@ -455,6 +455,34 @@
     )(scalars, lengths, *arrays)
 
 
+def split_blocks_kernel(in_ref, first_ref, second_ref):
+    count, both, _ = in_ref.shape
+    rows = both // 2
+    for block in range(count):
+        at = slice(block * rows, (block + 1) * rows)
+        first_ref[at] = in_ref[block, :rows]
+        second_ref[at] = in_ref[block, rows:]
+
+
+def split_blocks(blocks):
+    count, both, width = blocks.shape
+    lanes = width // 3 if width % 384 == 0 else width
+    shape = pltpu.HBM((count * both // 2, width), blocks.dtype)
+    out_spec = pl.BlockSpec((count * both // 2, lanes), lambda i: (0, i))
+    return pl.pallas_call(
+        split_blocks_kernel,
+        out_shape=(shape, shape),
+        grid_spec=pl.GridSpec(
+            grid=(width // lanes,),
+            in_specs=[pl.BlockSpec((count, both, lanes), lambda i: (0, 0, i))],
+            out_specs=[out_spec, out_spec],
+        ),
+        compiler_params=pltpu.CompilerParams(vmem_limit_bytes=24 << 20),
+        cost_estimate=pl.CostEstimate(flops=0, transcendentals=0, bytes_accessed=8 * blocks.size),
+        name="split_blocks",
+    )(blocks)
+
+
 def place_grads_kernel(
     order, scalars_ref, low_a_ref, low_b_ref, high_a_ref, high_b_ref, qkv_ref, pos_ref, out_ref, vec_ref
 ):
@@ -665,15 +693,12 @@
         return jnp.where(page == 0, out, out[::-1])
 
     half_of = lambda value, index: lax.dynamic_slice_in_dim(value, index * half, half, 0)
-    quarter = half // 2
     out_mine = half_of(output, low)
-    out_far = [swap(after(out_mine[:quarter], other), FAR)]
+    out_far = swap(after(out_mine, other), FAR)
 
     bits = [1 << k for k in range(dp_size.bit_length() - 1)]
-    send, give, _ = lax.optimization_barrier((send, give, out_far[0]))
+    give = after(give, out_far)
     near_sum = swap(send, NEAR)
-    out_far.append(swap(after(out_mine[quarter:], send), FAR))
-    out_far = jnp.concatenate(out_far, axis=0)
     mine = base + near_sum
 
     group_scalar = jnp.reshape(group, (1,))
@@ -682,7 +707,7 @@
     crossed = swap(jnp.concatenate([mine, ffn[ffn_rows:]], axis=0), FAR)
     ffn = ffn[:ffn_rows] + crossed[half:]
     far_mine = crossed[:half]
-    total = after(keep + group_swap(give, bits[0]), near_sum, out_far)
+    total = keep + group_swap(give, bits[0])
     more = bits[1:]
 
     def after_all(*values):
@@ -714,7 +739,8 @@
         got_lower = group_swap(lower, more[-1 - step])
         upper = jnp.concatenate([upper, got_upper], axis=0)
         lower = jnp.concatenate([lower, got_lower], axis=0)
-    upper, lower, _ = lax.optimization_barrier((upper, lower, rest))
+    grad_w_in, grad_w_back = split_blocks(gather(ffn).reshape(dp_size, ffn_rows, units))
+    upper, lower = after_all(upper, lower, rest, grad_w_in)[:2]
     parts = [upper, lower, group_swap(upper, bits[0]), group_swap(lower, bits[0])]
     grad_w_qkv, grad_w_pos, grad_w_out, vectors = place_grads(group_scalar, parts, columns, 8)
     grad_w_qkv, grad_w_pos = turn(grad_w_qkv), turn(grad_w_pos)
@@ -722,9 +748,6 @@
     grad_b_back, grad_gain_two, grad_shift_two = vectors[3], vectors[4], vectors[5]
     grad_b_in = vectors[6]
 
-    ffn = gather(ffn).reshape(dp_size, ffn_rows, units)
-    grad_w_in = ffn[:, :in_rows].reshape(width, units)
-    grad_w_back = ffn[:, in_rows:].reshape(units, width)
     return (
         layer_out,
         grad_tokens,

time: 421 us -> 410 us (0.974)
  waiting for transfers between devices: 255 us -> 236 us
  other arithmetic: 23.7 us -> 28.2 us
    ppermute x15 -> x14, waiting for transfers between devices: 199 us -> 181 us  [swap(): return lax.ppermute(value, MP, pairs)]
    slice x2 -> x0, local copies, waits for them, and re-layouts: 5.04 us -> none  [the longest x1 4.98 us: body(): grad_w_back = ffn[:, in_rows:].reshape(units, width)]
    unnamed x93 -> x90, local copies, waits for them, and re-layouts: 10.2 us -> 12.8 us
    ppermute x15 -> x14, starting transfers between devices: 24.1 us -> 23.1 us  [swap(): return lax.ppermute(value, MP, pairs)]
  transfers between devices with their start and end apart: 31 -> 30, of which waited for: 17 -> 19; matrix products, arithmetic and copies ran while one was open for 8% -> 10% of each run, Pallas kernels for 16% -> 16%
where the time goes in v7:
time: 410 us; the launch traced here: 409 us
  waiting for transfers between devices  236 us (58%)
  Pallas kernels  68.7 us (17%)
  starting transfers between devices  35.4 us (9%)
  other arithmetic  28.2 us (7%)
  local copies, waits for them, and re-layouts  26.2 us (6%)
  between operations  14.4 us (4%)
    ppermute x14, waiting for transfers between devices, swap(): return lax.ppermute(value, MP, pairs)  181 us
    ppermute x11, waiting for transfers between devices, group_swap(): return lax.ppermute(value, 'dp', pairs)  37.2 us
    pallas_call x1, Pallas kernels, attend_back(): pl.pallas_call(partial(attend_back_kernel, heads, count), out_shape=shape...  25.6 us
    ppermute x14, starting transfers between devices, swap(): return lax.ppermute(value, MP, pairs)  23.1 us
    pallas_call x4, Pallas kernels, on_chunk(): pl.pallas_call(without(kernel, inputs, len(before)), out_shape=shapes, gr...  22.7 us
    all_gather x4, waiting for transfers between devices, gather(): return lax.all_gather(value, 'dp', axis=0, tiled=True)  17.6 us
    unnamed x90, local copies, waits for them, and re-layouts  12.8 us
    ppermute x11, starting transfers between devices, group_swap(): return lax.ppermute(value, 'dp', pairs)  11.8 us
  transfers between devices with their start and end apart: 30, of which 19 were waited for; matrix products, arithmetic and copies ran while one was open for 10% of the time, Pallas kernels for 16%

profile of v7, /device:TPU:0, one launch (start us, length us, event | category | flops | bytes accessed | tf_op | source)
XLA Modules:
  0.0 409.4 jit_solution(3219753613299335734)
XLA Ops:
  8.1 4.1 %collective-permute-start.1 = (f32[24,768]{1,0:T(8,128)S(1)}, f32[24,768]{1,0:T(8,128)S(1)}, u32[]{:S(2)}, u32[]{:S(2)}) collective-permute-start(f32[24,768]{1,0:T(8,128)S(1)} %dynamic-slice_convert_fusion.1), channel_id=1, source_target_pairs={{0,2},{1,3},{2,0},{3,1},{4,6},{5,7},{6,4},{7,5},{8,10},{9,11},{10,... | collective-permute-start | bytes 221192 | tf_op jit(solution)/shard_map/ppermute | solution.py:586
  12.2 3.9 collective-permute-done.1
  22.0 10.0 %attend.1 = (f32[192,512]{1,0:T(8,128)S(1)}, bf16[192,512]{1,0:T(8,128)(2,1)S(1)}, bf16[5,192,512]{2,1,0:T(8,128)(2,1)S(1)}, bf16[512,768]{1,0:T(8,128)(2,1)S(1)}) custom-call(s32[2]{0:T(128)S(1)} %pad_add_fusion.scalars_ref.refs_0_, s32[2]{0:T(128)S(1)} %copy-done.14, bf16[2,512,768]{2,1,0:T(8,128)(2,1)S(1)} %copy-done.2, s32[2,2,512]{2,1,0:T(2,128)S(1)} %copy-done.15, ...), custom_call_target="tpu_custom_call" | custom-call | flops 2315255808 | bytes 5898240 | tf_op jit(solution)/shard_map/attend/pallas_call | solution.py:130
  33.9 1.6 collective-permute-start
  35.5 28.4 %collective-permute-done = f32[192,512]{1,0:T(8,128)S(1)} collective-permute-done((f32[192,512]{1,0:T(8,128)S(1)}, f32[192,512]{1,0:T(8,128)S(1)}, u32[]{:S(2)}, u32[]{:S(2)}) %collective-permute-start) | collective-permute-done | bytes 393248 | tf_op jit(solution)/shard_map/ppermute | solution.py:586
  63.9 1.9 slice.101
  70.4 16.2 %collective-permute-done.9 = f32[5,24,768]{2,1,0:T(8,128)S(1)} collective-permute-done((f32[5,24,768]{2,1,0:T(8,128)S(1)}, f32[5,24,768]{2,1,0:T(8,128)S(1)}, u32[]{:S(2)}, u32[]{:S(2)}) %collective-permute-start.9) | collective-permute-done | bytes 368672 | tf_op jit(solution)/shard_map/ppermute | solution.py:586
  88.6 17.5 %all-gather.7.cloned.1.call-done = f32[1536,768]{1,0:T(8,128)} async-done(((f32[192,768]{1,0:T(8,128)}), f32[1536,768]{1,0:T(8,128)}) %all-gather.7.cloned.1.call-update) | async-done | bytes 4718608 | tf_op jit(solution)/shard_map/all_gather | solution.py:597
  106.1 2.7 multiply_convert_fusion
  110.0 10.5 %collective-permute-done.2.refs_3_ = f32[512,768]{1,0:T(8,128)S(1)} collective-permute-done((f32[512,768]{1,0:T(8,128)S(1)}, f32[512,768]{1,0:T(8,128)S(1)}, u32[]{:S(2)}, u32[]{:S(2)}) %collective-permute-start.2) | collective-permute-done | bytes 1572896 | tf_op jit(solution)/shard_map/ppermute | solution.py:586
  121.7 5.1 %feed.2 = (f32[512,768]{1,0:T(8,128)}, f32[512,1]{1,0:T(8,128)S(1)}, bf16[512,768]{1,0:T(8,128)(2,1)S(1)}, bf16[512,1536]{1,0:T(8,128)(2,1)}, f32[512,1536]{1,0:T(8,128)}, /*index=5*/f32[256,768]{1,0:T(8,128)S(1)}) custom-call(s32[2]{0:T(128)S(1)} %pad_add_fusion.scalars_ref.refs_0_, bf16[2,512,768]{2,1,0:T(8,128)(2,1)} %refs_1_.5, f32[512,768]{1,0:T(8,128)} %copy-done.18, ...), custom_call_target="tpu_custom_call" | custom-call | flops 2415919104 | bytes 7864320 | tf_op jit(solution)/shard_map/feed/pallas_call | solution.py:242
  126.8 1.7 collective-permute-start.5
  128.6 5.4 %feed.3 = (f32[512,768]{1,0:T(8,128)}, f32[512,1]{1,0:T(8,128)S(1)}, bf16[512,768]{1,0:T(8,128)(2,1)S(1)}, bf16[512,1536]{1,0:T(8,128)(2,1)}, f32[512,1536]{1,0:T(8,128)}, /*index=5*/f32[256,768]{1,0:T(8,128)S(1)}) custom-call(s32[2]{0:T(128)S(1)} %pad_add_fusion.scalars_ref.refs_0_, ...), custom_call_target="tpu_custom_call", output_to_operand_aliasing={{0}: (12, {}), {1}: (13, {}), {2}: (14, {}), {3}: (15, {}),... | custom-call | flops 2415919104 | bytes 7864320 | tf_op jit(solution)/shard_map/feed/pallas_call | solution.py:242
  134.4 12.9 %collective-permute-done.5.refs_3_ = f32[256,768]{1,0:T(8,128)S(1)} collective-permute-done((f32[256,768]{1,0:T(8,128)S(1)}, f32[256,768]{1,0:T(8,128)S(1)}, u32[]{:S(2)}, u32[]{:S(2)}) %collective-permute-start.5) | collective-permute-done | bytes 786464 | tf_op jit(solution)/shard_map/ppermute | solution.py:586
  147.3 6.3 %feed_back.2 = (f32[512,768]{1,0:T(8,128)}, f32[512,768]{1,0:T(8,128)}, bf16[512,768]{1,0:T(8,128)(2,1)S(1)}, bf16[512,1536]{1,0:T(8,128)(2,1)}, f32[512,768]{1,...) custom-call(s32[2]{0:T(128)S(1)} %pad_add_fusion.scalars_ref.refs_0_, bf16[2,512,768]{2,1,0:T(8,128)(2,1)} %refs_1_.7, ...), custom_call_target="tpu_custom_call" | custom-call | flops 2415919104 | bytes 7864320 | tf_op jit(solution)/shard_map/feed_back/pallas_call | solution.py:242
  153.6 6.8 %collective-permute-done.4.refs_3_ = f32[256,768]{1,0:T(8,128)S(1)} collective-permute-done((f32[256,768]{1,0:T(8,128)S(1)}, f32[256,768]{1,0:T(8,128)S(1)}, u32[]{:S(2)}, u32[]{:S(2)}) %collective-permute-start.4) | collective-permute-done | bytes 786464 | tf_op jit(solution)/shard_map/ppermute | solution.py:586
  160.4 5.9 %feed_back.3 = (f32[512,768]{1,0:T(8,128)}, f32[512,768]{1,0:T(8,128)}, bf16[512,768]{1,0:T(8,128)(2,1)S(1)}, bf16[512,1536]{1,0:T(8,128)(2,1)}, f32[512,768]{1,...) custom-call(s32[2]{0:T(128)S(1)} %pad_add_fusion.scalars_ref.refs_0_, ...), custom_call_target="tpu_custom_call", output_to_operand_aliasing={{0}: (15, {}), {1}: (16, {}), {2}: (17, {}), {3}: (18, {}),... | custom-call | flops 2415919104 | bytes 7864320 | tf_op jit(solution)/shard_map/feed_back/pallas_call | solution.py:242
  167.7 5.6 %feed_grads.1 = f32[8,4,96,768]{3,2,1,0:T(8,128)} custom-call(bf16[512,768]{1,0:T(8,128)(2,1)S(1)} %get-tuple-element.98.low_ref, bf16[512,1536]{1,0:T(8,128)(2,1)S(1)} %copy-done.4, bf16[512,1536]{1,0:T(8,128)(2,1)S(1)} %copy-done.5, bf16[512,768]{1,0:T(8,128)(2,1)S(1)} %get-tuple-element.101.feed_ref), custom_call_target="tpu_custom_call" | custom-call | flops 2415919104 | bytes 9437184 | tf_op jit(solution)/shard_map/feed_grads/pallas_call | solution.py:282
  173.6 1.8 collective-permute-start.6
  177.1 29.6 %collective-permute-done.6.other_ref = f32[512,768]{1,0:T(8,128)} collective-permute-done((f32[512,768]{1,0:T(8,128)}, f32[512,768]{1,0:T(8,128)}, u32[]{:S(2)}, u32[]{:S(2)}) %collective-permute-start.6) | collective-permute-done | bytes 1572896 | tf_op jit(solution)/shard_map/ppermute | solution.py:586
  206.7 8.5 %collective-permute-start.7 = (f32[256,768]{1,0:T(8,128)S(1)}, f32[256,768]{1,0:T(8,128)}, u32[]{:S(2)}, u32[]{:S(2)}) collective-permute-start(f32[256,768]{1,0:T(8,128)S(1)} %constant_dynamic-slice_fusion), channel_id=1, source_target_pairs={{0,2},{1,3},{2,0},{3,1},{4,6},{5,7},{6,4},{7,5},{8,10},{9,11},{10,... | collective-permute-start | bytes 2359304 | tf_op jit(solution)/shard_map/ppermute | solution.py:586
  215.8 25.6 %attend_back.1 = (f32[256,768]{1,0:T(8,128)}, f32[256,768]{1,0:T(8,128)}, f32[4,304,768]{2,1,0:T(8,128)}, f32[4,304,768]{2,1,0:T(8,128)}) custom-call(s32[3]{0:T(128)} %pad_add_fusion.1.scalars_ref, s32[2]{0:T(128)} %lengths_ref.3, f32[512,768]{1,0:T(8,128)} %get-tuple-element.85.part_ref, f32[512,768]{1,0:T(8,128)} %collective-permute-done.6.other_ref, ...), custom_call_target="tpu_custom_call" | custom-call | flops 3321888768 | bytes 15728640 | tf_op jit(solution)/shard_map/attend_back/pallas_call | solution.py:425
  241.4 5.7 %collective-permute-done.7 = f32[256,768]{1,0:T(8,128)} collective-permute-done((f32[256,768]{1,0:T(8,128)S(1)}, f32[256,768]{1,0:T(8,128)}, u32[]{:S(2)}, u32[]{:S(2)}) %collective-permute-start.7) | collective-permute-done | bytes 786464 | tf_op jit(solution)/shard_map/ppermute | solution.py:586
  247.1 6.7 %collective-permute-done.12 = f32[4,304,768]{2,1,0:T(8,128)S(1)} collective-permute-done((f32[4,304,768]{2,1,0:T(8,128)}, f32[4,304,768]{2,1,0:T(8,128)S(1)}, u32[]{:S(2)}, u32[]{:S(2)}) %collective-permute-start.12) | collective-permute-done | bytes 3735584 | tf_op jit(solution)/shard_map/ppermute | solution.py:590
  253.8 2.8 add.64
  256.8 1.8 copy-done.17
  260.6 1.5 collective-permute-start.13
  263.6 3.7 collective-permute-done.10
  268.6 1.7 collective-permute-start.11
  270.3 1.7 collective-permute-start.8
  272.1 11.6 %collective-permute-done.13 = f32[2,152,768]{2,1,0:T(8,128)} collective-permute-done((f32[2,152,768]{2,1,0:T(8,128)}, f32[2,152,768]{2,1,0:T(8,128)}, u32[]{:S(2)}, u32[]{:S(2)}) %collective-permute-start.13) | collective-permute-done | bytes 933920 | tf_op jit(solution)/shard_map/ppermute | solution.py:590
  283.6 1.6 slice_add_fusion
  289.4 27.5 %collective-permute-done.8 = f32[256,768]{1,0:T(8,128)S(1)} collective-permute-done((f32[256,768]{1,0:T(8,128)}, f32[256,768]{1,0:T(8,128)S(1)}, u32[]{:S(2)}, u32[]{:S(2)}) %collective-permute-start.8) | collective-permute-done | bytes 786464 | tf_op jit(solution)/shard_map/ppermute | solution.py:586
  317.0 1.5 collective-permute-start.15
  318.5 1.5 collective-permute-start.18
  320.0 11.0 %collective-permute-done.11 = f32[448,768]{1,0:T(8,128)S(1)} collective-permute-done((f32[448,768]{1,0:T(8,128)S(1)}, f32[448,768]{1,0:T(8,128)S(1)}, u32[]{:S(2)}, u32[]{:S(2)}) %collective-permute-start.11) | collective-permute-done | bytes 1376288 | tf_op jit(solution)/shard_map/ppermute | solution.py:586
  335.8 21.9 %collective-permute-done.16 = f32[152,768]{1,0:T(8,128)S(1)} collective-permute-done((f32[152,768]{1,0:T(8,128)S(1)}, f32[152,768]{1,0:T(8,128)S(1)}, u32[]{:S(2)}, u32[]{:S(2)}) %collective-permute-start.16) | collective-permute-done | bytes 466976 | tf_op jit(solution)/shard_map/ppermute | solution.py:586
  358.8 1.6 collective-permute-start.21
  360.4 1.5 collective-permute-start.19
  363.2 9.8 %collective-permute-done.19 = f32[1,72,768]{2,1,0:T(8,128)S(1)} collective-permute-done((f32[1,72,768]{2,1,0:T(8,128)S(1)}, f32[1,72,768]{2,1,0:T(8,128)S(1)}, u32[]{:S(2)}, u32[]{:S(2)}) %collective-permute-start.19) | collective-permute-done | bytes 221216 | tf_op jit(solution)/shard_map/ppermute | solution.py:590
  373.6 1.6 collective-permute-start.22
  376.7 8.7 %collective-permute-done.20 = f32[2,72,768]{2,1,0:T(8,128)S(1)} collective-permute-done((f32[2,72,768]{2,1,0:T(8,128)S(1)}, f32[2,72,768]{2,1,0:T(8,128)S(1)}, u32[]{:S(2)}, u32[]{:S(2)}) %collective-permute-start.20) | collective-permute-done | bytes 442400 | tf_op jit(solution)/shard_map/ppermute | solution.py:590
  386.1 2.3 copy-done.6
  388.4 2.7 split_blocks.1
  391.1 2.8 collective-permute-done.17
  395.9 1.7 select_bitcast_fusion.1
  398.2 1.9 reverse_select_fusion
  400.0 2.2 place_grads.1
  (185 shorter events, 43.9 us)
Async XLA Ops:
  7.2 60.1 %all-gather.5.cloned.1.call-start = ((), (), s32[]{:S(2)}) async-start(), calls=%async_computation.1 | async-start | bytes 1327104 | tf_op jit(solution)/shard_map/all_gather | solution.py:597
  8.0 13.0 %copy-start.2 = (bf16[2,512,768]{2,1,0:T(8,128)(2,1)S(1)}, bf16[2,512,768]{2,1,0:T(8,128)(2,1)}, u32[]{:S(2)}) copy-start(bf16[2,512,768]{2,1,0:T(8,128)(2,1)} %refs_1_.5) | copy-start | bytes 4718596
  8.0 13.0 %copy-start.7 = (bf16[3,768,192]{1,2,0:T(8,128)(2,1)S(1)}, bf16[3,768,192]{1,2,0:T(8,128)(2,1)}, u32[]{:S(2)}) copy-start(bf16[3,768,192]{1,2,0:T(8,128)(2,1)} %param.20) | copy-start | bytes 2654212
  8.0 13.0 %copy-start.12 = (bf16[2,768,192]{1,2,0:T(8,128)(2,1)S(1)}, bf16[2,768,192]{1,2,0:T(8,128)(2,1)}, u32[]{:S(2)}) copy-start(bf16[2,768,192]{1,2,0:T(8,128)(2,1)} %param.21) | copy-start | bytes 1769476
  8.1 8.0 %collective-permute-start.1 = (f32[24,768]{1,0:T(8,128)S(1)}, f32[24,768]{1,0:T(8,128)S(1)}, u32[]{:S(2)}, u32[]{:S(2)}) collective-permute-start(f32[24,768]{1,0:T(8,128)S(1)} %dynamic-slice_convert_fusion.1), channel_id=1, source_target_pairs={{0,2},{1,3},{2,0},{3,1},{4,6},{5,7},{6,4},{7,5},{8,10},{9,11},{10,... | collective-permute-start | bytes 221192 | tf_op jit(solution)/shard_map/ppermute | solution.py:586
  16.8 89.4 %all-gather.7.cloned.1.call-start = ((), (), s32[]{:S(2)}) async-start(), calls=%async_computation.2 | async-start | bytes 5308416 | tf_op jit(solution)/shard_map/all_gather | solution.py:597
  19.6 44.3 %collective-permute-start.3 = (f32[200,768]{1,0:T(8,128)}, f32[200,768]{1,0:T(8,128)}, u32[]{:S(2)}, u32[]{:S(2)}) collective-permute-start(f32[200,768]{1,0:T(8,128)} %maximum_maximum_fusion), channel_id=1, source_target_pairs={{0,2},{1,3},{2,0},{3,1},{4,6},{5,7},{6,4},{7,5},{8,10},{9,11},{10,... | collective-permute-start | bytes 1843208 | tf_op jit(solution)/shard_map/ppermute | solution.py:586
  33.9 34.5 %copy-start.11 = (bf16[192,512]{1,0:T(8,128)(2,1)}, bf16[192,512]{1,0:T(8,128)(2,1)S(1)}, u32[]{:S(2)}) copy-start(bf16[192,512]{1,0:T(8,128)(2,1)S(1)} %get-tuple-element.67.mixed_ref) | copy-start | bytes 589828
  33.9 30.0 %collective-permute-start = (f32[192,512]{1,0:T(8,128)S(1)}, f32[192,512]{1,0:T(8,128)S(1)}, u32[]{:S(2)}, u32[]{:S(2)}) collective-permute-start(f32[192,512]{1,0:T(8,128)S(1)} %get-tuple-element.68), channel_id=1, source_target_pairs={{0,2},{1,3},{2,0},{3,1},{4,6},{5,7},{6,4},{7,5},{8,10},{9,11},{10,... | collective-permute-start | bytes 1179656 | tf_op jit(solution)/shard_map/ppermute | solution.py:586
  65.9 150.0 %all-gather.9.cloned.1.call-start = ((), (), s32[]{:S(2)}) async-start(), calls=%async_computation.3 | async-start | bytes 3317760 | tf_op jit(solution)/shard_map/all_gather | solution.py:597
  68.4 19.0 %copy-start.27 = (bf16[8,24,768]{2,1,0:T(8,128)(2,1)}, bf16[8,24,768]{2,1,0:T(8,128)(2,1)S(1)}, u32[]{:S(2)}) copy-start(bf16[8,24,768]{2,1,0:T(8,128)(2,1)S(1)} %fusion.5) | copy-start | bytes 884740
  68.5 19.3 %copy-start.39 = (f32[768]{0:T(1024)S(1)}, f32[768]{0:T(1024)}, u32[]{:S(2)}) copy-start(f32[768]{0:T(1024)} %param.24) | copy-start | bytes 9220
  68.5 19.3 %copy-start.40 = (f32[768]{0:T(1024)S(1)}, f32[768]{0:T(1024)}, u32[]{:S(2)}) copy-start(f32[768]{0:T(1024)} %param.25) | copy-start | bytes 9220
  68.5 19.3 %copy-start.41 = (f32[768]{0:T(1024)S(1)}, f32[768]{0:T(1024)}, u32[]{:S(2)}) copy-start(f32[768]{0:T(1024)} %param.23) | copy-start | bytes 9220
  68.5 20.1 %copy-start.38 = (f32[1,768]{1,0:T(1,128)S(1)}, f32[1,768]{1,0:T(1,128)}, u32[]{:S(2)}) copy-start(f32[1,768]{1,0:T(1,128)} %copy-done.37) | copy-start | bytes 9220
  69.1 39.7 %copy-start.18 = (f32[512,768]{1,0:T(8,128)}, f32[512,768]{1,0:T(8,128)S(1)}, u32[]{:S(2)}) copy-start(f32[512,768]{1,0:T(8,128)S(1)} %fusion.6.refs_2_) | copy-start | bytes 4718596
  70.3 16.3 %collective-permute-start.9 = (f32[5,24,768]{2,1,0:T(8,128)S(1)}, f32[5,24,768]{2,1,0:T(8,128)S(1)}, u32[]{:S(2)}, u32[]{:S(2)}) collective-permute-start(f32[5,24,768]{2,1,0:T(8,128)S(1)} %dynamic-slice_convert_fusion), channel_id=1, source_target_pairs={{0,2},{1,3},{2,0},{3,1},{4,6},{5,7},{6,4},{7,5},{8,10},{9,11},{10,... | collective-permute-start | bytes 1105928 | tf_op jit(solution)/shard_map/ppermute | solution.py:586
  87.4 180.0 %reduce-scatter.2.cloned.1.call-start = ((), (), s32[]{:S(2)}) async-start(), calls=%async_computation.4 | async-start | bytes 10616832 | tf_op jit(solution)/shard_map/reduce_scatter | solution.py:675
  87.7 32.8 %collective-permute-start.2 = (f32[512,768]{1,0:T(8,128)S(1)}, f32[512,768]{1,0:T(8,128)S(1)}, u32[]{:S(2)}, u32[]{:S(2)}) collective-permute-start(f32[512,768]{1,0:T(8,128)S(1)} %fusion.6.refs_2_), channel_id=1, source_target_pairs={{0,1},{1,0},{2,3},{3,2},{4,5},{5,4},{6,7},{7,6},{8,9},{9,8},{10,11... | collective-permute-start | bytes 4718600 | tf_op jit(solution)/shard_map/ppermute | solution.py:586
  87.8 72.6 %copy-start.13 = (f32[1,768]{1,0:T(1,128)}, f32[1,768]{1,0:T(1,128)S(1)}, u32[]{:S(2)}) copy-start(f32[1,768]{1,0:T(1,128)S(1)} %reshape.231.refs_5_.refs_6_.gain_ref) | copy-start | bytes 9220
  126.8 20.5 %collective-permute-start.5 = (f32[256,768]{1,0:T(8,128)S(1)}, f32[256,768]{1,0:T(8,128)S(1)}, u32[]{:S(2)}, u32[]{:S(2)}) collective-permute-start(f32[256,768]{1,0:T(8,128)S(1)} %get-tuple-element.78.refs_2_), channel_id=1, source_target_pairs={{0,1},{1,0},{2,3},{3,2},{4,5},{5,4},{6,7},{7,6},{8,9},{9,8},{10,11... | collective-permute-start | bytes 2359304 | tf_op jit(solution)/shard_map/ppermute | solution.py:586
  134.0 19.6 %copy-start.8 = (f32[512,1]{1,0:T(8,128)}, f32[512,1]{1,0:T(8,128)S(1)}, u32[]{:S(2)}) copy-start(f32[512,1]{1,0:T(8,128)S(1)} %get-tuple-element.88.scale_ref) | copy-start | bytes 6148
  134.0 26.4 %collective-permute-start.4 = (f32[256,768]{1,0:T(8,128)S(1)}, f32[256,768]{1,0:T(8,128)S(1)}, u32[]{:S(2)}, u32[]{:S(2)}) collective-permute-start(f32[256,768]{1,0:T(8,128)S(1)} %get-tuple-element.75.refs_2_), channel_id=1, source_target_pairs={{0,1},{1,0},{2,3},{3,2},{4,5},{5,4},{6,7},{7,6},{8,9},{9,8},{10,11... | collective-permute-start | bytes 2359304 | tf_op jit(solution)/shard_map/ppermute | solution.py:586
  173.3 212.7 %all-gather.11.cloned.1.call-start = ((), (), s32[]{:S(2)}) async-start(), calls=%async_computation.5 | async-start | bytes 5308416 | tf_op jit(solution)/shard_map/all_gather | solution.py:597
  173.6 33.1 %collective-permute-start.6 = (f32[512,768]{1,0:T(8,128)}, f32[512,768]{1,0:T(8,128)}, u32[]{:S(2)}, u32[]{:S(2)}) collective-permute-start(f32[512,768]{1,0:T(8,128)} %get-tuple-element.85.part_ref), channel_id=1, source_target_pairs={{0,1},{1,0},{2,3},{3,2},{4,5},{5,4},{6,7},{7,6},{8,9},{9,8},{10,11... | collective-permute-start | bytes 4718600 | tf_op jit(solution)/shard_map/ppermute | solution.py:586
  206.7 40.4 %collective-permute-start.7 = (f32[256,768]{1,0:T(8,128)S(1)}, f32[256,768]{1,0:T(8,128)}, u32[]{:S(2)}, u32[]{:S(2)}) collective-permute-start(f32[256,768]{1,0:T(8,128)S(1)} %constant_dynamic-slice_fusion), channel_id=1, source_target_pairs={{0,2},{1,3},{2,0},{3,1},{4,6},{5,7},{6,4},{7,5},{8,10},{9,11},{10,... | collective-permute-start | bytes 2359304 | tf_op jit(solution)/shard_map/ppermute | solution.py:586
  247.1 6.7 %collective-permute-start.12 = (f32[4,304,768]{2,1,0:T(8,128)}, f32[4,304,768]{2,1,0:T(8,128)S(1)}, u32[]{:S(2)}, u32[]{:S(2)}) collective-permute-start(f32[4,304,768]{2,1,0:T(8,128)} %get-tuple-element.104), channel_id=1, source_target_pairs={{0,4},{4,0},{8,12},{12,8},{16,20},{20,16},{24,28},{28,24},{1,5},{5... | collective-permute-start | bytes 11206664 | tf_op jit(solution)/shard_map/ppermute | solution.py:590
  247.1 20.2 %collective-permute-start.10 = (f32[256,768]{1,0:T(8,128)}, f32[256,768]{1,0:T(8,128)S(1)}, u32[]{:S(2)}, u32[]{:S(2)}) collective-permute-start(f32[256,768]{1,0:T(8,128)} %get-tuple-element.97), channel_id=1, source_target_pairs={{0,1},{1,0},{2,3},{3,2},{4,5},{5,4},{6,7},{7,6},{8,9},{9,8},{10,11... | collective-permute-start | bytes 2359304 | tf_op jit(solution)/shard_map/ppermute | solution.py:586
  260.6 23.0 %collective-permute-start.13 = (f32[2,152,768]{2,1,0:T(8,128)}, f32[2,152,768]{2,1,0:T(8,128)}, u32[]{:S(2)}, u32[]{:S(2)}) collective-permute-start(f32[2,152,768]{2,1,0:T(8,128)} %slice.139), channel_id=1, source_target_pairs={{0,16},{4,20},{8,24},{12,28},{16,0},{20,4},{24,8},{28,12},{1,17},{... | collective-permute-start | bytes 2801672 | tf_op jit(solution)/shard_map/ppermute | solution.py:590
  262.1 24.2 %collective-permute-start.14 = (f32[2,152,768]{2,1,0:T(8,128)}, f32[2,152,768]{2,1,0:T(8,128)}, u32[]{:S(2)}, u32[]{:S(2)}) collective-permute-start(f32[2,152,768]{2,1,0:T(8,128)} %slice_bitcast_fusion.1), channel_id=1, source_target_pairs={{0,8},{4,12},{8,0},{12,4},{16,24},{20,28},{24,16},{28,20},{1,9},{5... | collective-permute-start | bytes 2801672 | tf_op jit(solution)/shard_map/ppermute | solution.py:590
  268.6 62.4 %collective-permute-start.11 = (f32[448,768]{1,0:T(8,128)S(1)}, f32[448,768]{1,0:T(8,128)S(1)}, u32[]{:S(2)}, u32[]{:S(2)}) collective-permute-start(f32[448,768]{1,0:T(8,128)S(1)} %pad_maximum_fusion.6), channel_id=1, source_target_pairs={{0,2},{1,3},{2,0},{3,1},{4,6},{5,7},{6,4},{7,5},{8,10},{9,11},{10,... | collective-permute-start | bytes 4128776 | tf_op jit(solution)/shard_map/ppermute | solution.py:586
  270.3 46.6 %collective-permute-start.8 = (f32[256,768]{1,0:T(8,128)}, f32[256,768]{1,0:T(8,128)S(1)}, u32[]{:S(2)}, u32[]{:S(2)}) collective-permute-start(f32[256,768]{1,0:T(8,128)} %collective-permute-done.7), channel_id=1, source_target_pairs={{0,1},{1,0},{2,3},{3,2},{4,5},{5,4},{6,7},{7,6},{8,9},{9,8},{10,11... | collective-permute-start | bytes 2359304 | tf_op jit(solution)/shard_map/ppermute | solution.py:586
  286.3 45.8 %copy-start.28 = (f32[384,768]{1,0:T(8,128)S(1)}, f32[384,768]{1,0:T(8,128)}, u32[]{:S(2)}) copy-start(f32[384,768]{1,0:T(8,128)} %reduce-scatter.2.cloned.1.call-done) | copy-start | bytes 3538948
  288.6 44.4 %copy-start.20 = (f32[512,768]{1,0:T(8,128)S(1)}, f32[512,768]{1,0:T(8,128)}, u32[]{:S(2)}) copy-start(f32[512,768]{1,0:T(8,128)} %get-tuple-element.84) | copy-start | bytes 4718596
  289.4 43.7 %copy-start.26 = (f32[2,152,768]{2,1,0:T(8,128)S(1)}, f32[2,152,768]{2,1,0:T(8,128)}, u32[]{:S(2)}) copy-start(f32[2,152,768]{2,1,0:T(8,128)} %copy-done.25) | copy-start | bytes 2801668
  317.0 14.0 %copy-start.33 = (f32[256,768]{1,0:T(8,128)}, f32[256,768]{1,0:T(8,128)S(1)}, u32[]{:S(2)}) copy-start(f32[256,768]{1,0:T(8,128)S(1)} %collective-permute-done.8) | copy-start | bytes 2359300
  317.0 16.0 %collective-permute-start.15 = (f32[1,152,768]{2,1,0:T(8,128)}, f32[1,152,768]{2,1,0:T(8,128)}, u32[]{:S(2)}, u32[]{:S(2)}) collective-permute-start(f32[1,152,768]{2,1,0:T(8,128)} %slice.143), channel_id=1, source_target_pairs={{0,8},{4,12},{8,0},{12,4},{16,24},{20,28},{24,16},{28,20},{1,9},{5... | collective-permute-start | bytes 1400840 | tf_op jit(solution)/shard_map/ppermute | solution.py:590
  318.5 14.5 %collective-permute-start.18 = (f32[1,152,768]{2,1,0:T(8,128)}, f32[1,152,768]{2,1,0:T(8,128)}, u32[]{:S(2)}, u32[]{:S(2)}) collective-permute-start(f32[1,152,768]{2,1,0:T(8,128)} %slice_bitcast_fusion.4), channel_id=1, source_target_pairs={{0,16},{4,20},{8,24},{12,28},{16,0},{20,4},{24,8},{28,12},{1,17},{... | collective-permute-start | bytes 1400840 | tf_op jit(solution)/shard_map/ppermute | solution.py:590
  334.2 23.4 %collective-permute-start.16 = (f32[152,768]{1,0:T(8,128)S(1)}, f32[152,768]{1,0:T(8,128)S(1)}, u32[]{:S(2)}, u32[]{:S(2)}) collective-permute-start(f32[152,768]{1,0:T(8,128)S(1)} %fusion.13), channel_id=1, source_target_pairs={{0,2},{1,3},{2,0},{3,1},{4,6},{5,7},{6,4},{7,5},{8,10},{9,11},{10,... | collective-permute-start | bytes 1400840 | tf_op jit(solution)/shard_map/ppermute | solution.py:586
  334.5 23.1 %copy-start.24 = (f32[1,2,152,768]{3,2,1,0:T(8,128)S(1)}, f32[1,2,152,768]{3,2,1,0:T(8,128)}, u32[]{:S(2)}) copy-start(f32[1,2,152,768]{3,2,1,0:T(8,128)} %copy-done.23) | copy-start | bytes 2801668
  357.6 36.3 %collective-permute-start.17 = (f32[2,256,768]{2,1,0:T(8,128)}, f32[2,256,768]{2,1,0:T(8,128)}, u32[]{:S(2)}, u32[]{:S(2)}) collective-permute-start(f32[2,256,768]{2,1,0:T(8,128)} %pad_maximum_fusion.4), channel_id=1, source_target_pairs={{0,1},{1,0},{2,3},{3,2},{4,5},{5,4},{6,7},{7,6},{8,9},{9,8},{10,11... | collective-permute-start | bytes 4718600 | tf_op jit(solution)/shard_map/ppermute | solution.py:586
  358.8 14.8 %collective-permute-start.21 = (f32[1,80,768]{2,1,0:T(8,128)S(1)}, f32[1,80,768]{2,1,0:T(8,128)S(1)}, u32[]{:S(2)}, u32[]{:S(2)}) collective-permute-start(f32[1,80,768]{2,1,0:T(8,128)S(1)} %slice_bitcast_fusion.5), channel_id=1, source_target_pairs={{0,16},{4,20},{8,24},{12,28},{16,0},{20,4},{24,8},{28,12},{1,17},{... | collective-permute-start | bytes 737288 | tf_op jit(solution)/shard_map/ppermute | solution.py:590
  360.4 14.8 %copy-start.34 = (f32[256,768]{1,0:T(8,128)S(1)}, f32[256,768]{1,0:T(8,128)}, u32[]{:S(2)}) copy-start(f32[256,768]{1,0:T(8,128)} %copy-done.33) | copy-start | bytes 2359300
  360.4 12.6 %collective-permute-start.19 = (f32[1,72,768]{2,1,0:T(8,128)S(1)}, f32[1,72,768]{2,1,0:T(8,128)S(1)}, u32[]{:S(2)}, u32[]{:S(2)}) collective-permute-start(f32[1,72,768]{2,1,0:T(8,128)S(1)} %slice_bitcast_fusion.6), channel_id=1, source_target_pairs={{0,8},{4,12},{8,0},{12,4},{16,24},{20,28},{24,16},{28,20},{1,9},{5... | collective-permute-start | bytes 663560 | tf_op jit(solution)/shard_map/ppermute | solution.py:590
  373.0 12.4 %collective-permute-start.20 = (f32[2,72,768]{2,1,0:T(8,128)S(1)}, f32[2,72,768]{2,1,0:T(8,128)S(1)}, u32[]{:S(2)}, u32[]{:S(2)}) collective-permute-start(f32[2,72,768]{2,1,0:T(8,128)S(1)} %pad_maximum_fusion.10), channel_id=1, source_target_pairs={{0,16},{4,20},{8,24},{12,28},{16,0},{20,4},{24,8},{28,12},{1,17},{... | collective-permute-start | bytes 1327112 | tf_op jit(solution)/shard_map/ppermute | solution.py:590
  373.6 12.3 %collective-permute-start.22 = (f32[2,80,768]{2,1,0:T(8,128)S(1)}, f32[2,80,768]{2,1,0:T(8,128)S(1)}, u32[]{:S(2)}, u32[]{:S(2)}) collective-permute-start(f32[2,80,768]{2,1,0:T(8,128)S(1)} %pad_maximum_fusion.9), channel_id=1, source_target_pairs={{0,8},{4,12},{8,0},{12,4},{16,24},{20,28},{24,16},{28,20},{1,9},{5... | collective-permute-start | bytes 1474568 | tf_op jit(solution)/shard_map/ppermute | solution.py:590
  393.9 6.1 %collective-permute-start.24 = (f32[4,80,768]{2,1,0:T(8,128)S(1)}, f32[4,80,768]{2,1,0:T(8,128)S(1)}, u32[]{:S(2)}, u32[]{:S(2)}) collective-permute-start(f32[4,80,768]{2,1,0:T(8,128)S(1)} %pad_maximum_fusion.7.low_b_ref), channel_id=1, source_target_pairs={{0,4},{4,0},{8,12},{12,8},{16,20},{20,16},{24,28},{28,24},{1,5},{5... | collective-permute-start | bytes 2949128 | tf_op jit(solution)/shard_map/ppermute | solution.py:590
  395.4 4.7 %collective-permute-start.23 = (f32[4,72,768]{2,1,0:T(8,128)S(1)}, f32[4,72,768]{2,1,0:T(8,128)S(1)}, u32[]{:S(2)}, u32[]{:S(2)}) collective-permute-start(f32[4,72,768]{2,1,0:T(8,128)S(1)} %pad_maximum_fusion.8.low_a_ref), channel_id=1, source_target_pairs={{0,4},{4,0},{8,12},{12,8},{16,20},{20,16},{24,28},{28,24},{1,5},{5... | collective-permute-start | bytes 2654216 | tf_op jit(solution)/shard_map/ppermute | solution.py:590
  (28 other events, 119.4 us)
Sparse Core Ops, SparseCore 0:
  16.9 25.2 all-gather.4
  66.0 40.0 all-gather.6
  108.0 31.4 all-gather.8
  173.4 80.6 reduce-scatter.1
  333.1 45.6 all-gather.10

commit v8 on v7

--- a/solution.py
+++ b/solution.py
@@ -455,6 +455,35 @@
     )(scalars, lengths, *arrays)
 
 
+def spread_kernel(scalars_ref, *refs):
+    *pieces, out_ref = refs
+    if len(pieces) == 3:
+        pieces = [pieces[0], pieces[1], pieces[2].at[0], pieces[2].at[1]]
+    mine_ref, far_ref, rest_mine_ref, rest_far_ref = pieces
+    for step, ref in enumerate((mine_ref, rest_mine_ref, far_ref, rest_far_ref)):
+
+        @pl.when(pl.program_id(0) == step)
+        def _():
+            out_ref[0] = ref[...].astype(out_ref.dtype)
+
+
+def spread(scalars, pieces, kind):
+    half, width = pieces[0].shape
+    return pl.pallas_call(
+        spread_kernel,
+        out_shape=pltpu.HBM((2, 2 * half, width), kind),
+        grid_spec=pltpu.PrefetchScalarGridSpec(
+            num_scalar_prefetch=1,
+            grid=(4,),
+            in_specs=[pl.BlockSpec(memory_space=pltpu.VMEM)] * len(pieces),
+            out_specs=pl.BlockSpec((1, half, width), lambda i, s: (s[0] ^ (i // 2), s[1] ^ (i % 2), 0)),
+        ),
+        compiler_params=pltpu.CompilerParams(vmem_limit_bytes=16 << 20),
+        cost_estimate=pl.CostEstimate(flops=0, transcendentals=0, bytes_accessed=32 * half * width),
+        name="spread",
+    )(scalars, *pieces)
+
+
 def split_blocks_kernel(in_ref, first_ref, second_ref):
     count, both, _ = in_ref.shape
     rows = both // 2
@@ -622,7 +651,7 @@
     w_out_far = gather(out_rows).reshape(dp_size, -1, width)[:, : columns // dp_size]
     w_out_far = arrived(w_out_far.reshape(columns, width)).astype(bf16)
     mixed_far = swap(mixed_send, FAR)
-    far_rows = after(far_rows, mixed_far)
+    far_rows = after(far_rows, mixed_send)
     count = unit_rows.shape[0]
     b_in_two = jnp.stack([b_in, far_rows[count]])
     blocks = arrived(gather(far_rows[:count])).reshape(dp_size, count, -1)
@@ -686,12 +715,6 @@
     arrays += [proj, w_qkv, blocks, rows, pos_rows, mixed, mixed_far, vectors]
     send, base, keep, give = attend_back(dp_size, jnp.stack([page, low, group]), lengths, arrays)
 
-    def spread(mine, far, rest):
-        both = jnp.stack([mine, far])
-        out = jnp.stack([jnp.where(low == 0, both, rest), jnp.where(low == 0, rest, both)], axis=1)
-        out = out.reshape(pages, length, width)
-        return jnp.where(page == 0, out, out[::-1])
-
     half_of = lambda value, index: lax.dynamic_slice_in_dim(value, index * half, half, 0)
     out_mine = half_of(output, low)
     out_far = swap(after(out_mine, other), FAR)
@@ -728,13 +751,15 @@
     ffn = after(ffn, got_upper, got_lower)
 
     rest = swap(after(jnp.stack([mine, far_mine]), far_sum), NEAR)
-    grad_tokens = spread(mine, far_mine, rest)
+    grad_tokens = spread(scalars, (mine, far_mine, rest), f32)
     out_rest = half_of(output, 1 - low)
-    layer_out = spread(out_mine, arrived(out_far), jnp.stack([out_rest, arrived(out_turned)])).astype(bf16)
+    layer_out = spread(scalars, (out_mine, out_far, out_rest, after(out_turned, far_sum)), bf16)
     total = upper + far_sum
     cut = total.shape[0] // 16 * 8
     upper, lower = total[None, :cut], total[None, cut:]
     for step in range(len(more)):
+        if step:
+            upper, lower = after_all(upper, lower, layer_out)[:2]
         got_upper = group_swap(upper, more[step])
         got_lower = group_swap(lower, more[-1 - step])
         upper = jnp.concatenate([upper, got_upper], axis=0)

time: 410 us -> 406 us (level)
  other arithmetic: 28.2 us -> 19.2 us
  Pallas kernels: 68.7 us -> 75.3 us
    ppermute x14, waiting for transfers between devices: 181 us -> 199 us  [swap(): return lax.ppermute(value, MP, pairs)]
    all_gather x4, waiting for transfers between devices: 17.6 us -> 0.06 us  [gather(): return lax.all_gather(value, 'dp', axis=0, tiled=True)]
    pallas_call x0 -> x2, Pallas kernels: none -> 6.47 us  [spread(): pl.pallas_call(spread_kernel, out_shape=pltpu.HBM((2, 2 * half, width), k...]
    another operation x7 -> x2, other arithmetic: 8.49 us -> 3.95 us  [the longest x3 3.25 us: spread(): jnp.stack([jnp.where(low == 0, both, rest), jnp.where(low == 0, rest, bot...]
    unnamed x90 -> x92, local copies, waits for them, and re-layouts: 12.8 us -> 12.2 us
  transfers between devices with their start and end apart: 30 -> 30, of which waited for: 19 -> 20; matrix products, arithmetic and copies ran while one was open for 10% -> 8% of each run, Pallas kernels for 16% -> 18%
where the time goes in v8:
time: 406 us
  waiting for transfers between devices  237 us (58%)
  Pallas kernels  75.3 us (19%)
  starting transfers between devices  31.9 us (8%)
  local copies, waits for them, and re-layouts  26.7 us (7%)
  other arithmetic  19.2 us (5%)
  between operations  14.4 us (4%)
    ppermute x14, waiting for transfers between devices, swap(): return lax.ppermute(value, MP, pairs)  199 us
    ppermute x11, waiting for transfers between devices, group_swap(): return lax.ppermute(value, 'dp', pairs)  38.7 us
    pallas_call x1, Pallas kernels, attend_back(): pl.pallas_call(partial(attend_back_kernel, heads, count), out_shape=shape...  25.6 us
    pallas_call x4, Pallas kernels, on_chunk(): pl.pallas_call(without(kernel, inputs, len(before)), out_shape=shapes, gr...  22.8 us
    ppermute x14, starting transfers between devices, swap(): return lax.ppermute(value, MP, pairs)  19.3 us
    unnamed x92, local copies, waits for them, and re-layouts  12.2 us
    ppermute x11, starting transfers between devices, group_swap(): return lax.ppermute(value, 'dp', pairs)  12 us
    pallas_call x1, Pallas kernels, attend(): pl.pallas_call(partial(attend_kernel, columns // HEAD_DIM), out_shape=sha...  9.98 us
  transfers between devices with their start and end apart: 30, of which 20 were waited for; matrix products, arithmetic and copies ran while one was open for 8% of the time, Pallas kernels for 18%

profile of v8, /device:TPU:0, one launch (start us, length us, event | category | flops | bytes accessed | tf_op | source)
XLA Modules:
  0.0 405.5 jit_solution(9598929144683557502)
XLA Ops:
  8.1 4.1 %collective-permute-start.1 = (f32[24,768]{1,0:T(8,128)S(1)}, f32[24,768]{1,0:T(8,128)S(1)}, u32[]{:S(2)}, u32[]{:S(2)}) collective-permute-start(f32[24,768]{1,0:T(8,128)S(1)} %dynamic-slice_convert_fusion.1), channel_id=1, source_target_pairs={{0,2},{1,3},{2,0},{3,1},{4,6},{5,7},{6,4},{7,5},{8,10},{9,11},{10,... | collective-permute-start | bytes 221192 | tf_op jit(solution)/shard_map/ppermute | solution.py:615
  12.2 3.9 collective-permute-done.1
  22.0 10.0 %attend.1 = (f32[192,512]{1,0:T(8,128)S(1)}, bf16[192,512]{1,0:T(8,128)(2,1)S(1)}, bf16[5,192,512]{2,1,0:T(8,128)(2,1)S(1)}, bf16[512,768]{1,0:T(8,128)(2,1)S(1)}) custom-call(s32[2]{0:T(128)S(1)} %pad_add_fusion.scalars_ref.refs_0_, s32[2]{0:T(128)S(1)} %copy-done.18, bf16[2,512,768]{2,1,0:T(8,128)(2,1)S(1)} %copy-done.2, s32[2,2,512]{2,1,0:T(2,128)S(1)} %copy-done.21, ...), custom_call_target="tpu_custom_call" | custom-call | flops 2315255808 | bytes 5898240 | tf_op jit(solution)/shard_map/attend/pallas_call | solution.py:130
  34.6 12.6 %collective-permute-done.3 = f32[200,768]{1,0:T(8,128)} collective-permute-done((f32[200,768]{1,0:T(8,128)}, f32[200,768]{1,0:T(8,128)}, u32[]{:S(2)}, u32[]{:S(2)}) %collective-permute-start.3) | collective-permute-done | bytes 614432 | tf_op jit(solution)/shard_map/ppermute | solution.py:615
  47.2 2.0 slice.101
  50.6 19.8 %collective-permute-done = f32[192,512]{1,0:T(8,128)S(1)} collective-permute-done((f32[192,512]{1,0:T(8,128)S(1)}, f32[192,512]{1,0:T(8,128)S(1)}, u32[]{:S(2)}, u32[]{:S(2)}) %collective-permute-start) | collective-permute-done | bytes 393248 | tf_op jit(solution)/shard_map/ppermute | solution.py:615
  73.6 13.9 %collective-permute-done.9 = f32[5,24,768]{2,1,0:T(8,128)S(1)} collective-permute-done((f32[5,24,768]{2,1,0:T(8,128)S(1)}, f32[5,24,768]{2,1,0:T(8,128)S(1)}, u32[]{:S(2)}, u32[]{:S(2)}) %collective-permute-start.9) | collective-permute-done | bytes 368672 | tf_op jit(solution)/shard_map/ppermute | solution.py:615
  89.4 2.7 multiply_convert_fusion
  93.3 29.0 %collective-permute-done.2.refs_3_ = f32[512,768]{1,0:T(8,128)} collective-permute-done((f32[512,768]{1,0:T(8,128)S(1)}, f32[512,768]{1,0:T(8,128)}, u32[]{:S(2)}, u32[]{:S(2)}) %collective-permute-start.2) | collective-permute-done | bytes 1572896 | tf_op jit(solution)/shard_map/ppermute | solution.py:615
  122.4 5.2 %feed.2 = (f32[512,768]{1,0:T(8,128)}, f32[512,1]{1,0:T(8,128)S(1)}, bf16[512,768]{1,0:T(8,128)(2,1)S(1)}, bf16[512,1536]{1,0:T(8,128)(2,1)}, f32[512,1536]{1,0:T(8,128)}, /*index=5*/f32[256,768]{1,0:T(8,128)S(1)}) custom-call(s32[2]{0:T(128)S(1)} %pad_add_fusion.scalars_ref.refs_0_, bf16[2,512,768]{2,1,0:T(8,128)(2,1)} %refs_1_.5, f32[512,768]{1,0:T(8,128)} %copy-done.24, ...), custom_call_target="tpu_custom_call" | custom-call | flops 2415919104 | bytes 7864320 | tf_op jit(solution)/shard_map/feed/pallas_call | solution.py:242
  127.6 1.7 collective-permute-start.5
  129.3 5.4 %feed.3 = (f32[512,768]{1,0:T(8,128)}, f32[512,1]{1,0:T(8,128)S(1)}, bf16[512,768]{1,0:T(8,128)(2,1)S(1)}, bf16[512,1536]{1,0:T(8,128)(2,1)}, f32[512,1536]{1,0:T(8,128)}, /*index=5*/f32[256,768]{1,0:T(8,128)S(1)}) custom-call(s32[2]{0:T(128)S(1)} %pad_add_fusion.scalars_ref.refs_0_, ...), custom_call_target="tpu_custom_call", output_to_operand_aliasing={{0}: (12, {}), {1}: (13, {}), {2}: (14, {}), {3}: (15, {}),... | custom-call | flops 2415919104 | bytes 7864320 | tf_op jit(solution)/shard_map/feed/pallas_call | solution.py:242
  135.1 13.0 %collective-permute-done.5.refs_3_ = f32[256,768]{1,0:T(8,128)S(1)} collective-permute-done((f32[256,768]{1,0:T(8,128)S(1)}, f32[256,768]{1,0:T(8,128)S(1)}, u32[]{:S(2)}, u32[]{:S(2)}) %collective-permute-start.5) | collective-permute-done | bytes 786464 | tf_op jit(solution)/shard_map/ppermute | solution.py:615
  148.0 6.3 %feed_back.2 = (f32[512,768]{1,0:T(8,128)}, f32[512,768]{1,0:T(8,128)}, bf16[512,768]{1,0:T(8,128)(2,1)S(1)}, bf16[512,1536]{1,0:T(8,128)(2,1)}, f32[512,768]{1,...) custom-call(s32[2]{0:T(128)S(1)} %pad_add_fusion.scalars_ref.refs_0_, bf16[2,512,768]{2,1,0:T(8,128)(2,1)} %refs_1_.7, ...), custom_call_target="tpu_custom_call" | custom-call | flops 2415919104 | bytes 7864320 | tf_op jit(solution)/shard_map/feed_back/pallas_call | solution.py:242
  154.4 7.8 %collective-permute-done.4.refs_3_ = f32[256,768]{1,0:T(8,128)S(1)} collective-permute-done((f32[256,768]{1,0:T(8,128)S(1)}, f32[256,768]{1,0:T(8,128)S(1)}, u32[]{:S(2)}, u32[]{:S(2)}) %collective-permute-start.4) | collective-permute-done | bytes 786464 | tf_op jit(solution)/shard_map/ppermute | solution.py:615
  162.1 5.9 %feed_back.3 = (f32[512,768]{1,0:T(8,128)}, f32[512,768]{1,0:T(8,128)}, bf16[512,768]{1,0:T(8,128)(2,1)S(1)}, bf16[512,1536]{1,0:T(8,128)(2,1)}, f32[512,768]{1,...) custom-call(s32[2]{0:T(128)S(1)} %pad_add_fusion.scalars_ref.refs_0_, ...), custom_call_target="tpu_custom_call", output_to_operand_aliasing={{0}: (15, {}), {1}: (16, {}), {2}: (17, {}), {3}: (18, {}),... | custom-call | flops 2415919104 | bytes 7864320 | tf_op jit(solution)/shard_map/feed_back/pallas_call | solution.py:242
  169.5 5.6 %feed_grads.1 = f32[8,4,96,768]{3,2,1,0:T(8,128)} custom-call(bf16[512,768]{1,0:T(8,128)(2,1)S(1)} %get-tuple-element.107.low_ref, bf16[512,1536]{1,0:T(8,128)(2,1)S(1)} %copy-done.4, bf16[512,1536]{1,0:T(8,128)(2,1)S(1)} %copy-done.5, bf16[512,768]{1,0:T(8,128)(2,1)S(1)} %get-tuple-element.110.feed_ref), custom_call_target="tpu_custom_call" | custom-call | flops 2415919104 | bytes 9437184 | tf_op jit(solution)/shard_map/feed_grads/pallas_call | solution.py:282
  175.3 1.8 collective-permute-start.6
  180.2 29.1 %collective-permute-done.6.other_ref = f32[512,768]{1,0:T(8,128)} collective-permute-done((f32[512,768]{1,0:T(8,128)}, f32[512,768]{1,0:T(8,128)}, u32[]{:S(2)}, u32[]{:S(2)}) %collective-permute-start.6) | collective-permute-done | bytes 1572896 | tf_op jit(solution)/shard_map/ppermute | solution.py:615
  209.4 5.5 %collective-permute-start.7 = (f32[256,768]{1,0:T(8,128)S(1)}, f32[256,768]{1,0:T(8,128)S(1)}, u32[]{:S(2)}, u32[]{:S(2)}) collective-permute-start(f32[256,768]{1,0:T(8,128)S(1)} %get-tuple-element.89.refs_0_), channel_id=1, source_target_pairs={{0,2},{1,3},{2,0},{3,1},{4,6},{5,7},{6,4},{7,5},{8,10},{9,11},{10,... | collective-permute-start | bytes 2359304 | tf_op jit(solution)/shard_map/ppermute | solution.py:615
  215.6 25.6 %attend_back.1 = (f32[256,768]{1,0:T(8,128)}, f32[256,768]{1,0:T(8,128)}, f32[4,304,768]{2,1,0:T(8,128)}, f32[4,304,768]{2,1,0:T(8,128)}) custom-call(s32[3]{0:T(128)} %pad_add_fusion.1.scalars_ref, s32[2]{0:T(128)} %lengths_ref.3, f32[512,768]{1,0:T(8,128)} %get-tuple-element.88.part_ref, f32[512,768]{1,0:T(8,128)} %collective-permute-done.6.other_ref, ...), custom_call_target="tpu_custom_call" | custom-call | flops 3321888768 | bytes 15728640 | tf_op jit(solution)/shard_map/attend_back/pallas_call | solution.py:425
  241.2 3.9 collective-permute-done.7.refs_1_
  245.2 6.6 %collective-permute-done.10 = f32[4,304,768]{2,1,0:T(8,128)S(1)} collective-permute-done((f32[4,304,768]{2,1,0:T(8,128)}, f32[4,304,768]{2,1,0:T(8,128)S(1)}, u32[]{:S(2)}, u32[]{:S(2)}) %collective-permute-start.10) | collective-permute-done | bytes 3735584 | tf_op jit(solution)/shard_map/ppermute | solution.py:619
  251.8 2.8 add.63
  254.7 1.8 copy-done.23
  258.5 1.6 collective-permute-start.11
  260.1 1.6 collective-permute-start.12
  261.7 3.5 collective-permute-done.14
  266.6 1.8 collective-permute-start.15
  268.4 1.7 collective-permute-start.8
  270.1 11.5 %collective-permute-done.11 = f32[2,152,768]{2,1,0:T(8,128)} collective-permute-done((f32[2,152,768]{2,1,0:T(8,128)}, f32[2,152,768]{2,1,0:T(8,128)}, u32[]{:S(2)}, u32[]{:S(2)}) %collective-permute-start.11) | collective-permute-done | bytes 933920 | tf_op jit(solution)/shard_map/ppermute | solution.py:619
  281.6 1.6 slice_add_fusion
  286.5 28.4 %collective-permute-done.8.refs_3_ = f32[256,768]{1,0:T(8,128)S(1)} collective-permute-done((f32[256,768]{1,0:T(8,128)S(1)}, f32[256,768]{1,0:T(8,128)S(1)}, u32[]{:S(2)}, u32[]{:S(2)}) %collective-permute-start.8) | collective-permute-done | bytes 786464 | tf_op jit(solution)/shard_map/ppermute | solution.py:615
  317.3 1.5 collective-permute-start.18
  318.8 10.1 %collective-permute-done.15 = f32[448,768]{1,0:T(8,128)S(1)} collective-permute-done((f32[448,768]{1,0:T(8,128)S(1)}, f32[448,768]{1,0:T(8,128)S(1)}, u32[]{:S(2)}, u32[]{:S(2)}) %collective-permute-start.15) | collective-permute-done | bytes 1376288 | tf_op jit(solution)/shard_map/ppermute | solution.py:615
  334.2 21.3 %collective-permute-done.16 = f32[152,768]{1,0:T(8,128)S(1)} collective-permute-done((f32[152,768]{1,0:T(8,128)S(1)}, f32[152,768]{1,0:T(8,128)S(1)}, u32[]{:S(2)}, u32[]{:S(2)}) %collective-permute-start.16) | collective-permute-done | bytes 466976 | tf_op jit(solution)/shard_map/ppermute | solution.py:615
  355.6 1.7 collective-permute-start.19
  357.3 1.6 collective-permute-start.20
  358.9 2.3 spread.2
  361.2 6.9 %collective-permute-done.19 = f32[1,72,768]{2,1,0:T(8,128)S(1)} collective-permute-done((f32[1,72,768]{2,1,0:T(8,128)S(1)}, f32[1,72,768]{2,1,0:T(8,128)S(1)}, u32[]{:S(2)}, u32[]{:S(2)}) %collective-permute-start.19) | collective-permute-done | bytes 221216 | tf_op jit(solution)/shard_map/ppermute | solution.py:619
  368.2 2.7 collective-permute-done.20
  370.9 1.5 collective-permute-start.21
  373.0 10.6 %collective-permute-done.21 = f32[2,72,768]{2,1,0:T(8,128)S(1)} collective-permute-done((f32[2,72,768]{2,1,0:T(8,128)S(1)}, f32[2,72,768]{2,1,0:T(8,128)S(1)}, u32[]{:S(2)}, u32[]{:S(2)}) %collective-permute-start.21) | collective-permute-done | bytes 442400 | tf_op jit(solution)/shard_map/ppermute | solution.py:619
  384.2 2.3 copy-done.6
  386.5 2.7 split_blocks.1
  389.2 2.3 collective-permute-done.17.refs_2_
  392.0 4.1 %spread.3 = f32[2,512,768]{2,1,0:T(8,128)} custom-call(s32[2]{0:T(128)S(1)} %pad_add_fusion.scalars_ref.refs_0_, f32[256,768]{1,0:T(8,128)S(1)} %add.67.refs_0_, f32[256,768]{1,0:T(8,128)S(1)} %get-tuple-element.138.refs_1_, f32[2,256,768]{2,1,0:T(8,128)} %collective-permute-done.17.refs_2_), custom_call_target="tpu_custom_call" | custom-call | bytes 6291456 | tf_op jit(solution)/shard_map/spread/pallas_call | solution.py:472
  396.2 2.2 place_grads.1
  (178 shorter events, 39.7 us)
Async XLA Ops:
  7.2 63.3 %all-gather.5.cloned.1.call-start = ((), (), s32[]{:S(2)}) async-start(), calls=%async_computation.1 | async-start | bytes 1327104 | tf_op jit(solution)/shard_map/all_gather | solution.py:626
  8.1 8.0 %collective-permute-start.1 = (f32[24,768]{1,0:T(8,128)S(1)}, f32[24,768]{1,0:T(8,128)S(1)}, u32[]{:S(2)}, u32[]{:S(2)}) collective-permute-start(f32[24,768]{1,0:T(8,128)S(1)} %dynamic-slice_convert_fusion.1), channel_id=1, source_target_pairs={{0,2},{1,3},{2,0},{3,1},{4,6},{5,7},{6,4},{7,5},{8,10},{9,11},{10,... | collective-permute-start | bytes 221192 | tf_op jit(solution)/shard_map/ppermute | solution.py:615
  16.8 72.7 %all-gather.7.cloned.1.call-start = ((), (), s32[]{:S(2)}) async-start(), calls=%async_computation.2 | async-start | bytes 5308416 | tf_op jit(solution)/shard_map/all_gather | solution.py:626
  19.6 27.6 %collective-permute-start.3 = (f32[200,768]{1,0:T(8,128)}, f32[200,768]{1,0:T(8,128)}, u32[]{:S(2)}, u32[]{:S(2)}) collective-permute-start(f32[200,768]{1,0:T(8,128)} %maximum_maximum_fusion), channel_id=1, source_target_pairs={{0,2},{1,3},{2,0},{3,1},{4,6},{5,7},{6,4},{7,5},{8,10},{9,11},{10,... | collective-permute-start | bytes 1843208 | tf_op jit(solution)/shard_map/ppermute | solution.py:615
  34.6 37.0 %copy-start.15 = (bf16[192,512]{1,0:T(8,128)(2,1)}, bf16[192,512]{1,0:T(8,128)(2,1)S(1)}, u32[]{:S(2)}) copy-start(bf16[192,512]{1,0:T(8,128)(2,1)S(1)} %get-tuple-element.70.mixed_ref) | copy-start | bytes 589828
  49.2 166.4 %all-gather.9.cloned.1.call-start = ((), (), s32[]{:S(2)}) async-start(), calls=%async_computation.3 | async-start | bytes 3317760 | tf_op jit(solution)/shard_map/all_gather | solution.py:626
  49.2 21.2 %collective-permute-start = (f32[192,512]{1,0:T(8,128)S(1)}, f32[192,512]{1,0:T(8,128)S(1)}, u32[]{:S(2)}, u32[]{:S(2)}) collective-permute-start(f32[192,512]{1,0:T(8,128)S(1)} %copy-done.20), channel_id=1, source_target_pairs={{0,2},{1,3},{2,0},{3,1},{4,6},{5,7},{6,4},{7,5},{8,10},{9,11},{10,... | collective-permute-start | bytes 1179656 | tf_op jit(solution)/shard_map/ppermute | solution.py:615
  50.6 21.1 %copy-start.35 = (bf16[192,768]{1,0:T(8,128)(2,1)S(1)}, bf16[192,768]{1,0:T(8,128)(2,1)}, u32[]{:S(2)}) copy-start(bf16[192,768]{1,0:T(8,128)(2,1)} %w_out_ref.1) | copy-start | bytes 884740
  71.6 16.9 %copy-start.40 = (f32[768]{0:T(1024)S(1)}, f32[768]{0:T(1024)}, u32[]{:S(2)}) copy-start(f32[768]{0:T(1024)} %param.24) | copy-start | bytes 9220
  71.7 16.9 %copy-start.41 = (f32[768]{0:T(1024)S(1)}, f32[768]{0:T(1024)}, u32[]{:S(2)}) copy-start(f32[768]{0:T(1024)} %param.25) | copy-start | bytes 9220
  71.7 17.0 %copy-start.42 = (f32[768]{0:T(1024)S(1)}, f32[768]{0:T(1024)}, u32[]{:S(2)}) copy-start(f32[768]{0:T(1024)} %param.23) | copy-start | bytes 9220
  72.3 19.9 %copy-start.24 = (f32[512,768]{1,0:T(8,128)}, f32[512,768]{1,0:T(8,128)S(1)}, u32[]{:S(2)}) copy-start(f32[512,768]{1,0:T(8,128)S(1)} %fusion.3.refs_2_) | copy-start | bytes 4718596
  73.5 14.0 %collective-permute-start.9 = (f32[5,24,768]{2,1,0:T(8,128)S(1)}, f32[5,24,768]{2,1,0:T(8,128)S(1)}, u32[]{:S(2)}, u32[]{:S(2)}) collective-permute-start(f32[5,24,768]{2,1,0:T(8,128)S(1)} %dynamic-slice_convert_fusion), channel_id=1, source_target_pairs={{0,2},{1,3},{2,0},{3,1},{4,6},{5,7},{6,4},{7,5},{8,10},{9,11},{10,... | collective-permute-start | bytes 1105928 | tf_op jit(solution)/shard_map/ppermute | solution.py:615
  88.3 177.1 %reduce-scatter.2.cloned.1.call-start = ((), (), s32[]{:S(2)}) async-start(), calls=%async_computation.4 | async-start | bytes 10616832 | tf_op jit(solution)/shard_map/reduce_scatter | solution.py:704
  88.5 33.9 %collective-permute-start.2 = (f32[512,768]{1,0:T(8,128)S(1)}, f32[512,768]{1,0:T(8,128)}, u32[]{:S(2)}, u32[]{:S(2)}) collective-permute-start(f32[512,768]{1,0:T(8,128)S(1)} %fusion.3.refs_2_), channel_id=1, source_target_pairs={{0,1},{1,0},{2,3},{3,2},{4,5},{5,4},{6,7},{7,6},{8,9},{9,8},{10,11... | collective-permute-start | bytes 4718600 | tf_op jit(solution)/shard_map/ppermute | solution.py:615
  88.6 73.5 %copy-start.17 = (f32[1,768]{1,0:T(1,128)}, f32[1,768]{1,0:T(1,128)S(1)}, u32[]{:S(2)}) copy-start(f32[1,768]{1,0:T(1,128)S(1)} %reshape.107.refs_5_.refs_6_.gain_ref) | copy-start | bytes 9220
  92.2 30.2 %copy-start = (bf16[768,768]{1,0:T(8,128)(2,1)S(1)}, bf16[768,768]{1,0:T(8,128)(2,1)}, u32[]{:S(2)}) copy-start(bf16[768,768]{1,0:T(8,128)(2,1)} %refs_11_.3) | copy-start | bytes 3538948
  92.2 30.2 %copy-start.1 = (bf16[768,768]{1,0:T(8,128)(2,1)S(1)}, bf16[768,768]{1,0:T(8,128)(2,1)}, u32[]{:S(2)}) copy-start(bf16[768,768]{1,0:T(8,128)(2,1)} %refs_13_.3) | copy-start | bytes 3538948
  127.6 20.5 %collective-permute-start.5 = (f32[256,768]{1,0:T(8,128)S(1)}, f32[256,768]{1,0:T(8,128)S(1)}, u32[]{:S(2)}, u32[]{:S(2)}) collective-permute-start(f32[256,768]{1,0:T(8,128)S(1)} %get-tuple-element.81.refs_2_), channel_id=1, source_target_pairs={{0,1},{1,0},{2,3},{3,2},{4,5},{5,4},{6,7},{7,6},{8,9},{9,8},{10,11... | collective-permute-start | bytes 2359304 | tf_op jit(solution)/shard_map/ppermute | solution.py:615
  134.7 19.6 %copy-start.8 = (f32[512,1]{1,0:T(8,128)}, f32[512,1]{1,0:T(8,128)S(1)}, u32[]{:S(2)}) copy-start(f32[512,1]{1,0:T(8,128)S(1)} %get-tuple-element.91.scale_ref) | copy-start | bytes 6148
  134.7 27.4 %collective-permute-start.4 = (f32[256,768]{1,0:T(8,128)S(1)}, f32[256,768]{1,0:T(8,128)S(1)}, u32[]{:S(2)}, u32[]{:S(2)}) collective-permute-start(f32[256,768]{1,0:T(8,128)S(1)} %get-tuple-element.78.refs_2_), channel_id=1, source_target_pairs={{0,1},{1,0},{2,3},{3,2},{4,5},{5,4},{6,7},{7,6},{8,9},{9,8},{10,11... | collective-permute-start | bytes 2359304 | tf_op jit(solution)/shard_map/ppermute | solution.py:615
  175.1 209.1 %all-gather.11.cloned.1.call-start = ((), (), s32[]{:S(2)}) async-start(), calls=%async_computation.5 | async-start | bytes 5308416 | tf_op jit(solution)/shard_map/all_gather | solution.py:626
  175.3 34.0 %collective-permute-start.6 = (f32[512,768]{1,0:T(8,128)}, f32[512,768]{1,0:T(8,128)}, u32[]{:S(2)}, u32[]{:S(2)}) collective-permute-start(f32[512,768]{1,0:T(8,128)} %get-tuple-element.88.part_ref), channel_id=1, source_target_pairs={{0,1},{1,0},{2,3},{3,2},{4,5},{5,4},{6,7},{7,6},{8,9},{9,8},{10,11... | collective-permute-start | bytes 4718600 | tf_op jit(solution)/shard_map/ppermute | solution.py:615
  209.4 35.7 %collective-permute-start.7 = (f32[256,768]{1,0:T(8,128)S(1)}, f32[256,768]{1,0:T(8,128)S(1)}, u32[]{:S(2)}, u32[]{:S(2)}) collective-permute-start(f32[256,768]{1,0:T(8,128)S(1)} %get-tuple-element.89.refs_0_), channel_id=1, source_target_pairs={{0,2},{1,3},{2,0},{3,1},{4,6},{5,7},{6,4},{7,5},{8,10},{9,11},{10,... | collective-permute-start | bytes 2359304 | tf_op jit(solution)/shard_map/ppermute | solution.py:615
  245.0 23.3 %copy-start.11 = (f32[256,768]{1,0:T(8,128)}, f32[256,768]{1,0:T(8,128)S(1)}, u32[]{:S(2)}) copy-start(f32[256,768]{1,0:T(8,128)S(1)} %collective-permute-done.7.refs_1_) | copy-start | bytes 2359300
  245.1 6.7 %collective-permute-start.10 = (f32[4,304,768]{2,1,0:T(8,128)}, f32[4,304,768]{2,1,0:T(8,128)S(1)}, u32[]{:S(2)}, u32[]{:S(2)}) collective-permute-start(f32[4,304,768]{2,1,0:T(8,128)} %get-tuple-element.101), channel_id=1, source_target_pairs={{0,4},{4,0},{8,12},{12,8},{16,20},{20,16},{24,28},{28,24},{1,5},{5... | collective-permute-start | bytes 11206664 | tf_op jit(solution)/shard_map/ppermute | solution.py:619
  245.1 20.2 %collective-permute-start.14 = (f32[256,768]{1,0:T(8,128)}, f32[256,768]{1,0:T(8,128)S(1)}, u32[]{:S(2)}, u32[]{:S(2)}) collective-permute-start(f32[256,768]{1,0:T(8,128)} %get-tuple-element.106), channel_id=1, source_target_pairs={{0,1},{1,0},{2,3},{3,2},{4,5},{5,4},{6,7},{7,6},{8,9},{9,8},{10,11... | collective-permute-start | bytes 2359304 | tf_op jit(solution)/shard_map/ppermute | solution.py:615
  258.5 23.1 %collective-permute-start.11 = (f32[2,152,768]{2,1,0:T(8,128)}, f32[2,152,768]{2,1,0:T(8,128)}, u32[]{:S(2)}, u32[]{:S(2)}) collective-permute-start(f32[2,152,768]{2,1,0:T(8,128)} %slice.137), channel_id=1, source_target_pairs={{0,16},{4,20},{8,24},{12,28},{16,0},{20,4},{24,8},{28,12},{1,17},{... | collective-permute-start | bytes 2801672 | tf_op jit(solution)/shard_map/ppermute | solution.py:619
  260.1 24.2 %collective-permute-start.12 = (f32[2,152,768]{2,1,0:T(8,128)}, f32[2,152,768]{2,1,0:T(8,128)}, u32[]{:S(2)}, u32[]{:S(2)}) collective-permute-start(f32[2,152,768]{2,1,0:T(8,128)} %slice_bitcast_fusion.1), channel_id=1, source_target_pairs={{0,8},{4,12},{8,0},{12,4},{16,24},{20,28},{24,16},{28,20},{1,9},{5... | collective-permute-start | bytes 2801672 | tf_op jit(solution)/shard_map/ppermute | solution.py:619
  266.5 17.7 %copy-start.26 = (f32[4,152,768]{2,1,0:T(8,128)S(1)}, f32[4,152,768]{2,1,0:T(8,128)}, u32[]{:S(2)}) copy-start(f32[4,152,768]{2,1,0:T(8,128)} %copy-done.25) | copy-start | bytes 5603332
  266.6 62.4 %collective-permute-start.15 = (f32[448,768]{1,0:T(8,128)S(1)}, f32[448,768]{1,0:T(8,128)S(1)}, u32[]{:S(2)}, u32[]{:S(2)}) collective-permute-start(f32[448,768]{1,0:T(8,128)S(1)} %pad_maximum_fusion.2), channel_id=1, source_target_pairs={{0,2},{1,3},{2,0},{3,1},{4,6},{5,7},{6,4},{7,5},{8,10},{9,11},{10,... | collective-permute-start | bytes 4128776 | tf_op jit(solution)/shard_map/ppermute | solution.py:615
  268.4 46.5 %collective-permute-start.8 = (f32[256,768]{1,0:T(8,128)S(1)}, f32[256,768]{1,0:T(8,128)S(1)}, u32[]{:S(2)}, u32[]{:S(2)}) collective-permute-start(f32[256,768]{1,0:T(8,128)S(1)} %collective-permute-done.7.refs_1_), channel_id=1, source_target_pairs={{0,1},{1,0},{2,3},{3,2},{4,5},{5,4},{6,7},{7,6},{8,9},{9,8},{10,11... | collective-permute-start | bytes 2359304 | tf_op jit(solution)/shard_map/ppermute | solution.py:615
  284.3 45.7 %copy-start.31 = (f32[384,768]{1,0:T(8,128)S(1)}, f32[384,768]{1,0:T(8,128)}, u32[]{:S(2)}) copy-start(f32[384,768]{1,0:T(8,128)} %reduce-scatter.2.cloned.1.call-done) | copy-start | bytes 3538948
  285.7 29.3 %copy-start.27 = (f32[1,2,152,768]{3,2,1,0:T(8,128)}, f32[1,2,152,768]{3,2,1,0:T(8,128)S(1)}, u32[]{:S(2)}) copy-start(f32[1,2,152,768]{3,2,1,0:T(8,128)S(1)} %fusion.1) | copy-start | bytes 2801668
  315.8 15.1 %collective-permute-start.13 = (f32[1,152,768]{2,1,0:T(8,128)}, f32[1,152,768]{2,1,0:T(8,128)S(1)}, u32[]{:S(2)}, u32[]{:S(2)}) collective-permute-start(f32[1,152,768]{2,1,0:T(8,128)} %slice.141), channel_id=1, source_target_pairs={{0,8},{4,12},{8,0},{12,4},{16,24},{20,28},{24,16},{28,20},{1,9},{5... | collective-permute-start | bytes 1400840 | tf_op jit(solution)/shard_map/ppermute | solution.py:619
  317.3 13.6 %collective-permute-start.18 = (f32[1,152,768]{2,1,0:T(8,128)}, f32[1,152,768]{2,1,0:T(8,128)S(1)}, u32[]{:S(2)}, u32[]{:S(2)}) collective-permute-start(f32[1,152,768]{2,1,0:T(8,128)} %slice_bitcast_fusion.3), channel_id=1, source_target_pairs={{0,16},{4,20},{8,24},{12,28},{16,0},{20,4},{24,8},{28,12},{1,17},{... | collective-permute-start | bytes 1400840 | tf_op jit(solution)/shard_map/ppermute | solution.py:619
  332.2 23.3 %collective-permute-start.16 = (f32[152,768]{1,0:T(8,128)S(1)}, f32[152,768]{1,0:T(8,128)S(1)}, u32[]{:S(2)}, u32[]{:S(2)}) collective-permute-start(f32[152,768]{1,0:T(8,128)S(1)} %fusion.10), channel_id=1, source_target_pairs={{0,2},{1,3},{2,0},{3,1},{4,6},{5,7},{6,4},{7,5},{8,10},{9,11},{10,... | collective-permute-start | bytes 1400840 | tf_op jit(solution)/shard_map/ppermute | solution.py:615
  332.9 22.6 %copy-start.28 = (f32[1,2,152,768]{3,2,1,0:T(8,128)S(1)}, f32[1,2,152,768]{3,2,1,0:T(8,128)}, u32[]{:S(2)}) copy-start(f32[1,2,152,768]{3,2,1,0:T(8,128)} %copy-done.27) | copy-start | bytes 2801668
  332.9 22.6 %copy-start.38 = (f32[1,152,768]{2,1,0:T(8,128)S(1)}, f32[1,152,768]{2,1,0:T(8,128)}, u32[]{:S(2)}) copy-start(f32[1,152,768]{2,1,0:T(8,128)} %copy-done.37) | copy-start | bytes 1400836
  334.2 24.7 %copy-start.12 = (f32[256,768]{1,0:T(8,128)S(1)}, f32[256,768]{1,0:T(8,128)}, u32[]{:S(2)}) copy-start(f32[256,768]{1,0:T(8,128)} %copy-done.11) | copy-start | bytes 2359300
  334.2 24.7 %copy-start.14 = (f32[256,768]{1,0:T(8,128)S(1)}, f32[256,768]{1,0:T(8,128)}, u32[]{:S(2)}) copy-start(f32[256,768]{1,0:T(8,128)} %copy-done.13) | copy-start | bytes 2359300
  355.5 36.0 %collective-permute-start.17 = (f32[2,256,768]{2,1,0:T(8,128)}, f32[2,256,768]{2,1,0:T(8,128)}, u32[]{:S(2)}, u32[]{:S(2)}) collective-permute-start(f32[2,256,768]{2,1,0:T(8,128)} %pad_maximum_fusion), channel_id=1, source_target_pairs={{0,1},{1,0},{2,3},{3,2},{4,5},{5,4},{6,7},{7,6},{8,9},{9,8},{10,11... | collective-permute-start | bytes 4718600 | tf_op jit(solution)/shard_map/ppermute | solution.py:615
  355.6 12.5 %collective-permute-start.19 = (f32[1,72,768]{2,1,0:T(8,128)S(1)}, f32[1,72,768]{2,1,0:T(8,128)S(1)}, u32[]{:S(2)}, u32[]{:S(2)}) collective-permute-start(f32[1,72,768]{2,1,0:T(8,128)S(1)} %slice_bitcast_fusion.5), channel_id=1, source_target_pairs={{0,8},{4,12},{8,0},{12,4},{16,24},{20,28},{24,16},{28,20},{1,9},{5... | collective-permute-start | bytes 663560 | tf_op jit(solution)/shard_map/ppermute | solution.py:619
  357.3 13.5 %collective-permute-start.20 = (f32[1,80,768]{2,1,0:T(8,128)S(1)}, f32[1,80,768]{2,1,0:T(8,128)S(1)}, u32[]{:S(2)}, u32[]{:S(2)}) collective-permute-start(f32[1,80,768]{2,1,0:T(8,128)S(1)} %slice_bitcast_fusion.4), channel_id=1, source_target_pairs={{0,16},{4,20},{8,24},{12,28},{16,0},{20,4},{24,8},{28,12},{1,17},{... | collective-permute-start | bytes 737288 | tf_op jit(solution)/shard_map/ppermute | solution.py:619
  370.9 12.6 %collective-permute-start.21 = (f32[2,72,768]{2,1,0:T(8,128)S(1)}, f32[2,72,768]{2,1,0:T(8,128)S(1)}, u32[]{:S(2)}, u32[]{:S(2)}) collective-permute-start(f32[2,72,768]{2,1,0:T(8,128)S(1)} %pad_maximum_fusion.6), channel_id=1, source_target_pairs={{0,16},{4,20},{8,24},{12,28},{16,0},{20,4},{24,8},{28,12},{1,17},{... | collective-permute-start | bytes 1327112 | tf_op jit(solution)/shard_map/ppermute | solution.py:619
  372.4 11.6 %collective-permute-start.22 = (f32[2,80,768]{2,1,0:T(8,128)S(1)}, f32[2,80,768]{2,1,0:T(8,128)S(1)}, u32[]{:S(2)}, u32[]{:S(2)}) collective-permute-start(f32[2,80,768]{2,1,0:T(8,128)S(1)} %pad_maximum_fusion.5), channel_id=1, source_target_pairs={{0,8},{4,12},{8,0},{12,4},{16,24},{20,28},{24,16},{28,20},{1,9},{5... | collective-permute-start | bytes 1474568 | tf_op jit(solution)/shard_map/ppermute | solution.py:619
  391.5 4.7 %collective-permute-start.24 = (f32[4,80,768]{2,1,0:T(8,128)S(1)}, f32[4,80,768]{2,1,0:T(8,128)S(1)}, u32[]{:S(2)}, u32[]{:S(2)}) collective-permute-start(f32[4,80,768]{2,1,0:T(8,128)S(1)} %pad_maximum_fusion.3.low_b_ref), channel_id=1, source_target_pairs={{0,4},{4,0},{8,12},{12,8},{16,20},{20,16},{24,28},{28,24},{1,5},{5... | collective-permute-start | bytes 2949128 | tf_op jit(solution)/shard_map/ppermute | solution.py:619
  391.5 4.7 %collective-permute-start.23 = (f32[4,72,768]{2,1,0:T(8,128)S(1)}, f32[4,72,768]{2,1,0:T(8,128)S(1)}, u32[]{:S(2)}, u32[]{:S(2)}) collective-permute-start(f32[4,72,768]{2,1,0:T(8,128)S(1)} %pad_maximum_fusion.4.low_a_ref), channel_id=1, source_target_pairs={{0,4},{4,0},{8,12},{12,8},{16,20},{20,16},{24,28},{28,24},{1,5},{5... | collective-permute-start | bytes 2654216 | tf_op jit(solution)/shard_map/ppermute | solution.py:619
  (29 other events, 139.3 us)
Sparse Core Ops, SparseCore 0:
  16.9 25.2 all-gather.4
  49.3 40.0 all-gather.6
  91.3 31.4 all-gather.8
  175.2 78.8 reduce-scatter.1
  331.0 46.1 all-gather.10

commit v9 on v8

--- a/solution.py
+++ b/solution.py
@@ -654,18 +654,18 @@
     far_rows = after(far_rows, mixed_send)
     count = unit_rows.shape[0]
     b_in_two = jnp.stack([b_in, far_rows[count]])
-    blocks = arrived(gather(far_rows[:count])).reshape(dp_size, count, -1)
+    blocks = arrived(gather(far_rows)).reshape(dp_size, count + 8, -1)
     in_rows = width // dp_size
     w_in_far = blocks[:, :in_rows].reshape(width, units).astype(bf16)
-    w_back_far = blocks[:, in_rows:].reshape(units, width).astype(bf16)
+    w_back_far = blocks[:, in_rows:count].reshape(units, width).astype(bf16)
 
     mixed_far = arrived(mixed_far).astype(bf16)
     part = mm_tn(jnp.concatenate([mixed, mixed_far], axis=0), jnp.concatenate([w_out, w_out_far], axis=0))
     other = swap(part, NEAR)
     head_rows = jnp.concatenate([w_qkv, w_pos], axis=0)
     count = columns // dp_size
-    head_rows = lax.dynamic_slice_in_dim(after(head_rows, part), group * count, count, 1)
-    blocks = gather(swap(head_rows.astype(f32), FAR).reshape(-1, width))
+    head_rows = lax.dynamic_slice_in_dim(head_rows, group * count, count, 1).astype(f32)
+    blocks = gather(swap(after(head_rows, part), FAR).reshape(-1, width))
     blocks = blocks.reshape(1, dp_size, 5, count, width)
 
     rows_f32 = jax.ShapeDtypeStruct((length, width), f32)

time: 406 us -> 402 us (level)
  waiting for transfers between devices: 237 us -> 226 us
  starting transfers between devices: 31.9 us -> 42.8 us
    ppermute x14, waiting for transfers between devices: 199 us -> 178 us  [swap(): return lax.ppermute(value, MP, pairs)]
    ppermute x14, starting transfers between devices: 19.3 us -> 30.7 us  [swap(): return lax.ppermute(value, MP, pairs)]
    all_gather x4, waiting for transfers between devices: 0.06 us -> 8.73 us  [gather(): return lax.all_gather(value, 'dp', axis=0, tiled=True)]
  transfers between devices with their start and end apart: 30 -> 30, of which waited for: 20 -> 21; matrix products, arithmetic and copies ran while one was open for 8% -> 7% of each run, Pallas kernels for 18% -> 18%
where the time goes in v9:
time: 402 us; the launch traced here: 401 us
  waiting for transfers between devices  226 us (56%)
  Pallas kernels  75.4 us (19%)
  starting transfers between devices  42.8 us (11%)
  local copies, waits for them, and re-layouts  24.8 us (6%)
  other arithmetic  17.6 us (4%)
  between operations  14.3 us (4%)
    ppermute x14, waiting for transfers between devices, swap(): return lax.ppermute(value, MP, pairs)  178 us
    ppermute x11, waiting for transfers between devices, group_swap(): return lax.ppermute(value, 'dp', pairs)  38.9 us
    ppermute x14, starting transfers between devices, swap(): return lax.ppermute(value, MP, pairs)  30.7 us
    pallas_call x1, Pallas kernels, attend_back(): pl.pallas_call(partial(attend_back_kernel, heads, count), out_shape=shape...  25.7 us
    pallas_call x4, Pallas kernels, on_chunk(): pl.pallas_call(without(kernel, inputs, len(before)), out_shape=shapes, gr...  22.8 us
    unnamed x92, local copies, waits for them, and re-layouts  12.2 us
    ppermute x11, starting transfers between devices, group_swap(): return lax.ppermute(value, 'dp', pairs)  11.5 us
    pallas_call x1, Pallas kernels, attend(): pl.pallas_call(partial(attend_kernel, columns // HEAD_DIM), out_shape=sha...  9.98 us
  transfers between devices with their start and end apart: 30, of which 21 were waited for; matrix products, arithmetic and copies ran while one was open for 7% of the time, Pallas kernels for 18%

profile of v9, /device:TPU:0, one launch (start us, length us, event | category | flops | bytes accessed | tf_op | source)
XLA Modules:
  0.0 401.1 jit_solution(6920643785480786349)
XLA Ops:
  8.1 4.1 %collective-permute-start.1 = (f32[24,768]{1,0:T(8,128)S(1)}, f32[24,768]{1,0:T(8,128)S(1)}, u32[]{:S(2)}, u32[]{:S(2)}) collective-permute-start(f32[24,768]{1,0:T(8,128)S(1)} %dynamic-slice_convert_fusion), channel_id=1, source_target_pairs={{0,2},{1,3},{2,0},{3,1},{4,6},{5,7},{6,4},{7,5},{8,10},{9,11},{10,... | collective-permute-start | bytes 221192 | tf_op jit(solution)/shard_map/ppermute | solution.py:615
  12.2 3.9 collective-permute-done.1
  22.0 10.0 %attend.1 = (f32[192,512]{1,0:T(8,128)S(1)}, bf16[192,512]{1,0:T(8,128)(2,1)S(1)}, bf16[5,192,512]{2,1,0:T(8,128)(2,1)S(1)}, bf16[512,768]{1,0:T(8,128)(2,1)S(1)}) custom-call(s32[2]{0:T(128)S(1)} %pad_add_fusion.scalars_ref.refs_0_, s32[2]{0:T(128)S(1)} %copy-done.18, bf16[2,512,768]{2,1,0:T(8,128)(2,1)S(1)} %copy-done.2, s32[2,2,512]{2,1,0:T(2,128)S(1)} %copy-done.20, ...), custom_call_target="tpu_custom_call" | custom-call | flops 2315255808 | bytes 5898240 | tf_op jit(solution)/shard_map/attend/pallas_call | solution.py:130
  34.6 12.6 %collective-permute-done.3 = f32[200,768]{1,0:T(8,128)} collective-permute-done((f32[200,768]{1,0:T(8,128)}, f32[200,768]{1,0:T(8,128)}, u32[]{:S(2)}, u32[]{:S(2)}) %collective-permute-start.3) | collective-permute-done | bytes 614432 | tf_op jit(solution)/shard_map/ppermute | solution.py:615
  48.1 8.1 %collective-permute-done = f32[192,512]{1,0:T(8,128)S(1)} collective-permute-done((f32[192,512]{1,0:T(8,128)}, f32[192,512]{1,0:T(8,128)S(1)}, u32[]{:S(2)}, u32[]{:S(2)}) %collective-permute-start) | collective-permute-done | bytes 393248 | tf_op jit(solution)/shard_map/ppermute | solution.py:615
  58.6 15.0 %collective-permute-done.9 = f32[5,24,768]{2,1,0:T(8,128)S(1)} collective-permute-done((f32[5,24,768]{2,1,0:T(8,128)S(1)}, f32[5,24,768]{2,1,0:T(8,128)S(1)}, u32[]{:S(2)}, u32[]{:S(2)}) %collective-permute-start.9) | collective-permute-done | bytes 368672 | tf_op jit(solution)/shard_map/ppermute | solution.py:615
  74.7 12.5 %collective-permute-start.2 = (f32[512,768]{1,0:T(8,128)S(1)}, f32[512,768]{1,0:T(8,128)}, u32[]{:S(2)}, u32[]{:S(2)}) collective-permute-start(f32[512,768]{1,0:T(8,128)S(1)} %fusion.3.refs_2_), channel_id=1, source_target_pairs={{0,1},{1,0},{2,3},{3,2},{4,5},{5,4},{6,7},{7,6},{8,9},{9,8},{10,11... | collective-permute-start | bytes 4718600 | tf_op jit(solution)/shard_map/ppermute | solution.py:615
  88.0 8.7 %all-gather.7.cloned.1.call-done = f32[1600,768]{1,0:T(8,128)} async-done(((f32[200,768]{1,0:T(8,128)}), f32[1600,768]{1,0:T(8,128)}) %all-gather.7.cloned.1.call-update) | async-done | bytes 4915216 | tf_op jit(solution)/shard_map/all_gather | solution.py:626
  96.7 2.8 multiply_convert_fusion
  100.7 19.9 %collective-permute-done.2.refs_3_ = f32[512,768]{1,0:T(8,128)} collective-permute-done((f32[512,768]{1,0:T(8,128)S(1)}, f32[512,768]{1,0:T(8,128)}, u32[]{:S(2)}, u32[]{:S(2)}) %collective-permute-start.2) | collective-permute-done | bytes 1572896 | tf_op jit(solution)/shard_map/ppermute | solution.py:615
  120.6 5.2 %feed.2 = (f32[512,768]{1,0:T(8,128)}, f32[512,1]{1,0:T(8,128)S(1)}, bf16[512,768]{1,0:T(8,128)(2,1)S(1)}, bf16[512,1536]{1,0:T(8,128)(2,1)}, f32[512,1536]{1,0:T(8,128)}, /*index=5*/f32[256,768]{1,0:T(8,128)S(1)}) custom-call(s32[2]{0:T(128)S(1)} %pad_add_fusion.scalars_ref.refs_0_, bf16[2,512,768]{2,1,0:T(8,128)(2,1)} %refs_1_.5, f32[512,768]{1,0:T(8,128)} %copy-done.23, ...), custom_call_target="tpu_custom_call" | custom-call | flops 2415919104 | bytes 7864320 | tf_op jit(solution)/shard_map/feed/pallas_call | solution.py:242
  125.7 1.7 collective-permute-start.5
  127.5 5.4 %feed.3 = (f32[512,768]{1,0:T(8,128)}, f32[512,1]{1,0:T(8,128)S(1)}, bf16[512,768]{1,0:T(8,128)(2,1)S(1)}, bf16[512,1536]{1,0:T(8,128)(2,1)}, f32[512,1536]{1,0:T(8,128)}, /*index=5*/f32[256,768]{1,0:T(8,128)S(1)}) custom-call(s32[2]{0:T(128)S(1)} %pad_add_fusion.scalars_ref.refs_0_, ...), custom_call_target="tpu_custom_call", output_to_operand_aliasing={{0}: (12, {}), {1}: (13, {}), {2}: (14, {}), {3}: (15, {}),... | custom-call | flops 2415919104 | bytes 7864320 | tf_op jit(solution)/shard_map/feed/pallas_call | solution.py:242
  133.3 12.9 %collective-permute-done.5.refs_3_ = f32[256,768]{1,0:T(8,128)S(1)} collective-permute-done((f32[256,768]{1,0:T(8,128)S(1)}, f32[256,768]{1,0:T(8,128)S(1)}, u32[]{:S(2)}, u32[]{:S(2)}) %collective-permute-start.5) | collective-permute-done | bytes 786464 | tf_op jit(solution)/shard_map/ppermute | solution.py:615
  146.2 6.3 %feed_back.2 = (f32[512,768]{1,0:T(8,128)}, f32[512,768]{1,0:T(8,128)}, bf16[512,768]{1,0:T(8,128)(2,1)S(1)}, bf16[512,1536]{1,0:T(8,128)(2,1)}, f32[512,768]{1,...) custom-call(s32[2]{0:T(128)S(1)} %pad_add_fusion.scalars_ref.refs_0_, bf16[2,512,768]{2,1,0:T(8,128)(2,1)} %refs_1_.7, ...), custom_call_target="tpu_custom_call" | custom-call | flops 2415919104 | bytes 7864320 | tf_op jit(solution)/shard_map/feed_back/pallas_call | solution.py:242
  152.5 7.6 %collective-permute-done.4.refs_3_ = f32[256,768]{1,0:T(8,128)S(1)} collective-permute-done((f32[256,768]{1,0:T(8,128)S(1)}, f32[256,768]{1,0:T(8,128)S(1)}, u32[]{:S(2)}, u32[]{:S(2)}) %collective-permute-start.4) | collective-permute-done | bytes 786464 | tf_op jit(solution)/shard_map/ppermute | solution.py:615
  160.1 5.9 %feed_back.3 = (f32[512,768]{1,0:T(8,128)}, f32[512,768]{1,0:T(8,128)}, bf16[512,768]{1,0:T(8,128)(2,1)S(1)}, bf16[512,1536]{1,0:T(8,128)(2,1)}, f32[512,768]{1,...) custom-call(s32[2]{0:T(128)S(1)} %pad_add_fusion.scalars_ref.refs_0_, ...), custom_call_target="tpu_custom_call", output_to_operand_aliasing={{0}: (15, {}), {1}: (16, {}), {2}: (17, {}), {3}: (18, {}),... | custom-call | flops 2415919104 | bytes 7864320 | tf_op jit(solution)/shard_map/feed_back/pallas_call | solution.py:242
  167.4 5.6 %feed_grads.1 = f32[8,4,96,768]{3,2,1,0:T(8,128)} custom-call(bf16[512,768]{1,0:T(8,128)(2,1)S(1)} %get-tuple-element.107.low_ref, bf16[512,1536]{1,0:T(8,128)(2,1)S(1)} %copy-done.4, bf16[512,1536]{1,0:T(8,128)(2,1)S(1)} %copy-done.5, bf16[512,768]{1,0:T(8,128)(2,1)S(1)} %get-tuple-element.110.feed_ref), custom_call_target="tpu_custom_call" | custom-call | flops 2415919104 | bytes 9437184 | tf_op jit(solution)/shard_map/feed_grads/pallas_call | solution.py:282
  173.3 1.7 collective-permute-start.6
  176.6 1.5 constant_dynamic-slice_fusion
  178.1 29.0 %collective-permute-done.6.other_ref = f32[512,768]{1,0:T(8,128)} collective-permute-done((f32[512,768]{1,0:T(8,128)}, f32[512,768]{1,0:T(8,128)}, u32[]{:S(2)}, u32[]{:S(2)}) %collective-permute-start.6) | collective-permute-done | bytes 1572896 | tf_op jit(solution)/shard_map/ppermute | solution.py:615
  207.1 4.1 %collective-permute-start.7 = (f32[256,768]{1,0:T(8,128)S(1)}, f32[256,768]{1,0:T(8,128)S(1)}, u32[]{:S(2)}, u32[]{:S(2)}) collective-permute-start(f32[256,768]{1,0:T(8,128)S(1)} %get-tuple-element.89.refs_0_), channel_id=1, source_target_pairs={{0,2},{1,3},{2,0},{3,1},{4,6},{5,7},{6,4},{7,5},{8,10},{9,11},{10,... | collective-permute-start | bytes 2359304 | tf_op jit(solution)/shard_map/ppermute | solution.py:615
  211.9 25.7 %attend_back.1 = (f32[256,768]{1,0:T(8,128)}, f32[256,768]{1,0:T(8,128)}, f32[4,304,768]{2,1,0:T(8,128)}, f32[4,304,768]{2,1,0:T(8,128)}) custom-call(s32[3]{0:T(128)} %pad_add_fusion.1.scalars_ref, s32[2]{0:T(128)} %lengths_ref.3, f32[512,768]{1,0:T(8,128)} %get-tuple-element.88.part_ref, f32[512,768]{1,0:T(8,128)} %collective-permute-done.6.other_ref, ...), custom_call_target="tpu_custom_call" | custom-call | flops 3321888768 | bytes 15728640 | tf_op jit(solution)/shard_map/attend_back/pallas_call | solution.py:425
  237.6 3.1 collective-permute-done.7.refs_1_
  240.9 6.5 %collective-permute-done.10 = f32[4,304,768]{2,1,0:T(8,128)S(1)} collective-permute-done((f32[4,304,768]{2,1,0:T(8,128)}, f32[4,304,768]{2,1,0:T(8,128)S(1)}, u32[]{:S(2)}, u32[]{:S(2)}) %collective-permute-start.10) | collective-permute-done | bytes 3735584 | tf_op jit(solution)/shard_map/ppermute | solution.py:619
  247.5 2.8 add.63
  250.4 1.8 copy-done.22
  254.2 1.6 collective-permute-start.11
  257.2 3.7 collective-permute-done.14
  262.2 1.9 collective-permute-start.15
  264.1 1.7 collective-permute-start.8
  265.9 11.4 %collective-permute-done.11 = f32[2,152,768]{2,1,0:T(8,128)} collective-permute-done((f32[2,152,768]{2,1,0:T(8,128)}, f32[2,152,768]{2,1,0:T(8,128)}, u32[]{:S(2)}, u32[]{:S(2)}) %collective-permute-start.11) | collective-permute-done | bytes 933920 | tf_op jit(solution)/shard_map/ppermute | solution.py:619
  277.3 1.6 slice_add_fusion
  282.2 28.4 %collective-permute-done.8.refs_3_ = f32[256,768]{1,0:T(8,128)S(1)} collective-permute-done((f32[256,768]{1,0:T(8,128)S(1)}, f32[256,768]{1,0:T(8,128)S(1)}, u32[]{:S(2)}, u32[]{:S(2)}) %collective-permute-start.8) | collective-permute-done | bytes 786464 | tf_op jit(solution)/shard_map/ppermute | solution.py:615
  311.5 1.5 collective-permute-start.13
  313.0 1.5 collective-permute-start.18
  314.5 10.1 %collective-permute-done.15 = f32[448,768]{1,0:T(8,128)S(1)} collective-permute-done((f32[448,768]{1,0:T(8,128)S(1)}, f32[448,768]{1,0:T(8,128)S(1)}, u32[]{:S(2)}, u32[]{:S(2)}) %collective-permute-start.15) | collective-permute-done | bytes 1376288 | tf_op jit(solution)/shard_map/ppermute | solution.py:615
  329.9 21.3 %collective-permute-done.16 = f32[152,768]{1,0:T(8,128)S(1)} collective-permute-done((f32[152,768]{1,0:T(8,128)S(1)}, f32[152,768]{1,0:T(8,128)S(1)}, u32[]{:S(2)}, u32[]{:S(2)}) %collective-permute-start.16) | collective-permute-done | bytes 466976 | tf_op jit(solution)/shard_map/ppermute | solution.py:615
  351.3 1.9 collective-permute-start.19
  354.5 2.3 spread.2
  356.8 7.2 %collective-permute-done.19 = f32[1,72,768]{2,1,0:T(8,128)S(1)} collective-permute-done((f32[1,72,768]{2,1,0:T(8,128)S(1)}, f32[1,72,768]{2,1,0:T(8,128)S(1)}, u32[]{:S(2)}, u32[]{:S(2)}) %collective-permute-start.19) | collective-permute-done | bytes 221216 | tf_op jit(solution)/shard_map/ppermute | solution.py:619
  364.0 2.8 collective-permute-done.20
  368.8 10.4 %collective-permute-done.21 = f32[2,72,768]{2,1,0:T(8,128)S(1)} collective-permute-done((f32[2,72,768]{2,1,0:T(8,128)S(1)}, f32[2,72,768]{2,1,0:T(8,128)S(1)}, u32[]{:S(2)}, u32[]{:S(2)}) %collective-permute-start.21) | collective-permute-done | bytes 442400 | tf_op jit(solution)/shard_map/ppermute | solution.py:619
  379.8 2.3 copy-done.6
  382.2 2.7 split_blocks.1
  384.9 2.2 collective-permute-done.17.refs_2_
  387.6 4.1 %spread.3 = f32[2,512,768]{2,1,0:T(8,128)} custom-call(s32[2]{0:T(128)S(1)} %pad_add_fusion.scalars_ref.refs_0_, f32[256,768]{1,0:T(8,128)S(1)} %add.67.refs_0_, f32[256,768]{1,0:T(8,128)S(1)} %get-tuple-element.138.refs_1_, f32[2,256,768]{2,1,0:T(8,128)} %collective-permute-done.17.refs_2_), custom_call_target="tpu_custom_call" | custom-call | bytes 6291456 | tf_op jit(solution)/shard_map/spread/pallas_call | solution.py:472
  391.8 2.2 place_grads.1
  (176 shorter events, 39.4 us)
Async XLA Ops:
  7.2 49.1 %all-gather.5.cloned.1.call-start = ((), (), s32[]{:S(2)}) async-start(), calls=%async_computation.1 | async-start | bytes 1327104 | tf_op jit(solution)/shard_map/all_gather | solution.py:626
  8.1 8.0 %collective-permute-start.1 = (f32[24,768]{1,0:T(8,128)S(1)}, f32[24,768]{1,0:T(8,128)S(1)}, u32[]{:S(2)}, u32[]{:S(2)}) collective-permute-start(f32[24,768]{1,0:T(8,128)S(1)} %dynamic-slice_convert_fusion), channel_id=1, source_target_pairs={{0,2},{1,3},{2,0},{3,1},{4,6},{5,7},{6,4},{7,5},{8,10},{9,11},{10,... | collective-permute-start | bytes 221192 | tf_op jit(solution)/shard_map/ppermute | solution.py:615
  16.8 79.9 %all-gather.7.cloned.1.call-start = ((), (), s32[]{:S(2)}) async-start(), calls=%async_computation.2 | async-start | bytes 5529600 | tf_op jit(solution)/shard_map/all_gather | solution.py:626
  19.6 27.6 %collective-permute-start.3 = (f32[200,768]{1,0:T(8,128)}, f32[200,768]{1,0:T(8,128)}, u32[]{:S(2)}, u32[]{:S(2)}) collective-permute-start(f32[200,768]{1,0:T(8,128)} %maximum_maximum_fusion), channel_id=1, source_target_pairs={{0,2},{1,3},{2,0},{3,1},{4,6},{5,7},{6,4},{7,5},{8,10},{9,11},{10,... | collective-permute-start | bytes 1843208 | tf_op jit(solution)/shard_map/ppermute | solution.py:615
  34.6 22.9 %copy-start.15 = (bf16[192,512]{1,0:T(8,128)(2,1)}, bf16[192,512]{1,0:T(8,128)(2,1)S(1)}, u32[]{:S(2)}) copy-start(bf16[192,512]{1,0:T(8,128)(2,1)S(1)} %get-tuple-element.70.mixed_ref) | copy-start | bytes 589828
  47.2 164.7 %all-gather.9.cloned.1.call-start = ((), (), s32[]{:S(2)}) async-start(), calls=%async_computation.3 | async-start | bytes 3317760 | tf_op jit(solution)/shard_map/all_gather | solution.py:626
  47.2 9.0 %collective-permute-start = (f32[192,512]{1,0:T(8,128)}, f32[192,512]{1,0:T(8,128)S(1)}, u32[]{:S(2)}, u32[]{:S(2)}) collective-permute-start(f32[192,512]{1,0:T(8,128)} %copy-done.19), channel_id=1, source_target_pairs={{0,2},{1,3},{2,0},{3,1},{4,6},{5,7},{6,4},{7,5},{8,10},{9,11},{10,... | collective-permute-start | bytes 1179656 | tf_op jit(solution)/shard_map/ppermute | solution.py:615
  57.5 42.0 %copy-start.29 = (bf16[8,24,768]{2,1,0:T(8,128)(2,1)}, bf16[8,24,768]{2,1,0:T(8,128)(2,1)S(1)}, u32[]{:S(2)}) copy-start(bf16[8,24,768]{2,1,0:T(8,128)(2,1)S(1)} %fusion.2) | copy-start | bytes 884740
  57.5 29.7 %copy-start.40 = (f32[768]{0:T(1024)S(1)}, f32[768]{0:T(1024)}, u32[]{:S(2)}) copy-start(f32[768]{0:T(1024)} %param.24) | copy-start | bytes 9220
  57.5 29.7 %copy-start.41 = (f32[768]{0:T(1024)S(1)}, f32[768]{0:T(1024)}, u32[]{:S(2)}) copy-start(f32[768]{0:T(1024)} %param.25) | copy-start | bytes 9220
  57.5 29.7 %copy-start.42 = (f32[768]{0:T(1024)S(1)}, f32[768]{0:T(1024)}, u32[]{:S(2)}) copy-start(f32[768]{0:T(1024)} %param.23) | copy-start | bytes 9220
  58.2 41.3 %copy-start.23 = (f32[512,768]{1,0:T(8,128)}, f32[512,768]{1,0:T(8,128)S(1)}, u32[]{:S(2)}) copy-start(f32[512,768]{1,0:T(8,128)S(1)} %fusion.3.refs_2_) | copy-start | bytes 4718596
  58.2 15.5 %collective-permute-start.9 = (f32[5,24,768]{2,1,0:T(8,128)S(1)}, f32[5,24,768]{2,1,0:T(8,128)S(1)}, u32[]{:S(2)}, u32[]{:S(2)}) collective-permute-start(f32[5,24,768]{2,1,0:T(8,128)S(1)} %copy-done.39), channel_id=1, source_target_pairs={{0,2},{1,3},{2,0},{3,1},{4,6},{5,7},{6,4},{7,5},{8,10},{9,11},{10,... | collective-permute-start | bytes 1105928 | tf_op jit(solution)/shard_map/ppermute | solution.py:615
  74.4 186.6 %reduce-scatter.2.cloned.1.call-start = ((), (), s32[]{:S(2)}) async-start(), calls=%async_computation.4 | async-start | bytes 10616832 | tf_op jit(solution)/shard_map/reduce_scatter | solution.py:704
  74.7 45.9 %collective-permute-start.2 = (f32[512,768]{1,0:T(8,128)S(1)}, f32[512,768]{1,0:T(8,128)}, u32[]{:S(2)}, u32[]{:S(2)}) collective-permute-start(f32[512,768]{1,0:T(8,128)S(1)} %fusion.3.refs_2_), channel_id=1, source_target_pairs={{0,1},{1,0},{2,3},{3,2},{4,5},{5,4},{6,7},{7,6},{8,9},{9,8},{10,11... | collective-permute-start | bytes 4718600 | tf_op jit(solution)/shard_map/ppermute | solution.py:615
  87.2 72.9 %copy-start.17 = (f32[1,768]{1,0:T(1,128)}, f32[1,768]{1,0:T(1,128)S(1)}, u32[]{:S(2)}) copy-start(f32[1,768]{1,0:T(1,128)S(1)} %reshape.107.refs_5_.refs_6_.gain_ref) | copy-start | bytes 9220
  99.5 21.1 %copy-start = (bf16[768,768]{1,0:T(8,128)(2,1)S(1)}, bf16[768,768]{1,0:T(8,128)(2,1)}, u32[]{:S(2)}) copy-start(bf16[768,768]{1,0:T(8,128)(2,1)} %refs_11_.3) | copy-start | bytes 3538948
  99.5 21.0 %copy-start.1 = (bf16[768,768]{1,0:T(8,128)(2,1)S(1)}, bf16[768,768]{1,0:T(8,128)(2,1)}, u32[]{:S(2)}) copy-start(bf16[768,768]{1,0:T(8,128)(2,1)} %refs_13_.3) | copy-start | bytes 3538948
  125.7 20.5 %collective-permute-start.5 = (f32[256,768]{1,0:T(8,128)S(1)}, f32[256,768]{1,0:T(8,128)S(1)}, u32[]{:S(2)}, u32[]{:S(2)}) collective-permute-start(f32[256,768]{1,0:T(8,128)S(1)} %get-tuple-element.81.refs_2_), channel_id=1, source_target_pairs={{0,1},{1,0},{2,3},{3,2},{4,5},{5,4},{6,7},{7,6},{8,9},{9,8},{10,11... | collective-permute-start | bytes 2359304 | tf_op jit(solution)/shard_map/ppermute | solution.py:615
  132.9 19.6 %copy-start.8 = (f32[512,1]{1,0:T(8,128)}, f32[512,1]{1,0:T(8,128)S(1)}, u32[]{:S(2)}) copy-start(f32[512,1]{1,0:T(8,128)S(1)} %get-tuple-element.91.scale_ref) | copy-start | bytes 6148
  132.9 27.2 %collective-permute-start.4 = (f32[256,768]{1,0:T(8,128)S(1)}, f32[256,768]{1,0:T(8,128)S(1)}, u32[]{:S(2)}, u32[]{:S(2)}) collective-permute-start(f32[256,768]{1,0:T(8,128)S(1)} %get-tuple-element.78.refs_2_), channel_id=1, source_target_pairs={{0,1},{1,0},{2,3},{3,2},{4,5},{5,4},{6,7},{7,6},{8,9},{9,8},{10,11... | collective-permute-start | bytes 2359304 | tf_op jit(solution)/shard_map/ppermute | solution.py:615
  173.0 206.8 %all-gather.11.cloned.1.call-start = ((), (), s32[]{:S(2)}) async-start(), calls=%async_computation.5 | async-start | bytes 5308416 | tf_op jit(solution)/shard_map/all_gather | solution.py:626
  173.3 33.8 %collective-permute-start.6 = (f32[512,768]{1,0:T(8,128)}, f32[512,768]{1,0:T(8,128)}, u32[]{:S(2)}, u32[]{:S(2)}) collective-permute-start(f32[512,768]{1,0:T(8,128)} %get-tuple-element.88.part_ref), channel_id=1, source_target_pairs={{0,1},{1,0},{2,3},{3,2},{4,5},{5,4},{6,7},{7,6},{8,9},{9,8},{10,11... | collective-permute-start | bytes 4718600 | tf_op jit(solution)/shard_map/ppermute | solution.py:615
  207.1 33.6 %collective-permute-start.7 = (f32[256,768]{1,0:T(8,128)S(1)}, f32[256,768]{1,0:T(8,128)S(1)}, u32[]{:S(2)}, u32[]{:S(2)}) collective-permute-start(f32[256,768]{1,0:T(8,128)S(1)} %get-tuple-element.89.refs_0_), channel_id=1, source_target_pairs={{0,2},{1,3},{2,0},{3,1},{4,6},{5,7},{6,4},{7,5},{8,10},{9,11},{10,... | collective-permute-start | bytes 2359304 | tf_op jit(solution)/shard_map/ppermute | solution.py:615
  240.7 23.4 %copy-start.11 = (f32[256,768]{1,0:T(8,128)}, f32[256,768]{1,0:T(8,128)S(1)}, u32[]{:S(2)}) copy-start(f32[256,768]{1,0:T(8,128)S(1)} %collective-permute-done.7.refs_1_) | copy-start | bytes 2359300
  240.7 6.7 %collective-permute-start.10 = (f32[4,304,768]{2,1,0:T(8,128)}, f32[4,304,768]{2,1,0:T(8,128)S(1)}, u32[]{:S(2)}, u32[]{:S(2)}) collective-permute-start(f32[4,304,768]{2,1,0:T(8,128)} %get-tuple-element.101), channel_id=1, source_target_pairs={{0,4},{4,0},{8,12},{12,8},{16,20},{20,16},{24,28},{28,24},{1,5},{5... | collective-permute-start | bytes 11206664 | tf_op jit(solution)/shard_map/ppermute | solution.py:619
  240.7 20.2 %collective-permute-start.14 = (f32[256,768]{1,0:T(8,128)}, f32[256,768]{1,0:T(8,128)S(1)}, u32[]{:S(2)}, u32[]{:S(2)}) collective-permute-start(f32[256,768]{1,0:T(8,128)} %get-tuple-element.106), channel_id=1, source_target_pairs={{0,1},{1,0},{2,3},{3,2},{4,5},{5,4},{6,7},{7,6},{8,9},{9,8},{10,11... | collective-permute-start | bytes 2359304 | tf_op jit(solution)/shard_map/ppermute | solution.py:615
  254.2 23.0 %collective-permute-start.11 = (f32[2,152,768]{2,1,0:T(8,128)}, f32[2,152,768]{2,1,0:T(8,128)}, u32[]{:S(2)}, u32[]{:S(2)}) collective-permute-start(f32[2,152,768]{2,1,0:T(8,128)} %slice.133), channel_id=1, source_target_pairs={{0,16},{4,20},{8,24},{12,28},{16,0},{20,4},{24,8},{28,12},{1,17},{... | collective-permute-start | bytes 2801672 | tf_op jit(solution)/shard_map/ppermute | solution.py:619
  255.8 24.1 %collective-permute-start.12 = (f32[2,152,768]{2,1,0:T(8,128)}, f32[2,152,768]{2,1,0:T(8,128)}, u32[]{:S(2)}, u32[]{:S(2)}) collective-permute-start(f32[2,152,768]{2,1,0:T(8,128)} %slice_bitcast_fusion.1), channel_id=1, source_target_pairs={{0,8},{4,12},{8,0},{12,4},{16,24},{20,28},{24,16},{28,20},{1,9},{5... | collective-permute-start | bytes 2801672 | tf_op jit(solution)/shard_map/ppermute | solution.py:619
  262.2 17.7 %copy-start.25 = (f32[4,152,768]{2,1,0:T(8,128)S(1)}, f32[4,152,768]{2,1,0:T(8,128)}, u32[]{:S(2)}) copy-start(f32[4,152,768]{2,1,0:T(8,128)} %copy-done.24) | copy-start | bytes 5603332
  262.2 62.4 %collective-permute-start.15 = (f32[448,768]{1,0:T(8,128)S(1)}, f32[448,768]{1,0:T(8,128)S(1)}, u32[]{:S(2)}, u32[]{:S(2)}) collective-permute-start(f32[448,768]{1,0:T(8,128)S(1)} %pad_maximum_fusion.1), channel_id=1, source_target_pairs={{0,2},{1,3},{2,0},{3,1},{4,6},{5,7},{6,4},{7,5},{8,10},{9,11},{10,... | collective-permute-start | bytes 4128776 | tf_op jit(solution)/shard_map/ppermute | solution.py:615
  264.1 46.5 %collective-permute-start.8 = (f32[256,768]{1,0:T(8,128)S(1)}, f32[256,768]{1,0:T(8,128)S(1)}, u32[]{:S(2)}, u32[]{:S(2)}) collective-permute-start(f32[256,768]{1,0:T(8,128)S(1)} %collective-permute-done.7.refs_1_), channel_id=1, source_target_pairs={{0,1},{1,0},{2,3},{3,2},{4,5},{5,4},{6,7},{7,6},{8,9},{9,8},{10,11... | collective-permute-start | bytes 2359304 | tf_op jit(solution)/shard_map/ppermute | solution.py:615
  279.9 45.8 %copy-start.30 = (f32[384,768]{1,0:T(8,128)S(1)}, f32[384,768]{1,0:T(8,128)}, u32[]{:S(2)}) copy-start(f32[384,768]{1,0:T(8,128)} %reduce-scatter.2.cloned.1.call-done) | copy-start | bytes 3538948
  281.3 29.3 %copy-start.26 = (f32[1,2,152,768]{3,2,1,0:T(8,128)}, f32[1,2,152,768]{3,2,1,0:T(8,128)S(1)}, u32[]{:S(2)}) copy-start(f32[1,2,152,768]{3,2,1,0:T(8,128)S(1)} %fusion.1) | copy-start | bytes 2801668
  311.5 15.1 %collective-permute-start.13 = (f32[1,152,768]{2,1,0:T(8,128)}, f32[1,152,768]{2,1,0:T(8,128)S(1)}, u32[]{:S(2)}, u32[]{:S(2)}) collective-permute-start(f32[1,152,768]{2,1,0:T(8,128)} %slice.137), channel_id=1, source_target_pairs={{0,8},{4,12},{8,0},{12,4},{16,24},{20,28},{24,16},{28,20},{1,9},{5... | collective-permute-start | bytes 1400840 | tf_op jit(solution)/shard_map/ppermute | solution.py:619
  313.0 13.6 %collective-permute-start.18 = (f32[1,152,768]{2,1,0:T(8,128)}, f32[1,152,768]{2,1,0:T(8,128)S(1)}, u32[]{:S(2)}, u32[]{:S(2)}) collective-permute-start(f32[1,152,768]{2,1,0:T(8,128)} %slice_bitcast_fusion.3), channel_id=1, source_target_pairs={{0,16},{4,20},{8,24},{12,28},{16,0},{20,4},{24,8},{28,12},{1,17},{... | collective-permute-start | bytes 1400840 | tf_op jit(solution)/shard_map/ppermute | solution.py:619
  327.9 23.2 %collective-permute-start.16 = (f32[152,768]{1,0:T(8,128)S(1)}, f32[152,768]{1,0:T(8,128)S(1)}, u32[]{:S(2)}, u32[]{:S(2)}) collective-permute-start(f32[152,768]{1,0:T(8,128)S(1)} %fusion.10), channel_id=1, source_target_pairs={{0,2},{1,3},{2,0},{3,1},{4,6},{5,7},{6,4},{7,5},{8,10},{9,11},{10,... | collective-permute-start | bytes 1400840 | tf_op jit(solution)/shard_map/ppermute | solution.py:615
  328.6 22.5 %copy-start.27 = (f32[1,2,152,768]{3,2,1,0:T(8,128)S(1)}, f32[1,2,152,768]{3,2,1,0:T(8,128)}, u32[]{:S(2)}) copy-start(f32[1,2,152,768]{3,2,1,0:T(8,128)} %copy-done.26) | copy-start | bytes 2801668
  328.6 22.5 %copy-start.37 = (f32[1,152,768]{2,1,0:T(8,128)S(1)}, f32[1,152,768]{2,1,0:T(8,128)}, u32[]{:S(2)}) copy-start(f32[1,152,768]{2,1,0:T(8,128)} %copy-done.36) | copy-start | bytes 1400836
  329.9 24.6 %copy-start.12 = (f32[256,768]{1,0:T(8,128)S(1)}, f32[256,768]{1,0:T(8,128)}, u32[]{:S(2)}) copy-start(f32[256,768]{1,0:T(8,128)} %copy-done.11) | copy-start | bytes 2359300
  329.9 24.6 %copy-start.14 = (f32[256,768]{1,0:T(8,128)S(1)}, f32[256,768]{1,0:T(8,128)}, u32[]{:S(2)}) copy-start(f32[256,768]{1,0:T(8,128)} %copy-done.13) | copy-start | bytes 2359300
  351.1 36.0 %collective-permute-start.17 = (f32[2,256,768]{2,1,0:T(8,128)}, f32[2,256,768]{2,1,0:T(8,128)}, u32[]{:S(2)}, u32[]{:S(2)}) collective-permute-start(f32[2,256,768]{2,1,0:T(8,128)} %pad_maximum_fusion), channel_id=1, source_target_pairs={{0,1},{1,0},{2,3},{3,2},{4,5},{5,4},{6,7},{7,6},{8,9},{9,8},{10,11... | collective-permute-start | bytes 4718600 | tf_op jit(solution)/shard_map/ppermute | solution.py:615
  351.3 12.7 %collective-permute-start.19 = (f32[1,72,768]{2,1,0:T(8,128)S(1)}, f32[1,72,768]{2,1,0:T(8,128)S(1)}, u32[]{:S(2)}, u32[]{:S(2)}) collective-permute-start(f32[1,72,768]{2,1,0:T(8,128)S(1)} %slice_bitcast_fusion.5), channel_id=1, source_target_pairs={{0,8},{4,12},{8,0},{12,4},{16,24},{20,28},{24,16},{28,20},{1,9},{5... | collective-permute-start | bytes 663560 | tf_op jit(solution)/shard_map/ppermute | solution.py:619
  353.2 13.6 %collective-permute-start.20 = (f32[1,80,768]{2,1,0:T(8,128)S(1)}, f32[1,80,768]{2,1,0:T(8,128)S(1)}, u32[]{:S(2)}, u32[]{:S(2)}) collective-permute-start(f32[1,80,768]{2,1,0:T(8,128)S(1)} %slice_bitcast_fusion.4), channel_id=1, source_target_pairs={{0,16},{4,20},{8,24},{12,28},{16,0},{20,4},{24,8},{28,12},{1,17},{... | collective-permute-start | bytes 737288 | tf_op jit(solution)/shard_map/ppermute | solution.py:619
  366.9 12.3 %collective-permute-start.21 = (f32[2,72,768]{2,1,0:T(8,128)S(1)}, f32[2,72,768]{2,1,0:T(8,128)S(1)}, u32[]{:S(2)}, u32[]{:S(2)}) collective-permute-start(f32[2,72,768]{2,1,0:T(8,128)S(1)} %pad_maximum_fusion.5), channel_id=1, source_target_pairs={{0,16},{4,20},{8,24},{12,28},{16,0},{20,4},{24,8},{28,12},{1,17},{... | collective-permute-start | bytes 1327112 | tf_op jit(solution)/shard_map/ppermute | solution.py:619
  368.0 11.7 %collective-permute-start.22 = (f32[2,80,768]{2,1,0:T(8,128)S(1)}, f32[2,80,768]{2,1,0:T(8,128)S(1)}, u32[]{:S(2)}, u32[]{:S(2)}) collective-permute-start(f32[2,80,768]{2,1,0:T(8,128)S(1)} %pad_maximum_fusion.4), channel_id=1, source_target_pairs={{0,8},{4,12},{8,0},{12,4},{16,24},{20,28},{24,16},{28,20},{1,9},{5... | collective-permute-start | bytes 1474568 | tf_op jit(solution)/shard_map/ppermute | solution.py:619
  387.1 4.7 %collective-permute-start.24 = (f32[4,80,768]{2,1,0:T(8,128)S(1)}, f32[4,80,768]{2,1,0:T(8,128)S(1)}, u32[]{:S(2)}, u32[]{:S(2)}) collective-permute-start(f32[4,80,768]{2,1,0:T(8,128)S(1)} %pad_maximum_fusion.2.low_b_ref), channel_id=1, source_target_pairs={{0,4},{4,0},{8,12},{12,8},{16,20},{20,16},{24,28},{28,24},{1,5},{5... | collective-permute-start | bytes 2949128 | tf_op jit(solution)/shard_map/ppermute | solution.py:619
  387.1 4.7 %collective-permute-start.23 = (f32[4,72,768]{2,1,0:T(8,128)S(1)}, f32[4,72,768]{2,1,0:T(8,128)S(1)}, u32[]{:S(2)}, u32[]{:S(2)}) collective-permute-start(f32[4,72,768]{2,1,0:T(8,128)S(1)} %pad_maximum_fusion.3.low_a_ref), channel_id=1, source_target_pairs={{0,4},{4,0},{8,12},{12,8},{16,20},{20,16},{24,28},{28,24},{1,5},{5... | collective-permute-start | bytes 2654216 | tf_op jit(solution)/shard_map/ppermute | solution.py:619
  (29 other events, 132.0 us)
Sparse Core Ops, SparseCore 0:
  16.9 25.2 all-gather.4
  47.3 49.3 all-gather.6
  99.2 31.4 all-gather.8
  173.1 77.5 reduce-scatter.1
  326.7 45.4 all-gather.10

commit v10 on v9

--- a/solution.py
+++ b/solution.py
@@ -236,7 +236,12 @@
     def rows_of(array):
         if array.shape[0] == length and len(array.shape) == 2:
             return pl.BlockSpec((rows, array.shape[1]), lambda i, s: (chunk, 0))
-        return pl.BlockSpec(array.shape, lambda i, s: (0,) * len(array.shape))
+        return pl.BlockSpec(memory_space=pltpu.VMEM)
+
+    def whole(shape):
+        if shape.shape[0] == length:
+            return rows_of(shape)
+        return pl.BlockSpec(shape.shape, lambda i, s: (0,) * len(shape.shape))
 
     inputs = 2 + len(arrays)
     return pl.pallas_call(
@@ -248,7 +253,7 @@
             in_specs=[pl.BlockSpec((1, rows, width), lambda i, s: (s[0], chunk, 0))]
             + [rows_of(array) for array in arrays]
             + [pl.BlockSpec(memory_space=pl.ANY)] * len(before),
-            out_specs=[rows_of(shape) for shape in shapes],
+            out_specs=[whole(shape) for shape in shapes],
         ),
         input_output_aliases={inputs + index: index for index in range(len(before))},
         compiler_params=pltpu.CompilerParams(vmem_limit_bytes=48 << 20),
@@ -455,33 +460,36 @@
     )(scalars, lengths, *arrays)
 
 
-def spread_kernel(scalars_ref, *refs):
-    *pieces, out_ref = refs
-    if len(pieces) == 3:
-        pieces = [pieces[0], pieces[1], pieces[2].at[0], pieces[2].at[1]]
-    mine_ref, far_ref, rest_mine_ref, rest_far_ref = pieces
-    for step, ref in enumerate((mine_ref, rest_mine_ref, far_ref, rest_far_ref)):
+def spread_kernel(count, scalars_ref, *refs):
+    out_ref = refs[-1]
+    pieces = [refs[0].at[0], refs[0].at[1]] if len(refs[0].shape) == 3 else refs[:count]
+    for step, ref in enumerate(pieces):
 
         @pl.when(pl.program_id(0) == step)
         def _():
             out_ref[0] = ref[...].astype(out_ref.dtype)
 
 
-def spread(scalars, pieces, kind):
-    half, width = pieces[0].shape
+def spread(scalars, pieces, kind, start, onto=()):
+    half, width = pieces[0].shape[-2:]
+    count = max(len(pieces), 2)
     return pl.pallas_call(
-        spread_kernel,
+        partial(spread_kernel, count),
         out_shape=pltpu.HBM((2, 2 * half, width), kind),
         grid_spec=pltpu.PrefetchScalarGridSpec(
             num_scalar_prefetch=1,
-            grid=(4,),
-            in_specs=[pl.BlockSpec(memory_space=pltpu.VMEM)] * len(pieces),
-            out_specs=pl.BlockSpec((1, half, width), lambda i, s: (s[0] ^ (i // 2), s[1] ^ (i % 2), 0)),
-        ),
+            grid=(count,),
+            in_specs=[pl.BlockSpec(memory_space=pltpu.VMEM)] * len(pieces)
+            + [pl.BlockSpec(memory_space=pltpu.HBM)] * len(onto),
+            out_specs=pl.BlockSpec(
+                (1, half, width), lambda i, s: (s[0] ^ ((start + i) % 2), s[1] ^ ((start + i) // 2), 0)
+            ),
+        ),
+        input_output_aliases={1 + len(pieces): 0} if onto else {},
         compiler_params=pltpu.CompilerParams(vmem_limit_bytes=16 << 20),
         cost_estimate=pl.CostEstimate(flops=0, transcendentals=0, bytes_accessed=32 * half * width),
         name="spread",
-    )(scalars, *pieces)
+    )(scalars, *pieces, *onto)
 
 
 def split_blocks_kernel(in_ref, first_ref, second_ref):
@@ -751,15 +759,16 @@
     ffn = after(ffn, got_upper, got_lower)
 
     rest = swap(after(jnp.stack([mine, far_mine]), far_sum), NEAR)
-    grad_tokens = spread(scalars, (mine, far_mine, rest), f32)
+    grad_half = spread(scalars, (mine, far_mine), f32, 0)
+    grad_tokens = spread(scalars, (rest,), f32, 2, (grad_half,))
     out_rest = half_of(output, 1 - low)
-    layer_out = spread(scalars, (out_mine, out_far, out_rest, after(out_turned, far_sum)), bf16)
+    layer_out = spread(scalars, (out_mine, out_far, out_rest, after(out_turned, far_sum)), bf16, 0)
     total = upper + far_sum
     cut = total.shape[0] // 16 * 8
     upper, lower = total[None, :cut], total[None, cut:]
     for step in range(len(more)):
         if step:
-            upper, lower = after_all(upper, lower, layer_out)[:2]
+            upper, lower = after_all(upper, lower, layer_out, grad_half)[:2]
         got_upper = group_swap(upper, more[step])
         got_lower = group_swap(lower, more[-1 - step])
         upper = jnp.concatenate([upper, got_upper], axis=0)

time: 402 us -> 401 us (level)
    unnamed x92 -> x84, local copies, waits for them, and re-layouts: 12.2 us -> 12.2 us
  transfers between devices with their start and end apart: 30 -> 30, of which waited for: 21 -> 22; matrix products, arithmetic and copies ran while one was open for 7% -> 7% of each run, Pallas kernels for 18% -> 19%
where the time goes in v10:
time: 401 us; the launch traced here: 400 us
  waiting for transfers between devices  223 us (56%)
  Pallas kernels  76.3 us (19%)
  starting transfers between devices  43 us (11%)
  local copies, waits for them, and re-layouts  24.7 us (6%)
  other arithmetic  18.7 us (5%)
  between operations  14.3 us (4%)
    ppermute x14, waiting for transfers between devices, swap(): return lax.ppermute(value, MP, pairs)  177 us
    ppermute x11, waiting for transfers between devices, group_swap(): return lax.ppermute(value, 'dp', pairs)  36.7 us
    ppermute x14, starting transfers between devices, swap(): return lax.ppermute(value, MP, pairs)  30.8 us
    pallas_call x1, Pallas kernels, attend_back(): pl.pallas_call(partial(attend_back_kernel, heads, count), out_shape=shape...  25.7 us
    pallas_call x4, Pallas kernels, on_chunk(): pl.pallas_call(without(kernel, inputs, len(before)), out_shape=shapes, gr...  22.8 us
    unnamed x84, local copies, waits for them, and re-layouts  12.2 us
    ppermute x11, starting transfers between devices, group_swap(): return lax.ppermute(value, 'dp', pairs)  11.5 us
    pallas_call x1, Pallas kernels, attend(): pl.pallas_call(partial(attend_kernel, columns // HEAD_DIM), out_shape=sha...  9.98 us
  transfers between devices with their start and end apart: 30, of which 22 were waited for; matrix products, arithmetic and copies ran while one was open for 7% of the time, Pallas kernels for 19%

profile of v10, /device:TPU:0, one launch (start us, length us, event | category | flops | bytes accessed | tf_op | source)
XLA Modules:
  0.0 400.3 jit_solution(560330409834289405)
XLA Ops:
  8.1 4.1 %collective-permute-start.1 = (f32[24,768]{1,0:T(8,128)S(1)}, f32[24,768]{1,0:T(8,128)S(1)}, u32[]{:S(2)}, u32[]{:S(2)}) collective-permute-start(f32[24,768]{1,0:T(8,128)S(1)} %dynamic-slice_convert_fusion), channel_id=1, source_target_pairs={{0,2},{1,3},{2,0},{3,1},{4,6},{5,7},{6,4},{7,5},{8,10},{9,11},{10,... | collective-permute-start | bytes 221192 | tf_op jit(solution)/shard_map/ppermute | solution.py:623
  12.2 3.9 collective-permute-done.1
  22.0 10.0 %attend.1 = (f32[192,512]{1,0:T(8,128)S(1)}, bf16[192,512]{1,0:T(8,128)(2,1)S(1)}, bf16[5,192,512]{2,1,0:T(8,128)(2,1)S(1)}, bf16[512,768]{1,0:T(8,128)(2,1)S(1)}) custom-call(s32[2]{0:T(128)S(1)} %pad_add_fusion.scalars_ref.refs_0_, s32[2]{0:T(128)S(1)} %copy-done.16, bf16[2,512,768]{2,1,0:T(8,128)(2,1)S(1)} %copy-done.2, s32[2,2,512]{2,1,0:T(2,128)S(1)} %copy-done.18, ...), custom_call_target="tpu_custom_call" | custom-call | flops 2315255808 | bytes 5898240 | tf_op jit(solution)/shard_map/attend/pallas_call | solution.py:130
  34.7 12.5 %collective-permute-done.3 = f32[200,768]{1,0:T(8,128)} collective-permute-done((f32[200,768]{1,0:T(8,128)}, f32[200,768]{1,0:T(8,128)}, u32[]{:S(2)}, u32[]{:S(2)}) %collective-permute-start.3) | collective-permute-done | bytes 614432 | tf_op jit(solution)/shard_map/ppermute | solution.py:623
  48.1 8.1 %collective-permute-done = f32[192,512]{1,0:T(8,128)S(1)} collective-permute-done((f32[192,512]{1,0:T(8,128)}, f32[192,512]{1,0:T(8,128)S(1)}, u32[]{:S(2)}, u32[]{:S(2)}) %collective-permute-start) | collective-permute-done | bytes 393248 | tf_op jit(solution)/shard_map/ppermute | solution.py:623
  58.6 15.0 %collective-permute-done.9 = f32[5,24,768]{2,1,0:T(8,128)S(1)} collective-permute-done((f32[5,24,768]{2,1,0:T(8,128)S(1)}, f32[5,24,768]{2,1,0:T(8,128)S(1)}, u32[]{:S(2)}, u32[]{:S(2)}) %collective-permute-start.9) | collective-permute-done | bytes 368672 | tf_op jit(solution)/shard_map/ppermute | solution.py:623
  74.7 12.5 %collective-permute-start.2 = (f32[512,768]{1,0:T(8,128)S(1)}, f32[512,768]{1,0:T(8,128)}, u32[]{:S(2)}, u32[]{:S(2)}) collective-permute-start(f32[512,768]{1,0:T(8,128)S(1)} %fusion.3.refs_2_), channel_id=1, source_target_pairs={{0,1},{1,0},{2,3},{3,2},{4,5},{5,4},{6,7},{7,6},{8,9},{9,8},{10,11... | collective-permute-start | bytes 4718600 | tf_op jit(solution)/shard_map/ppermute | solution.py:623
  88.0 8.7 %all-gather.7.cloned.1.call-done = f32[1600,768]{1,0:T(8,128)} async-done(((f32[200,768]{1,0:T(8,128)}), f32[1600,768]{1,0:T(8,128)}) %all-gather.7.cloned.1.call-update) | async-done | bytes 4915216 | tf_op jit(solution)/shard_map/all_gather | solution.py:634
  96.7 2.8 multiply_convert_fusion
  100.7 19.9 %collective-permute-done.2.refs_3_ = f32[512,768]{1,0:T(8,128)} collective-permute-done((f32[512,768]{1,0:T(8,128)S(1)}, f32[512,768]{1,0:T(8,128)}, u32[]{:S(2)}, u32[]{:S(2)}) %collective-permute-start.2) | collective-permute-done | bytes 1572896 | tf_op jit(solution)/shard_map/ppermute | solution.py:623
  120.6 5.2 %feed.2 = (f32[512,768]{1,0:T(8,128)}, f32[512,1]{1,0:T(8,128)S(1)}, bf16[512,768]{1,0:T(8,128)(2,1)S(1)}, bf16[512,1536]{1,0:T(8,128)(2,1)}, f32[512,1536]{1,0:T(8,128)}, /*index=5*/f32[256,768]{1,0:T(8,128)S(1)}) custom-call(s32[2]{0:T(128)S(1)} %pad_add_fusion.scalars_ref.refs_0_, bf16[2,512,768]{2,1,0:T(8,128)(2,1)} %refs_1_.5, f32[512,768]{1,0:T(8,128)} %copy-done.21, ...), custom_call_target="tpu_custom_call" | custom-call | flops 2415919104 | bytes 7864320 | tf_op jit(solution)/shard_map/feed/pallas_call | solution.py:247
  125.7 1.7 collective-permute-start.5
  127.5 5.4 %feed.3 = (f32[512,768]{1,0:T(8,128)}, f32[512,1]{1,0:T(8,128)S(1)}, bf16[512,768]{1,0:T(8,128)(2,1)S(1)}, bf16[512,1536]{1,0:T(8,128)(2,1)}, f32[512,1536]{1,0:T(8,128)}, /*index=5*/f32[256,768]{1,0:T(8,128)S(1)}) custom-call(s32[2]{0:T(128)S(1)} %pad_add_fusion.scalars_ref.refs_0_, ...), custom_call_target="tpu_custom_call", output_to_operand_aliasing={{0}: (12, {}), {1}: (13, {}), {2}: (14, {}), {3}: (15, {}),... | custom-call | flops 2415919104 | bytes 7864320 | tf_op jit(solution)/shard_map/feed/pallas_call | solution.py:247
  133.3 12.9 %collective-permute-done.5.refs_3_ = f32[256,768]{1,0:T(8,128)S(1)} collective-permute-done((f32[256,768]{1,0:T(8,128)S(1)}, f32[256,768]{1,0:T(8,128)S(1)}, u32[]{:S(2)}, u32[]{:S(2)}) %collective-permute-start.5) | collective-permute-done | bytes 786464 | tf_op jit(solution)/shard_map/ppermute | solution.py:623
  146.2 6.3 %feed_back.2 = (f32[512,768]{1,0:T(8,128)}, f32[512,768]{1,0:T(8,128)}, bf16[512,768]{1,0:T(8,128)(2,1)S(1)}, bf16[512,1536]{1,0:T(8,128)(2,1)}, f32[512,768]{1,...) custom-call(s32[2]{0:T(128)S(1)} %pad_add_fusion.scalars_ref.refs_0_, bf16[2,512,768]{2,1,0:T(8,128)(2,1)} %refs_1_.7, ...), custom_call_target="tpu_custom_call" | custom-call | flops 2415919104 | bytes 7864320 | tf_op jit(solution)/shard_map/feed_back/pallas_call | solution.py:247
  152.5 7.6 %collective-permute-done.4.refs_3_ = f32[256,768]{1,0:T(8,128)S(1)} collective-permute-done((f32[256,768]{1,0:T(8,128)S(1)}, f32[256,768]{1,0:T(8,128)S(1)}, u32[]{:S(2)}, u32[]{:S(2)}) %collective-permute-start.4) | collective-permute-done | bytes 786464 | tf_op jit(solution)/shard_map/ppermute | solution.py:623
  160.1 5.9 %feed_back.3 = (f32[512,768]{1,0:T(8,128)}, f32[512,768]{1,0:T(8,128)}, bf16[512,768]{1,0:T(8,128)(2,1)S(1)}, bf16[512,1536]{1,0:T(8,128)(2,1)}, f32[512,768]{1,...) custom-call(s32[2]{0:T(128)S(1)} %pad_add_fusion.scalars_ref.refs_0_, ...), custom_call_target="tpu_custom_call", output_to_operand_aliasing={{0}: (15, {}), {1}: (16, {}), {2}: (17, {}), {3}: (18, {}),... | custom-call | flops 2415919104 | bytes 7864320 | tf_op jit(solution)/shard_map/feed_back/pallas_call | solution.py:247
  167.4 5.6 %feed_grads.1 = f32[8,4,96,768]{3,2,1,0:T(8,128)} custom-call(bf16[512,768]{1,0:T(8,128)(2,1)S(1)} %get-tuple-element.107.low_ref, bf16[512,1536]{1,0:T(8,128)(2,1)S(1)} %copy-done.4, bf16[512,1536]{1,0:T(8,128)(2,1)S(1)} %copy-done.5, bf16[512,768]{1,0:T(8,128)(2,1)S(1)} %get-tuple-element.110.feed_ref), custom_call_target="tpu_custom_call" | custom-call | flops 2415919104 | bytes 9437184 | tf_op jit(solution)/shard_map/feed_grads/pallas_call | solution.py:287
  173.3 1.7 collective-permute-start.6
  176.6 1.5 constant_dynamic-slice_fusion
  178.1 29.0 %collective-permute-done.6.other_ref = f32[512,768]{1,0:T(8,128)} collective-permute-done((f32[512,768]{1,0:T(8,128)}, f32[512,768]{1,0:T(8,128)}, u32[]{:S(2)}, u32[]{:S(2)}) %collective-permute-start.6) | collective-permute-done | bytes 1572896 | tf_op jit(solution)/shard_map/ppermute | solution.py:623
  207.1 4.1 %collective-permute-start.7 = (f32[256,768]{1,0:T(8,128)S(1)}, f32[256,768]{1,0:T(8,128)S(1)}, u32[]{:S(2)}, u32[]{:S(2)}) collective-permute-start(f32[256,768]{1,0:T(8,128)S(1)} %get-tuple-element.89.refs_0_), channel_id=1, source_target_pairs={{0,2},{1,3},{2,0},{3,1},{4,6},{5,7},{6,4},{7,5},{8,10},{9,11},{10,... | collective-permute-start | bytes 2359304 | tf_op jit(solution)/shard_map/ppermute | solution.py:623
  211.9 25.7 %attend_back.1 = (f32[256,768]{1,0:T(8,128)}, f32[256,768]{1,0:T(8,128)}, f32[4,304,768]{2,1,0:T(8,128)}, f32[4,304,768]{2,1,0:T(8,128)}) custom-call(s32[3]{0:T(128)} %pad_add_fusion.1.scalars_ref, s32[2]{0:T(128)} %lengths_ref.3, f32[512,768]{1,0:T(8,128)} %get-tuple-element.88.part_ref, f32[512,768]{1,0:T(8,128)} %collective-permute-done.6.other_ref, ...), custom_call_target="tpu_custom_call" | custom-call | flops 3321888768 | bytes 15728640 | tf_op jit(solution)/shard_map/attend_back/pallas_call | solution.py:430
  237.6 3.1 collective-permute-done.7.refs_1_
  240.9 6.6 %collective-permute-done.10 = f32[4,304,768]{2,1,0:T(8,128)S(1)} collective-permute-done((f32[4,304,768]{2,1,0:T(8,128)}, f32[4,304,768]{2,1,0:T(8,128)S(1)}, u32[]{:S(2)}, u32[]{:S(2)}) %collective-permute-start.10) | collective-permute-done | bytes 3735584 | tf_op jit(solution)/shard_map/ppermute | solution.py:627
  247.5 2.8 add.63
  250.4 1.8 copy-done.20
  254.2 1.6 collective-permute-start.11
  257.2 3.7 collective-permute-done.14
  262.2 1.9 collective-permute-start.15
  264.1 1.7 collective-permute-start.8
  265.8 11.4 %collective-permute-done.11 = f32[2,152,768]{2,1,0:T(8,128)} collective-permute-done((f32[2,152,768]{2,1,0:T(8,128)}, f32[2,152,768]{2,1,0:T(8,128)}, u32[]{:S(2)}, u32[]{:S(2)}) %collective-permute-start.11) | collective-permute-done | bytes 933920 | tf_op jit(solution)/shard_map/ppermute | solution.py:627
  277.2 1.6 slice_add_fusion
  282.1 28.5 %collective-permute-done.8.refs_3_ = f32[256,768]{1,0:T(8,128)S(1)} collective-permute-done((f32[256,768]{1,0:T(8,128)S(1)}, f32[256,768]{1,0:T(8,128)S(1)}, u32[]{:S(2)}, u32[]{:S(2)}) %collective-permute-start.8) | collective-permute-done | bytes 786464 | tf_op jit(solution)/shard_map/ppermute | solution.py:623
  311.5 1.5 collective-permute-start.13
  314.5 10.1 %collective-permute-done.15 = f32[448,768]{1,0:T(8,128)S(1)} collective-permute-done((f32[448,768]{1,0:T(8,128)S(1)}, f32[448,768]{1,0:T(8,128)S(1)}, u32[]{:S(2)}, u32[]{:S(2)}) %collective-permute-start.15) | collective-permute-done | bytes 1376288 | tf_op jit(solution)/shard_map/ppermute | solution.py:623
  330.0 21.2 %collective-permute-done.16 = f32[152,768]{1,0:T(8,128)S(1)} collective-permute-done((f32[152,768]{1,0:T(8,128)S(1)}, f32[152,768]{1,0:T(8,128)S(1)}, u32[]{:S(2)}, u32[]{:S(2)}) %collective-permute-start.16) | collective-permute-done | bytes 466976 | tf_op jit(solution)/shard_map/ppermute | solution.py:623
  352.3 1.9 collective-permute-start.19
  355.5 1.8 spread.4.refs_1_
  357.3 2.3 spread.3
  359.6 5.4 %collective-permute-done.19 = f32[1,72,768]{2,1,0:T(8,128)S(1)} collective-permute-done((f32[1,72,768]{2,1,0:T(8,128)S(1)}, f32[1,72,768]{2,1,0:T(8,128)S(1)}, u32[]{:S(2)}, u32[]{:S(2)}) %collective-permute-start.19) | collective-permute-done | bytes 221216 | tf_op jit(solution)/shard_map/ppermute | solution.py:627
  365.1 2.8 collective-permute-done.20
  369.9 9.3 %collective-permute-done.21 = f32[2,72,768]{2,1,0:T(8,128)S(1)} collective-permute-done((f32[2,72,768]{2,1,0:T(8,128)S(1)}, f32[2,72,768]{2,1,0:T(8,128)S(1)}, u32[]{:S(2)}, u32[]{:S(2)}) %collective-permute-start.21) | collective-permute-done | bytes 442400 | tf_op jit(solution)/shard_map/ppermute | solution.py:627
  380.5 2.3 copy-done.6
  382.8 2.7 split_blocks.1
  385.5 1.7 collective-permute-done.17.refs_0_
  387.7 3.2 spread.5
  391.0 2.2 place_grads.1
  (169 shorter events, 42.9 us)
Async XLA Ops:
  7.2 49.1 %all-gather.5.cloned.1.call-start = ((), (), s32[]{:S(2)}) async-start(), calls=%async_computation.1 | async-start | bytes 1327104 | tf_op jit(solution)/shard_map/all_gather | solution.py:634
  8.0 13.0 %copy-start.2 = (bf16[2,512,768]{2,1,0:T(8,128)(2,1)S(1)}, bf16[2,512,768]{2,1,0:T(8,128)(2,1)}, u32[]{:S(2)}) copy-start(bf16[2,512,768]{2,1,0:T(8,128)(2,1)} %refs_1_.5) | copy-start | bytes 4718596
  8.0 13.0 %copy-start.7 = (bf16[3,768,192]{1,2,0:T(8,128)(2,1)S(1)}, bf16[3,768,192]{1,2,0:T(8,128)(2,1)}, u32[]{:S(2)}) copy-start(bf16[3,768,192]{1,2,0:T(8,128)(2,1)} %param.20) | copy-start | bytes 2654212
  8.0 13.0 %copy-start.14 = (bf16[2,768,192]{1,2,0:T(8,128)(2,1)S(1)}, bf16[2,768,192]{1,2,0:T(8,128)(2,1)}, u32[]{:S(2)}) copy-start(bf16[2,768,192]{1,2,0:T(8,128)(2,1)} %param.21) | copy-start | bytes 1769476
  8.0 13.0 %copy-start.16 = (s32[2]{0:T(128)S(1)}, s32[2]{0:T(128)}, u32[]{:S(2)}) copy-start(s32[2]{0:T(128)} %lengths_ref.3) | copy-start | bytes 28
  8.1 8.0 %collective-permute-start.1 = (f32[24,768]{1,0:T(8,128)S(1)}, f32[24,768]{1,0:T(8,128)S(1)}, u32[]{:S(2)}, u32[]{:S(2)}) collective-permute-start(f32[24,768]{1,0:T(8,128)S(1)} %dynamic-slice_convert_fusion), channel_id=1, source_target_pairs={{0,2},{1,3},{2,0},{3,1},{4,6},{5,7},{6,4},{7,5},{8,10},{9,11},{10,... | collective-permute-start | bytes 221192 | tf_op jit(solution)/shard_map/ppermute | solution.py:623
  16.8 79.9 %all-gather.7.cloned.1.call-start = ((), (), s32[]{:S(2)}) async-start(), calls=%async_computation.2 | async-start | bytes 5529600 | tf_op jit(solution)/shard_map/all_gather | solution.py:634
  19.6 27.6 %collective-permute-start.3 = (f32[200,768]{1,0:T(8,128)}, f32[200,768]{1,0:T(8,128)}, u32[]{:S(2)}, u32[]{:S(2)}) collective-permute-start(f32[200,768]{1,0:T(8,128)} %maximum_maximum_fusion), channel_id=1, source_target_pairs={{0,2},{1,3},{2,0},{3,1},{4,6},{5,7},{6,4},{7,5},{8,10},{9,11},{10,... | collective-permute-start | bytes 1843208 | tf_op jit(solution)/shard_map/ppermute | solution.py:623
  34.7 22.9 %copy-start.13 = (bf16[192,512]{1,0:T(8,128)(2,1)}, bf16[192,512]{1,0:T(8,128)(2,1)S(1)}, u32[]{:S(2)}) copy-start(bf16[192,512]{1,0:T(8,128)(2,1)S(1)} %get-tuple-element.70.mixed_ref) | copy-start | bytes 589828
  47.2 164.7 %all-gather.9.cloned.1.call-start = ((), (), s32[]{:S(2)}) async-start(), calls=%async_computation.3 | async-start | bytes 3317760 | tf_op jit(solution)/shard_map/all_gather | solution.py:634
  47.2 9.0 %collective-permute-start = (f32[192,512]{1,0:T(8,128)}, f32[192,512]{1,0:T(8,128)S(1)}, u32[]{:S(2)}, u32[]{:S(2)}) collective-permute-start(f32[192,512]{1,0:T(8,128)} %copy-done.17), channel_id=1, source_target_pairs={{0,2},{1,3},{2,0},{3,1},{4,6},{5,7},{6,4},{7,5},{8,10},{9,11},{10,... | collective-permute-start | bytes 1179656 | tf_op jit(solution)/shard_map/ppermute | solution.py:623
  57.5 42.0 %copy-start.27 = (bf16[8,24,768]{2,1,0:T(8,128)(2,1)}, bf16[8,24,768]{2,1,0:T(8,128)(2,1)S(1)}, u32[]{:S(2)}) copy-start(bf16[8,24,768]{2,1,0:T(8,128)(2,1)S(1)} %fusion.2) | copy-start | bytes 884740
  57.5 29.7 %copy-start.36 = (f32[768]{0:T(1024)S(1)}, f32[768]{0:T(1024)}, u32[]{:S(2)}) copy-start(f32[768]{0:T(1024)} %param.24) | copy-start | bytes 9220
  57.5 29.7 %copy-start.37 = (f32[768]{0:T(1024)S(1)}, f32[768]{0:T(1024)}, u32[]{:S(2)}) copy-start(f32[768]{0:T(1024)} %param.25) | copy-start | bytes 9220
  57.5 29.7 %copy-start.38 = (f32[768]{0:T(1024)S(1)}, f32[768]{0:T(1024)}, u32[]{:S(2)}) copy-start(f32[768]{0:T(1024)} %param.23) | copy-start | bytes 9220
  58.2 41.3 %copy-start.21 = (f32[512,768]{1,0:T(8,128)}, f32[512,768]{1,0:T(8,128)S(1)}, u32[]{:S(2)}) copy-start(f32[512,768]{1,0:T(8,128)S(1)} %fusion.3.refs_2_) | copy-start | bytes 4718596
  58.2 15.5 %collective-permute-start.9 = (f32[5,24,768]{2,1,0:T(8,128)S(1)}, f32[5,24,768]{2,1,0:T(8,128)S(1)}, u32[]{:S(2)}, u32[]{:S(2)}) collective-permute-start(f32[5,24,768]{2,1,0:T(8,128)S(1)} %copy-done.35), channel_id=1, source_target_pairs={{0,2},{1,3},{2,0},{3,1},{4,6},{5,7},{6,4},{7,5},{8,10},{9,11},{10,... | collective-permute-start | bytes 1105928 | tf_op jit(solution)/shard_map/ppermute | solution.py:623
  74.4 186.6 %reduce-scatter.2.cloned.1.call-start = ((), (), s32[]{:S(2)}) async-start(), calls=%async_computation.4 | async-start | bytes 10616832 | tf_op jit(solution)/shard_map/reduce_scatter | solution.py:712
  74.7 45.9 %collective-permute-start.2 = (f32[512,768]{1,0:T(8,128)S(1)}, f32[512,768]{1,0:T(8,128)}, u32[]{:S(2)}, u32[]{:S(2)}) collective-permute-start(f32[512,768]{1,0:T(8,128)S(1)} %fusion.3.refs_2_), channel_id=1, source_target_pairs={{0,1},{1,0},{2,3},{3,2},{4,5},{5,4},{6,7},{7,6},{8,9},{9,8},{10,11... | collective-permute-start | bytes 4718600 | tf_op jit(solution)/shard_map/ppermute | solution.py:623
  87.2 72.9 %copy-start.15 = (f32[1,768]{1,0:T(1,128)}, f32[1,768]{1,0:T(1,128)S(1)}, u32[]{:S(2)}) copy-start(f32[1,768]{1,0:T(1,128)S(1)} %reshape.107.refs_5_.refs_6_.gain_ref) | copy-start | bytes 9220
  99.5 21.1 %copy-start = (bf16[768,768]{1,0:T(8,128)(2,1)S(1)}, bf16[768,768]{1,0:T(8,128)(2,1)}, u32[]{:S(2)}) copy-start(bf16[768,768]{1,0:T(8,128)(2,1)} %refs_11_.3) | copy-start | bytes 3538948
  99.5 21.0 %copy-start.1 = (bf16[768,768]{1,0:T(8,128)(2,1)S(1)}, bf16[768,768]{1,0:T(8,128)(2,1)}, u32[]{:S(2)}) copy-start(bf16[768,768]{1,0:T(8,128)(2,1)} %refs_13_.3) | copy-start | bytes 3538948
  125.7 20.5 %collective-permute-start.5 = (f32[256,768]{1,0:T(8,128)S(1)}, f32[256,768]{1,0:T(8,128)S(1)}, u32[]{:S(2)}, u32[]{:S(2)}) collective-permute-start(f32[256,768]{1,0:T(8,128)S(1)} %get-tuple-element.81.refs_2_), channel_id=1, source_target_pairs={{0,1},{1,0},{2,3},{3,2},{4,5},{5,4},{6,7},{7,6},{8,9},{9,8},{10,11... | collective-permute-start | bytes 2359304 | tf_op jit(solution)/shard_map/ppermute | solution.py:623
  132.9 19.6 %copy-start.8 = (f32[512,1]{1,0:T(8,128)}, f32[512,1]{1,0:T(8,128)S(1)}, u32[]{:S(2)}) copy-start(f32[512,1]{1,0:T(8,128)S(1)} %get-tuple-element.91.scale_ref) | copy-start | bytes 6148
  132.9 27.2 %collective-permute-start.4 = (f32[256,768]{1,0:T(8,128)S(1)}, f32[256,768]{1,0:T(8,128)S(1)}, u32[]{:S(2)}, u32[]{:S(2)}) collective-permute-start(f32[256,768]{1,0:T(8,128)S(1)} %get-tuple-element.78.refs_2_), channel_id=1, source_target_pairs={{0,1},{1,0},{2,3},{3,2},{4,5},{5,4},{6,7},{7,6},{8,9},{9,8},{10,11... | collective-permute-start | bytes 2359304 | tf_op jit(solution)/shard_map/ppermute | solution.py:623
  173.0 207.4 %all-gather.11.cloned.1.call-start = ((), (), s32[]{:S(2)}) async-start(), calls=%async_computation.5 | async-start | bytes 5308416 | tf_op jit(solution)/shard_map/all_gather | solution.py:634
  173.3 33.8 %collective-permute-start.6 = (f32[512,768]{1,0:T(8,128)}, f32[512,768]{1,0:T(8,128)}, u32[]{:S(2)}, u32[]{:S(2)}) collective-permute-start(f32[512,768]{1,0:T(8,128)} %get-tuple-element.88.part_ref), channel_id=1, source_target_pairs={{0,1},{1,0},{2,3},{3,2},{4,5},{5,4},{6,7},{7,6},{8,9},{9,8},{10,11... | collective-permute-start | bytes 4718600 | tf_op jit(solution)/shard_map/ppermute | solution.py:623
  207.1 33.7 %collective-permute-start.7 = (f32[256,768]{1,0:T(8,128)S(1)}, f32[256,768]{1,0:T(8,128)S(1)}, u32[]{:S(2)}, u32[]{:S(2)}) collective-permute-start(f32[256,768]{1,0:T(8,128)S(1)} %get-tuple-element.89.refs_0_), channel_id=1, source_target_pairs={{0,2},{1,3},{2,0},{3,1},{4,6},{5,7},{6,4},{7,5},{8,10},{9,11},{10,... | collective-permute-start | bytes 2359304 | tf_op jit(solution)/shard_map/ppermute | solution.py:623
  240.7 6.7 %collective-permute-start.10 = (f32[4,304,768]{2,1,0:T(8,128)}, f32[4,304,768]{2,1,0:T(8,128)S(1)}, u32[]{:S(2)}, u32[]{:S(2)}) collective-permute-start(f32[4,304,768]{2,1,0:T(8,128)} %get-tuple-element.101), channel_id=1, source_target_pairs={{0,4},{4,0},{8,12},{12,8},{16,20},{20,16},{24,28},{28,24},{1,5},{5... | collective-permute-start | bytes 11206664 | tf_op jit(solution)/shard_map/ppermute | solution.py:627
  240.7 20.2 %collective-permute-start.14 = (f32[256,768]{1,0:T(8,128)}, f32[256,768]{1,0:T(8,128)S(1)}, u32[]{:S(2)}, u32[]{:S(2)}) collective-permute-start(f32[256,768]{1,0:T(8,128)} %get-tuple-element.106), channel_id=1, source_target_pairs={{0,1},{1,0},{2,3},{3,2},{4,5},{5,4},{6,7},{7,6},{8,9},{9,8},{10,11... | collective-permute-start | bytes 2359304 | tf_op jit(solution)/shard_map/ppermute | solution.py:623
  254.2 23.0 %collective-permute-start.11 = (f32[2,152,768]{2,1,0:T(8,128)}, f32[2,152,768]{2,1,0:T(8,128)}, u32[]{:S(2)}, u32[]{:S(2)}) collective-permute-start(f32[2,152,768]{2,1,0:T(8,128)} %slice.133), channel_id=1, source_target_pairs={{0,16},{4,20},{8,24},{12,28},{16,0},{20,4},{24,8},{28,12},{1,17},{... | collective-permute-start | bytes 2801672 | tf_op jit(solution)/shard_map/ppermute | solution.py:627
  255.8 24.1 %collective-permute-start.12 = (f32[2,152,768]{2,1,0:T(8,128)}, f32[2,152,768]{2,1,0:T(8,128)}, u32[]{:S(2)}, u32[]{:S(2)}) collective-permute-start(f32[2,152,768]{2,1,0:T(8,128)} %slice_bitcast_fusion.1), channel_id=1, source_target_pairs={{0,8},{4,12},{8,0},{12,4},{16,24},{20,28},{24,16},{28,20},{1,9},{5... | collective-permute-start | bytes 2801672 | tf_op jit(solution)/shard_map/ppermute | solution.py:627
  262.2 17.7 %copy-start.23 = (f32[4,152,768]{2,1,0:T(8,128)S(1)}, f32[4,152,768]{2,1,0:T(8,128)}, u32[]{:S(2)}) copy-start(f32[4,152,768]{2,1,0:T(8,128)} %copy-done.22) | copy-start | bytes 5603332
  262.2 62.4 %collective-permute-start.15 = (f32[448,768]{1,0:T(8,128)S(1)}, f32[448,768]{1,0:T(8,128)S(1)}, u32[]{:S(2)}, u32[]{:S(2)}) collective-permute-start(f32[448,768]{1,0:T(8,128)S(1)} %pad_maximum_fusion.1), channel_id=1, source_target_pairs={{0,2},{1,3},{2,0},{3,1},{4,6},{5,7},{6,4},{7,5},{8,10},{9,11},{10,... | collective-permute-start | bytes 4128776 | tf_op jit(solution)/shard_map/ppermute | solution.py:623
  264.1 46.5 %collective-permute-start.8 = (f32[256,768]{1,0:T(8,128)S(1)}, f32[256,768]{1,0:T(8,128)S(1)}, u32[]{:S(2)}, u32[]{:S(2)}) collective-permute-start(f32[256,768]{1,0:T(8,128)S(1)} %collective-permute-done.7.refs_1_), channel_id=1, source_target_pairs={{0,1},{1,0},{2,3},{3,2},{4,5},{5,4},{6,7},{7,6},{8,9},{9,8},{10,11... | collective-permute-start | bytes 2359304 | tf_op jit(solution)/shard_map/ppermute | solution.py:623
  279.9 45.8 %copy-start.28 = (f32[384,768]{1,0:T(8,128)S(1)}, f32[384,768]{1,0:T(8,128)}, u32[]{:S(2)}) copy-start(f32[384,768]{1,0:T(8,128)} %reduce-scatter.2.cloned.1.call-done) | copy-start | bytes 3538948
  281.3 29.3 %copy-start.24 = (f32[1,2,152,768]{3,2,1,0:T(8,128)}, f32[1,2,152,768]{3,2,1,0:T(8,128)S(1)}, u32[]{:S(2)}) copy-start(f32[1,2,152,768]{3,2,1,0:T(8,128)S(1)} %fusion.1) | copy-start | bytes 2801668
  311.5 15.1 %collective-permute-start.13 = (f32[1,152,768]{2,1,0:T(8,128)}, f32[1,152,768]{2,1,0:T(8,128)}, u32[]{:S(2)}, u32[]{:S(2)}) collective-permute-start(f32[1,152,768]{2,1,0:T(8,128)} %slice.137), channel_id=1, source_target_pairs={{0,8},{4,12},{8,0},{12,4},{16,24},{20,28},{24,16},{28,20},{1,9},{5... | collective-permute-start | bytes 1400840 | tf_op jit(solution)/shard_map/ppermute | solution.py:627
  313.0 13.6 %collective-permute-start.18 = (f32[1,152,768]{2,1,0:T(8,128)}, f32[1,152,768]{2,1,0:T(8,128)}, u32[]{:S(2)}, u32[]{:S(2)}) collective-permute-start(f32[1,152,768]{2,1,0:T(8,128)} %slice_bitcast_fusion.3), channel_id=1, source_target_pairs={{0,16},{4,20},{8,24},{12,28},{16,0},{20,4},{24,8},{28,12},{1,17},{... | collective-permute-start | bytes 1400840 | tf_op jit(solution)/shard_map/ppermute | solution.py:627
  327.9 23.2 %collective-permute-start.16 = (f32[152,768]{1,0:T(8,128)S(1)}, f32[152,768]{1,0:T(8,128)S(1)}, u32[]{:S(2)}, u32[]{:S(2)}) collective-permute-start(f32[152,768]{1,0:T(8,128)S(1)} %fusion.10), channel_id=1, source_target_pairs={{0,2},{1,3},{2,0},{3,1},{4,6},{5,7},{6,4},{7,5},{8,10},{9,11},{10,... | collective-permute-start | bytes 1400840 | tf_op jit(solution)/shard_map/ppermute | solution.py:623
  328.7 22.4 %copy-start.25 = (f32[1,2,152,768]{3,2,1,0:T(8,128)S(1)}, f32[1,2,152,768]{3,2,1,0:T(8,128)}, u32[]{:S(2)}) copy-start(f32[1,2,152,768]{3,2,1,0:T(8,128)} %copy-done.24) | copy-start | bytes 2801668
  351.2 36.0 %collective-permute-start.17 = (f32[2,256,768]{2,1,0:T(8,128)}, f32[2,256,768]{2,1,0:T(8,128)}, u32[]{:S(2)}, u32[]{:S(2)}) collective-permute-start(f32[2,256,768]{2,1,0:T(8,128)} %pad_maximum_fusion), channel_id=1, source_target_pairs={{0,1},{1,0},{2,3},{3,2},{4,5},{5,4},{6,7},{7,6},{8,9},{9,8},{10,11... | collective-permute-start | bytes 4718600 | tf_op jit(solution)/shard_map/ppermute | solution.py:623
  352.3 12.7 %collective-permute-start.19 = (f32[1,72,768]{2,1,0:T(8,128)S(1)}, f32[1,72,768]{2,1,0:T(8,128)S(1)}, u32[]{:S(2)}, u32[]{:S(2)}) collective-permute-start(f32[1,72,768]{2,1,0:T(8,128)S(1)} %slice_bitcast_fusion.5), channel_id=1, source_target_pairs={{0,8},{4,12},{8,0},{12,4},{16,24},{20,28},{24,16},{28,20},{1,9},{5... | collective-permute-start | bytes 663560 | tf_op jit(solution)/shard_map/ppermute | solution.py:627
  354.3 13.6 %collective-permute-start.20 = (f32[1,80,768]{2,1,0:T(8,128)S(1)}, f32[1,80,768]{2,1,0:T(8,128)S(1)}, u32[]{:S(2)}, u32[]{:S(2)}) collective-permute-start(f32[1,80,768]{2,1,0:T(8,128)S(1)} %slice_bitcast_fusion.4), channel_id=1, source_target_pairs={{0,16},{4,20},{8,24},{12,28},{16,0},{20,4},{24,8},{28,12},{1,17},{... | collective-permute-start | bytes 737288 | tf_op jit(solution)/shard_map/ppermute | solution.py:627
  368.0 11.2 %collective-permute-start.21 = (f32[2,72,768]{2,1,0:T(8,128)S(1)}, f32[2,72,768]{2,1,0:T(8,128)S(1)}, u32[]{:S(2)}, u32[]{:S(2)}) collective-permute-start(f32[2,72,768]{2,1,0:T(8,128)S(1)} %pad_maximum_fusion.5), channel_id=1, source_target_pairs={{0,16},{4,20},{8,24},{12,28},{16,0},{20,4},{24,8},{28,12},{1,17},{... | collective-permute-start | bytes 1327112 | tf_op jit(solution)/shard_map/ppermute | solution.py:627
  369.1 11.3 %collective-permute-start.22 = (f32[2,80,768]{2,1,0:T(8,128)S(1)}, f32[2,80,768]{2,1,0:T(8,128)S(1)}, u32[]{:S(2)}, u32[]{:S(2)}) collective-permute-start(f32[2,80,768]{2,1,0:T(8,128)S(1)} %pad_maximum_fusion.4), channel_id=1, source_target_pairs={{0,8},{4,12},{8,0},{12,4},{16,24},{20,28},{24,16},{28,20},{1,9},{5... | collective-permute-start | bytes 1474568 | tf_op jit(solution)/shard_map/ppermute | solution.py:627
  387.2 3.8 collective-permute-start.24
  387.2 3.8 collective-permute-start.23
  (25 other events, 80.8 us)
Sparse Core Ops, SparseCore 0:
  16.9 25.2 all-gather.4
  47.3 49.3 all-gather.6
  99.2 31.4 all-gather.8
  173.1 77.5 reduce-scatter.1
  326.7 44.9 all-gather.10

commit v11 on v10

--- a/solution.py
+++ b/solution.py
@@ -467,7 +467,9 @@
 
         @pl.when(pl.program_id(0) == step)
         def _():
-            out_ref[0] = ref[...].astype(out_ref.dtype)
+            rows = out_ref.shape[1]
+            at = pl.ds(pl.multiple_of(pl.program_id(1) * rows, rows), rows)
+            out_ref[0] = ref[at].astype(out_ref.dtype)
 
 
 def spread(scalars, pieces, kind, start, onto=()):
@@ -478,11 +480,12 @@
         out_shape=pltpu.HBM((2, 2 * half, width), kind),
         grid_spec=pltpu.PrefetchScalarGridSpec(
             num_scalar_prefetch=1,
-            grid=(count,),
+            grid=(count, 2),
             in_specs=[pl.BlockSpec(memory_space=pltpu.VMEM)] * len(pieces)
             + [pl.BlockSpec(memory_space=pltpu.HBM)] * len(onto),
             out_specs=pl.BlockSpec(
-                (1, half, width), lambda i, s: (s[0] ^ ((start + i) % 2), s[1] ^ ((start + i) // 2), 0)
+                (1, half // 2, width),
+                lambda i, j, s: (s[0] ^ ((start + i) % 2), 2 * (s[1] ^ ((start + i) // 2)) + j, 0),
             ),
         ),
         input_output_aliases={1 + len(pieces): 0} if onto else {},

time: 401 us -> 402 us (level)
  transfers between devices with their start and end apart: 30 -> 30, of which waited for: 22 -> 21; matrix products, arithmetic and copies ran while one was open for 7% -> 7% of each run, Pallas kernels for 19% -> 19%
where the time goes in v11:
time: 402 us; the launch traced here: 401 us
  waiting for transfers between devices  221 us (55%)
  Pallas kernels  78.5 us (20%)
  starting transfers between devices  43 us (11%)
  local copies, waits for them, and re-layouts  24.7 us (6%)
  other arithmetic  18.7 us (5%)
  between operations  14.3 us (4%)
    ppermute x14, waiting for transfers between devices, swap(): return lax.ppermute(value, MP, pairs)  177 us
    ppermute x11, waiting for transfers between devices, group_swap(): return lax.ppermute(value, 'dp', pairs)  34.9 us
    ppermute x14, starting transfers between devices, swap(): return lax.ppermute(value, MP, pairs)  30.8 us
    pallas_call x1, Pallas kernels, attend_back(): pl.pallas_call(partial(attend_back_kernel, heads, count), out_shape=shape...  25.7 us
    pallas_call x4, Pallas kernels, on_chunk(): pl.pallas_call(without(kernel, inputs, len(before)), out_shape=shapes, gr...  22.8 us
    unnamed x84, local copies, waits for them, and re-layouts  12.2 us
    ppermute x11, starting transfers between devices, group_swap(): return lax.ppermute(value, 'dp', pairs)  11.5 us
    pallas_call x1, Pallas kernels, attend(): pl.pallas_call(partial(attend_kernel, columns // HEAD_DIM), out_shape=sha...  9.98 us
  transfers between devices with their start and end apart: 30, of which 21 were waited for; matrix products, arithmetic and copies ran while one was open for 7% of the time, Pallas kernels for 19%

profile of v11, /device:TPU:0, one launch (start us, length us, event | category | flops | bytes accessed | tf_op | source)
XLA Modules:
  0.0 400.7 jit_solution(14120451803161775011)
XLA Ops:
  8.1 4.1 %collective-permute-start.1 = (f32[24,768]{1,0:T(8,128)S(1)}, f32[24,768]{1,0:T(8,128)S(1)}, u32[]{:S(2)}, u32[]{:S(2)}) collective-permute-start(f32[24,768]{1,0:T(8,128)S(1)} %dynamic-slice_convert_fusion), channel_id=1, source_target_pairs={{0,2},{1,3},{2,0},{3,1},{4,6},{5,7},{6,4},{7,5},{8,10},{9,11},{10,... | collective-permute-start | bytes 221192 | tf_op jit(solution)/shard_map/ppermute | solution.py:626
  12.2 3.9 collective-permute-done.1
  22.0 10.0 %attend.1 = (f32[192,512]{1,0:T(8,128)S(1)}, bf16[192,512]{1,0:T(8,128)(2,1)S(1)}, bf16[5,192,512]{2,1,0:T(8,128)(2,1)S(1)}, bf16[512,768]{1,0:T(8,128)(2,1)S(1)}) custom-call(s32[2]{0:T(128)S(1)} %pad_add_fusion.scalars_ref.refs_0_, s32[2]{0:T(128)S(1)} %copy-done.16, bf16[2,512,768]{2,1,0:T(8,128)(2,1)S(1)} %copy-done.2, s32[2,2,512]{2,1,0:T(2,128)S(1)} %copy-done.18, ...), custom_call_target="tpu_custom_call" | custom-call | flops 2315255808 | bytes 5898240 | tf_op jit(solution)/shard_map/attend/pallas_call | solution.py:130
  34.7 12.5 %collective-permute-done.3 = f32[200,768]{1,0:T(8,128)} collective-permute-done((f32[200,768]{1,0:T(8,128)}, f32[200,768]{1,0:T(8,128)}, u32[]{:S(2)}, u32[]{:S(2)}) %collective-permute-start.3) | collective-permute-done | bytes 614432 | tf_op jit(solution)/shard_map/ppermute | solution.py:626
  48.1 8.1 %collective-permute-done = f32[192,512]{1,0:T(8,128)S(1)} collective-permute-done((f32[192,512]{1,0:T(8,128)}, f32[192,512]{1,0:T(8,128)S(1)}, u32[]{:S(2)}, u32[]{:S(2)}) %collective-permute-start) | collective-permute-done | bytes 393248 | tf_op jit(solution)/shard_map/ppermute | solution.py:626
  58.6 15.0 %collective-permute-done.9 = f32[5,24,768]{2,1,0:T(8,128)S(1)} collective-permute-done((f32[5,24,768]{2,1,0:T(8,128)S(1)}, f32[5,24,768]{2,1,0:T(8,128)S(1)}, u32[]{:S(2)}, u32[]{:S(2)}) %collective-permute-start.9) | collective-permute-done | bytes 368672 | tf_op jit(solution)/shard_map/ppermute | solution.py:626
  74.7 12.5 %collective-permute-start.2 = (f32[512,768]{1,0:T(8,128)S(1)}, f32[512,768]{1,0:T(8,128)}, u32[]{:S(2)}, u32[]{:S(2)}) collective-permute-start(f32[512,768]{1,0:T(8,128)S(1)} %fusion.3.refs_2_), channel_id=1, source_target_pairs={{0,1},{1,0},{2,3},{3,2},{4,5},{5,4},{6,7},{7,6},{8,9},{9,8},{10,11... | collective-permute-start | bytes 4718600 | tf_op jit(solution)/shard_map/ppermute | solution.py:626
  88.0 8.7 %all-gather.7.cloned.1.call-done = f32[1600,768]{1,0:T(8,128)} async-done(((f32[200,768]{1,0:T(8,128)}), f32[1600,768]{1,0:T(8,128)}) %all-gather.7.cloned.1.call-update) | async-done | bytes 4915216 | tf_op jit(solution)/shard_map/all_gather | solution.py:637
  96.7 2.8 multiply_convert_fusion
  100.7 19.9 %collective-permute-done.2.refs_3_ = f32[512,768]{1,0:T(8,128)} collective-permute-done((f32[512,768]{1,0:T(8,128)S(1)}, f32[512,768]{1,0:T(8,128)}, u32[]{:S(2)}, u32[]{:S(2)}) %collective-permute-start.2) | collective-permute-done | bytes 1572896 | tf_op jit(solution)/shard_map/ppermute | solution.py:626
  120.6 5.2 %feed.2 = (f32[512,768]{1,0:T(8,128)}, f32[512,1]{1,0:T(8,128)S(1)}, bf16[512,768]{1,0:T(8,128)(2,1)S(1)}, bf16[512,1536]{1,0:T(8,128)(2,1)}, f32[512,1536]{1,0:T(8,128)}, /*index=5*/f32[256,768]{1,0:T(8,128)S(1)}) custom-call(s32[2]{0:T(128)S(1)} %pad_add_fusion.scalars_ref.refs_0_, bf16[2,512,768]{2,1,0:T(8,128)(2,1)} %refs_1_.5, f32[512,768]{1,0:T(8,128)} %copy-done.21, ...), custom_call_target="tpu_custom_call" | custom-call | flops 2415919104 | bytes 7864320 | tf_op jit(solution)/shard_map/feed/pallas_call | solution.py:247
  125.7 1.7 collective-permute-start.5
  127.5 5.4 %feed.3 = (f32[512,768]{1,0:T(8,128)}, f32[512,1]{1,0:T(8,128)S(1)}, bf16[512,768]{1,0:T(8,128)(2,1)S(1)}, bf16[512,1536]{1,0:T(8,128)(2,1)}, f32[512,1536]{1,0:T(8,128)}, /*index=5*/f32[256,768]{1,0:T(8,128)S(1)}) custom-call(s32[2]{0:T(128)S(1)} %pad_add_fusion.scalars_ref.refs_0_, ...), custom_call_target="tpu_custom_call", output_to_operand_aliasing={{0}: (12, {}), {1}: (13, {}), {2}: (14, {}), {3}: (15, {}),... | custom-call | flops 2415919104 | bytes 7864320 | tf_op jit(solution)/shard_map/feed/pallas_call | solution.py:247
  133.3 12.9 %collective-permute-done.5.refs_3_ = f32[256,768]{1,0:T(8,128)S(1)} collective-permute-done((f32[256,768]{1,0:T(8,128)S(1)}, f32[256,768]{1,0:T(8,128)S(1)}, u32[]{:S(2)}, u32[]{:S(2)}) %collective-permute-start.5) | collective-permute-done | bytes 786464 | tf_op jit(solution)/shard_map/ppermute | solution.py:626
  146.2 6.3 %feed_back.2 = (f32[512,768]{1,0:T(8,128)}, f32[512,768]{1,0:T(8,128)}, bf16[512,768]{1,0:T(8,128)(2,1)S(1)}, bf16[512,1536]{1,0:T(8,128)(2,1)}, f32[512,768]{1,...) custom-call(s32[2]{0:T(128)S(1)} %pad_add_fusion.scalars_ref.refs_0_, bf16[2,512,768]{2,1,0:T(8,128)(2,1)} %refs_1_.7, ...), custom_call_target="tpu_custom_call" | custom-call | flops 2415919104 | bytes 7864320 | tf_op jit(solution)/shard_map/feed_back/pallas_call | solution.py:247
  152.5 7.6 %collective-permute-done.4.refs_3_ = f32[256,768]{1,0:T(8,128)S(1)} collective-permute-done((f32[256,768]{1,0:T(8,128)S(1)}, f32[256,768]{1,0:T(8,128)S(1)}, u32[]{:S(2)}, u32[]{:S(2)}) %collective-permute-start.4) | collective-permute-done | bytes 786464 | tf_op jit(solution)/shard_map/ppermute | solution.py:626
  160.1 5.9 %feed_back.3 = (f32[512,768]{1,0:T(8,128)}, f32[512,768]{1,0:T(8,128)}, bf16[512,768]{1,0:T(8,128)(2,1)S(1)}, bf16[512,1536]{1,0:T(8,128)(2,1)}, f32[512,768]{1,...) custom-call(s32[2]{0:T(128)S(1)} %pad_add_fusion.scalars_ref.refs_0_, ...), custom_call_target="tpu_custom_call", output_to_operand_aliasing={{0}: (15, {}), {1}: (16, {}), {2}: (17, {}), {3}: (18, {}),... | custom-call | flops 2415919104 | bytes 7864320 | tf_op jit(solution)/shard_map/feed_back/pallas_call | solution.py:247
  167.4 5.6 %feed_grads.1 = f32[8,4,96,768]{3,2,1,0:T(8,128)} custom-call(bf16[512,768]{1,0:T(8,128)(2,1)S(1)} %get-tuple-element.107.low_ref, bf16[512,1536]{1,0:T(8,128)(2,1)S(1)} %copy-done.4, bf16[512,1536]{1,0:T(8,128)(2,1)S(1)} %copy-done.5, bf16[512,768]{1,0:T(8,128)(2,1)S(1)} %get-tuple-element.110.feed_ref), custom_call_target="tpu_custom_call" | custom-call | flops 2415919104 | bytes 9437184 | tf_op jit(solution)/shard_map/feed_grads/pallas_call | solution.py:287
  173.3 1.7 collective-permute-start.6
  176.6 1.5 constant_dynamic-slice_fusion
  178.1 29.0 %collective-permute-done.6.other_ref = f32[512,768]{1,0:T(8,128)} collective-permute-done((f32[512,768]{1,0:T(8,128)}, f32[512,768]{1,0:T(8,128)}, u32[]{:S(2)}, u32[]{:S(2)}) %collective-permute-start.6) | collective-permute-done | bytes 1572896 | tf_op jit(solution)/shard_map/ppermute | solution.py:626
  207.1 4.1 %collective-permute-start.7 = (f32[256,768]{1,0:T(8,128)S(1)}, f32[256,768]{1,0:T(8,128)S(1)}, u32[]{:S(2)}, u32[]{:S(2)}) collective-permute-start(f32[256,768]{1,0:T(8,128)S(1)} %get-tuple-element.89.refs_0_), channel_id=1, source_target_pairs={{0,2},{1,3},{2,0},{3,1},{4,6},{5,7},{6,4},{7,5},{8,10},{9,11},{10,... | collective-permute-start | bytes 2359304 | tf_op jit(solution)/shard_map/ppermute | solution.py:626
  211.9 25.7 %attend_back.1 = (f32[256,768]{1,0:T(8,128)}, f32[256,768]{1,0:T(8,128)}, f32[4,304,768]{2,1,0:T(8,128)}, f32[4,304,768]{2,1,0:T(8,128)}) custom-call(s32[3]{0:T(128)} %pad_add_fusion.1.scalars_ref, s32[2]{0:T(128)} %lengths_ref.3, f32[512,768]{1,0:T(8,128)} %get-tuple-element.88.part_ref, f32[512,768]{1,0:T(8,128)} %collective-permute-done.6.other_ref, ...), custom_call_target="tpu_custom_call" | custom-call | flops 3321888768 | bytes 15728640 | tf_op jit(solution)/shard_map/attend_back/pallas_call | solution.py:430
  237.6 3.1 collective-permute-done.7.refs_1_
  240.9 6.6 %collective-permute-done.10 = f32[4,304,768]{2,1,0:T(8,128)S(1)} collective-permute-done((f32[4,304,768]{2,1,0:T(8,128)}, f32[4,304,768]{2,1,0:T(8,128)S(1)}, u32[]{:S(2)}, u32[]{:S(2)}) %collective-permute-start.10) | collective-permute-done | bytes 3735584 | tf_op jit(solution)/shard_map/ppermute | solution.py:630
  247.5 2.8 add.63
  250.4 1.8 copy-done.20
  254.2 1.6 collective-permute-start.11
  257.2 3.7 collective-permute-done.14
  262.2 1.9 collective-permute-start.15
  264.1 1.7 collective-permute-start.8
  265.8 11.4 %collective-permute-done.11 = f32[2,152,768]{2,1,0:T(8,128)} collective-permute-done((f32[2,152,768]{2,1,0:T(8,128)}, f32[2,152,768]{2,1,0:T(8,128)}, u32[]{:S(2)}, u32[]{:S(2)}) %collective-permute-start.11) | collective-permute-done | bytes 933920 | tf_op jit(solution)/shard_map/ppermute | solution.py:630
  277.2 1.6 slice_add_fusion
  282.1 28.5 %collective-permute-done.8.refs_3_ = f32[256,768]{1,0:T(8,128)S(1)} collective-permute-done((f32[256,768]{1,0:T(8,128)S(1)}, f32[256,768]{1,0:T(8,128)S(1)}, u32[]{:S(2)}, u32[]{:S(2)}) %collective-permute-start.8) | collective-permute-done | bytes 786464 | tf_op jit(solution)/shard_map/ppermute | solution.py:626
  311.5 1.5 collective-permute-start.13
  314.5 10.1 %collective-permute-done.15 = f32[448,768]{1,0:T(8,128)S(1)} collective-permute-done((f32[448,768]{1,0:T(8,128)S(1)}, f32[448,768]{1,0:T(8,128)S(1)}, u32[]{:S(2)}, u32[]{:S(2)}) %collective-permute-start.15) | collective-permute-done | bytes 1376288 | tf_op jit(solution)/shard_map/ppermute | solution.py:626
  330.0 21.2 %collective-permute-done.16 = f32[152,768]{1,0:T(8,128)S(1)} collective-permute-done((f32[152,768]{1,0:T(8,128)S(1)}, f32[152,768]{1,0:T(8,128)S(1)}, u32[]{:S(2)}, u32[]{:S(2)}) %collective-permute-start.16) | collective-permute-done | bytes 466976 | tf_op jit(solution)/shard_map/ppermute | solution.py:626
  352.3 1.9 collective-permute-start.19
  355.5 2.3 spread.4.refs_1_
  357.8 3.5 spread.3
  361.4 3.7 collective-permute-done.19
  365.1 2.8 collective-permute-done.20
  369.9 9.3 %collective-permute-done.21 = f32[2,72,768]{2,1,0:T(8,128)S(1)} collective-permute-done((f32[2,72,768]{2,1,0:T(8,128)S(1)}, f32[2,72,768]{2,1,0:T(8,128)S(1)}, u32[]{:S(2)}, u32[]{:S(2)}) %collective-permute-start.21) | collective-permute-done | bytes 442400 | tf_op jit(solution)/shard_map/ppermute | solution.py:630
  380.5 2.3 copy-done.6
  382.8 2.7 split_blocks.1
  385.5 1.7 collective-permute-done.17.refs_0_
  387.7 3.7 spread.5
  391.4 2.2 place_grads.1
  (169 shorter events, 42.7 us)
Async XLA Ops:
  7.2 49.1 %all-gather.5.cloned.1.call-start = ((), (), s32[]{:S(2)}) async-start(), calls=%async_computation.1 | async-start | bytes 1327104 | tf_op jit(solution)/shard_map/all_gather | solution.py:637
  8.0 13.0 %copy-start.2 = (bf16[2,512,768]{2,1,0:T(8,128)(2,1)S(1)}, bf16[2,512,768]{2,1,0:T(8,128)(2,1)}, u32[]{:S(2)}) copy-start(bf16[2,512,768]{2,1,0:T(8,128)(2,1)} %refs_1_.5) | copy-start | bytes 4718596
  8.0 13.0 %copy-start.7 = (bf16[3,768,192]{1,2,0:T(8,128)(2,1)S(1)}, bf16[3,768,192]{1,2,0:T(8,128)(2,1)}, u32[]{:S(2)}) copy-start(bf16[3,768,192]{1,2,0:T(8,128)(2,1)} %param.20) | copy-start | bytes 2654212
  8.0 13.0 %copy-start.14 = (bf16[2,768,192]{1,2,0:T(8,128)(2,1)S(1)}, bf16[2,768,192]{1,2,0:T(8,128)(2,1)}, u32[]{:S(2)}) copy-start(bf16[2,768,192]{1,2,0:T(8,128)(2,1)} %param.21) | copy-start | bytes 1769476
  8.0 13.0 %copy-start.16 = (s32[2]{0:T(128)S(1)}, s32[2]{0:T(128)}, u32[]{:S(2)}) copy-start(s32[2]{0:T(128)} %lengths_ref.3) | copy-start | bytes 28
  8.1 8.0 %collective-permute-start.1 = (f32[24,768]{1,0:T(8,128)S(1)}, f32[24,768]{1,0:T(8,128)S(1)}, u32[]{:S(2)}, u32[]{:S(2)}) collective-permute-start(f32[24,768]{1,0:T(8,128)S(1)} %dynamic-slice_convert_fusion), channel_id=1, source_target_pairs={{0,2},{1,3},{2,0},{3,1},{4,6},{5,7},{6,4},{7,5},{8,10},{9,11},{10,... | collective-permute-start | bytes 221192 | tf_op jit(solution)/shard_map/ppermute | solution.py:626
  16.8 79.9 %all-gather.7.cloned.1.call-start = ((), (), s32[]{:S(2)}) async-start(), calls=%async_computation.2 | async-start | bytes 5529600 | tf_op jit(solution)/shard_map/all_gather | solution.py:637
  19.6 27.6 %collective-permute-start.3 = (f32[200,768]{1,0:T(8,128)}, f32[200,768]{1,0:T(8,128)}, u32[]{:S(2)}, u32[]{:S(2)}) collective-permute-start(f32[200,768]{1,0:T(8,128)} %maximum_maximum_fusion), channel_id=1, source_target_pairs={{0,2},{1,3},{2,0},{3,1},{4,6},{5,7},{6,4},{7,5},{8,10},{9,11},{10,... | collective-permute-start | bytes 1843208 | tf_op jit(solution)/shard_map/ppermute | solution.py:626
  34.7 22.9 %copy-start.13 = (bf16[192,512]{1,0:T(8,128)(2,1)}, bf16[192,512]{1,0:T(8,128)(2,1)S(1)}, u32[]{:S(2)}) copy-start(bf16[192,512]{1,0:T(8,128)(2,1)S(1)} %get-tuple-element.70.mixed_ref) | copy-start | bytes 589828
  47.2 164.7 %all-gather.9.cloned.1.call-start = ((), (), s32[]{:S(2)}) async-start(), calls=%async_computation.3 | async-start | bytes 3317760 | tf_op jit(solution)/shard_map/all_gather | solution.py:637
  47.2 9.0 %collective-permute-start = (f32[192,512]{1,0:T(8,128)}, f32[192,512]{1,0:T(8,128)S(1)}, u32[]{:S(2)}, u32[]{:S(2)}) collective-permute-start(f32[192,512]{1,0:T(8,128)} %copy-done.17), channel_id=1, source_target_pairs={{0,2},{1,3},{2,0},{3,1},{4,6},{5,7},{6,4},{7,5},{8,10},{9,11},{10,... | collective-permute-start | bytes 1179656 | tf_op jit(solution)/shard_map/ppermute | solution.py:626
  57.5 42.0 %copy-start.27 = (bf16[8,24,768]{2,1,0:T(8,128)(2,1)}, bf16[8,24,768]{2,1,0:T(8,128)(2,1)S(1)}, u32[]{:S(2)}) copy-start(bf16[8,24,768]{2,1,0:T(8,128)(2,1)S(1)} %fusion.2) | copy-start | bytes 884740
  57.5 29.7 %copy-start.36 = (f32[768]{0:T(1024)S(1)}, f32[768]{0:T(1024)}, u32[]{:S(2)}) copy-start(f32[768]{0:T(1024)} %param.24) | copy-start | bytes 9220
  57.5 29.7 %copy-start.37 = (f32[768]{0:T(1024)S(1)}, f32[768]{0:T(1024)}, u32[]{:S(2)}) copy-start(f32[768]{0:T(1024)} %param.25) | copy-start | bytes 9220
  57.5 29.7 %copy-start.38 = (f32[768]{0:T(1024)S(1)}, f32[768]{0:T(1024)}, u32[]{:S(2)}) copy-start(f32[768]{0:T(1024)} %param.23) | copy-start | bytes 9220
  58.2 41.3 %copy-start.21 = (f32[512,768]{1,0:T(8,128)}, f32[512,768]{1,0:T(8,128)S(1)}, u32[]{:S(2)}) copy-start(f32[512,768]{1,0:T(8,128)S(1)} %fusion.3.refs_2_) | copy-start | bytes 4718596
  58.2 15.5 %collective-permute-start.9 = (f32[5,24,768]{2,1,0:T(8,128)S(1)}, f32[5,24,768]{2,1,0:T(8,128)S(1)}, u32[]{:S(2)}, u32[]{:S(2)}) collective-permute-start(f32[5,24,768]{2,1,0:T(8,128)S(1)} %copy-done.35), channel_id=1, source_target_pairs={{0,2},{1,3},{2,0},{3,1},{4,6},{5,7},{6,4},{7,5},{8,10},{9,11},{10,... | collective-permute-start | bytes 1105928 | tf_op jit(solution)/shard_map/ppermute | solution.py:626
  74.4 186.6 %reduce-scatter.2.cloned.1.call-start = ((), (), s32[]{:S(2)}) async-start(), calls=%async_computation.4 | async-start | bytes 10616832 | tf_op jit(solution)/shard_map/reduce_scatter | solution.py:715
  74.7 45.9 %collective-permute-start.2 = (f32[512,768]{1,0:T(8,128)S(1)}, f32[512,768]{1,0:T(8,128)}, u32[]{:S(2)}, u32[]{:S(2)}) collective-permute-start(f32[512,768]{1,0:T(8,128)S(1)} %fusion.3.refs_2_), channel_id=1, source_target_pairs={{0,1},{1,0},{2,3},{3,2},{4,5},{5,4},{6,7},{7,6},{8,9},{9,8},{10,11... | collective-permute-start | bytes 4718600 | tf_op jit(solution)/shard_map/ppermute | solution.py:626
  87.2 72.9 %copy-start.15 = (f32[1,768]{1,0:T(1,128)}, f32[1,768]{1,0:T(1,128)S(1)}, u32[]{:S(2)}) copy-start(f32[1,768]{1,0:T(1,128)S(1)} %reshape.107.refs_5_.refs_6_.gain_ref) | copy-start | bytes 9220
  99.5 21.1 %copy-start = (bf16[768,768]{1,0:T(8,128)(2,1)S(1)}, bf16[768,768]{1,0:T(8,128)(2,1)}, u32[]{:S(2)}) copy-start(bf16[768,768]{1,0:T(8,128)(2,1)} %refs_11_.3) | copy-start | bytes 3538948
  99.5 21.0 %copy-start.1 = (bf16[768,768]{1,0:T(8,128)(2,1)S(1)}, bf16[768,768]{1,0:T(8,128)(2,1)}, u32[]{:S(2)}) copy-start(bf16[768,768]{1,0:T(8,128)(2,1)} %refs_13_.3) | copy-start | bytes 3538948
  125.7 20.5 %collective-permute-start.5 = (f32[256,768]{1,0:T(8,128)S(1)}, f32[256,768]{1,0:T(8,128)S(1)}, u32[]{:S(2)}, u32[]{:S(2)}) collective-permute-start(f32[256,768]{1,0:T(8,128)S(1)} %get-tuple-element.81.refs_2_), channel_id=1, source_target_pairs={{0,1},{1,0},{2,3},{3,2},{4,5},{5,4},{6,7},{7,6},{8,9},{9,8},{10,11... | collective-permute-start | bytes 2359304 | tf_op jit(solution)/shard_map/ppermute | solution.py:626
  132.9 19.6 %copy-start.8 = (f32[512,1]{1,0:T(8,128)}, f32[512,1]{1,0:T(8,128)S(1)}, u32[]{:S(2)}) copy-start(f32[512,1]{1,0:T(8,128)S(1)} %get-tuple-element.91.scale_ref) | copy-start | bytes 6148
  132.9 27.2 %collective-permute-start.4 = (f32[256,768]{1,0:T(8,128)S(1)}, f32[256,768]{1,0:T(8,128)S(1)}, u32[]{:S(2)}, u32[]{:S(2)}) collective-permute-start(f32[256,768]{1,0:T(8,128)S(1)} %get-tuple-element.78.refs_2_), channel_id=1, source_target_pairs={{0,1},{1,0},{2,3},{3,2},{4,5},{5,4},{6,7},{7,6},{8,9},{9,8},{10,11... | collective-permute-start | bytes 2359304 | tf_op jit(solution)/shard_map/ppermute | solution.py:626
  173.0 207.4 %all-gather.11.cloned.1.call-start = ((), (), s32[]{:S(2)}) async-start(), calls=%async_computation.5 | async-start | bytes 5308416 | tf_op jit(solution)/shard_map/all_gather | solution.py:637
  173.3 33.8 %collective-permute-start.6 = (f32[512,768]{1,0:T(8,128)}, f32[512,768]{1,0:T(8,128)}, u32[]{:S(2)}, u32[]{:S(2)}) collective-permute-start(f32[512,768]{1,0:T(8,128)} %get-tuple-element.88.part_ref), channel_id=1, source_target_pairs={{0,1},{1,0},{2,3},{3,2},{4,5},{5,4},{6,7},{7,6},{8,9},{9,8},{10,11... | collective-permute-start | bytes 4718600 | tf_op jit(solution)/shard_map/ppermute | solution.py:626
  207.1 33.7 %collective-permute-start.7 = (f32[256,768]{1,0:T(8,128)S(1)}, f32[256,768]{1,0:T(8,128)S(1)}, u32[]{:S(2)}, u32[]{:S(2)}) collective-permute-start(f32[256,768]{1,0:T(8,128)S(1)} %get-tuple-element.89.refs_0_), channel_id=1, source_target_pairs={{0,2},{1,3},{2,0},{3,1},{4,6},{5,7},{6,4},{7,5},{8,10},{9,11},{10,... | collective-permute-start | bytes 2359304 | tf_op jit(solution)/shard_map/ppermute | solution.py:626
  240.7 6.7 %collective-permute-start.10 = (f32[4,304,768]{2,1,0:T(8,128)}, f32[4,304,768]{2,1,0:T(8,128)S(1)}, u32[]{:S(2)}, u32[]{:S(2)}) collective-permute-start(f32[4,304,768]{2,1,0:T(8,128)} %get-tuple-element.101), channel_id=1, source_target_pairs={{0,4},{4,0},{8,12},{12,8},{16,20},{20,16},{24,28},{28,24},{1,5},{5... | collective-permute-start | bytes 11206664 | tf_op jit(solution)/shard_map/ppermute | solution.py:630
  240.7 20.2 %collective-permute-start.14 = (f32[256,768]{1,0:T(8,128)}, f32[256,768]{1,0:T(8,128)S(1)}, u32[]{:S(2)}, u32[]{:S(2)}) collective-permute-start(f32[256,768]{1,0:T(8,128)} %get-tuple-element.106), channel_id=1, source_target_pairs={{0,1},{1,0},{2,3},{3,2},{4,5},{5,4},{6,7},{7,6},{8,9},{9,8},{10,11... | collective-permute-start | bytes 2359304 | tf_op jit(solution)/shard_map/ppermute | solution.py:626
  254.2 23.0 %collective-permute-start.11 = (f32[2,152,768]{2,1,0:T(8,128)}, f32[2,152,768]{2,1,0:T(8,128)}, u32[]{:S(2)}, u32[]{:S(2)}) collective-permute-start(f32[2,152,768]{2,1,0:T(8,128)} %slice.133), channel_id=1, source_target_pairs={{0,16},{4,20},{8,24},{12,28},{16,0},{20,4},{24,8},{28,12},{1,17},{... | collective-permute-start | bytes 2801672 | tf_op jit(solution)/shard_map/ppermute | solution.py:630
  255.8 24.1 %collective-permute-start.12 = (f32[2,152,768]{2,1,0:T(8,128)}, f32[2,152,768]{2,1,0:T(8,128)}, u32[]{:S(2)}, u32[]{:S(2)}) collective-permute-start(f32[2,152,768]{2,1,0:T(8,128)} %slice_bitcast_fusion.1), channel_id=1, source_target_pairs={{0,8},{4,12},{8,0},{12,4},{16,24},{20,28},{24,16},{28,20},{1,9},{5... | collective-permute-start | bytes 2801672 | tf_op jit(solution)/shard_map/ppermute | solution.py:630
  262.2 17.7 %copy-start.23 = (f32[4,152,768]{2,1,0:T(8,128)S(1)}, f32[4,152,768]{2,1,0:T(8,128)}, u32[]{:S(2)}) copy-start(f32[4,152,768]{2,1,0:T(8,128)} %copy-done.22) | copy-start | bytes 5603332
  262.2 62.4 %collective-permute-start.15 = (f32[448,768]{1,0:T(8,128)S(1)}, f32[448,768]{1,0:T(8,128)S(1)}, u32[]{:S(2)}, u32[]{:S(2)}) collective-permute-start(f32[448,768]{1,0:T(8,128)S(1)} %pad_maximum_fusion.1), channel_id=1, source_target_pairs={{0,2},{1,3},{2,0},{3,1},{4,6},{5,7},{6,4},{7,5},{8,10},{9,11},{10,... | collective-permute-start | bytes 4128776 | tf_op jit(solution)/shard_map/ppermute | solution.py:626
  264.1 46.5 %collective-permute-start.8 = (f32[256,768]{1,0:T(8,128)S(1)}, f32[256,768]{1,0:T(8,128)S(1)}, u32[]{:S(2)}, u32[]{:S(2)}) collective-permute-start(f32[256,768]{1,0:T(8,128)S(1)} %collective-permute-done.7.refs_1_), channel_id=1, source_target_pairs={{0,1},{1,0},{2,3},{3,2},{4,5},{5,4},{6,7},{7,6},{8,9},{9,8},{10,11... | collective-permute-start | bytes 2359304 | tf_op jit(solution)/shard_map/ppermute | solution.py:626
  279.9 45.8 %copy-start.28 = (f32[384,768]{1,0:T(8,128)S(1)}, f32[384,768]{1,0:T(8,128)}, u32[]{:S(2)}) copy-start(f32[384,768]{1,0:T(8,128)} %reduce-scatter.2.cloned.1.call-done) | copy-start | bytes 3538948
  281.3 29.3 %copy-start.24 = (f32[1,2,152,768]{3,2,1,0:T(8,128)}, f32[1,2,152,768]{3,2,1,0:T(8,128)S(1)}, u32[]{:S(2)}) copy-start(f32[1,2,152,768]{3,2,1,0:T(8,128)S(1)} %fusion.1) | copy-start | bytes 2801668
  311.5 15.1 %collective-permute-start.13 = (f32[1,152,768]{2,1,0:T(8,128)}, f32[1,152,768]{2,1,0:T(8,128)}, u32[]{:S(2)}, u32[]{:S(2)}) collective-permute-start(f32[1,152,768]{2,1,0:T(8,128)} %slice.137), channel_id=1, source_target_pairs={{0,8},{4,12},{8,0},{12,4},{16,24},{20,28},{24,16},{28,20},{1,9},{5... | collective-permute-start | bytes 1400840 | tf_op jit(solution)/shard_map/ppermute | solution.py:630
  313.0 13.6 %collective-permute-start.18 = (f32[1,152,768]{2,1,0:T(8,128)}, f32[1,152,768]{2,1,0:T(8,128)}, u32[]{:S(2)}, u32[]{:S(2)}) collective-permute-start(f32[1,152,768]{2,1,0:T(8,128)} %slice_bitcast_fusion.3), channel_id=1, source_target_pairs={{0,16},{4,20},{8,24},{12,28},{16,0},{20,4},{24,8},{28,12},{1,17},{... | collective-permute-start | bytes 1400840 | tf_op jit(solution)/shard_map/ppermute | solution.py:630
  327.9 23.2 %collective-permute-start.16 = (f32[152,768]{1,0:T(8,128)S(1)}, f32[152,768]{1,0:T(8,128)S(1)}, u32[]{:S(2)}, u32[]{:S(2)}) collective-permute-start(f32[152,768]{1,0:T(8,128)S(1)} %fusion.10), channel_id=1, source_target_pairs={{0,2},{1,3},{2,0},{3,1},{4,6},{5,7},{6,4},{7,5},{8,10},{9,11},{10,... | collective-permute-start | bytes 1400840 | tf_op jit(solution)/shard_map/ppermute | solution.py:626
  328.7 22.4 %copy-start.25 = (f32[1,2,152,768]{3,2,1,0:T(8,128)S(1)}, f32[1,2,152,768]{3,2,1,0:T(8,128)}, u32[]{:S(2)}) copy-start(f32[1,2,152,768]{3,2,1,0:T(8,128)} %copy-done.24) | copy-start | bytes 2801668
  351.2 36.0 %collective-permute-start.17 = (f32[2,256,768]{2,1,0:T(8,128)}, f32[2,256,768]{2,1,0:T(8,128)}, u32[]{:S(2)}, u32[]{:S(2)}) collective-permute-start(f32[2,256,768]{2,1,0:T(8,128)} %pad_maximum_fusion), channel_id=1, source_target_pairs={{0,1},{1,0},{2,3},{3,2},{4,5},{5,4},{6,7},{7,6},{8,9},{9,8},{10,11... | collective-permute-start | bytes 4718600 | tf_op jit(solution)/shard_map/ppermute | solution.py:626
  352.3 12.7 %collective-permute-start.19 = (f32[1,72,768]{2,1,0:T(8,128)S(1)}, f32[1,72,768]{2,1,0:T(8,128)S(1)}, u32[]{:S(2)}, u32[]{:S(2)}) collective-permute-start(f32[1,72,768]{2,1,0:T(8,128)S(1)} %slice_bitcast_fusion.5), channel_id=1, source_target_pairs={{0,8},{4,12},{8,0},{12,4},{16,24},{20,28},{24,16},{28,20},{1,9},{5... | collective-permute-start | bytes 663560 | tf_op jit(solution)/shard_map/ppermute | solution.py:630
  354.3 13.6 %collective-permute-start.20 = (f32[1,80,768]{2,1,0:T(8,128)S(1)}, f32[1,80,768]{2,1,0:T(8,128)S(1)}, u32[]{:S(2)}, u32[]{:S(2)}) collective-permute-start(f32[1,80,768]{2,1,0:T(8,128)S(1)} %slice_bitcast_fusion.4), channel_id=1, source_target_pairs={{0,16},{4,20},{8,24},{12,28},{16,0},{20,4},{24,8},{28,12},{1,17},{... | collective-permute-start | bytes 737288 | tf_op jit(solution)/shard_map/ppermute | solution.py:630
  368.0 11.2 %collective-permute-start.21 = (f32[2,72,768]{2,1,0:T(8,128)S(1)}, f32[2,72,768]{2,1,0:T(8,128)S(1)}, u32[]{:S(2)}, u32[]{:S(2)}) collective-permute-start(f32[2,72,768]{2,1,0:T(8,128)S(1)} %pad_maximum_fusion.5), channel_id=1, source_target_pairs={{0,16},{4,20},{8,24},{12,28},{16,0},{20,4},{24,8},{28,12},{1,17},{... | collective-permute-start | bytes 1327112 | tf_op jit(solution)/shard_map/ppermute | solution.py:630
  369.1 11.3 %collective-permute-start.22 = (f32[2,80,768]{2,1,0:T(8,128)S(1)}, f32[2,80,768]{2,1,0:T(8,128)S(1)}, u32[]{:S(2)}, u32[]{:S(2)}) collective-permute-start(f32[2,80,768]{2,1,0:T(8,128)S(1)} %pad_maximum_fusion.4), channel_id=1, source_target_pairs={{0,8},{4,12},{8,0},{12,4},{16,24},{20,28},{24,16},{28,20},{1,9},{5... | collective-permute-start | bytes 1474568 | tf_op jit(solution)/shard_map/ppermute | solution.py:630
  387.2 4.2 %collective-permute-start.24 = (f32[4,80,768]{2,1,0:T(8,128)S(1)}, f32[4,80,768]{2,1,0:T(8,128)S(1)}, u32[]{:S(2)}, u32[]{:S(2)}) collective-permute-start(f32[4,80,768]{2,1,0:T(8,128)S(1)} %pad_maximum_fusion.2.low_b_ref), channel_id=1, source_target_pairs={{0,4},{4,0},{8,12},{12,8},{16,20},{20,16},{24,28},{28,24},{1,5},{5... | collective-permute-start | bytes 2949128 | tf_op jit(solution)/shard_map/ppermute | solution.py:630
  387.2 4.2 %collective-permute-start.23 = (f32[4,72,768]{2,1,0:T(8,128)S(1)}, f32[4,72,768]{2,1,0:T(8,128)S(1)}, u32[]{:S(2)}, u32[]{:S(2)}) collective-permute-start(f32[4,72,768]{2,1,0:T(8,128)S(1)} %pad_maximum_fusion.3.low_a_ref), channel_id=1, source_target_pairs={{0,4},{4,0},{8,12},{12,8},{16,20},{20,16},{24,28},{28,24},{1,5},{5... | collective-permute-start | bytes 2654216 | tf_op jit(solution)/shard_map/ppermute | solution.py:630
  (25 other events, 81.3 us)
Sparse Core Ops, SparseCore 0:
  16.9 25.2 all-gather.4
  47.3 49.3 all-gather.6
  99.2 31.4 all-gather.8
  173.1 77.5 reduce-scatter.1
  326.7 44.9 all-gather.10
